TPU v7x, 32 devices: a whole 2x2x4 slice. The times are simulated.
32 devices in a mesh: groups: 2 (over x), tile: 8 (over z, y), section: 2 (over core).
Axes of the slice: x: 2, y: 2, z: 4, core: 2. Of those that a mesh axis runs over, the one named last changes fastest.
Arguments:
- frames: bfloat16 [2, 128, 8192], P(None, ('groups', 'tile', 'section')), parts along dimension 1, may hold values from -6 to 6
- start_fine: bfloat16 [128, 32768], P(('groups', 'tile', 'section')), parts along dimension 0, may hold values from -0.8984375 to 0.8984375
- start_coarse: bfloat16 [64, 49152], P(('groups', 'tile', 'section')), parts along dimension 0, may hold values from -0.8984375 to 0.8984375
- enc_stem: bfloat16 [16, 64], replicated, may hold values from -1.5 to 1.5
- enc_fine_x: bfloat16 [3, 3, 64, 192], replicated, may hold values from -0.25 to 0.25
- enc_fine_h: bfloat16 [3, 3, 64, 192], replicated, may hold values from -0.25 to 0.25
- enc_down: bfloat16 [3, 3, 64, 192], replicated, may hold values from -0.25 to 0.25
- enc_coarse_x: bfloat16 [3, 3, 192, 576], replicated, may hold values from -0.15625 to 0.15625
- enc_coarse_h: bfloat16 [3, 3, 192, 576], replicated, may hold values from -0.15625 to 0.15625
- fc_coarse_h: bfloat16 [3, 3, 192, 576], replicated, may hold values from -0.15625 to 0.15625
- fc_up: bfloat16 [3, 3, 192, 64], replicated, may hold values from -0.25 to 0.25
- fc_fine_x: bfloat16 [3, 3, 64, 192], replicated, may hold values from -0.25 to 0.25
- fc_fine_h: bfloat16 [3, 3, 64, 192], replicated, may hold values from -0.25 to 0.25
- fc_head: bfloat16 [64, 16], replicated, may hold values from -0.75 to 0.75
Outputs:
- forecast: bfloat16 [2, 128, 8192], P(None, ('groups', 'tile', 'section')), parts along dimension 1
There are 2 independent parts, one for each index of `groups`. A program takes and returns all parts, laid end to end along the dimension named above; an argument that names none is the same for every part. Nothing has to cross between parts.
All inputs are finite; a program needn't handle non-finite values.
Results may differ from a plain program's by a relative error of at most 0.007.
Values may be sent and summed in bfloat16 or wider, within the bound.
No kernel may reach another device: no remote copies, remote signals or barrier semaphores. Data moves between devices by JAX's collectives and lax.ppermute only.
A program may use at most 64 MiB of HBM per device.

v0:
```python
import jax
import jax.numpy as jnp
from jax import lax
from jax.experimental import pallas as pl
from jax.experimental.pallas import tpu as pltpu
from jax.sharding import PartitionSpec as P

C1 = 64
C2 = 192
PATCH = 16
FRAMES = 2
HORIZON = 2
COLS = 512
SUB = 16
FB = COLS // SUB
CB = COLS // 2 // SUB
LANES = 128
BF = jnp.bfloat16
F32 = jnp.float32
LINE = ("tile", "section")


def leaky(values):
    return jnp.where(values > 0, values, 0.2 * values)


def low_half(shape):
    return lax.broadcasted_iota(jnp.int32, shape, len(shape) - 1) < 64


def swap_halves(x):
    flat = x.reshape(-1, LANES)
    return pltpu.roll(flat, 64, 1).reshape(x.shape)


def swap_bf(x):
    return swap_halves(x.astype(F32)).astype(BF)


def sigmoid(x):
    return 0.5 * jnp.tanh(0.5 * x) + 0.5


def shift_sub(x, by):
    wide = x.astype(F32)
    row = lax.broadcasted_iota(jnp.int32, wide.shape, 0)
    if by > 0:
        moved = jnp.where(row == 0, 0.0, pltpu.roll(wide, 1, 0))
    else:
        moved = jnp.where(row == SUB - 1, 0.0, pltpu.roll(wide, SUB - 1, 0))
    return moved.astype(BF)


def seal(ref, idx, blocks):
    ref[idx, 0] = shift_sub(ref[idx, blocks], 1)
    ref[idx, blocks + 1] = shift_sub(ref[idx, 1], -1)


def fine_patches(ref, idx, lo, count):
    parts = [
        ref[idx + dr, pl.ds(lo + dj, count)].reshape(count * SUB, LANES)
        for dr in (-1, 0, 1)
        for dj in (0, 1, 2)
    ]
    return jnp.concatenate(parts, axis=-1)


def fine_gru(src, idx, weight, valid, emit):
    count = 16
    for lo in range(0, FB, count):
        acc = jnp.dot(fine_patches(src, idx, lo, count), weight[...], preferred_element_type=F32)
        gates = sigmoid(acc[:, :LANES])
        cand = acc[:, LANES:]
        cand = jnp.tanh(cand + swap_halves(gates * cand))
        old = src[idx, pl.ds(1 + lo, count)].reshape(count * SUB, LANES).astype(F32)
        new = (1.0 - gates) * cand + gates * old
        new = jnp.where(valid, new, 0.0).astype(BF)
        emit(lo, count, new.reshape(count, SUB, LANES))


def down_row(src, idx, weight):
    parts = []
    for dr in (-1, 0, 1):
        row = src[idx + dr].reshape(FB // 2 + 1, 2, SUB, LANES)
        for tap in (row[:CB, 0], row[:CB, 1], row[1:, 0]):
            parts.append(tap.reshape(CB * SUB, LANES))
    lhs = jnp.concatenate(parts, axis=-1)
    return jnp.dot(lhs, weight[...], preferred_element_type=F32)


def coarse_forms(t0, t1):
    lo = low_half(t0.shape)
    r0, r1 = swap_halves(t0), swap_halves(t1)
    return (
        t0.astype(BF),
        jnp.where(lo, t1, 0.0).astype(BF),
        jnp.where(lo, 0.0, r0).astype(BF),
        jnp.where(lo, r0, r1).astype(BF),
    )


def put_forms(ref, idx, forms):
    for k, tile in enumerate(forms):
        ref[idx, 1 : CB + 1, :, k * LANES : (k + 1) * LANES] = tile.reshape(CB, SUB, LANES)
    seal(ref, idx, CB)


def put_packed(ref, idx, tiles):
    t = [tiles(i).astype(F32) for i in range(3)]
    r = [swap_halves(x) for x in t]
    lo = low_half(t[0].shape)
    even = (t[0], jnp.where(lo, t[1], 0.0), jnp.where(lo, 0.0, r[0]), jnp.where(lo, r[0], r[1]))
    odd = (
        jnp.where(lo, r[1], r[2]),
        jnp.where(lo, r[2], 0.0),
        jnp.where(lo, 0.0, t[1]),
        t[2],
    )
    for k in range(4):
        both = jnp.stack([even[k].astype(BF), odd[k].astype(BF)], axis=1)
        ref[idx, 1 : CB + 1, :, k * LANES : (k + 1) * LANES] = both.reshape(CB, SUB, LANES)
    seal(ref, idx, CB)


def pack_forms(forms):
    f = [x.reshape(CB // 2, 2, SUB, LANES) for x in forms]
    lo = low_half((CB // 2, SUB, LANES))
    return (f[0][:, 0], jnp.where(lo, f[1][:, 0], f[2][:, 1]), f[3][:, 1])


def coarse_patches(ref, idx):
    def tile(dr, dj, k):
        return ref[idx + dr, dj : dj + CB, :, k * LANES : (k + 1) * LANES].reshape(CB * SUB, LANES)

    lo = low_half((CB * SUB, LANES))

    def aligned(dr):
        return [
            tile(dr, 0, 0),
            jnp.where(lo, tile(dr, 0, 1), tile(dr, 1, 2)),
            tile(dr, 1, 3),
            tile(dr, 2, 0),
        ]

    parts = aligned(-1)
    parts.append(jnp.where(lo, tile(-1, 2, 1), tile(0, 0, 2)))
    parts += [tile(0, 0, 3), tile(0, 1, 0), jnp.where(lo, tile(0, 1, 1), tile(0, 2, 2)), tile(0, 2, 3)]
    parts += aligned(1)
    parts.append(tile(1, 2, 1))
    return jnp.concatenate(parts, axis=-1)[:, : 9 * C2]


def coarse_gru(x_ref, x_idx, h_ref, h_idx, w_x, w_h, acc_x, acc_h, valid):
    width = 3 * C2
    acc_h[:, :width] = jnp.dot(coarse_patches(h_ref, h_idx), w_h[...], preferred_element_type=F32)
    if x_ref is not None:
        acc_x[:, :width] = jnp.dot(coarse_patches(x_ref, x_idx), w_x[...], preferred_element_type=F32)

    def part(ref, k):
        return ref[:, k * LANES : (k + 1) * LANES]

    gates = []
    for k in range(3):
        mixed = part(acc_h, k)
        if x_ref is not None:
            mixed = part(acc_x, k) + mixed
        gates.append(sigmoid(mixed))
    lo = low_half(gates[0].shape)
    g1, g2 = swap_halves(gates[1]), swap_halves(gates[2])
    update = (jnp.where(lo, g1, g2), g2)
    out = []
    for k in range(2):
        cand = gates[k] * part(acc_h, 3 + k)
        if x_ref is not None:
            cand = part(acc_x, 3 + k) + cand
        cand = jnp.tanh(cand)
        old = h_ref[h_idx, 1 : CB + 1, :, k * LANES : (k + 1) * LANES].reshape(CB * SUB, LANES).astype(F32)
        new = (1.0 - update[k]) * cand + update[k] * old
        out.append(jnp.where(valid, new, 0.0).astype(BF).astype(F32))
    return coarse_forms(out[0], out[1])


def in_grid(row, rows):
    return jnp.logical_and(row >= 0, row < rows)


def fine_encoder_body(
    where_ref, own, outer, inner, fr_own, fr_outer, fr_inner, w_stem, w_gru, w_down,
    state_out, low_own, low_outer, low_inner, p1, p2, p3, stem2,
):
    upper = where_ref[0] == 0
    first = where_ref[1] * 4
    rows = where_ref[2] * 4
    lo = low_half((1, SUB, LANES))

    def pick(own_ref, outer_ref, inner_ref, idx, lanes, frame=None):
        def at(ref, r):
            return ref[r, :, lanes] if frame is None else ref[frame, r, :, lanes]

        if 3 <= idx < 7:
            return at(own_ref, idx - 3)
        r = idx + 1 if idx < 3 else idx - 7
        a, b = at(outer_ref, r), at(inner_ref, r)
        return jnp.where(upper, a, b) if idx < 3 else jnp.where(upper, b, a)

    for frame in range(FRAMES):
        for t in range(4):
            lanes = slice(t * LANES, (t + 1) * LANES)
            patches = jnp.concatenate(
                [pick(fr_own, fr_outer, fr_inner, idx, lanes, frame) for idx in range(9)], axis=0
            )
            for half in range(2):
                acc = jnp.dot(patches, w_stem[:, half * 512 : half * 512 + 512], preferred_element_type=F32)
                acc = leaky(acc).astype(BF)
                for k in range(4):
                    block = acc[:, k * LANES : (k + 1) * LANES].reshape(9, SUB, LANES)
                    at = 8 * t + 4 * half + k
                    if frame == 0:
                        p1[:, 1 + at] = block
                    else:
                        stem2[:, at] = block
    for idx in range(9):
        for k in range(FB // 2):
            pair = pick(own, outer, inner, idx, slice(k * LANES, (k + 1) * LANES))
            p1[idx, 1 + 2 * k] = jnp.where(lo[0], p1[idx, 1 + 2 * k], swap_bf(pair))
            p1[idx, 2 + 2 * k] = jnp.where(lo[0], p1[idx, 2 + 2 * k], pair)
        seal(p1, idx, FB)

    @pl.loop(1, 8)
    def _(idx):
        def emit(lo_block, count, new):
            stems = stem2[idx, pl.ds(lo_block, count)]
            p2[idx, pl.ds(1 + lo_block, count)] = jnp.where(lo, stems, new)

        fine_gru(p1, idx, w_gru, in_grid(first + idx - 3, rows), emit)
        seal(p2, idx, FB)

    @pl.loop(2, 7)
    def _(idx):
        def emit(lo_block, count, new):
            p3[idx, pl.ds(1 + lo_block, count)] = jnp.where(lo, jnp.zeros_like(new), new)

        fine_gru(p2, idx, w_gru, in_grid(first + idx - 3, rows), emit)
        seal(p3, idx, FB)

    def lowered(src, p):
        acc = leaky(down_row(src, 3 + 2 * p, w_down)).astype(BF).astype(F32)
        return pack_forms(coarse_forms(acc[:, :LANES], acc[:, LANES:]))

    def put(ref, at, tiles):
        for k, tile in enumerate(tiles):
            ref[at, :, :, k * LANES : (k + 1) * LANES] = tile

    for p in range(2):
        tiles = lowered(p2, p)
        put(low_own, p, tiles)
        put(low_outer, p, tiles)
        put(low_inner, p, tiles)
    for p in range(2):
        tiles = lowered(p3, p)
        put(low_own, 2 + p, tiles)
        to_outer = upper if p == 0 else jnp.logical_not(upper)

        @pl.when(to_outer)
        def _():
            put(low_outer, 2, tiles)

        @pl.when(jnp.logical_not(to_outer))
        def _():
            put(low_inner, 2, tiles)

    for r in range(4):
        for k in range(FB // 2):
            state_out[r, k] = jnp.where(lo[0], swap_bf(p3[3 + r, 1 + 2 * k]), p3[3 + r, 2 + 2 * k])


def zero_tail(acc):
    acc[:, 4 * LANES :] = jnp.zeros((CB * SUB, LANES), F32)


def packed_tiles(ref, at):
    return lambda i: ref[at, :, :, i * LANES : (i + 1) * LANES]


def coarse_encoder_body(
    where_ref, own, outer, inner, low_own, low_outer, low_inner, w_x, w_h,
    state_out, x1, x2, h0, h1, acc_x, acc_h,
):
    upper = where_ref[0] == 0
    first = where_ref[1] * 2
    rows = where_ref[2] * 2
    zero_tail(acc_x)
    zero_tail(acc_h)

    def raw_tiles(get):
        def tiles(i):
            return jnp.stack([get(slice((3 * k + i) * LANES, (3 * k + i + 1) * LANES)) for k in range(CB // 2)])

        return tiles

    for idx in range(6):
        if 2 <= idx < 4:
            put_packed(h0, idx, raw_tiles(lambda lanes: own[idx - 2, :, lanes]))
            put_packed(x1, idx, packed_tiles(low_own, idx - 2))
            continue
        r = idx if idx < 2 else idx - 4
        first_ref, second_ref = (outer, inner) if idx < 2 else (inner, outer)
        put_packed(
            h0, idx, raw_tiles(lambda lanes: jnp.where(upper, first_ref[r, :, lanes], second_ref[r, :, lanes]))
        )
        low_a, low_b = (low_outer, low_inner) if idx < 2 else (low_inner, low_outer)
        put_packed(x1, idx, lambda i: jnp.where(upper, packed_tiles(low_a, r)(i), packed_tiles(low_b, r)(i)))
    put_packed(x2, 1, packed_tiles(low_own, 2))
    put_packed(x2, 2, packed_tiles(low_own, 3))
    put_packed(x2, 0, lambda i: jnp.where(upper, packed_tiles(low_outer, 2)(i), packed_tiles(low_inner, 2)(i)))
    put_packed(x2, 3, lambda i: jnp.where(upper, packed_tiles(low_inner, 2)(i), packed_tiles(low_outer, 2)(i)))

    @pl.loop(0, 4)
    def _(idx):
        forms = coarse_gru(x1, idx + 1, h0, idx + 1, w_x, w_h, acc_x, acc_h, in_grid(first + idx - 1, rows))
        put_forms(h1, idx, forms)

    @pl.loop(0, 2)
    def _(idx):
        forms = coarse_gru(x2, idx + 1, h1, idx + 1, w_x, w_h, acc_x, acc_h, in_grid(first + idx, rows))
        for k, tile in enumerate(pack_forms(forms)):
            state_out[idx, :, :, k * LANES : (k + 1) * LANES] = tile


def raise_pair(src, idx, weight):
    def tile(dr, dj, k):
        return src[idx + dr, 1 + dj : 1 + dj + CB, :, k * LANES : (k + 1) * LANES].reshape(CB * SUB, LANES)

    lo = low_half((CB * SUB, LANES))
    parts = []
    for dr in (0, 1):
        parts += [tile(dr, 0, 0), jnp.where(lo, tile(dr, 0, 1), tile(dr, 1, 2)), tile(dr, 1, 3)]
    return jnp.dot(jnp.concatenate(parts, axis=-1), weight[...], preferred_element_type=F32)


def forecaster_body(
    where_ref, c_own, c_outer, c_inner, c_third, f_own, f_outer, f_inner, w_h, w_up, w_gru, w_head,
    out, h2, s1, s2, pf1, pf2, states, acc_h,
):
    upper = where_ref[0] == 0
    first_c = where_ref[1] * 2
    rows_c = where_ref[2] * 2
    first_f = where_ref[1] * 4
    rows_f = where_ref[2] * 4
    lo = low_half((1, SUB, LANES))
    zero_tail(acc_h)

    put_packed(h2, 3, packed_tiles(c_own, 0))
    put_packed(h2, 4, packed_tiles(c_own, 1))

    def either(a, b):
        return lambda i: jnp.where(upper, a(i), b(i))

    put_packed(h2, 0, either(packed_tiles(c_outer, 0), packed_tiles(c_third, 0)))
    put_packed(h2, 1, either(packed_tiles(c_outer, 1), packed_tiles(c_inner, 0)))
    put_packed(h2, 2, either(packed_tiles(c_outer, 2), packed_tiles(c_inner, 1)))
    put_packed(h2, 5, either(packed_tiles(c_inner, 0), packed_tiles(c_outer, 0)))
    put_packed(h2, 6, either(packed_tiles(c_inner, 1), packed_tiles(c_outer, 1)))
    put_packed(h2, 7, either(packed_tiles(c_third, 0), packed_tiles(c_outer, 2)))

    for idx in range(8):
        for k in range(FB // 2):
            if 2 <= idx < 6:
                pair = f_own[idx - 2, k]
            elif idx < 2:
                pair = jnp.where(upper, f_outer[2 + idx, k], f_inner[2 + idx, k])
            else:
                pair = jnp.where(upper, f_inner[idx - 6, k], f_outer[idx - 6, k])
            pf1[idx, 1 + 2 * k] = swap_bf(pair)
            pf1[idx, 2 + 2 * k] = pair

    @pl.loop(0, 6)
    def _(idx):
        forms = coarse_gru(None, 0, h2, idx + 1, None, w_h, None, acc_h, in_grid(first_c + idx - 2, rows_c))
        put_forms(s1, idx, forms)

    @pl.loop(0, 4)
    def _(idx):
        forms = coarse_gru(None, 0, s1, idx + 1, None, w_h, None, acc_h, in_grid(first_c + idx - 1, rows_c))
        put_forms(s2, idx, forms)

    s2[4] = jnp.zeros(s2.shape[1:], BF)

    def raise_rows(src, idx, fine, at, coarse_row):
        acc = raise_pair(src, idx, w_up)
        acc = jnp.where(in_grid(coarse_row, rows_c), leaky(acc), 0.0)
        for half, row in enumerate(at):
            if row is None:
                continue
            tile = acc[:, half * LANES : (half + 1) * LANES]
            even = tile.astype(BF).reshape(CB, SUB, LANES)
            odd = swap_halves(tile).astype(BF).reshape(CB, SUB, LANES)
            both = jnp.stack([even, odd], axis=1).reshape(FB, SUB, LANES)
            fine[row, 1 : FB + 1] = jnp.where(lo, both, fine[row, 1 : FB + 1])

    @pl.loop(0, 4)
    def _(k):
        raise_rows(s1, k + 1, pf1, (2 * k, 2 * k + 1), first_c + k - 1)
        seal(pf1, 2 * k, FB)
        seal(pf1, 2 * k + 1, FB)

    @pl.loop(0, 6)
    def _(idx):
        def emit(lo_block, count, new):
            pf2[idx, pl.ds(1 + lo_block, count)] = new

        fine_gru(pf1, idx + 1, w_gru, in_grid(first_f + idx - 1, rows_f), emit)

    def head(step, ref, base):
        for t in range(4):
            lhs = jnp.concatenate(
                [ref[base : base + 4, 1 + 8 * t + k].reshape(4 * SUB, LANES) for k in range(8)], axis=-1
            )
            acc = jnp.dot(lhs, w_head[...], preferred_element_type=F32).astype(BF)
            out[step, :, :, t * LANES : (t + 1) * LANES] = acc.reshape(4, SUB, LANES)

    head(0, pf2, 1)

    raise_rows(s2, 0, pf2, (None, 0), first_c - 1)
    raise_rows(s2, 1, pf2, (1, 2), first_c)
    raise_rows(s2, 2, pf2, (3, 4), first_c + 1)
    raise_rows(s2, 3, pf2, (5, None), first_c + 2)
    for idx in range(6):
        seal(pf2, idx, FB)

    @pl.loop(0, 4)
    def _(idx):
        def emit(lo_block, count, new):
            states[idx, pl.ds(1 + lo_block, count)] = new

        fine_gru(pf2, idx + 1, w_gru, True, emit)

    head(1, states, 0)


def fine_weight(kernel_x, kernel_h):
    x = kernel_x.reshape(9, C1, 3 * C1)
    h = kernel_h.reshape(9, C1, 3 * C1)
    none = jnp.zeros((9, C1, C1), BF)
    top = jnp.concatenate([x[..., : 2 * C1], none, x[..., 2 * C1 :]], axis=-1)
    low = jnp.concatenate([h, none], axis=-1)
    return jnp.concatenate([top, low], axis=1).reshape(9 * LANES, 2 * LANES)


def down_weight(kernel):
    k = kernel.reshape(9, C1, C2)
    return jnp.pad(k, ((0, 0), (C1, 0), (0, 2 * LANES - C2))).reshape(9 * LANES, 2 * LANES)


def up_weight(kernel):
    none = jnp.zeros((C2, C1), BF)

    def rows(even, odd):
        def group(a):
            if a is None:
                return [none, none], [none, none]
            return [kernel[a, 1], kernel[a, 0]], [none, kernel[a, 2]]

        e, o = group(even), group(odd)
        return [jnp.concatenate(e[i] + o[i], axis=-1) for i in range(2)]

    return jnp.concatenate(rows(1, 0) + rows(None, 2), axis=0)


def stem_weight(kernel):
    eye = jnp.eye(8, dtype=BF)
    wide = jnp.pad(kernel, ((0, 0), (0, LANES - C1)))
    return (eye[:, None, :, None] * wide[None, :, None, :]).reshape(8 * PATCH, 8 * LANES)


def head_weight(kernel):
    eye = jnp.eye(8, dtype=BF)
    tall = jnp.pad(kernel, ((LANES - C1, 0), (0, 0)))
    return (eye[:, None, :, None] * tall[None, :, None, :]).reshape(8 * LANES, 8 * PATCH)


def call(body, name, args, outs, scratch):
    return pl.pallas_call(
        body,
        name=name,
        out_shape=[jax.ShapeDtypeStruct(s, BF) for s in outs],
        in_specs=[pl.BlockSpec(memory_space=pltpu.SMEM)]
        + [pl.BlockSpec(memory_space=pltpu.VMEM)] * (len(args) - 1),
        out_specs=[pl.BlockSpec(memory_space=pltpu.VMEM)] * len(outs),
        scratch_shapes=scratch,
        compiler_params=pltpu.CompilerParams(vmem_limit_bytes=48 * 1024 * 1024),
    )(*args)


def on_device(
    frames,
    start_fine,
    start_coarse,
    enc_stem,
    enc_fine_x,
    enc_fine_h,
    enc_down,
    enc_coarse_x,
    enc_coarse_h,
    fc_coarse_h,
    fc_up,
    fc_fine_x,
    fc_fine_h,
    fc_head,
):
    count = lax.axis_size(LINE)
    section = lax.axis_index("section")
    position = lax.axis_index(LINE)
    where = jnp.stack([section, position, jnp.int32(count)]).astype(jnp.int32)
    across = [(i, i + 1) for i in range(1, count - 1, 2)]
    across = across + [(b, a) for a, b in across]

    def outer_swap(x):
        return lax.ppermute(x, LINE, across)

    def inner_swap(x):
        return lax.ppermute(x, "section", [(0, 1), (1, 0)])

    fine = start_fine.reshape(4, SUB, FB * C1)
    coarse = start_coarse.reshape(2, SUB, CB * C2)
    patches = frames.reshape(FRAMES, 4, SUB, FB * PATCH)
    fine_o, fr_o = outer_swap(fine), outer_swap(patches)
    fine_i, fr_i = inner_swap(fine), inner_swap(patches)
    coarse_o, coarse_i = outer_swap(coarse), inner_swap(coarse)

    w_enc = fine_weight(enc_fine_x, enc_fine_h)
    w_fc = fine_weight(fc_fine_x, fc_fine_h)

    def fine_buf(rows):
        return pltpu.VMEM((rows, FB + 2, SUB, LANES), BF)

    def coarse_buf(rows):
        return pltpu.VMEM((rows, CB + 2, SUB, 4 * LANES), BF)

    acc_buf = pltpu.VMEM((CB * SUB, 5 * LANES), F32)
    packed = (CB // 2, SUB, 3 * LANES)

    state_f, low_own, low_o, low_i = call(
        fine_encoder_body,
        "fine_encoder",
        [where, fine, fine_o, fine_i, patches, fr_o, fr_i, stem_weight(enc_stem), w_enc, down_weight(enc_down)],
        [(4, FB // 2, SUB, LANES), (4,) + packed, (3,) + packed, (3,) + packed],
        [fine_buf(9), fine_buf(9), fine_buf(9), pltpu.VMEM((9, FB, SUB, LANES), BF)],
    )
    got_o, got_i = outer_swap(low_o), inner_swap(low_i)
    state_fo, state_fi = outer_swap(state_f), inner_swap(state_f)

    flat = (9 * C2, 3 * C2)
    (state_c,) = call(
        coarse_encoder_body,
        "coarse_encoder",
        [where, coarse, coarse_o, coarse_i, low_own, got_o, got_i, enc_coarse_x.reshape(flat), enc_coarse_h.reshape(flat)],
        [(2,) + packed],
        [coarse_buf(6), coarse_buf(4), coarse_buf(6), coarse_buf(4), acc_buf, acc_buf],
    )
    state_ci = inner_swap(state_c)
    near = jnp.where(section == 0, state_ci[0], state_ci[1])[None]
    send = jnp.where(
        section == 0,
        jnp.concatenate([state_c, near], axis=0),
        jnp.concatenate([near, state_c], axis=0),
    )
    state_co = outer_swap(send)
    third = inner_swap(jnp.where(section == 0, state_co[2], state_co[0])[None])

    (out,) = call(
        forecaster_body,
        "forecaster",
        [where, state_c, state_co, state_ci, third, state_f, state_fo, state_fi,
         fc_coarse_h.reshape(flat), up_weight(fc_up), w_fc, head_weight(fc_head)],
        [(HORIZON, 4, SUB, FB * PATCH)],
        [coarse_buf(8), coarse_buf(6), coarse_buf(5), fine_buf(8), fine_buf(6), fine_buf(4), acc_buf],
    )
    return out.reshape(HORIZON, 4, COLS * PATCH)


def solution(mesh):
    line = ("groups", "tile", "section")
    return jax.shard_map(
        on_device,
        mesh=mesh,
        in_specs=(P(None, line, None), P(line, None), P(line, None)) + (P(),) * 11,
        out_specs=P(None, line, None),
        check_vma=False,
    )
```

profile of v0, /device:TPU:19, one launch (start us, length us, event | category | flops | bytes accessed | tf_op | source)
XLA Modules:
  0.0 104.4 jit_solution(12550759261833038670)
XLA Ops:
  0.0 1.2 %copy.55 = bf16[1,4,16,2048]{3,2,1,0:T(8,128)(2,1)S(1)} copy(bf16[1,4,16,2048]{3,1,2,0:T(4,128)(2,1)} %bitcast.67) | data formatting | bytes 524288
  1.2 3.7 %collective-permute-start.2 = (bf16[4,16,2048]{2,1,0:T(8,128)(2,1)S(1)}, bf16[4,16,2048]{2,1,0:T(8,128)(2,1)S(1)}, u32[]{:S(2)}, u32[]{:S(2)}) collective-permute-start(bf16[4,16,2048]{2,1,0:T(8,128)(2,1)S(1)} %bitcast.50), channel_id=1, source_target_pairs={{1,2},{3,4},{5,6},{7,8},{9,10},{11,12},{13,14},{2,1},{4,3},{6,5},{... | collective-permute-start | bytes 786440 | tf_op jit(solution)/shard_map/ppermute | solution.py:519
  5.0 1.0 reshape.65.fr_own
  6.0 3.5 %collective-permute-start.4 = (bf16[2,4,16,512]{3,2,1,0:T(8,128)(2,1)S(1)}, bf16[2,4,16,512]{3,2,1,0:T(8,128)(2,1)S(1)}, u32[]{:S(2)}, u32[]{:S(2)}) collective-permute-start(bf16[2,4,16,512]{3,2,1,0:T(8,128)(2,1)S(1)} %reshape.65.fr_own), channel_id=1, source_target_pairs={{1,2},{3,4},{5,6},{7,8},{9,10},{11,12},{13,14},{2,1},{4,3},{6,5},{... | collective-permute-start | bytes 393224 | tf_op jit(solution)/shard_map/ppermute | solution.py:519
  9.6 0.9 slice.68
  10.8 1.3 %fusion.4 = (bf16[9,128,256]{2,1,0:T(8,128)(2,1)S(1)}, bf16[9,128,256]{2,1,0:T(8,128)(2,1)S(1)}) fusion(bf16[9,64,192]{2,1,0:T(8,128)(2,1)S(1)} %bitcast.60, bf16[9,64,64]{2,1,0:T(8,128)(2,1)S(1)} %slice.75, bf16[9,64,128]{2,1,0:T(8,128)(2,1)S(1)} %slice.74, bf16[128,256]{1,0:T(8,128)(2,1)S(1)} %pad.39.clone, bf16[9,64,192]{2,1,0:T(8,128)(2,1)} %bitcast.61, ...), kind=kLoop, calls=%fused_computation.6 | loop fusion | flops 5308416 | bytes 2129920 | tf_op jit(solution)/shard_map/concatenate | solution.py:447
  12.2 1.0 pad.16
  13.3 1.2 %collective-permute-done.4.fr_outer = bf16[2,4,16,512]{3,2,1,0:T(8,128)(2,1)S(1)} collective-permute-done((bf16[2,4,16,512]{3,2,1,0:T(8,128)(2,1)S(1)}, bf16[2,4,16,512]{3,2,1,0:T(8,128)(2,1)S(1)}, u32[]{:S(2)}, u32[]{:S(2)}) %collective-permute-start.4) | collective-permute-done | bytes 131104 | tf_op jit(solution)/shard_map/ppermute | solution.py:519
  14.6 10.8 %fine_encoder.1 = (bf16[4,16,16,128]{3,2,1,0:T(8,128)(2,1)S(1)}, bf16[4,8,16,384]{3,2,1,0:T(8,128)(2,1)S(1)}, bf16[3,8,16,384]{3,2,1,0:T(8,128)(2,1)S(1)}, bf16[3,8,16,384]{3,2,1,0:T(8,128)(2,1)S(1)}) custom-call(s32[3]{0:T(128)S(1)} %pad_add_fusion.where_ref, bf16[4,16,2048]{2,1,0:T(8,128)(2,1)S(1)} %bitcast.52, ...), custom_call_target="tpu_custom_call" | custom-call | tf_op jit(solution)/shard_map/fine_encoder/pallas_call | solution.py:483
  25.5 3.6 %collective-permute-start.6 = (bf16[3,8,16,384]{3,2,1,0:T(8,128)(2,1)S(1)}, bf16[3,8,16,384]{3,2,1,0:T(8,128)(2,1)S(1)}, u32[]{:S(2)}, u32[]{:S(2)}) collective-permute-start(bf16[3,8,16,384]{3,2,1,0:T(8,128)(2,1)S(1)} %get-tuple-element.10), channel_id=1, source_target_pairs={{1,2},{3,4},{5,6},{7,8},{9,10},{11,12},{13,14},{2,1},{4,3},{6,5},{... | collective-permute-start | bytes 884744 | tf_op jit(solution)/shard_map/ppermute | solution.py:519
  29.3 2.1 %collective-permute-start = (bf16[2,16,3072]{2,1,0:T(8,128)(2,1)S(1)}, bf16[2,16,3072]{2,1,0:T(8,128)(2,1)S(1)}, u32[]{:S(2)}, u32[]{:S(2)}) collective-permute-start(bf16[2,16,3072]{2,1,0:T(8,128)(2,1)S(1)} %bitcast.54), channel_id=1, source_target_pairs={{1,2},{3,4},{5,6},{7,8},{9,10},{11,12},{13,14},{2,1},{4,3},{6,5},{... | collective-permute-start | bytes 589832 | tf_op jit(solution)/shard_map/ppermute | solution.py:519
  31.7 8.7 %collective-permute-done.outer = bf16[2,16,3072]{2,1,0:T(8,128)(2,1)S(1)} collective-permute-done((bf16[2,16,3072]{2,1,0:T(8,128)(2,1)S(1)}, bf16[2,16,3072]{2,1,0:T(8,128)(2,1)S(1)}, u32[]{:S(2)}, u32[]{:S(2)}) %collective-permute-start) | collective-permute-done | bytes 196640 | tf_op jit(solution)/shard_map/ppermute | solution.py:519
  40.4 1.6 %copy-done.1 = bf16[3,3,192,576]{3,2,1,0:T(8,128)(2,1)S(1)} copy-done((bf16[3,3,192,576]{3,2,1,0:T(8,128)(2,1)S(1)}, bf16[3,3,192,576]{3,2,1,0:T(8,128)(2,1)}, u32[]{:S(2)}) %copy-start.1) | copy-done | bytes 1990680
  42.0 12.2 %coarse_encoder.1.c_own = bf16[2,8,16,384]{3,2,1,0:T(8,128)(2,1)S(1)} custom-call(s32[3]{0:T(128)S(1)} %pad_add_fusion.where_ref, bf16[2,16,3072]{2,1,0:T(8,128)(2,1)S(1)} %bitcast.56, bf16[2,16,3072]{2,1,0:T(8,128)(2,1)S(1)} %collective-permute-done.outer, bf16[2,16,3072]{2,1,0:T(8,128)(2,1)S(1)} %collective-permute-done.1.inner, ...), custom_call_target="tpu_custom_call" | custom-call | tf_op jit(solution)/shard_map/coarse_encoder/pallas_call | solution.py:483
  54.3 1.4 %collective-permute-done.8.c_inner = bf16[2,8,16,384]{3,2,1,0:T(8,128)(2,1)S(1)} collective-permute-done((bf16[2,8,16,384]{3,2,1,0:T(8,128)(2,1)S(1)}, bf16[2,8,16,384]{3,2,1,0:T(8,128)(2,1)S(1)}, u32[]{:S(2)}, u32[]{:S(2)}) %collective-permute-start.8) | collective-permute-done | bytes 196640 | tf_op jit(solution)/shard_map/ppermute | solution.py:522
  56.4 0.8 maximum_select_fusion
  57.2 3.9 %collective-permute-start.9 = (bf16[3,8,16,384]{3,2,1,0:T(8,128)(2,1)}, bf16[3,8,16,384]{3,2,1,0:T(8,128)(2,1)S(1)}, u32[]{:S(2)}, u32[]{:S(2)}) collective-permute-start(bf16[3,8,16,384]{3,2,1,0:T(8,128)(2,1)} %maximum_select_fusion), channel_id=1, source_target_pairs={{1,2},{3,4},{5,6},{7,8},{9,10},{11,12},{13,14},{2,1},{4,3},{6,5},{... | collective-permute-start | bytes 884744 | tf_op jit(solution)/shard_map/ppermute | solution.py:519
  61.1 0.7 copy.36
  61.9 0.7 copy.37
  63.3 0.7 copy.39
  66.9 0.7 copy.44
  67.8 0.8 copy.53
  68.5 1.8 %copy.35.w_head = bf16[1024,128]{1,0:T(8,128)(2,1)} copy(bf16[1024,128]{0,1:T(8,128)(2,1)} %bitcast.59) | data formatting | bytes 524288 | tf_op jit(solution)/shard_map/mul | solution.py:479
  70.3 2.2 %collective-permute-start.11 = (bf16[4,16,16,128]{3,2,1,0:T(8,128)(2,1)S(1)}, bf16[4,16,16,128]{3,2,1,0:T(8,128)(2,1)S(1)}, u32[]{:S(2)}, u32[]{:S(2)}) collective-permute-start(bf16[4,16,16,128]{3,2,1,0:T(8,128)(2,1)S(1)} %get-tuple-element.12.f_own), channel_id=1, source_target_pairs={{1,2},{3,4},{5,6},{7,8},{9,10},{11,12},{13,14},{2,1},{4,3},{6,5},{... | collective-permute-start | bytes 786440 | tf_op jit(solution)/shard_map/ppermute | solution.py:519
  72.5 0.8 collective-permute-start.12
  74.1 1.2 %fusion.5.w_up = bf16[768,256]{1,0:T(8,128)(2,1)S(1)} fusion(bf16[192,64]{1,0:T(8,128)(2,1)} %bitcast.76, bf16[192,64]{1,0:T(8,128)(2,1)} %bitcast.75, bf16[192,64]{1,0:T(8,128)(2,1)} %bitcast.74, bf16[192,128]{1,0:T(8,128)(2,1)S(1)} %concatenate.50, bf16[192,64]{1,0:T(8,128)(2,1)} %bitcast.73, bf16[192,64]{1,0:T(8,128)(2,1)S(1)} %broadcast_in_dim.2, ...), kind=kLoop, calls=%fused_computation.7 | loop fusion | flops 5111808 | bytes 688128 | tf_op jit(solution)/shard_map/concatenate | solution.py:467
  75.3 5.7 %collective-permute-done.11.f_outer = bf16[4,16,16,128]{3,2,1,0:T(8,128)(2,1)S(1)} collective-permute-done((bf16[4,16,16,128]{3,2,1,0:T(8,128)(2,1)S(1)}, bf16[4,16,16,128]{3,2,1,0:T(8,128)(2,1)S(1)}, u32[]{:S(2)}, u32[]{:S(2)}) %collective-permute-start.11) | collective-permute-done | bytes 262176 | tf_op jit(solution)/shard_map/ppermute | solution.py:519
  81.0 0.9 copy-done.3
  81.9 1.0 copy-done.5
  82.9 0.9 copy-done.7
  83.8 19.9 %forecaster.1 = bf16[2,4,16,512]{3,2,1,0:T(8,128)(2,1)S(1)} custom-call(s32[3]{0:T(128)S(1)} %copy-done.9, bf16[2,8,16,384]{3,2,1,0:T(8,128)(2,1)S(1)} %coarse_encoder.1.c_own, bf16[3,8,16,384]{3,2,1,0:T(8,128)(2,1)S(1)} %copy-done.5, bf16[2,8,16,384]{3,2,1,0:T(8,128)(2,1)S(1)} %copy-done.7, bf16[1,8,16,384]{3,2,1,0:T(8,128)(2,1)S(1)} %collective-permute-done.10.c_third, ...), custom_call_target="tpu_custom_call" | custom-call | tf_op jit(solution)/shard_map/forecaster/pallas_call | solution.py:483
  103.7 0.7 reshape.77
  (69 shorter events, 6.3 us)
Async XLA Ops:
  0.0 10.5 %copy-start.11 = (bf16[3,3,64,192]{3,2,1,0:T(8,128)(2,1)S(1)}, bf16[3,3,64,192]{3,2,1,0:T(8,128)(2,1)}, u32[]{:S(2)}) copy-start(bf16[3,3,64,192]{3,2,1,0:T(8,128)(2,1)} %param.18) | copy-start | bytes 663556
  0.0 10.6 %copy-start.12 = (bf16[3,3,64,192]{3,2,1,0:T(8,128)(2,1)S(1)}, bf16[3,3,64,192]{3,2,1,0:T(8,128)(2,1)}, u32[]{:S(2)}) copy-start(bf16[3,3,64,192]{3,2,1,0:T(8,128)(2,1)} %param.25) | copy-start | bytes 663556
  0.0 10.7 %copy-start.15 = (bf16[16,64]{1,0:T(8,128)(2,1)S(1)}, bf16[16,64]{1,0:T(8,128)(2,1)}, u32[]{:S(2)}) copy-start(bf16[16,64]{1,0:T(8,128)(2,1)} %param.17) | copy-start | bytes 6148
  0.0 10.8 %copy-start.10 = (bf16[3,3,64,192]{3,2,1,0:T(8,128)(2,1)S(1)}, bf16[3,3,64,192]{3,2,1,0:T(8,128)(2,1)}, u32[]{:S(2)}) copy-start(bf16[3,3,64,192]{3,2,1,0:T(8,128)(2,1)} %param.26) | copy-start | bytes 663556
  1.2 13.4 %collective-permute-start.2 = (bf16[4,16,2048]{2,1,0:T(8,128)(2,1)S(1)}, bf16[4,16,2048]{2,1,0:T(8,128)(2,1)S(1)}, u32[]{:S(2)}, u32[]{:S(2)}) collective-permute-start(bf16[4,16,2048]{2,1,0:T(8,128)(2,1)S(1)} %bitcast.50), channel_id=1, source_target_pairs={{1,2},{3,4},{5,6},{7,8},{9,10},{11,12},{13,14},{2,1},{4,3},{6,5},{... | collective-permute-start | bytes 786440 | tf_op jit(solution)/shard_map/ppermute | solution.py:519
  4.9 9.7 %collective-permute-start.3 = (bf16[4,16,2048]{2,1,0:T(8,128)(2,1)S(1)}, bf16[4,16,2048]{2,1,0:T(8,128)(2,1)S(1)}, u32[]{:S(2)}, u32[]{:S(2)}) collective-permute-start(bf16[4,16,2048]{2,1,0:T(8,128)(2,1)S(1)} %bitcast.51), channel_id=1, source_target_pairs={{0,1},{1,0},{2,3},{3,2},{4,5},{5,4},{6,7},{7,6},{8,9},{9,8},{10,11... | collective-permute-start | bytes 786440 | tf_op jit(solution)/shard_map/ppermute | solution.py:522
  6.0 8.6 %collective-permute-start.4 = (bf16[2,4,16,512]{3,2,1,0:T(8,128)(2,1)S(1)}, bf16[2,4,16,512]{3,2,1,0:T(8,128)(2,1)S(1)}, u32[]{:S(2)}, u32[]{:S(2)}) collective-permute-start(bf16[2,4,16,512]{3,2,1,0:T(8,128)(2,1)S(1)} %reshape.65.fr_own), channel_id=1, source_target_pairs={{1,2},{3,4},{5,6},{7,8},{9,10},{11,12},{13,14},{2,1},{4,3},{6,5},{... | collective-permute-start | bytes 393224 | tf_op jit(solution)/shard_map/ppermute | solution.py:519
  9.5 5.1 %collective-permute-start.5 = (bf16[2,4,16,512]{3,2,1,0:T(8,128)(2,1)S(1)}, bf16[2,4,16,512]{3,2,1,0:T(8,128)(2,1)S(1)}, u32[]{:S(2)}, u32[]{:S(2)}) collective-permute-start(bf16[2,4,16,512]{3,2,1,0:T(8,128)(2,1)S(1)} %reshape.65.fr_own), channel_id=1, source_target_pairs={{0,1},{1,0},{2,3},{3,2},{4,5},{5,4},{6,7},{7,6},{8,9},{9,8},{10,11... | collective-permute-start | bytes 393224 | tf_op jit(solution)/shard_map/ppermute | solution.py:522
  13.3 27.1 %copy-start.8 = (s32[3]{0:T(128)}, s32[3]{0:T(128)S(1)}, u32[]{:S(2)}) copy-start(s32[3]{0:T(128)S(1)} %pad_add_fusion.where_ref) | copy-start | bytes 40
  14.6 14.6 %copy-start.14 = (bf16[2,49152]{1,0:T(2,128)(2,1)S(1)}, bf16[2,49152]{1,0:T(2,128)(2,1)}, u32[]{:S(2)}) copy-start(bf16[2,49152]{1,0:T(2,128)(2,1)} %param.16) | copy-start | bytes 589828
  14.6 25.8 %copy-start = (bf16[3,3,192,576]{3,2,1,0:T(8,128)(2,1)S(1)}, bf16[3,3,192,576]{3,2,1,0:T(8,128)(2,1)}, u32[]{:S(2)}) copy-start(bf16[3,3,192,576]{3,2,1,0:T(8,128)(2,1)} %param.21) | copy-start | bytes 5971972
  25.5 14.9 %collective-permute-start.6 = (bf16[3,8,16,384]{3,2,1,0:T(8,128)(2,1)S(1)}, bf16[3,8,16,384]{3,2,1,0:T(8,128)(2,1)S(1)}, u32[]{:S(2)}, u32[]{:S(2)}) collective-permute-start(bf16[3,8,16,384]{3,2,1,0:T(8,128)(2,1)S(1)} %get-tuple-element.10), channel_id=1, source_target_pairs={{1,2},{3,4},{5,6},{7,8},{9,10},{11,12},{13,14},{2,1},{4,3},{6,5},{... | collective-permute-start | bytes 884744 | tf_op jit(solution)/shard_map/ppermute | solution.py:519
  29.1 11.3 %collective-permute-start.7 = (bf16[3,8,16,384]{3,2,1,0:T(8,128)(2,1)S(1)}, bf16[3,8,16,384]{3,2,1,0:T(8,128)(2,1)S(1)}, u32[]{:S(2)}, u32[]{:S(2)}) collective-permute-start(bf16[3,8,16,384]{3,2,1,0:T(8,128)(2,1)S(1)} %get-tuple-element.11), channel_id=1, source_target_pairs={{0,1},{1,0},{2,3},{3,2},{4,5},{5,4},{6,7},{7,6},{8,9},{9,8},{10,11... | collective-permute-start | bytes 884744 | tf_op jit(solution)/shard_map/ppermute | solution.py:522
  29.3 11.1 %collective-permute-start = (bf16[2,16,3072]{2,1,0:T(8,128)(2,1)S(1)}, bf16[2,16,3072]{2,1,0:T(8,128)(2,1)S(1)}, u32[]{:S(2)}, u32[]{:S(2)}) collective-permute-start(bf16[2,16,3072]{2,1,0:T(8,128)(2,1)S(1)} %bitcast.54), channel_id=1, source_target_pairs={{1,2},{3,4},{5,6},{7,8},{9,10},{11,12},{13,14},{2,1},{4,3},{6,5},{... | collective-permute-start | bytes 589832 | tf_op jit(solution)/shard_map/ppermute | solution.py:519
  31.3 9.0 %collective-permute-start.1 = (bf16[2,16,3072]{2,1,0:T(8,128)(2,1)S(1)}, bf16[2,16,3072]{2,1,0:T(8,128)(2,1)S(1)}, u32[]{:S(2)}, u32[]{:S(2)}) collective-permute-start(bf16[2,16,3072]{2,1,0:T(8,128)(2,1)S(1)} %bitcast.55), channel_id=1, source_target_pairs={{0,1},{1,0},{2,3},{3,2},{4,5},{5,4},{6,7},{7,6},{8,9},{9,8},{10,11... | collective-permute-start | bytes 589832 | tf_op jit(solution)/shard_map/ppermute | solution.py:522
  40.4 1.6 %copy-start.1 = (bf16[3,3,192,576]{3,2,1,0:T(8,128)(2,1)S(1)}, bf16[3,3,192,576]{3,2,1,0:T(8,128)(2,1)}, u32[]{:S(2)}) copy-start(bf16[3,3,192,576]{3,2,1,0:T(8,128)(2,1)} %param.22) | copy-start | bytes 5971972
  42.0 19.1 %copy-start.13 = (bf16[3,3,192,64]{2,3,1,0:T(8,128)(2,1)S(1)}, bf16[3,3,192,64]{2,3,1,0:T(8,128)(2,1)}, u32[]{:S(2)}) copy-start(bf16[3,3,192,64]{2,3,1,0:T(8,128)(2,1)} %param.24) | copy-start | bytes 663556
  54.2 13.4 %copy-start.16 = (bf16[64,16]{0,1:T(8,128)(2,1)S(1)}, bf16[64,16]{0,1:T(8,128)(2,1)}, u32[]{:S(2)}) copy-start(bf16[64,16]{0,1:T(8,128)(2,1)} %param.27) | copy-start | bytes 6148
  54.2 1.5 %collective-permute-start.8 = (bf16[2,8,16,384]{3,2,1,0:T(8,128)(2,1)S(1)}, bf16[2,8,16,384]{3,2,1,0:T(8,128)(2,1)S(1)}, u32[]{:S(2)}, u32[]{:S(2)}) collective-permute-start(bf16[2,8,16,384]{3,2,1,0:T(8,128)(2,1)S(1)} %coarse_encoder.1.c_own), channel_id=1, source_target_pairs={{0,1},{1,0},{2,3},{3,2},{4,5},{5,4},{6,7},{7,6},{8,9},{9,8},{10,11... | collective-permute-start | bytes 589832 | tf_op jit(solution)/shard_map/ppermute | solution.py:522
  55.7 0.7 copy-start.6
  57.2 16.2 %collective-permute-start.9 = (bf16[3,8,16,384]{3,2,1,0:T(8,128)(2,1)}, bf16[3,8,16,384]{3,2,1,0:T(8,128)(2,1)S(1)}, u32[]{:S(2)}, u32[]{:S(2)}) collective-permute-start(bf16[3,8,16,384]{3,2,1,0:T(8,128)(2,1)} %maximum_select_fusion), channel_id=1, source_target_pairs={{1,2},{3,4},{5,6},{7,8},{9,10},{11,12},{13,14},{2,1},{4,3},{6,5},{... | collective-permute-start | bytes 884744 | tf_op jit(solution)/shard_map/ppermute | solution.py:519
  67.8 13.2 %copy-start.2 = (bf16[3,3,192,576]{3,2,1,0:T(8,128)(2,1)S(1)}, bf16[3,3,192,576]{3,2,1,0:T(8,128)(2,1)}, u32[]{:S(2)}) copy-start(bf16[3,3,192,576]{3,2,1,0:T(8,128)(2,1)} %param.23) | copy-start | bytes 5971972
  70.3 10.6 %copy-start.9 = (s32[3]{0:T(128)S(1)}, s32[3]{0:T(128)}, u32[]{:S(2)}) copy-start(s32[3]{0:T(128)} %copy-done.8) | copy-start | bytes 40
  70.3 10.6 %collective-permute-start.11 = (bf16[4,16,16,128]{3,2,1,0:T(8,128)(2,1)S(1)}, bf16[4,16,16,128]{3,2,1,0:T(8,128)(2,1)S(1)}, u32[]{:S(2)}, u32[]{:S(2)}) collective-permute-start(bf16[4,16,16,128]{3,2,1,0:T(8,128)(2,1)S(1)} %get-tuple-element.12.f_own), channel_id=1, source_target_pairs={{1,2},{3,4},{5,6},{7,8},{9,10},{11,12},{13,14},{2,1},{4,3},{6,5},{... | collective-permute-start | bytes 786440 | tf_op jit(solution)/shard_map/ppermute | solution.py:519
  72.5 8.4 %collective-permute-start.12 = (bf16[4,16,16,128]{3,2,1,0:T(8,128)(2,1)S(1)}, bf16[4,16,16,128]{3,2,1,0:T(8,128)(2,1)S(1)}, u32[]{:S(2)}, u32[]{:S(2)}) collective-permute-start(bf16[4,16,16,128]{3,2,1,0:T(8,128)(2,1)S(1)} %get-tuple-element.12.f_own), channel_id=1, source_target_pairs={{0,1},{1,0},{2,3},{3,2},{4,5},{5,4},{6,7},{7,6},{8,9},{9,8},{10,11... | collective-permute-start | bytes 786440 | tf_op jit(solution)/shard_map/ppermute | solution.py:522
  73.4 0.7 copy-start.4
  73.4 7.6 %collective-permute-start.10 = (bf16[1,8,16,384]{3,2,1,0:T(8,128)(2,1)S(1)}, bf16[1,8,16,384]{3,2,1,0:T(8,128)(2,1)S(1)}, u32[]{:S(2)}, u32[]{:S(2)}) collective-permute-start(bf16[1,8,16,384]{3,2,1,0:T(8,128)(2,1)S(1)} %slice_select_fusion), channel_id=1, source_target_pairs={{0,1},{1,0},{2,3},{3,2},{4,5},{5,4},{6,7},{7,6},{8,9},{9,8},{10,11... | collective-permute-start | bytes 294920 | tf_op jit(solution)/shard_map/ppermute | solution.py:522
  81.0 1.0 copy-start.3
  81.9 1.0 copy-start.5
  82.9 0.9 copy-start.7
where the time goes:
time: 105 us; the launch traced here: 104 us
  Pallas kernels  42.9 us (41%)
  starting transfers between devices  20.7 us (20%)
  local copies, waits for them, and re-layouts  20 us (19%)
  waiting for transfers between devices  17 us (16%)
  other arithmetic  3.5 us (3%)
    pallas_call x3, Pallas kernels, call(): pl.pallas_call(body, name=name, out_shape=[jax.ShapeDtypeStruct(s, BF) fo...  42.9 us
    ppermute x6, starting transfers between devices, outer_swap(): return lax.ppermute(x, LINE, across)  19.1 us
    ppermute x6, waiting for transfers between devices, outer_swap(): return lax.ppermute(x, LINE, across)  15.6 us
    unnamed x47, local copies, waits for them, and re-layouts  14.2 us
  transfers between devices with their start and end apart: 13, of which 4 were waited for; matrix products, arithmetic and copies ran while one was open for 14% of the time, Pallas kernels for 0%

commit v1 on v0

--- a/solution.py
+++ b/solution.py
@@ -18,6 +18,8 @@
 BF = jnp.bfloat16
 F32 = jnp.float32
 LINE = ("tile", "section")
+PAIRS = CB // 2
+ROW_TILES = 3 * PAIRS
 
 
 def leaky(values):
@@ -185,30 +187,25 @@
 
 
 def fine_encoder_body(
-    where_ref, own, outer, inner, fr_own, fr_outer, fr_inner, w_stem, w_gru, w_down,
-    state_out, low_own, low_outer, low_inner, p1, p2, p3, stem2,
+    where_ref, own, outer, inner, w_stem, w_gru, w_down,
+    state_out, low_own, to_outer, to_inner, p1, p2, p3, stem2,
 ):
     upper = where_ref[0] == 0
     first = where_ref[1] * 4
     rows = where_ref[2] * 4
     lo = low_half((1, SUB, LANES))
 
-    def pick(own_ref, outer_ref, inner_ref, idx, lanes, frame=None):
-        def at(ref, r):
-            return ref[r, :, lanes] if frame is None else ref[frame, r, :, lanes]
-
+    def pick(idx, lanes):
         if 3 <= idx < 7:
-            return at(own_ref, idx - 3)
+            return own[idx - 3, :, lanes]
         r = idx + 1 if idx < 3 else idx - 7
-        a, b = at(outer_ref, r), at(inner_ref, r)
+        a, b = outer[r, :, lanes], inner[r, :, lanes]
         return jnp.where(upper, a, b) if idx < 3 else jnp.where(upper, b, a)
 
     for frame in range(FRAMES):
         for t in range(4):
-            lanes = slice(t * LANES, (t + 1) * LANES)
-            patches = jnp.concatenate(
-                [pick(fr_own, fr_outer, fr_inner, idx, lanes, frame) for idx in range(9)], axis=0
-            )
+            at = FB * C1 + frame * FB * PATCH + t * LANES
+            patches = jnp.concatenate([pick(idx, slice(at, at + LANES)) for idx in range(9)], axis=0)
             for half in range(2):
                 acc = jnp.dot(patches, w_stem[:, half * 512 : half * 512 + 512], preferred_element_type=F32)
                 acc = leaky(acc).astype(BF)
@@ -221,7 +218,7 @@
                         stem2[:, at] = block
     for idx in range(9):
         for k in range(FB // 2):
-            pair = pick(own, outer, inner, idx, slice(k * LANES, (k + 1) * LANES))
+            pair = pick(idx, slice(k * LANES, (k + 1) * LANES))
             p1[idx, 1 + 2 * k] = jnp.where(lo[0], p1[idx, 1 + 2 * k], swap_bf(pair))
             p1[idx, 2 + 2 * k] = jnp.where(lo[0], p1[idx, 2 + 2 * k], pair)
         seal(p1, idx, FB)
@@ -249,29 +246,35 @@
 
     def put(ref, at, tiles):
         for k, tile in enumerate(tiles):
-            ref[at, :, :, k * LANES : (k + 1) * LANES] = tile
+            base = at * ROW_TILES + k * PAIRS
+            ref[base : base + PAIRS] = tile
 
     for p in range(2):
         tiles = lowered(p2, p)
         put(low_own, p, tiles)
-        put(low_outer, p, tiles)
-        put(low_inner, p, tiles)
+        put(to_outer, p, tiles)
+        put(to_inner, p, tiles)
     for p in range(2):
         tiles = lowered(p3, p)
         put(low_own, 2 + p, tiles)
-        to_outer = upper if p == 0 else jnp.logical_not(upper)
-
-        @pl.when(to_outer)
+        outward = upper if p == 0 else jnp.logical_not(upper)
+
+        @pl.when(outward)
         def _():
-            put(low_outer, 2, tiles)
-
-        @pl.when(jnp.logical_not(to_outer))
+            put(to_outer, 2, tiles)
+
+        @pl.when(jnp.logical_not(outward))
         def _():
-            put(low_inner, 2, tiles)
+            put(to_inner, 2, tiles)
 
     for r in range(4):
         for k in range(FB // 2):
             state_out[r, k] = jnp.where(lo[0], swap_bf(p3[3 + r, 1 + 2 * k]), p3[3 + r, 2 + 2 * k])
+    base = 3 * ROW_TILES
+    for top, ref in ((upper, to_outer), (jnp.logical_not(upper), to_inner)):
+        start = jnp.where(top, 0, 2)
+        for r in range(2):
+            ref[base + r * FB // 2 : base + (r + 1) * FB // 2] = state_out[start + r]
 
 
 def zero_tail(acc):
@@ -279,13 +282,17 @@
 
 
 def packed_tiles(ref, at):
-    return lambda i: ref[at, :, :, i * LANES : (i + 1) * LANES]
+    return lambda i: ref[at * ROW_TILES + i * PAIRS : at * ROW_TILES + (i + 1) * PAIRS]
 
 
 def coarse_encoder_body(
-    where_ref, own, outer, inner, low_own, low_outer, low_inner, w_x, w_h,
-    state_out, x1, x2, h0, h1, acc_x, acc_h,
+    where_ref, own, outer, inner, low_own, low_outer, low_inner, w_x_hbm, w_h_hbm,
+    state_out, x1, x2, h0, h1, acc_x, acc_h, w_x, w_h, sems,
 ):
+    fetch_h = pltpu.make_async_copy(w_h_hbm, w_h, sems.at[0])
+    fetch_x = pltpu.make_async_copy(w_x_hbm, w_x, sems.at[1])
+    fetch_h.start()
+    fetch_x.start()
     upper = where_ref[0] == 0
     first = where_ref[1] * 2
     rows = where_ref[2] * 2
@@ -300,13 +307,13 @@
 
     for idx in range(6):
         if 2 <= idx < 4:
-            put_packed(h0, idx, raw_tiles(lambda lanes: own[idx - 2, :, lanes]))
+            put_packed(h0, idx, raw_tiles(lambda lanes: own[2 + idx, :, lanes]))
             put_packed(x1, idx, packed_tiles(low_own, idx - 2))
             continue
         r = idx if idx < 2 else idx - 4
         first_ref, second_ref = (outer, inner) if idx < 2 else (inner, outer)
         put_packed(
-            h0, idx, raw_tiles(lambda lanes: jnp.where(upper, first_ref[r, :, lanes], second_ref[r, :, lanes]))
+            h0, idx, raw_tiles(lambda lanes: jnp.where(upper, first_ref[4 + r, :, lanes], second_ref[4 + r, :, lanes]))
         )
         low_a, low_b = (low_outer, low_inner) if idx < 2 else (low_inner, low_outer)
         put_packed(x1, idx, lambda i: jnp.where(upper, packed_tiles(low_a, r)(i), packed_tiles(low_b, r)(i)))
@@ -315,6 +322,9 @@
     put_packed(x2, 0, lambda i: jnp.where(upper, packed_tiles(low_outer, 2)(i), packed_tiles(low_inner, 2)(i)))
     put_packed(x2, 3, lambda i: jnp.where(upper, packed_tiles(low_inner, 2)(i), packed_tiles(low_outer, 2)(i)))
 
+    fetch_h.wait()
+    fetch_x.wait()
+
     @pl.loop(0, 4)
     def _(idx):
         forms = coarse_gru(x1, idx + 1, h0, idx + 1, w_x, w_h, acc_x, acc_h, in_grid(first + idx - 1, rows))
@@ -324,7 +334,7 @@
     def _(idx):
         forms = coarse_gru(x2, idx + 1, h1, idx + 1, w_x, w_h, acc_x, acc_h, in_grid(first + idx, rows))
         for k, tile in enumerate(pack_forms(forms)):
-            state_out[idx, :, :, k * LANES : (k + 1) * LANES] = tile
+            state_out[pl.ds(idx * ROW_TILES + k * PAIRS, PAIRS)] = tile
 
 
 def raise_pair(src, idx, weight):
@@ -339,9 +349,11 @@
 
 
 def forecaster_body(
-    where_ref, c_own, c_outer, c_inner, c_third, f_own, f_outer, f_inner, w_h, w_up, w_gru, w_head,
-    out, h2, s1, s2, pf1, pf2, states, acc_h,
+    where_ref, c_own, c_outer, c_inner, c_third, f_own, f_outer, f_inner, w_h_hbm, w_up, w_gru, w_head,
+    out, h2, s1, s2, pf1, pf2, states, acc_h, w_h, sem,
 ):
+    fetch_h = pltpu.make_async_copy(w_h_hbm, w_h, sem)
+    fetch_h.start()
     upper = where_ref[0] == 0
     first_c = where_ref[1] * 2
     rows_c = where_ref[2] * 2
@@ -363,16 +375,20 @@
     put_packed(h2, 6, either(packed_tiles(c_inner, 1), packed_tiles(c_outer, 1)))
     put_packed(h2, 7, either(packed_tiles(c_third, 0), packed_tiles(c_outer, 2)))
 
+    base = 3 * ROW_TILES
     for idx in range(8):
         for k in range(FB // 2):
             if 2 <= idx < 6:
                 pair = f_own[idx - 2, k]
             elif idx < 2:
-                pair = jnp.where(upper, f_outer[2 + idx, k], f_inner[2 + idx, k])
+                pair = jnp.where(upper, f_outer[base + idx * FB // 2 + k], f_inner[base + idx * FB // 2 + k])
             else:
-                pair = jnp.where(upper, f_inner[idx - 6, k], f_outer[idx - 6, k])
+                at = base + (idx - 6) * FB // 2 + k
+                pair = jnp.where(upper, f_inner[at], f_outer[at])
             pf1[idx, 1 + 2 * k] = swap_bf(pair)
             pf1[idx, 2 + 2 * k] = pair
+
+    fetch_h.wait()
 
     @pl.loop(0, 6)
     def _(idx):
@@ -438,45 +454,50 @@
     head(1, states, 0)
 
 
-def fine_weight(kernel_x, kernel_h):
-    x = kernel_x.reshape(9, C1, 3 * C1)
-    h = kernel_h.reshape(9, C1, 3 * C1)
-    none = jnp.zeros((9, C1, C1), BF)
-    top = jnp.concatenate([x[..., : 2 * C1], none, x[..., 2 * C1 :]], axis=-1)
-    low = jnp.concatenate([h, none], axis=-1)
-    return jnp.concatenate([top, low], axis=1).reshape(9 * LANES, 2 * LANES)
-
-
-def down_weight(kernel):
-    k = kernel.reshape(9, C1, C2)
-    return jnp.pad(k, ((0, 0), (C1, 0), (0, 2 * LANES - C2))).reshape(9 * LANES, 2 * LANES)
-
-
-def up_weight(kernel):
-    none = jnp.zeros((C2, C1), BF)
-
-    def rows(even, odd):
-        def group(a):
-            if a is None:
-                return [none, none], [none, none]
-            return [kernel[a, 1], kernel[a, 0]], [none, kernel[a, 2]]
-
-        e, o = group(even), group(odd)
-        return [jnp.concatenate(e[i] + o[i], axis=-1) for i in range(2)]
-
-    return jnp.concatenate(rows(1, 0) + rows(None, 2), axis=0)
-
-
-def stem_weight(kernel):
-    eye = jnp.eye(8, dtype=BF)
-    wide = jnp.pad(kernel, ((0, 0), (0, LANES - C1)))
-    return (eye[:, None, :, None] * wide[None, :, None, :]).reshape(8 * PATCH, 8 * LANES)
-
-
-def head_weight(kernel):
-    eye = jnp.eye(8, dtype=BF)
-    tall = jnp.pad(kernel, ((LANES - C1, 0), (0, 0)))
-    return (eye[:, None, :, None] * tall[None, :, None, :]).reshape(8 * LANES, 8 * PATCH)
+def to_upper(x):
+    return jnp.concatenate([jnp.zeros(x.shape, F32), x.astype(F32)], axis=-1).astype(BF)
+
+
+def to_lower(x):
+    return jnp.concatenate([x.astype(F32), jnp.zeros(x.shape, F32)], axis=-1).astype(BF)
+
+
+def prepare_body(
+    stem, enc_x, enc_h, down, up, fc_x, fc_h, head, w_stem, w_enc, w_down, w_up, w_fc, w_head
+):
+    for kx, kh, w in ((enc_x, enc_h, w_enc), (fc_x, fc_h, w_fc)):
+        for k in range(9):
+            at = k * LANES
+            w[at : at + C1, :LANES] = kx[k, :, :LANES]
+            w[at : at + C1, LANES:] = to_upper(kx[k, :, LANES:])
+            w[at + C1 : at + LANES, :LANES] = kh[k, :, :LANES]
+            w[at + C1 : at + LANES, LANES:] = to_lower(kh[k, :, LANES:])
+    for k in range(9):
+        at = k * LANES
+        w_down[at : at + C1] = jnp.zeros((C1, 2 * LANES), BF)
+        w_down[at + C1 : at + LANES, :LANES] = down[k, :, :LANES]
+        w_down[at + C1 : at + LANES, LANES:] = to_lower(down[k, :, LANES:])
+
+    def tap(a, b):
+        return jnp.zeros((C2, C1), F32) if a is None else up[3 * a + b].astype(F32)
+
+    none = (None, None)
+    for g, taps in enumerate((
+        ((1, 1), (1, 0), (0, 1), (0, 0)),
+        (none, (1, 2), none, (0, 2)),
+        (none, none, (2, 1), (2, 0)),
+        (none, none, none, (2, 2)),
+    )):
+        for n in range(2):
+            pair = jnp.concatenate([tap(*taps[2 * n]), tap(*taps[2 * n + 1])], axis=-1)
+            w_up[g * C2 : (g + 1) * C2, n * LANES : (n + 1) * LANES] = pair.astype(BF)
+
+    w_stem[...] = jnp.zeros(w_stem.shape, BF)
+    w_head[...] = jnp.zeros(w_head.shape, BF)
+    wide = to_lower(stem[...])
+    for k in range(8):
+        w_stem[k * PATCH : (k + 1) * PATCH, k * LANES : (k + 1) * LANES] = wide
+        w_head[k * LANES + C1 : (k + 1) * LANES, k * PATCH : (k + 1) * PATCH] = head[...]
 
 
 def call(body, name, args, outs, scratch):
@@ -484,12 +505,11 @@
         body,
         name=name,
         out_shape=[jax.ShapeDtypeStruct(s, BF) for s in outs],
-        in_specs=[pl.BlockSpec(memory_space=pltpu.SMEM)]
-        + [pl.BlockSpec(memory_space=pltpu.VMEM)] * (len(args) - 1),
+        in_specs=[pl.BlockSpec(memory_space=space) for _, space in args],
         out_specs=[pl.BlockSpec(memory_space=pltpu.VMEM)] * len(outs),
         scratch_shapes=scratch,
-        compiler_params=pltpu.CompilerParams(vmem_limit_bytes=48 * 1024 * 1024),
-    )(*args)
+        compiler_params=pltpu.CompilerParams(vmem_limit_bytes=24 * 1024 * 1024),
+    )(*[arg for arg, _ in args])
 
 
 def on_device(
@@ -522,14 +542,17 @@
         return lax.ppermute(x, "section", [(0, 1), (1, 0)])
 
     fine = start_fine.reshape(4, SUB, FB * C1)
+    patches = frames.reshape(FRAMES, 4, SUB, FB * PATCH)
     coarse = start_coarse.reshape(2, SUB, CB * C2)
-    patches = frames.reshape(FRAMES, 4, SUB, FB * PATCH)
-    fine_o, fr_o = outer_swap(fine), outer_swap(patches)
-    fine_i, fr_i = inner_swap(fine), inner_swap(patches)
-    coarse_o, coarse_i = outer_swap(coarse), inner_swap(coarse)
-
-    w_enc = fine_weight(enc_fine_x, enc_fine_h)
-    w_fc = fine_weight(fc_fine_x, fc_fine_h)
+    own = jnp.concatenate([fine, patches[0], patches[1]], axis=-1)
+    own = jnp.concatenate([own, coarse], axis=0)
+    outer, inner = outer_swap(own), inner_swap(own)
+
+    def on_chip(*values):
+        return [(value, pltpu.VMEM) for value in values]
+
+    def in_hbm(*values):
+        return [(value, pltpu.HBM) for value in values]
 
     def fine_buf(rows):
         return pltpu.VMEM((rows, FB + 2, SUB, LANES), BF)
@@ -537,44 +560,74 @@
     def coarse_buf(rows):
         return pltpu.VMEM((rows, CB + 2, SUB, 4 * LANES), BF)
 
+    place = [(where, pltpu.SMEM)]
     acc_buf = pltpu.VMEM((CB * SUB, 5 * LANES), F32)
-    packed = (CB // 2, SUB, 3 * LANES)
-
-    state_f, low_own, low_o, low_i = call(
+    flat = (9 * C2, 3 * C2)
+    big = pltpu.VMEM(flat, BF)
+
+    w_stem, w_enc, w_down, w_up, w_fc, w_head = call(
+        prepare_body,
+        "prepare",
+        on_chip(
+            enc_stem,
+            enc_fine_x.reshape(9, C1, 3 * C1),
+            enc_fine_h.reshape(9, C1, 3 * C1),
+            enc_down.reshape(9, C1, C2),
+            fc_up.reshape(9, C2, C1),
+            fc_fine_x.reshape(9, C1, 3 * C1),
+            fc_fine_h.reshape(9, C1, 3 * C1),
+            fc_head,
+        ),
+        [
+            (8 * PATCH, 8 * LANES),
+            (9 * LANES, 2 * LANES),
+            (9 * LANES, 2 * LANES),
+            (4 * C2, 2 * LANES),
+            (9 * LANES, 2 * LANES),
+            (8 * LANES, 8 * PATCH),
+        ],
+        [],
+    )
+    halo = (3 * ROW_TILES + FB, SUB, LANES)
+    state_f, low_own, to_outer, to_inner = call(
         fine_encoder_body,
         "fine_encoder",
-        [where, fine, fine_o, fine_i, patches, fr_o, fr_i, stem_weight(enc_stem), w_enc, down_weight(enc_down)],
-        [(4, FB // 2, SUB, LANES), (4,) + packed, (3,) + packed, (3,) + packed],
+        place + on_chip(own, outer, inner, w_stem, w_enc, w_down),
+        [(4, FB // 2, SUB, LANES), (4 * ROW_TILES, SUB, LANES), halo, halo],
         [fine_buf(9), fine_buf(9), fine_buf(9), pltpu.VMEM((9, FB, SUB, LANES), BF)],
     )
-    got_o, got_i = outer_swap(low_o), inner_swap(low_i)
-    state_fo, state_fi = outer_swap(state_f), inner_swap(state_f)
-
-    flat = (9 * C2, 3 * C2)
+    got_o, got_i = outer_swap(to_outer), inner_swap(to_inner)
+
     (state_c,) = call(
         coarse_encoder_body,
         "coarse_encoder",
-        [where, coarse, coarse_o, coarse_i, low_own, got_o, got_i, enc_coarse_x.reshape(flat), enc_coarse_h.reshape(flat)],
-        [(2,) + packed],
-        [coarse_buf(6), coarse_buf(4), coarse_buf(6), coarse_buf(4), acc_buf, acc_buf],
+        place
+        + on_chip(own, outer, inner, low_own, got_o, got_i)
+        + in_hbm(enc_coarse_x.reshape(flat), enc_coarse_h.reshape(flat)),
+        [(2 * ROW_TILES, SUB, LANES)],
+        [coarse_buf(6), coarse_buf(4), coarse_buf(6), coarse_buf(4), acc_buf, acc_buf, big, big,
+         pltpu.SemaphoreType.DMA((2,))],
     )
     state_ci = inner_swap(state_c)
-    near = jnp.where(section == 0, state_ci[0], state_ci[1])[None]
+    near = jnp.where(section == 0, state_ci[:ROW_TILES], state_ci[ROW_TILES:])
     send = jnp.where(
         section == 0,
         jnp.concatenate([state_c, near], axis=0),
         jnp.concatenate([near, state_c], axis=0),
     )
     state_co = outer_swap(send)
-    third = inner_swap(jnp.where(section == 0, state_co[2], state_co[0])[None])
+    third = inner_swap(jnp.where(section == 0, state_co[2 * ROW_TILES :], state_co[:ROW_TILES]))
 
     (out,) = call(
         forecaster_body,
         "forecaster",
-        [where, state_c, state_co, state_ci, third, state_f, state_fo, state_fi,
-         fc_coarse_h.reshape(flat), up_weight(fc_up), w_fc, head_weight(fc_head)],
+        place
+        + on_chip(state_c, state_co, state_ci, third, state_f, got_o, got_i)
+        + in_hbm(fc_coarse_h.reshape(flat))
+        + on_chip(w_up, w_fc, w_head),
         [(HORIZON, 4, SUB, FB * PATCH)],
-        [coarse_buf(8), coarse_buf(6), coarse_buf(5), fine_buf(8), fine_buf(6), fine_buf(4), acc_buf],
+        [coarse_buf(8), coarse_buf(6), coarse_buf(5), fine_buf(8), fine_buf(6), fine_buf(4), acc_buf, big,
+         pltpu.SemaphoreType.DMA],
     )
     return out.reshape(HORIZON, 4, COLS * PATCH)
 

time: 105 us -> 92 us (0.88)
  starting transfers between devices: 20.7 us -> 11.1 us
  local copies, waits for them, and re-layouts: 20 us -> 10.6 us
  waiting for transfers between devices: 17 us -> 25 us
  other arithmetic: 3.5 us -> 0.19 us
  Pallas kernels: 42.9 us -> 44.1 us
    ppermute x6 -> x3, starting transfers between devices: 19.1 us -> 10.1 us  [outer_swap(): return lax.ppermute(x, LINE, across)]
    ppermute x6 -> x3, waiting for transfers between devices: 15.6 us -> 22.3 us  [outer_swap(): return lax.ppermute(x, LINE, across)]
    unnamed x47 -> x38, local copies, waits for them, and re-layouts: 14.2 us -> 8.95 us
    concatenate x2 -> x1, other arithmetic: 2.45 us -> 0.04 us  [on_device(): own = jnp.concatenate([own, coarse], axis=0)]
    mul x1 -> x0, local copies, waits for them, and re-layouts: 1.79 us -> none  [head_weight(): eye[:, None, :, None] * tall[None, :, None, :]]
    ppermute x7 -> x4, waiting for transfers between devices: 1.44 us -> 2.71 us  [inner_swap(): return lax.ppermute(x, 'section', [(0, 1), (1, 0)])]
    pallas_call x3 -> x4, Pallas kernels: 42.9 us -> 44.1 us  [call(): pl.pallas_call(body, name=name, out_shape=[jax.ShapeDtypeStruct(s, BF) fo...]
    pad x3 -> x0, local copies, waits for them, and re-layouts: 1.1 us -> none  [the longest x1 1.02 us: down_weight(): jnp.pad(k, ((0, 0), (C1, 0), (0, 2 * LANES - C2)))]
  transfers between devices with their start and end apart: 13 -> 7, of which waited for: 4 -> 5; matrix products, arithmetic and copies ran while one was open for 14% -> 0% of each run, Pallas kernels for 0% -> 1%
where the time goes in v1:
time: 92 us; the launch traced here: 91.3 us
  Pallas kernels  44.1 us (48%)
  waiting for transfers between devices  25 us (27%)
  starting transfers between devices  11.1 us (12%)
  local copies, waits for them, and re-layouts  10.6 us (12%)
    pallas_call x4, Pallas kernels, call(): pl.pallas_call(body, name=name, out_shape=[jax.ShapeDtypeStruct(s, BF) fo...  44.1 us
    ppermute x3, waiting for transfers between devices, outer_swap(): return lax.ppermute(x, LINE, across)  22.3 us
    ppermute x3, starting transfers between devices, outer_swap(): return lax.ppermute(x, LINE, across)  10.1 us
    unnamed x38, local copies, waits for them, and re-layouts  8.95 us
    ppermute x4, waiting for transfers between devices, inner_swap(): return lax.ppermute(x, 'section', [(0, 1), (1, 0)])  2.71 us
  transfers between devices with their start and end apart: 7, of which 5 were waited for; matrix products, arithmetic and copies ran while one was open for 0% of the time, Pallas kernels for 1%

profile of v1, /device:TPU:19, one launch (start us, length us, event | category | flops | bytes accessed | tf_op | source)
XLA Modules:
  0.0 91.3 jit_solution(3487084265967747634)
XLA Ops:
  0.0 0.9 %fusion = (bf16[1,4,8192]{2,1,0:T(4,128)(2,1)S(1)}, bf16[1,4,8192]{2,1,0:T(4,128)(2,1)S(1)}) fusion(bf16[2,4,8192]{2,1,0:T(4,128)(2,1)} %param.14), kind=kLoop, calls=%fused_computation.9 | loop fusion | bytes 262144 | tf_op jit(solution)/shard_map/slice | solution.py:547
  0.9 0.0 copy-start.16
  0.9 0.0 copy-start.15
  0.9 1.0 %copy.26 = bf16[1,2,16,3072]{3,2,1,0:T(8,128)(2,1)S(1)} copy(bf16[1,2,16,3072]{3,1,2,0:T(2,128)(2,1)} %bitcast.43) | data formatting | bytes 393216
  2.0 1.1 %copy.25 = bf16[1,4,16,2048]{3,2,1,0:T(8,128)(2,1)S(1)} copy(bf16[1,4,16,2048]{3,1,2,0:T(4,128)(2,1)} %bitcast.40) | data formatting | bytes 524288
  3.1 0.0 copy-start.14
  3.2 0.7 collective-permute-start.1
  3.9 3.0 %collective-permute-start = (bf16[6,16,3072]{2,1,0:T(8,128)(2,1)S(1)}, bf16[6,16,3072]{2,1,0:T(8,128)(2,1)S(1)}, u32[]{:S(2)}, u32[]{:S(2)}) collective-permute-start(bf16[6,16,3072]{2,1,0:T(8,128)(2,1)S(1)} %pad_maximum_fusion.own), channel_id=1, source_target_pairs={{1,2},{3,4},{5,6},{7,8},{9,10},{11,12},{13,14},{2,1},{4,3},{6,5},{... | collective-permute-start | bytes 1769480 | tf_op jit(solution)/shard_map/ppermute | solution.py:539
  7.0 0.1 copy.16.head
  7.1 0.3 copy.15
  7.4 1.0 %copy-done.5 = bf16[3,3,64,192]{3,2,1,0:T(8,128)(2,1)S(1)} copy-done((bf16[3,3,64,192]{3,2,1,0:T(8,128)(2,1)S(1)}, bf16[3,3,64,192]{3,2,1,0:T(8,128)(2,1)}, u32[]{:S(2)}) %copy-start.5) | copy-done | bytes 221208
  8.3 1.0 %copy-done.6 = bf16[3,3,64,192]{3,2,1,0:T(8,128)(2,1)S(1)} copy-done((bf16[3,3,64,192]{3,2,1,0:T(8,128)(2,1)S(1)}, bf16[3,3,64,192]{3,2,1,0:T(8,128)(2,1)}, u32[]{:S(2)}) %copy-start.6) | copy-done | bytes 221208
  9.3 1.0 %copy-done.7 = bf16[3,3,64,192]{3,2,1,0:T(8,128)(2,1)S(1)} copy-done((bf16[3,3,64,192]{3,2,1,0:T(8,128)(2,1)S(1)}, bf16[3,3,64,192]{3,2,1,0:T(8,128)(2,1)}, u32[]{:S(2)}) %copy-start.7) | copy-done | bytes 221208
  10.2 1.0 %copy-done.8 = bf16[3,3,64,192]{3,2,1,0:T(8,128)(2,1)S(1)} copy-done((bf16[3,3,64,192]{3,2,1,0:T(8,128)(2,1)S(1)}, bf16[3,3,64,192]{3,2,1,0:T(8,128)(2,1)}, u32[]{:S(2)}) %copy-start.8) | copy-done | bytes 221208
  11.2 1.0 %copy-done.9 = bf16[3,3,64,192]{3,2,1,0:T(8,128)(2,1)S(1)} copy-done((bf16[3,3,64,192]{3,2,1,0:T(8,128)(2,1)S(1)}, bf16[3,3,64,192]{3,2,1,0:T(8,128)(2,1)}, u32[]{:S(2)}) %copy-start.9) | copy-done | bytes 221208
  12.2 0.5 prepare.1
  12.7 0.1 pad_add_fusion.where_ref
  12.8 8.7 %collective-permute-done.outer = bf16[6,16,3072]{2,1,0:T(8,128)(2,1)S(1)} collective-permute-done((bf16[6,16,3072]{2,1,0:T(8,128)(2,1)S(1)}, bf16[6,16,3072]{2,1,0:T(8,128)(2,1)S(1)}, u32[]{:S(2)}, u32[]{:S(2)}) %collective-permute-start) | collective-permute-done | bytes 589856 | tf_op jit(solution)/shard_map/ppermute | solution.py:539
  21.4 10.9 %fine_encoder.1 = (bf16[4,16,16,128]{3,2,1,0:T(8,128)(2,1)S(1)}, bf16[96,16,128]{2,1,0:T(8,128)(2,1)S(1)}, bf16[104,16,128]{2,1,0:T(8,128)(2,1)S(1)}, bf16[104,16,128]{2,1,0:T(8,128)(2,1)S(1)}) custom-call(s32[3]{0:T(128)S(1)} %pad_add_fusion.where_ref, bf16[6,16,3072]{2,1,0:T(8,128)(2,1)S(1)} %pad_maximum_fusion.own, ...), custom_call_target="tpu_custom_call" | custom-call | tf_op jit(solution)/shard_map/fine_encoder/pallas_call | solution.py:504
  32.4 3.1 %collective-permute-start.2 = (bf16[104,16,128]{2,1,0:T(8,128)(2,1)S(1)}, bf16[104,16,128]{2,1,0:T(8,128)(2,1)S(1)}, u32[]{:S(2)}, u32[]{:S(2)}) collective-permute-start(bf16[104,16,128]{2,1,0:T(8,128)(2,1)S(1)} %get-tuple-element.19), channel_id=1, source_target_pairs={{1,2},{3,4},{5,6},{7,8},{9,10},{11,12},{13,14},{2,1},{4,3},{6,5},{... | collective-permute-start | bytes 1277960 | tf_op jit(solution)/shard_map/ppermute | solution.py:539
  35.4 0.1 collective-permute-start.3
  35.5 6.3 %collective-permute-done.2.low_outer.f_outer = bf16[104,16,128]{2,1,0:T(8,128)(2,1)S(1)} collective-permute-done((bf16[104,16,128]{2,1,0:T(8,128)(2,1)S(1)}, bf16[104,16,128]{2,1,0:T(8,128)(2,1)S(1)}, u32[]{:S(2)}, u32[]{:S(2)}) %collective-permute-start.2) | collective-permute-done | bytes 426016 | tf_op jit(solution)/shard_map/ppermute | solution.py:539
  41.8 12.5 %coarse_encoder.1.c_own = bf16[48,16,128]{2,1,0:T(8,128)(2,1)S(1)} custom-call(s32[3]{0:T(128)S(1)} %pad_add_fusion.where_ref, bf16[6,16,3072]{2,1,0:T(8,128)(2,1)S(1)} %pad_maximum_fusion.own, bf16[6,16,3072]{2,1,0:T(8,128)(2,1)S(1)} %collective-permute-done.outer, bf16[6,16,3072]{2,1,0:T(8,128)(2,1)S(1)} %collective-permute-done.1.inner, ...), custom_call_target="tpu_custom_call" | custom-call | tf_op jit(solution)/shard_map/coarse_encoder/pallas_call | solution.py:504
  54.3 0.1 collective-permute-start.4
  54.4 1.4 %collective-permute-done.4.c_inner = bf16[48,16,128]{2,1,0:T(8,128)(2,1)S(1)} collective-permute-done((bf16[48,16,128]{2,1,0:T(8,128)(2,1)S(1)}, bf16[48,16,128]{2,1,0:T(8,128)(2,1)S(1)}, u32[]{:S(2)}, u32[]{:S(2)}) %collective-permute-start.4) | collective-permute-done | bytes 196640 | tf_op jit(solution)/shard_map/ppermute | solution.py:542
  55.9 4.0 %collective-permute-start.5 = (bf16[72,16,128]{2,1,0:T(8,128)(2,1)S(1)}, bf16[72,16,128]{2,1,0:T(8,128)(2,1)S(1)}, u32[]{:S(2)}, u32[]{:S(2)}) collective-permute-start(bf16[72,16,128]{2,1,0:T(8,128)(2,1)S(1)} %maximum_select_fusion), channel_id=1, source_target_pairs={{1,2},{3,4},{5,6},{7,8},{9,10},{11,12},{13,14},{2,1},{4,3},{6,5},{... | collective-permute-start | bytes 884744 | tf_op jit(solution)/shard_map/ppermute | solution.py:539
  60.0 7.4 %collective-permute-done.5.c_outer = bf16[72,16,128]{2,1,0:T(8,128)(2,1)S(1)} collective-permute-done((bf16[72,16,128]{2,1,0:T(8,128)(2,1)S(1)}, bf16[72,16,128]{2,1,0:T(8,128)(2,1)S(1)}, u32[]{:S(2)}, u32[]{:S(2)}) %collective-permute-start.5) | collective-permute-done | bytes 294944 | tf_op jit(solution)/shard_map/ppermute | solution.py:539
  67.4 0.1 collective-permute-start.6
  67.4 1.3 %collective-permute-done.6.c_third = bf16[24,16,128]{2,1,0:T(8,128)(2,1)S(1)} collective-permute-done((bf16[24,16,128]{2,1,0:T(8,128)(2,1)S(1)}, bf16[24,16,128]{2,1,0:T(8,128)(2,1)S(1)}, u32[]{:S(2)}, u32[]{:S(2)}) %collective-permute-start.6) | collective-permute-done | bytes 98336 | tf_op jit(solution)/shard_map/ppermute | solution.py:542
  68.7 1.6 %copy-done.2 = bf16[3,3,192,576]{3,2,1,0:T(8,128)(2,1)S(1)} copy-done((bf16[3,3,192,576]{3,2,1,0:T(8,128)(2,1)S(1)}, bf16[3,3,192,576]{3,2,1,0:T(8,128)(2,1)}, u32[]{:S(2)}) %copy-start.2) | copy-done | bytes 1990680
  70.4 20.2 %forecaster.1 = bf16[2,4,16,512]{3,2,1,0:T(8,128)(2,1)S(1)} custom-call(s32[3]{0:T(128)S(1)} %pad_add_fusion.where_ref, bf16[48,16,128]{2,1,0:T(8,128)(2,1)S(1)} %coarse_encoder.1.c_own, bf16[72,16,128]{2,1,0:T(8,128)(2,1)S(1)} %collective-permute-done.5.c_outer, bf16[48,16,128]{2,1,0:T(8,128)(2,1)S(1)} %collective-permute-done.4.c_inner, ...), custom_call_target="tpu_custom_call" | custom-call | tf_op jit(solution)/shard_map/forecaster/pallas_call | solution.py:504
  90.6 0.7 reshape.52
  (32 shorter events, 0.2 us)
Async XLA Ops:
  0.9 6.0 %copy-start.16 = (bf16[64,16]{0,1:T(8,128)(2,1)S(1)}, bf16[64,16]{0,1:T(8,128)(2,1)}, u32[]{:S(2)}) copy-start(bf16[64,16]{0,1:T(8,128)(2,1)} %param.27) | copy-start | bytes 6148
  0.9 6.1 %copy-start.15 = (bf16[3,3,192,64]{2,3,1,0:T(8,128)(2,1)S(1)}, bf16[3,3,192,64]{2,3,1,0:T(8,128)(2,1)}, u32[]{:S(2)}) copy-start(bf16[3,3,192,64]{2,3,1,0:T(8,128)(2,1)} %param.24) | copy-start | bytes 663556
  3.1 4.3 %copy-start.14 = (bf16[16,64]{1,0:T(8,128)(2,1)S(1)}, bf16[16,64]{1,0:T(8,128)(2,1)}, u32[]{:S(2)}) copy-start(bf16[16,64]{1,0:T(8,128)(2,1)} %stem.1) | copy-start | bytes 6148
  3.2 9.6 %collective-permute-start.1 = (bf16[6,16,3072]{2,1,0:T(8,128)(2,1)S(1)}, bf16[6,16,3072]{2,1,0:T(8,128)(2,1)S(1)}, u32[]{:S(2)}, u32[]{:S(2)}) collective-permute-start(bf16[6,16,3072]{2,1,0:T(8,128)(2,1)S(1)} %pad_maximum_fusion.own), channel_id=1, source_target_pairs={{0,1},{1,0},{2,3},{3,2},{4,5},{5,4},{6,7},{7,6},{8,9},{9,8},{10,11... | collective-permute-start | bytes 1769480 | tf_op jit(solution)/shard_map/ppermute | solution.py:542
  3.9 17.5 %collective-permute-start = (bf16[6,16,3072]{2,1,0:T(8,128)(2,1)S(1)}, bf16[6,16,3072]{2,1,0:T(8,128)(2,1)S(1)}, u32[]{:S(2)}, u32[]{:S(2)}) collective-permute-start(bf16[6,16,3072]{2,1,0:T(8,128)(2,1)S(1)} %pad_maximum_fusion.own), channel_id=1, source_target_pairs={{1,2},{3,4},{5,6},{7,8},{9,10},{11,12},{13,14},{2,1},{4,3},{6,5},{... | collective-permute-start | bytes 1769480 | tf_op jit(solution)/shard_map/ppermute | solution.py:539
  7.3 1.0 %copy-start.5 = (bf16[3,3,64,192]{3,2,1,0:T(8,128)(2,1)S(1)}, bf16[3,3,64,192]{3,2,1,0:T(8,128)(2,1)}, u32[]{:S(2)}) copy-start(bf16[3,3,64,192]{3,2,1,0:T(8,128)(2,1)} %param.18) | copy-start | bytes 663556
  8.3 1.0 %copy-start.6 = (bf16[3,3,64,192]{3,2,1,0:T(8,128)(2,1)S(1)}, bf16[3,3,64,192]{3,2,1,0:T(8,128)(2,1)}, u32[]{:S(2)}) copy-start(bf16[3,3,64,192]{3,2,1,0:T(8,128)(2,1)} %param.19) | copy-start | bytes 663556
  9.3 1.0 %copy-start.7 = (bf16[3,3,64,192]{3,2,1,0:T(8,128)(2,1)S(1)}, bf16[3,3,64,192]{3,2,1,0:T(8,128)(2,1)}, u32[]{:S(2)}) copy-start(bf16[3,3,64,192]{3,2,1,0:T(8,128)(2,1)} %param.20) | copy-start | bytes 663556
  10.2 1.0 %copy-start.8 = (bf16[3,3,64,192]{3,2,1,0:T(8,128)(2,1)S(1)}, bf16[3,3,64,192]{3,2,1,0:T(8,128)(2,1)}, u32[]{:S(2)}) copy-start(bf16[3,3,64,192]{3,2,1,0:T(8,128)(2,1)} %param.25) | copy-start | bytes 663556
  11.2 1.0 %copy-start.9 = (bf16[3,3,64,192]{3,2,1,0:T(8,128)(2,1)S(1)}, bf16[3,3,64,192]{3,2,1,0:T(8,128)(2,1)}, u32[]{:S(2)}) copy-start(bf16[3,3,64,192]{3,2,1,0:T(8,128)(2,1)} %param.26) | copy-start | bytes 663556
  12.2 29.7 %copy-start.1 = (bf16[3,3,192,576]{3,2,1,0:T(8,128)(2,1)S(1)}, bf16[3,3,192,576]{3,2,1,0:T(8,128)(2,1)}, u32[]{:S(2)}) copy-start(bf16[3,3,192,576]{3,2,1,0:T(8,128)(2,1)} %param.22) | copy-start | bytes 5971972
  12.7 19.7 %copy-start.3 = (bf16[768,256]{1,0:T(8,128)(2,1)}, bf16[768,256]{1,0:T(8,128)(2,1)S(1)}, u32[]{:S(2)}) copy-start(bf16[768,256]{1,0:T(8,128)(2,1)S(1)} %get-tuple-element.22.w_up) | copy-start | bytes 1179652
  12.7 19.7 %copy-start.10 = (bf16[1024,128]{1,0:T(8,128)(2,1)}, bf16[1024,128]{1,0:T(8,128)(2,1)S(1)}, u32[]{:S(2)}) copy-start(bf16[1024,128]{1,0:T(8,128)(2,1)S(1)} %get-tuple-element.24.w_head) | copy-start | bytes 786436
  21.4 20.4 %copy-start = (bf16[3,3,192,576]{3,2,1,0:T(8,128)(2,1)S(1)}, bf16[3,3,192,576]{3,2,1,0:T(8,128)(2,1)}, u32[]{:S(2)}) copy-start(bf16[3,3,192,576]{3,2,1,0:T(8,128)(2,1)} %param.21) | copy-start | bytes 5971972
  32.4 22.0 %copy-start.12 = (bf16[4,16,16,128]{3,2,1,0:T(8,128)(2,1)}, bf16[4,16,16,128]{3,2,1,0:T(8,128)(2,1)S(1)}, u32[]{:S(2)}) copy-start(bf16[4,16,16,128]{3,2,1,0:T(8,128)(2,1)S(1)} %get-tuple-element.21.f_own) | copy-start | bytes 786436
  32.4 9.4 %collective-permute-start.2 = (bf16[104,16,128]{2,1,0:T(8,128)(2,1)S(1)}, bf16[104,16,128]{2,1,0:T(8,128)(2,1)S(1)}, u32[]{:S(2)}, u32[]{:S(2)}) collective-permute-start(bf16[104,16,128]{2,1,0:T(8,128)(2,1)S(1)} %get-tuple-element.19), channel_id=1, source_target_pairs={{1,2},{3,4},{5,6},{7,8},{9,10},{11,12},{13,14},{2,1},{4,3},{6,5},{... | collective-permute-start | bytes 1277960 | tf_op jit(solution)/shard_map/ppermute | solution.py:539
  35.4 6.4 %collective-permute-start.3 = (bf16[104,16,128]{2,1,0:T(8,128)(2,1)S(1)}, bf16[104,16,128]{2,1,0:T(8,128)(2,1)S(1)}, u32[]{:S(2)}, u32[]{:S(2)}) collective-permute-start(bf16[104,16,128]{2,1,0:T(8,128)(2,1)S(1)} %get-tuple-element.20), channel_id=1, source_target_pairs={{0,1},{1,0},{2,3},{3,2},{4,5},{5,4},{6,7},{7,6},{8,9},{9,8},{10,11... | collective-permute-start | bytes 1277960 | tf_op jit(solution)/shard_map/ppermute | solution.py:542
  54.3 14.4 %copy-start.4 = (bf16[768,256]{1,0:T(8,128)(2,1)S(1)}, bf16[768,256]{1,0:T(8,128)(2,1)}, u32[]{:S(2)}) copy-start(bf16[768,256]{1,0:T(8,128)(2,1)} %copy-done.3) | copy-start | bytes 1179652
  54.3 14.4 %copy-start.11 = (bf16[1024,128]{1,0:T(8,128)(2,1)S(1)}, bf16[1024,128]{1,0:T(8,128)(2,1)}, u32[]{:S(2)}) copy-start(bf16[1024,128]{1,0:T(8,128)(2,1)} %copy-done.10) | copy-start | bytes 786436
  54.3 1.5 %collective-permute-start.4 = (bf16[48,16,128]{2,1,0:T(8,128)(2,1)S(1)}, bf16[48,16,128]{2,1,0:T(8,128)(2,1)S(1)}, u32[]{:S(2)}, u32[]{:S(2)}) collective-permute-start(bf16[48,16,128]{2,1,0:T(8,128)(2,1)S(1)} %coarse_encoder.1.c_own), channel_id=1, source_target_pairs={{0,1},{1,0},{2,3},{3,2},{4,5},{5,4},{6,7},{7,6},{8,9},{9,8},{10,11... | collective-permute-start | bytes 589832 | tf_op jit(solution)/shard_map/ppermute | solution.py:542
  54.4 14.3 %copy-start.13 = (bf16[4,16,16,128]{3,2,1,0:T(8,128)(2,1)S(1)}, bf16[4,16,16,128]{3,2,1,0:T(8,128)(2,1)}, u32[]{:S(2)}) copy-start(bf16[4,16,16,128]{3,2,1,0:T(8,128)(2,1)} %copy-done.12) | copy-start | bytes 786436
  55.9 11.4 %collective-permute-start.5 = (bf16[72,16,128]{2,1,0:T(8,128)(2,1)S(1)}, bf16[72,16,128]{2,1,0:T(8,128)(2,1)S(1)}, u32[]{:S(2)}, u32[]{:S(2)}) collective-permute-start(bf16[72,16,128]{2,1,0:T(8,128)(2,1)S(1)} %maximum_select_fusion), channel_id=1, source_target_pairs={{1,2},{3,4},{5,6},{7,8},{9,10},{11,12},{13,14},{2,1},{4,3},{6,5},{... | collective-permute-start | bytes 884744 | tf_op jit(solution)/shard_map/ppermute | solution.py:539
  67.4 1.4 %collective-permute-start.6 = (bf16[24,16,128]{2,1,0:T(8,128)(2,1)S(1)}, bf16[24,16,128]{2,1,0:T(8,128)(2,1)S(1)}, u32[]{:S(2)}, u32[]{:S(2)}) collective-permute-start(bf16[24,16,128]{2,1,0:T(8,128)(2,1)S(1)} %slice_select_fusion), channel_id=1, source_target_pairs={{0,1},{1,0},{2,3},{3,2},{4,5},{5,4},{6,7},{7,6},{8,9},{9,8},{10,11... | collective-permute-start | bytes 294920 | tf_op jit(solution)/shard_map/ppermute | solution.py:542
  68.7 1.6 %copy-start.2 = (bf16[3,3,192,576]{3,2,1,0:T(8,128)(2,1)S(1)}, bf16[3,3,192,576]{3,2,1,0:T(8,128)(2,1)}, u32[]{:S(2)}) copy-start(bf16[3,3,192,576]{3,2,1,0:T(8,128)(2,1)} %param.23) | copy-start | bytes 5971972

commit v2 on v1

--- a/solution.py
+++ b/solution.py
@@ -4,6 +4,7 @@
 from jax.experimental import pallas as pl
 from jax.experimental.pallas import tpu as pltpu
 from jax.sharding import PartitionSpec as P
+
 
 C1 = 64
 C2 = 192
@@ -154,7 +155,8 @@
 
 def coarse_gru(x_ref, x_idx, h_ref, h_idx, w_x, w_h, acc_x, acc_h, valid):
     width = 3 * C2
-    acc_h[:, :width] = jnp.dot(coarse_patches(h_ref, h_idx), w_h[...], preferred_element_type=F32)
+    if w_h is not None:
+        acc_h[:, :width] = jnp.dot(coarse_patches(h_ref, h_idx), w_h[...], preferred_element_type=F32)
     if x_ref is not None:
         acc_x[:, :width] = jnp.dot(coarse_patches(x_ref, x_idx), w_x[...], preferred_element_type=F32)
 
@@ -188,7 +190,7 @@
 
 def fine_encoder_body(
     where_ref, own, outer, inner, w_stem, w_gru, w_down,
-    state_out, low_own, to_outer, to_inner, p1, p2, p3, stem2,
+    state_out, low_own, to_outer, to_inner, state_outer, state_inner, p1, p2, p3, stem2,
 ):
     upper = where_ref[0] == 0
     first = where_ref[1] * 4
@@ -198,7 +200,7 @@
     def pick(idx, lanes):
         if 3 <= idx < 7:
             return own[idx - 3, :, lanes]
-        r = idx + 1 if idx < 3 else idx - 7
+        r = idx if idx < 3 else idx - 7
         a, b = outer[r, :, lanes], inner[r, :, lanes]
         return jnp.where(upper, a, b) if idx < 3 else jnp.where(upper, b, a)
 
@@ -270,11 +272,10 @@
     for r in range(4):
         for k in range(FB // 2):
             state_out[r, k] = jnp.where(lo[0], swap_bf(p3[3 + r, 1 + 2 * k]), p3[3 + r, 2 + 2 * k])
-    base = 3 * ROW_TILES
-    for top, ref in ((upper, to_outer), (jnp.logical_not(upper), to_inner)):
+    for top, ref in ((upper, state_outer), (jnp.logical_not(upper), state_inner)):
         start = jnp.where(top, 0, 2)
         for r in range(2):
-            ref[base + r * FB // 2 : base + (r + 1) * FB // 2] = state_out[start + r]
+            ref[r] = state_out[start + r]
 
 
 def zero_tail(acc):
@@ -285,49 +286,57 @@
     return lambda i: ref[at * ROW_TILES + i * PAIRS : at * ROW_TILES + (i + 1) * PAIRS]
 
 
+def raw_tiles(get):
+    def tiles(i):
+        return jnp.stack([get(slice((3 * k + i) * LANES, (3 * k + i + 1) * LANES)) for k in range(PAIRS)])
+
+    return tiles
+
+
+def coarse_state_body(where_ref, own, outer, inner, w_h, acc_out, h_out, h0):
+    upper = where_ref[0] == 0
+    for idx in range(6):
+        if 2 <= idx < 4:
+            put_packed(h0, idx, raw_tiles(lambda lanes: own[idx - 2, :, lanes]))
+            continue
+        r = idx if idx < 2 else idx - 4
+        a, b = (outer, inner) if idx < 2 else (inner, outer)
+        put_packed(h0, idx, raw_tiles(lambda lanes: jnp.where(upper, a[r, :, lanes], b[r, :, lanes])))
+
+    @pl.loop(0, 4)
+    def _(idx):
+        acc_out[idx, :, : 3 * C2] = jnp.dot(coarse_patches(h0, idx + 1), w_h[...], preferred_element_type=F32)
+        acc_out[idx, :, 4 * LANES + C1 :] = jnp.zeros((CB * SUB, C1), F32)
+        h_out[idx] = h0[idx + 1]
+
+
 def coarse_encoder_body(
-    where_ref, own, outer, inner, low_own, low_outer, low_inner, w_x_hbm, w_h_hbm,
-    state_out, x1, x2, h0, h1, acc_x, acc_h, w_x, w_h, sems,
+    where_ref, low_own, low_outer, low_inner, acc_first, h_first, w_x, w_h,
+    state_out, x1, x2, h1, acc_x, acc_h,
 ):
-    fetch_h = pltpu.make_async_copy(w_h_hbm, w_h, sems.at[0])
-    fetch_x = pltpu.make_async_copy(w_x_hbm, w_x, sems.at[1])
-    fetch_h.start()
-    fetch_x.start()
     upper = where_ref[0] == 0
     first = where_ref[1] * 2
     rows = where_ref[2] * 2
     zero_tail(acc_x)
     zero_tail(acc_h)
 
-    def raw_tiles(get):
-        def tiles(i):
-            return jnp.stack([get(slice((3 * k + i) * LANES, (3 * k + i + 1) * LANES)) for k in range(CB // 2)])
-
-        return tiles
-
     for idx in range(6):
         if 2 <= idx < 4:
-            put_packed(h0, idx, raw_tiles(lambda lanes: own[2 + idx, :, lanes]))
             put_packed(x1, idx, packed_tiles(low_own, idx - 2))
             continue
         r = idx if idx < 2 else idx - 4
-        first_ref, second_ref = (outer, inner) if idx < 2 else (inner, outer)
-        put_packed(
-            h0, idx, raw_tiles(lambda lanes: jnp.where(upper, first_ref[4 + r, :, lanes], second_ref[4 + r, :, lanes]))
-        )
-        low_a, low_b = (low_outer, low_inner) if idx < 2 else (low_inner, low_outer)
-        put_packed(x1, idx, lambda i: jnp.where(upper, packed_tiles(low_a, r)(i), packed_tiles(low_b, r)(i)))
+        a, b = (low_outer, low_inner) if idx < 2 else (low_inner, low_outer)
+        put_packed(x1, idx, lambda i: jnp.where(upper, packed_tiles(a, r)(i), packed_tiles(b, r)(i)))
     put_packed(x2, 1, packed_tiles(low_own, 2))
     put_packed(x2, 2, packed_tiles(low_own, 3))
     put_packed(x2, 0, lambda i: jnp.where(upper, packed_tiles(low_outer, 2)(i), packed_tiles(low_inner, 2)(i)))
     put_packed(x2, 3, lambda i: jnp.where(upper, packed_tiles(low_inner, 2)(i), packed_tiles(low_outer, 2)(i)))
 
-    fetch_h.wait()
-    fetch_x.wait()
-
     @pl.loop(0, 4)
     def _(idx):
-        forms = coarse_gru(x1, idx + 1, h0, idx + 1, w_x, w_h, acc_x, acc_h, in_grid(first + idx - 1, rows))
+        forms = coarse_gru(
+            x1, idx + 1, h_first, idx, w_x, None, acc_x, acc_first.at[idx], in_grid(first + idx - 1, rows)
+        )
         put_forms(h1, idx, forms)
 
     @pl.loop(0, 2)
@@ -349,11 +358,9 @@
 
 
 def forecaster_body(
-    where_ref, c_own, c_outer, c_inner, c_third, f_own, f_outer, f_inner, w_h_hbm, w_up, w_gru, w_head,
-    out, h2, s1, s2, pf1, pf2, states, acc_h, w_h, sem,
+    where_ref, c_own, c_outer, c_inner, c_third, f_own, f_outer, f_inner, w_h, w_up, w_gru, w_head,
+    out, h2, s1, s2, pf1, pf2, states, acc_h,
 ):
-    fetch_h = pltpu.make_async_copy(w_h_hbm, w_h, sem)
-    fetch_h.start()
     upper = where_ref[0] == 0
     first_c = where_ref[1] * 2
     rows_c = where_ref[2] * 2
@@ -375,20 +382,16 @@
     put_packed(h2, 6, either(packed_tiles(c_inner, 1), packed_tiles(c_outer, 1)))
     put_packed(h2, 7, either(packed_tiles(c_third, 0), packed_tiles(c_outer, 2)))
 
-    base = 3 * ROW_TILES
     for idx in range(8):
         for k in range(FB // 2):
             if 2 <= idx < 6:
                 pair = f_own[idx - 2, k]
             elif idx < 2:
-                pair = jnp.where(upper, f_outer[base + idx * FB // 2 + k], f_inner[base + idx * FB // 2 + k])
+                pair = jnp.where(upper, f_outer[idx, k], f_inner[idx, k])
             else:
-                at = base + (idx - 6) * FB // 2 + k
-                pair = jnp.where(upper, f_inner[at], f_outer[at])
+                pair = jnp.where(upper, f_inner[idx - 6, k], f_outer[idx - 6, k])
             pf1[idx, 1 + 2 * k] = swap_bf(pair)
             pf1[idx, 2 + 2 * k] = pair
-
-    fetch_h.wait()
 
     @pl.loop(0, 6)
     def _(idx):
@@ -500,11 +503,10 @@
         w_head[k * LANES + C1 : (k + 1) * LANES, k * PATCH : (k + 1) * PATCH] = head[...]
 
 
-def call(body, name, args, outs, scratch):
+def call(body, args, outs, scratch):
     return pl.pallas_call(
         body,
-        name=name,
-        out_shape=[jax.ShapeDtypeStruct(s, BF) for s in outs],
+        out_shape=[s if isinstance(s, jax.ShapeDtypeStruct) else jax.ShapeDtypeStruct(s, BF) for s in outs],
         in_specs=[pl.BlockSpec(memory_space=space) for _, space in args],
         out_specs=[pl.BlockSpec(memory_space=pltpu.VMEM)] * len(outs),
         scratch_shapes=scratch,
@@ -545,14 +547,11 @@
     patches = frames.reshape(FRAMES, 4, SUB, FB * PATCH)
     coarse = start_coarse.reshape(2, SUB, CB * C2)
     own = jnp.concatenate([fine, patches[0], patches[1]], axis=-1)
-    own = jnp.concatenate([own, coarse], axis=0)
-    outer, inner = outer_swap(own), inner_swap(own)
+    outer = outer_swap(lax.dynamic_slice_in_dim(own, section, 3, 0))
+    inner = inner_swap(lax.dynamic_slice_in_dim(own, 1 - section, 3, 0))
 
     def on_chip(*values):
         return [(value, pltpu.VMEM) for value in values]
-
-    def in_hbm(*values):
-        return [(value, pltpu.HBM) for value in values]
 
     def fine_buf(rows):
         return pltpu.VMEM((rows, FB + 2, SUB, LANES), BF)
@@ -563,11 +562,9 @@
     place = [(where, pltpu.SMEM)]
     acc_buf = pltpu.VMEM((CB * SUB, 5 * LANES), F32)
     flat = (9 * C2, 3 * C2)
-    big = pltpu.VMEM(flat, BF)
 
     w_stem, w_enc, w_down, w_up, w_fc, w_head = call(
         prepare_body,
-        "prepare",
         on_chip(
             enc_stem,
             enc_fine_x.reshape(9, C1, 3 * C1),
@@ -588,25 +585,32 @@
         ],
         [],
     )
-    halo = (3 * ROW_TILES + FB, SUB, LANES)
-    state_f, low_own, to_outer, to_inner = call(
+    coarse_o, coarse_i = outer_swap(coarse), inner_swap(coarse)
+
+    halo = (3 * ROW_TILES, SUB, LANES)
+    edge = (2, FB // 2, SUB, LANES)
+    state_f, low_own, to_outer, to_inner, state_fo, state_fi = call(
         fine_encoder_body,
-        "fine_encoder",
         place + on_chip(own, outer, inner, w_stem, w_enc, w_down),
-        [(4, FB // 2, SUB, LANES), (4 * ROW_TILES, SUB, LANES), halo, halo],
+        [(4, FB // 2, SUB, LANES), (4 * ROW_TILES, SUB, LANES), halo, halo, edge, edge],
         [fine_buf(9), fine_buf(9), fine_buf(9), pltpu.VMEM((9, FB, SUB, LANES), BF)],
     )
     got_o, got_i = outer_swap(to_outer), inner_swap(to_inner)
+
+    acc_first, h_first = call(
+        coarse_state_body,
+        place + on_chip(coarse, coarse_o, coarse_i, enc_coarse_h.reshape(flat)),
+        [jax.ShapeDtypeStruct((4, CB * SUB, 5 * LANES), F32), (4, CB + 2, SUB, 4 * LANES)],
+        [coarse_buf(6)],
+    )
+    state_fo, state_fi = outer_swap(state_fo), inner_swap(state_fi)
 
     (state_c,) = call(
         coarse_encoder_body,
-        "coarse_encoder",
         place
-        + on_chip(own, outer, inner, low_own, got_o, got_i)
-        + in_hbm(enc_coarse_x.reshape(flat), enc_coarse_h.reshape(flat)),
+        + on_chip(low_own, got_o, got_i, acc_first, h_first, enc_coarse_x.reshape(flat), enc_coarse_h.reshape(flat)),
         [(2 * ROW_TILES, SUB, LANES)],
-        [coarse_buf(6), coarse_buf(4), coarse_buf(6), coarse_buf(4), acc_buf, acc_buf, big, big,
-         pltpu.SemaphoreType.DMA((2,))],
+        [coarse_buf(6), coarse_buf(4), coarse_buf(4), acc_buf, acc_buf],
     )
     state_ci = inner_swap(state_c)
     near = jnp.where(section == 0, state_ci[:ROW_TILES], state_ci[ROW_TILES:])
@@ -620,14 +624,11 @@
 
     (out,) = call(
         forecaster_body,
-        "forecaster",
         place
-        + on_chip(state_c, state_co, state_ci, third, state_f, got_o, got_i)
-        + in_hbm(fc_coarse_h.reshape(flat))
+        + on_chip(state_c, state_co, state_ci, third, state_f, state_fo, state_fi, fc_coarse_h.reshape(flat))
         + on_chip(w_up, w_fc, w_head),
         [(HORIZON, 4, SUB, FB * PATCH)],
-        [coarse_buf(8), coarse_buf(6), coarse_buf(5), fine_buf(8), fine_buf(6), fine_buf(4), acc_buf, big,
-         pltpu.SemaphoreType.DMA],
+        [coarse_buf(8), coarse_buf(6), coarse_buf(5), fine_buf(8), fine_buf(6), fine_buf(4), acc_buf],
     )
     return out.reshape(HORIZON, 4, COLS * PATCH)
 

time: 92 us -> 93.7 us (1.018)
  starting transfers between devices: 11.1 us -> 17 us
  waiting for transfers between devices: 25 us -> 19.6 us
    ppermute x3 -> x5, starting transfers between devices: 10.1 us -> 15.2 us  [outer_swap(): return lax.ppermute(x, LINE, across)]
    ppermute x3 -> x5, waiting for transfers between devices: 22.3 us -> 18.1 us  [outer_swap(): return lax.ppermute(x, LINE, across)]
    ppermute x4 -> x6, waiting for transfers between devices: 2.71 us -> 1.44 us  [inner_swap(): return lax.ppermute(x, 'section', [(0, 1), (1, 0)])]
    unnamed x38 -> x41, local copies, waits for them, and re-layouts: 8.95 us -> 8.31 us
    pallas_call x4 -> x5, Pallas kernels: 44.1 us -> 44.7 us  [call(): pl.pallas_call(body, out_shape=[s if isinstance(s, jax.ShapeDtypeStruct)...]
  transfers between devices with their start and end apart: 7 -> 11, of which waited for: 5 -> 5; matrix products, arithmetic and copies ran while one was open for 0% -> 1% of each run, Pallas kernels for 1% -> 5%
where the time goes in v2:
time: 93.7 us; the launch traced here: 92.6 us
  Pallas kernels  44.7 us (48%)
  waiting for transfers between devices  19.6 us (21%)
  starting transfers between devices  17 us (18%)
  local copies, waits for them, and re-layouts  10.9 us (12%)
    pallas_call x5, Pallas kernels, call(): pl.pallas_call(body, out_shape=[s if isinstance(s, jax.ShapeDtypeStruct)...  44.7 us
    ppermute x5, waiting for transfers between devices, outer_swap(): return lax.ppermute(x, LINE, across)  18.1 us
    ppermute x5, starting transfers between devices, outer_swap(): return lax.ppermute(x, LINE, across)  15.2 us
    unnamed x41, local copies, waits for them, and re-layouts  8.31 us
  transfers between devices with their start and end apart: 11, of which 5 were waited for; matrix products, arithmetic and copies ran while one was open for 1% of the time, Pallas kernels for 5%

profile of v2, /device:TPU:19, one launch (start us, length us, event | category | flops | bytes accessed | tf_op | source)
XLA Modules:
  0.0 92.6 jit_solution(13368212067408642495)
XLA Ops:
  0.0 1.0 %fusion = (bf16[1,4,8192]{2,1,0:T(4,128)(2,1)S(1)}, bf16[1,4,8192]{2,1,0:T(4,128)(2,1)S(1)}) fusion(bf16[2,4,8192]{2,1,0:T(4,128)(2,1)} %param.14), kind=kLoop, calls=%fused_computation.10 | loop fusion | bytes 262144 | tf_op jit(solution)/shard_map/slice | solution.py:549
  1.0 1.1 %bitcast_dynamic-update-slice_fusion = bf16[4,16,3072]{2,1,0:T(8,128)(2,1)S(1)} fusion(bf16[1,4,16,2048]{3,1,2,0:T(4,128)(2,1)} %bitcast.41), kind=kLoop, calls=%fused_computation.1 | loop fusion | bytes 524288
  2.2 0.9 constant_dynamic-slice_fusion
  3.0 0.7 collective-permute-start.1
  3.7 3.0 %collective-permute-start = (bf16[3,16,3072]{2,1,0:T(8,128)(2,1)}, bf16[3,16,3072]{2,1,0:T(8,128)(2,1)S(1)}, u32[]{:S(2)}, u32[]{:S(2)}) collective-permute-start(bf16[3,16,3072]{2,1,0:T(8,128)(2,1)} %get-tuple-element.34), channel_id=1, source_target_pairs={{1,2},{3,4},{5,6},{7,8},{9,10},{11,12},{13,14},{2,1},{4,3},{6,5},{... | collective-permute-start | bytes 884744 | tf_op jit(solution)/shard_map/ppermute | solution.py:541
  6.8 0.1 copy.16.head
  6.9 0.3 copy.15
  7.2 1.0 %copy-done.6 = bf16[3,3,64,192]{3,2,1,0:T(8,128)(2,1)S(1)} copy-done((bf16[3,3,64,192]{3,2,1,0:T(8,128)(2,1)S(1)}, bf16[3,3,64,192]{3,2,1,0:T(8,128)(2,1)}, u32[]{:S(2)}) %copy-start.6) | copy-done | bytes 221208
  8.2 1.0 %copy-done.7 = bf16[3,3,64,192]{3,2,1,0:T(8,128)(2,1)S(1)} copy-done((bf16[3,3,64,192]{3,2,1,0:T(8,128)(2,1)S(1)}, bf16[3,3,64,192]{3,2,1,0:T(8,128)(2,1)}, u32[]{:S(2)}) %copy-start.7) | copy-done | bytes 221208
  9.1 1.0 %copy-done.8 = bf16[3,3,64,192]{3,2,1,0:T(8,128)(2,1)S(1)} copy-done((bf16[3,3,64,192]{3,2,1,0:T(8,128)(2,1)S(1)}, bf16[3,3,64,192]{3,2,1,0:T(8,128)(2,1)}, u32[]{:S(2)}) %copy-start.8) | copy-done | bytes 221208
  10.1 1.0 %copy-done.9 = bf16[3,3,64,192]{3,2,1,0:T(8,128)(2,1)S(1)} copy-done((bf16[3,3,64,192]{3,2,1,0:T(8,128)(2,1)S(1)}, bf16[3,3,64,192]{3,2,1,0:T(8,128)(2,1)}, u32[]{:S(2)}) %copy-start.9) | copy-done | bytes 221208
  11.0 0.5 shard_map.136
  11.6 0.1 pad_add_fusion.where_ref
  11.6 3.5 %collective-permute-done.outer = bf16[3,16,3072]{2,1,0:T(8,128)(2,1)S(1)} collective-permute-done((bf16[3,16,3072]{2,1,0:T(8,128)(2,1)}, bf16[3,16,3072]{2,1,0:T(8,128)(2,1)S(1)}, u32[]{:S(2)}, u32[]{:S(2)}) %collective-permute-start) | collective-permute-done | bytes 294944 | tf_op jit(solution)/shard_map/ppermute | solution.py:541
  15.1 10.9 %shard_map.137 = (bf16[4,16,16,128]{3,2,1,0:T(8,128)(2,1)S(1)}, bf16[96,16,128]{2,1,0:T(8,128)(2,1)S(1)}, bf16[72,16,128]{2,1,0:T(8,128)(2,1)S(1)}, bf16[72,16,1...) custom-call(s32[3]{0:T(128)S(1)} %pad_add_fusion.where_ref, ...), custom_call_target="tpu_custom_call" | custom-call | tf_op jit(solution)/shard_map/pallas_call | solution.py:507
  26.0 3.2 %collective-permute-start.2 = (bf16[72,16,128]{2,1,0:T(8,128)(2,1)S(1)}, bf16[72,16,128]{2,1,0:T(8,128)(2,1)S(1)}, u32[]{:S(2)}, u32[]{:S(2)}) collective-permute-start(bf16[72,16,128]{2,1,0:T(8,128)(2,1)S(1)} %get-tuple-element.23), channel_id=1, source_target_pairs={{1,2},{3,4},{5,6},{7,8},{9,10},{11,12},{13,14},{2,1},{4,3},{6,5},{... | collective-permute-start | bytes 884744 | tf_op jit(solution)/shard_map/ppermute | solution.py:541
  29.4 0.5 collective-permute-start.5
  29.9 2.5 %collective-permute-start.4 = (bf16[2,16,3072]{2,1,0:T(8,128)(2,1)S(1)}, bf16[2,16,3072]{2,1,0:T(8,128)(2,1)S(1)}, u32[]{:S(2)}, u32[]{:S(2)}) collective-permute-start(bf16[2,16,3072]{2,1,0:T(8,128)(2,1)S(1)} %bitcast.34), channel_id=1, source_target_pairs={{1,2},{3,4},{5,6},{7,8},{9,10},{11,12},{13,14},{2,1},{4,3},{6,5},{... | collective-permute-start | bytes 589832 | tf_op jit(solution)/shard_map/ppermute | solution.py:541
  32.4 7.2 %collective-permute-done.4.outer = bf16[2,16,3072]{2,1,0:T(8,128)(2,1)S(1)} collective-permute-done((bf16[2,16,3072]{2,1,0:T(8,128)(2,1)S(1)}, bf16[2,16,3072]{2,1,0:T(8,128)(2,1)S(1)}, u32[]{:S(2)}, u32[]{:S(2)}) %collective-permute-start.4) | collective-permute-done | bytes 196640 | tf_op jit(solution)/shard_map/ppermute | solution.py:541
  39.7 4.4 %shard_map.138 = (f32[4,256,640]{2,1,0:T(8,128)S(1)}, bf16[4,18,16,512]{3,2,1,0:T(8,128)(2,1)S(1)}) custom-call(s32[3]{0:T(128)S(1)} %pad_add_fusion.where_ref, bf16[2,16,3072]{2,1,0:T(8,128)(2,1)S(1)} %bitcast.35, bf16[2,16,3072]{2,1,0:T(8,128)(2,1)S(1)} %collective-permute-done.4.outer, bf16[2,16,3072]{2,1,0:T(8,128)(2,1)S(1)} %collective-permute-done.5.inner, ...), custom_call_target="tpu_custom_call" | custom-call | tf_op jit(solution)/shard_map/pallas_call | solution.py:507
  44.2 8.6 %shard_map.139.c_own = bf16[48,16,128]{2,1,0:T(8,128)(2,1)S(1)} custom-call(s32[3]{0:T(128)S(1)} %pad_add_fusion.where_ref, bf16[96,16,128]{2,1,0:T(8,128)(2,1)S(1)} %get-tuple-element.22.low_own, bf16[72,16,128]{2,1,0:T(8,128)(2,1)S(1)} %collective-permute-done.2.low_outer, bf16[72,16,128]{2,1,0:T(8,128)(2,1)S(1)} %collective-permute-done.3.low_inner, ...), custom_call_target="tpu_custom_call" | custom-call | tf_op jit(solution)/shard_map/pallas_call | solution.py:507
  52.9 1.4 %collective-permute-done.6.c_inner = bf16[48,16,128]{2,1,0:T(8,128)(2,1)S(1)} collective-permute-done((bf16[48,16,128]{2,1,0:T(8,128)(2,1)S(1)}, bf16[48,16,128]{2,1,0:T(8,128)(2,1)S(1)}, u32[]{:S(2)}, u32[]{:S(2)}) %collective-permute-start.6) | collective-permute-done | bytes 196640 | tf_op jit(solution)/shard_map/ppermute | solution.py:544
  54.3 4.4 %collective-permute-start.7 = (bf16[72,16,128]{2,1,0:T(8,128)(2,1)S(1)}, bf16[72,16,128]{2,1,0:T(8,128)(2,1)S(1)}, u32[]{:S(2)}, u32[]{:S(2)}) collective-permute-start(bf16[72,16,128]{2,1,0:T(8,128)(2,1)S(1)} %maximum_select_fusion), channel_id=1, source_target_pairs={{1,2},{3,4},{5,6},{7,8},{9,10},{11,12},{13,14},{2,1},{4,3},{6,5},{... | collective-permute-start | bytes 884744 | tf_op jit(solution)/shard_map/ppermute | solution.py:541
  58.7 2.1 %collective-permute-start.9 = (bf16[2,16,16,128]{3,2,1,0:T(8,128)(2,1)S(1)}, bf16[2,16,16,128]{3,2,1,0:T(8,128)(2,1)S(1)}, u32[]{:S(2)}, u32[]{:S(2)}) collective-permute-start(bf16[2,16,16,128]{3,2,1,0:T(8,128)(2,1)S(1)} %get-tuple-element.28), channel_id=1, source_target_pairs={{1,2},{3,4},{5,6},{7,8},{9,10},{11,12},{13,14},{2,1},{4,3},{6,5},{... | collective-permute-start | bytes 393224 | tf_op jit(solution)/shard_map/ppermute | solution.py:541
  60.9 0.4 collective-permute-start.10
  61.2 6.1 %collective-permute-done.7.c_outer = bf16[72,16,128]{2,1,0:T(8,128)(2,1)S(1)} collective-permute-done((bf16[72,16,128]{2,1,0:T(8,128)(2,1)S(1)}, bf16[72,16,128]{2,1,0:T(8,128)(2,1)S(1)}, u32[]{:S(2)}, u32[]{:S(2)}) %collective-permute-start.7) | collective-permute-done | bytes 294944 | tf_op jit(solution)/shard_map/ppermute | solution.py:541
  67.4 1.3 %collective-permute-done.9.f_outer = bf16[2,16,16,128]{3,2,1,0:T(8,128)(2,1)S(1)} collective-permute-done((bf16[2,16,16,128]{3,2,1,0:T(8,128)(2,1)S(1)}, bf16[2,16,16,128]{3,2,1,0:T(8,128)(2,1)S(1)}, u32[]{:S(2)}, u32[]{:S(2)}) %collective-permute-start.9) | collective-permute-done | bytes 131104 | tf_op jit(solution)/shard_map/ppermute | solution.py:541
  68.7 1.0 %copy-done.4 = bf16[768,256]{1,0:T(8,128)(2,1)S(1)} copy-done((bf16[768,256]{1,0:T(8,128)(2,1)S(1)}, bf16[768,256]{1,0:T(8,128)(2,1)}, u32[]{:S(2)}) %copy-start.4) | copy-done | bytes 393240
  69.7 0.9 %copy-done.11 = bf16[1024,128]{1,0:T(8,128)(2,1)S(1)} copy-done((bf16[1024,128]{1,0:T(8,128)(2,1)S(1)}, bf16[1024,128]{1,0:T(8,128)(2,1)}, u32[]{:S(2)}) %copy-start.11) | copy-done | bytes 262168
  70.7 0.9 %copy-done.13 = bf16[4,16,16,128]{3,2,1,0:T(8,128)(2,1)S(1)} copy-done((bf16[4,16,16,128]{3,2,1,0:T(8,128)(2,1)S(1)}, bf16[4,16,16,128]{3,2,1,0:T(8,128)(2,1)}, u32[]{:S(2)}) %copy-start.13) | copy-done | bytes 262168
  71.6 20.2 %shard_map.140 = bf16[2,4,16,512]{3,2,1,0:T(8,128)(2,1)S(1)} custom-call(s32[3]{0:T(128)S(1)} %pad_add_fusion.where_ref, bf16[48,16,128]{2,1,0:T(8,128)(2,1)S(1)} %shard_map.139.c_own, bf16[72,16,128]{2,1,0:T(8,128)(2,1)S(1)} %collective-permute-done.7.c_outer, bf16[48,16,128]{2,1,0:T(8,128)(2,1)S(1)} %collective-permute-done.6.c_inner, ...), custom_call_target="tpu_custom_call" | custom-call | tf_op jit(solution)/shard_map/pallas_call | solution.py:507
  91.8 0.7 reshape.53
  (44 shorter events, 0.4 us)
Async XLA Ops:
  0.0 6.8 %copy-start.17 = (bf16[64,16]{0,1:T(8,128)(2,1)S(1)}, bf16[64,16]{0,1:T(8,128)(2,1)}, u32[]{:S(2)}) copy-start(bf16[64,16]{0,1:T(8,128)(2,1)} %param.27) | copy-start | bytes 6148
  0.0 6.9 %copy-start.15 = (bf16[3,3,192,64]{2,3,1,0:T(8,128)(2,1)S(1)}, bf16[3,3,192,64]{2,3,1,0:T(8,128)(2,1)}, u32[]{:S(2)}) copy-start(bf16[3,3,192,64]{2,3,1,0:T(8,128)(2,1)} %param.24) | copy-start | bytes 663556
  0.0 7.2 %copy-start.5 = (bf16[3,3,64,192]{3,2,1,0:T(8,128)(2,1)S(1)}, bf16[3,3,64,192]{3,2,1,0:T(8,128)(2,1)}, u32[]{:S(2)}) copy-start(bf16[3,3,64,192]{3,2,1,0:T(8,128)(2,1)} %param.18) | copy-start | bytes 663556
  0.0 7.2 %copy-start.14 = (bf16[16,64]{1,0:T(8,128)(2,1)S(1)}, bf16[16,64]{1,0:T(8,128)(2,1)}, u32[]{:S(2)}) copy-start(bf16[16,64]{1,0:T(8,128)(2,1)} %stem.1) | copy-start | bytes 6148
  3.0 8.6 %collective-permute-start.1 = (bf16[3,16,3072]{2,1,0:T(8,128)(2,1)}, bf16[3,16,3072]{2,1,0:T(8,128)(2,1)S(1)}, u32[]{:S(2)}, u32[]{:S(2)}) collective-permute-start(bf16[3,16,3072]{2,1,0:T(8,128)(2,1)} %get-tuple-element.33), channel_id=1, source_target_pairs={{0,1},{1,0},{2,3},{3,2},{4,5},{5,4},{6,7},{7,6},{8,9},{9,8},{10,11... | collective-permute-start | bytes 884744 | tf_op jit(solution)/shard_map/ppermute | solution.py:544
  3.7 11.4 %collective-permute-start = (bf16[3,16,3072]{2,1,0:T(8,128)(2,1)}, bf16[3,16,3072]{2,1,0:T(8,128)(2,1)S(1)}, u32[]{:S(2)}, u32[]{:S(2)}) collective-permute-start(bf16[3,16,3072]{2,1,0:T(8,128)(2,1)} %get-tuple-element.34), channel_id=1, source_target_pairs={{1,2},{3,4},{5,6},{7,8},{9,10},{11,12},{13,14},{2,1},{4,3},{6,5},{... | collective-permute-start | bytes 884744 | tf_op jit(solution)/shard_map/ppermute | solution.py:541
  6.9 22.4 %copy-start.16 = (bf16[2,49152]{1,0:T(2,128)(2,1)S(1)}, bf16[2,49152]{1,0:T(2,128)(2,1)}, u32[]{:S(2)}) copy-start(bf16[2,49152]{1,0:T(2,128)(2,1)} %param.16) | copy-start | bytes 589828
  7.2 1.0 %copy-start.6 = (bf16[3,3,64,192]{3,2,1,0:T(8,128)(2,1)S(1)}, bf16[3,3,64,192]{3,2,1,0:T(8,128)(2,1)}, u32[]{:S(2)}) copy-start(bf16[3,3,64,192]{3,2,1,0:T(8,128)(2,1)} %param.19) | copy-start | bytes 663556
  8.2 1.0 %copy-start.7 = (bf16[3,3,64,192]{3,2,1,0:T(8,128)(2,1)S(1)}, bf16[3,3,64,192]{3,2,1,0:T(8,128)(2,1)}, u32[]{:S(2)}) copy-start(bf16[3,3,64,192]{3,2,1,0:T(8,128)(2,1)} %param.20) | copy-start | bytes 663556
  9.1 1.0 %copy-start.8 = (bf16[3,3,64,192]{3,2,1,0:T(8,128)(2,1)S(1)}, bf16[3,3,64,192]{3,2,1,0:T(8,128)(2,1)}, u32[]{:S(2)}) copy-start(bf16[3,3,64,192]{3,2,1,0:T(8,128)(2,1)} %param.25) | copy-start | bytes 663556
  10.1 1.0 %copy-start.9 = (bf16[3,3,64,192]{3,2,1,0:T(8,128)(2,1)S(1)}, bf16[3,3,64,192]{3,2,1,0:T(8,128)(2,1)}, u32[]{:S(2)}) copy-start(bf16[3,3,64,192]{3,2,1,0:T(8,128)(2,1)} %param.26) | copy-start | bytes 663556
  11.0 28.6 %copy-start = (bf16[3,3,192,576]{3,2,1,0:T(8,128)(2,1)S(1)}, bf16[3,3,192,576]{3,2,1,0:T(8,128)(2,1)}, u32[]{:S(2)}) copy-start(bf16[3,3,192,576]{3,2,1,0:T(8,128)(2,1)} %param.22) | copy-start | bytes 5971972
  11.5 28.1 %copy-start.3 = (bf16[768,256]{1,0:T(8,128)(2,1)}, bf16[768,256]{1,0:T(8,128)(2,1)S(1)}, u32[]{:S(2)}) copy-start(bf16[768,256]{1,0:T(8,128)(2,1)S(1)} %get-tuple-element.30.w_up) | copy-start | bytes 1179652
  11.5 28.1 %copy-start.10 = (bf16[1024,128]{1,0:T(8,128)(2,1)}, bf16[1024,128]{1,0:T(8,128)(2,1)S(1)}, u32[]{:S(2)}) copy-start(bf16[1024,128]{1,0:T(8,128)(2,1)S(1)} %get-tuple-element.32.w_head) | copy-start | bytes 786436
  26.0 18.1 %copy-start.12 = (bf16[4,16,16,128]{3,2,1,0:T(8,128)(2,1)}, bf16[4,16,16,128]{3,2,1,0:T(8,128)(2,1)S(1)}, u32[]{:S(2)}) copy-start(bf16[4,16,16,128]{3,2,1,0:T(8,128)(2,1)S(1)} %get-tuple-element.27.f_own) | copy-start | bytes 786436
  26.0 18.1 %copy-start.2 = (bf16[3,3,192,576]{3,2,1,0:T(8,128)(2,1)S(1)}, bf16[3,3,192,576]{3,2,1,0:T(8,128)(2,1)}, u32[]{:S(2)}) copy-start(bf16[3,3,192,576]{3,2,1,0:T(8,128)(2,1)} %param.21) | copy-start | bytes 5971972
  26.0 18.1 %collective-permute-start.2 = (bf16[72,16,128]{2,1,0:T(8,128)(2,1)S(1)}, bf16[72,16,128]{2,1,0:T(8,128)(2,1)S(1)}, u32[]{:S(2)}, u32[]{:S(2)}) collective-permute-start(bf16[72,16,128]{2,1,0:T(8,128)(2,1)S(1)} %get-tuple-element.23), channel_id=1, source_target_pairs={{1,2},{3,4},{5,6},{7,8},{9,10},{11,12},{13,14},{2,1},{4,3},{6,5},{... | collective-permute-start | bytes 884744 | tf_op jit(solution)/shard_map/ppermute | solution.py:541
  29.2 14.9 %collective-permute-start.3 = (bf16[72,16,128]{2,1,0:T(8,128)(2,1)S(1)}, bf16[72,16,128]{2,1,0:T(8,128)(2,1)S(1)}, u32[]{:S(2)}, u32[]{:S(2)}) collective-permute-start(bf16[72,16,128]{2,1,0:T(8,128)(2,1)S(1)} %get-tuple-element.24), channel_id=1, source_target_pairs={{0,1},{1,0},{2,3},{3,2},{4,5},{5,4},{6,7},{7,6},{8,9},{9,8},{10,11... | collective-permute-start | bytes 884744 | tf_op jit(solution)/shard_map/ppermute | solution.py:544
  29.4 3.1 %collective-permute-start.5 = (bf16[2,16,3072]{2,1,0:T(8,128)(2,1)S(1)}, bf16[2,16,3072]{2,1,0:T(8,128)(2,1)S(1)}, u32[]{:S(2)}, u32[]{:S(2)}) collective-permute-start(bf16[2,16,3072]{2,1,0:T(8,128)(2,1)S(1)} %bitcast.33), channel_id=1, source_target_pairs={{0,1},{1,0},{2,3},{3,2},{4,5},{5,4},{6,7},{7,6},{8,9},{9,8},{10,11... | collective-permute-start | bytes 589832 | tf_op jit(solution)/shard_map/ppermute | solution.py:544
  29.9 9.8 %collective-permute-start.4 = (bf16[2,16,3072]{2,1,0:T(8,128)(2,1)S(1)}, bf16[2,16,3072]{2,1,0:T(8,128)(2,1)S(1)}, u32[]{:S(2)}, u32[]{:S(2)}) collective-permute-start(bf16[2,16,3072]{2,1,0:T(8,128)(2,1)S(1)} %bitcast.34), channel_id=1, source_target_pairs={{1,2},{3,4},{5,6},{7,8},{9,10},{11,12},{13,14},{2,1},{4,3},{6,5},{... | collective-permute-start | bytes 589832 | tf_op jit(solution)/shard_map/ppermute | solution.py:541
  44.2 24.5 %copy-start.1 = (bf16[3,3,192,576]{3,2,1,0:T(8,128)(2,1)S(1)}, bf16[3,3,192,576]{3,2,1,0:T(8,128)(2,1)}, u32[]{:S(2)}) copy-start(bf16[3,3,192,576]{3,2,1,0:T(8,128)(2,1)} %param.23) | copy-start | bytes 5971972
  52.8 1.5 %collective-permute-start.6 = (bf16[48,16,128]{2,1,0:T(8,128)(2,1)S(1)}, bf16[48,16,128]{2,1,0:T(8,128)(2,1)S(1)}, u32[]{:S(2)}, u32[]{:S(2)}) collective-permute-start(bf16[48,16,128]{2,1,0:T(8,128)(2,1)S(1)} %shard_map.139.c_own), channel_id=1, source_target_pairs={{0,1},{1,0},{2,3},{3,2},{4,5},{5,4},{6,7},{7,6},{8,9},{9,8},{10,11... | collective-permute-start | bytes 589832 | tf_op jit(solution)/shard_map/ppermute | solution.py:544
  54.3 13.0 %collective-permute-start.7 = (bf16[72,16,128]{2,1,0:T(8,128)(2,1)S(1)}, bf16[72,16,128]{2,1,0:T(8,128)(2,1)S(1)}, u32[]{:S(2)}, u32[]{:S(2)}) collective-permute-start(bf16[72,16,128]{2,1,0:T(8,128)(2,1)S(1)} %maximum_select_fusion), channel_id=1, source_target_pairs={{1,2},{3,4},{5,6},{7,8},{9,10},{11,12},{13,14},{2,1},{4,3},{6,5},{... | collective-permute-start | bytes 884744 | tf_op jit(solution)/shard_map/ppermute | solution.py:541
  58.7 10.0 %collective-permute-start.9 = (bf16[2,16,16,128]{3,2,1,0:T(8,128)(2,1)S(1)}, bf16[2,16,16,128]{3,2,1,0:T(8,128)(2,1)S(1)}, u32[]{:S(2)}, u32[]{:S(2)}) collective-permute-start(bf16[2,16,16,128]{3,2,1,0:T(8,128)(2,1)S(1)} %get-tuple-element.28), channel_id=1, source_target_pairs={{1,2},{3,4},{5,6},{7,8},{9,10},{11,12},{13,14},{2,1},{4,3},{6,5},{... | collective-permute-start | bytes 393224 | tf_op jit(solution)/shard_map/ppermute | solution.py:541
  60.9 7.9 %collective-permute-start.10 = (bf16[2,16,16,128]{3,2,1,0:T(8,128)(2,1)S(1)}, bf16[2,16,16,128]{3,2,1,0:T(8,128)(2,1)S(1)}, u32[]{:S(2)}, u32[]{:S(2)}) collective-permute-start(bf16[2,16,16,128]{3,2,1,0:T(8,128)(2,1)S(1)} %get-tuple-element.29), channel_id=1, source_target_pairs={{0,1},{1,0},{2,3},{3,2},{4,5},{5,4},{6,7},{7,6},{8,9},{9,8},{10,11... | collective-permute-start | bytes 393224 | tf_op jit(solution)/shard_map/ppermute | solution.py:544
  67.3 1.4 %collective-permute-start.8 = (bf16[24,16,128]{2,1,0:T(8,128)(2,1)S(1)}, bf16[24,16,128]{2,1,0:T(8,128)(2,1)S(1)}, u32[]{:S(2)}, u32[]{:S(2)}) collective-permute-start(bf16[24,16,128]{2,1,0:T(8,128)(2,1)S(1)} %slice_select_fusion), channel_id=1, source_target_pairs={{0,1},{1,0},{2,3},{3,2},{4,5},{5,4},{6,7},{7,6},{8,9},{9,8},{10,11... | collective-permute-start | bytes 294920 | tf_op jit(solution)/shard_map/ppermute | solution.py:544
  68.7 1.0 %copy-start.4 = (bf16[768,256]{1,0:T(8,128)(2,1)S(1)}, bf16[768,256]{1,0:T(8,128)(2,1)}, u32[]{:S(2)}) copy-start(bf16[768,256]{1,0:T(8,128)(2,1)} %copy-done.3) | copy-start | bytes 1179652
  69.7 0.9 %copy-start.11 = (bf16[1024,128]{1,0:T(8,128)(2,1)S(1)}, bf16[1024,128]{1,0:T(8,128)(2,1)}, u32[]{:S(2)}) copy-start(bf16[1024,128]{1,0:T(8,128)(2,1)} %copy-done.10) | copy-start | bytes 786436
  70.7 0.9 %copy-start.13 = (bf16[4,16,16,128]{3,2,1,0:T(8,128)(2,1)S(1)}, bf16[4,16,16,128]{3,2,1,0:T(8,128)(2,1)}, u32[]{:S(2)}) copy-start(bf16[4,16,16,128]{3,2,1,0:T(8,128)(2,1)} %copy-done.12) | copy-start | bytes 786436

commit v3 on v2

--- a/solution.py
+++ b/solution.py
@@ -184,17 +184,32 @@
     return coarse_forms(out[0], out[1])
 
 
+def place(per_device):
+    upper = lax.axis_index("section") == 0
+    line = lax.axis_index("tile") * lax.axis_size("section") + lax.axis_index("section")
+    return upper, line * per_device, lax.axis_size(LINE) * per_device
+
+
 def in_grid(row, rows):
     return jnp.logical_and(row >= 0, row < rows)
 
 
+def pack_body(fine, first, second, own, to_outer, to_inner):
+    upper, _, _ = place(4)
+    for r in range(4):
+        own[r, :, : FB * C1] = fine[r]
+        own[r, :, FB * C1 : FB * (C1 + PATCH)] = first[r]
+        own[r, :, FB * (C1 + PATCH) :] = second[r]
+    for r in range(3):
+        to_outer[r] = jnp.where(upper, own[r], own[r + 1])
+        to_inner[r] = jnp.where(upper, own[r + 1], own[r])
+
+
 def fine_encoder_body(
-    where_ref, own, outer, inner, w_stem, w_gru, w_down,
+    own, outer, inner, w_stem, w_gru, w_down,
     state_out, low_own, to_outer, to_inner, state_outer, state_inner, p1, p2, p3, stem2,
 ):
-    upper = where_ref[0] == 0
-    first = where_ref[1] * 4
-    rows = where_ref[2] * 4
+    upper, first, rows = place(4)
     lo = low_half((1, SUB, LANES))
 
     def pick(idx, lanes):
@@ -293,8 +308,8 @@
     return tiles
 
 
-def coarse_state_body(where_ref, own, outer, inner, w_h, acc_out, h_out, h0):
-    upper = where_ref[0] == 0
+def coarse_state_body(own, outer, inner, w_h, acc_out, h_out, h0):
+    upper, _, _ = place(2)
     for idx in range(6):
         if 2 <= idx < 4:
             put_packed(h0, idx, raw_tiles(lambda lanes: own[idx - 2, :, lanes]))
@@ -311,12 +326,10 @@
 
 
 def coarse_encoder_body(
-    where_ref, low_own, low_outer, low_inner, acc_first, h_first, w_x, w_h,
+    low_own, low_outer, low_inner, acc_first, h_first, w_x, w_h,
     state_out, x1, x2, h1, acc_x, acc_h,
 ):
-    upper = where_ref[0] == 0
-    first = where_ref[1] * 2
-    rows = where_ref[2] * 2
+    upper, first, rows = place(2)
     zero_tail(acc_x)
     zero_tail(acc_h)
 
@@ -342,8 +355,9 @@
     @pl.loop(0, 2)
     def _(idx):
         forms = coarse_gru(x2, idx + 1, h1, idx + 1, w_x, w_h, acc_x, acc_h, in_grid(first + idx, rows))
+        slot = jnp.where(upper, idx, 1 - idx)
         for k, tile in enumerate(pack_forms(forms)):
-            state_out[pl.ds(idx * ROW_TILES + k * PAIRS, PAIRS)] = tile
+            state_out[pl.ds(slot * ROW_TILES + k * PAIRS, PAIRS)] = tile
 
 
 def raise_pair(src, idx, weight):
@@ -358,29 +372,25 @@
 
 
 def forecaster_body(
-    where_ref, c_own, c_outer, c_inner, c_third, f_own, f_outer, f_inner, w_h, w_up, w_gru, w_head,
+    c_own, c_outer, c_inner, c_third, f_own, f_outer, f_inner, w_h, w_up, w_gru, w_head,
     out, h2, s1, s2, pf1, pf2, states, acc_h,
 ):
-    upper = where_ref[0] == 0
-    first_c = where_ref[1] * 2
-    rows_c = where_ref[2] * 2
-    first_f = where_ref[1] * 4
-    rows_f = where_ref[2] * 4
+    upper, first_c, rows_c = place(2)
+    _, first_f, rows_f = place(4)
     lo = low_half((1, SUB, LANES))
     zero_tail(acc_h)
 
-    put_packed(h2, 3, packed_tiles(c_own, 0))
-    put_packed(h2, 4, packed_tiles(c_own, 1))
-
-    def either(a, b):
-        return lambda i: jnp.where(upper, a(i), b(i))
-
-    put_packed(h2, 0, either(packed_tiles(c_outer, 0), packed_tiles(c_third, 0)))
-    put_packed(h2, 1, either(packed_tiles(c_outer, 1), packed_tiles(c_inner, 0)))
-    put_packed(h2, 2, either(packed_tiles(c_outer, 2), packed_tiles(c_inner, 1)))
-    put_packed(h2, 5, either(packed_tiles(c_inner, 0), packed_tiles(c_outer, 0)))
-    put_packed(h2, 6, either(packed_tiles(c_inner, 1), packed_tiles(c_outer, 1)))
-    put_packed(h2, 7, either(packed_tiles(c_third, 0), packed_tiles(c_outer, 2)))
+    def either(a, i, b, j):
+        return lambda t: jnp.where(upper, packed_tiles(a, i)(t), packed_tiles(b, j)(t))
+
+    put_packed(h2, 0, either(c_outer, 2, c_third, 0))
+    put_packed(h2, 1, either(c_outer, 1, c_inner, 0))
+    put_packed(h2, 2, either(c_outer, 0, c_inner, 1))
+    put_packed(h2, 3, either(c_own, 0, c_own, 1))
+    put_packed(h2, 4, either(c_own, 1, c_own, 0))
+    put_packed(h2, 5, either(c_inner, 1, c_outer, 0))
+    put_packed(h2, 6, either(c_inner, 0, c_outer, 1))
+    put_packed(h2, 7, either(c_third, 0, c_outer, 2))
 
     for idx in range(8):
         for k in range(FB // 2):
@@ -465,24 +475,47 @@
     return jnp.concatenate([x.astype(F32), jnp.zeros(x.shape, F32)], axis=-1).astype(BF)
 
 
-def prepare_body(
-    stem, enc_x, enc_h, down, up, fc_x, fc_h, head, w_stem, w_enc, w_down, w_up, w_fc, w_head
-):
-    for kx, kh, w in ((enc_x, enc_h, w_enc), (fc_x, fc_h, w_fc)):
-        for k in range(9):
-            at = k * LANES
-            w[at : at + C1, :LANES] = kx[k, :, :LANES]
-            w[at : at + C1, LANES:] = to_upper(kx[k, :, LANES:])
-            w[at + C1 : at + LANES, :LANES] = kh[k, :, :LANES]
-            w[at + C1 : at + LANES, LANES:] = to_lower(kh[k, :, LANES:])
+def fetch_all(given, copies, sems):
+    fetches = [pltpu.make_async_copy(src, dst, sems.at[i]) for i, (src, dst) in enumerate(zip(given, copies))]
+    for fetch in fetches:
+        fetch.start()
+    for fetch in fetches:
+        fetch.wait()
+
+
+def arrange_gru(kx, kh, w):
+    for k in range(9):
+        at = k * LANES
+        w[at : at + C1, :LANES] = kx[k, :, :LANES]
+        w[at : at + C1, LANES:] = to_upper(kx[k, :, LANES:])
+        w[at + C1 : at + LANES, :LANES] = kh[k, :, :LANES]
+        w[at + C1 : at + LANES, LANES:] = to_lower(kh[k, :, LANES:])
+
+
+def prepare_encoder_body(*refs):
+    given, (w_stem, w_enc, w_down), copies, sems = refs[:4], refs[4:7], refs[7:11], refs[11]
+    fetch_all(given, copies, sems)
+    stem, enc_x, enc_h, down = copies
+    arrange_gru(enc_x, enc_h, w_enc)
     for k in range(9):
         at = k * LANES
         w_down[at : at + C1] = jnp.zeros((C1, 2 * LANES), BF)
         w_down[at + C1 : at + LANES, :LANES] = down[k, :, :LANES]
         w_down[at + C1 : at + LANES, LANES:] = to_lower(down[k, :, LANES:])
+    w_stem[...] = jnp.zeros(w_stem.shape, BF)
+    wide = to_lower(stem[...])
+    for k in range(8):
+        w_stem[k * PATCH : (k + 1) * PATCH, k * LANES : (k + 1) * LANES] = wide
+
+
+def prepare_forecaster_body(*refs):
+    given, (w_up, w_fc, w_head), copies, sems = refs[:4], refs[4:7], refs[7:11], refs[11]
+    fetch_all(given, copies, sems)
+    up, fc_x, fc_h, head = copies
+    arrange_gru(fc_x, fc_h, w_fc)
 
     def tap(a, b):
-        return jnp.zeros((C2, C1), F32) if a is None else up[3 * a + b].astype(F32)
+        return jnp.zeros((C2, C1), F32) if a is None else up[3 * a + b].astype(F32).T
 
     none = (None, None)
     for g, taps in enumerate((
@@ -495,12 +528,10 @@
             pair = jnp.concatenate([tap(*taps[2 * n]), tap(*taps[2 * n + 1])], axis=-1)
             w_up[g * C2 : (g + 1) * C2, n * LANES : (n + 1) * LANES] = pair.astype(BF)
 
-    w_stem[...] = jnp.zeros(w_stem.shape, BF)
     w_head[...] = jnp.zeros(w_head.shape, BF)
-    wide = to_lower(stem[...])
+    tall = head[...].astype(F32).T.astype(BF)
     for k in range(8):
-        w_stem[k * PATCH : (k + 1) * PATCH, k * LANES : (k + 1) * LANES] = wide
-        w_head[k * LANES + C1 : (k + 1) * LANES, k * PATCH : (k + 1) * PATCH] = head[...]
+        w_head[k * LANES + C1 : (k + 1) * LANES, k * PATCH : (k + 1) * PATCH] = tall
 
 
 def call(body, args, outs, scratch):
@@ -531,9 +562,6 @@
     fc_head,
 ):
     count = lax.axis_size(LINE)
-    section = lax.axis_index("section")
-    position = lax.axis_index(LINE)
-    where = jnp.stack([section, position, jnp.int32(count)]).astype(jnp.int32)
     across = [(i, i + 1) for i in range(1, count - 1, 2)]
     across = across + [(b, a) for a, b in across]
 
@@ -546,9 +574,6 @@
     fine = start_fine.reshape(4, SUB, FB * C1)
     patches = frames.reshape(FRAMES, 4, SUB, FB * PATCH)
     coarse = start_coarse.reshape(2, SUB, CB * C2)
-    own = jnp.concatenate([fine, patches[0], patches[1]], axis=-1)
-    outer = outer_swap(lax.dynamic_slice_in_dim(own, section, 3, 0))
-    inner = inner_swap(lax.dynamic_slice_in_dim(own, 1 - section, 3, 0))
 
     def on_chip(*values):
         return [(value, pltpu.VMEM) for value in values]
@@ -559,31 +584,30 @@
     def coarse_buf(rows):
         return pltpu.VMEM((rows, CB + 2, SUB, 4 * LANES), BF)
 
-    place = [(where, pltpu.SMEM)]
+    rows = (3, SUB, FB * (C1 + FRAMES * PATCH))
+    own, to_outer, to_inner = call(pack_body, on_chip(fine, patches[0], patches[1]), [(4,) + rows[1:], rows, rows], [])
+    outer, inner = outer_swap(to_outer), inner_swap(to_inner)
+
     acc_buf = pltpu.VMEM((CB * SUB, 5 * LANES), F32)
     flat = (9 * C2, 3 * C2)
 
-    w_stem, w_enc, w_down, w_up, w_fc, w_head = call(
-        prepare_body,
-        on_chip(
-            enc_stem,
-            enc_fine_x.reshape(9, C1, 3 * C1),
-            enc_fine_h.reshape(9, C1, 3 * C1),
-            enc_down.reshape(9, C1, C2),
-            fc_up.reshape(9, C2, C1),
-            fc_fine_x.reshape(9, C1, 3 * C1),
-            fc_fine_h.reshape(9, C1, 3 * C1),
-            fc_head,
-        ),
-        [
-            (8 * PATCH, 8 * LANES),
-            (9 * LANES, 2 * LANES),
-            (9 * LANES, 2 * LANES),
-            (4 * C2, 2 * LANES),
-            (9 * LANES, 2 * LANES),
-            (8 * LANES, 8 * PATCH),
-        ],
-        [],
+    def prepare(body, values, outs):
+        scratch = [pltpu.VMEM(value.shape, BF) for value in values]
+        return call(
+            body, [(value, pl.ANY) for value in values], outs, scratch + [pltpu.SemaphoreType.DMA((len(values),))]
+        )
+
+    kernel = (9, C1, 3 * C1)
+    wide = (9 * LANES, 2 * LANES)
+    w_stem, w_enc, w_down = prepare(
+        prepare_encoder_body,
+        [enc_stem, enc_fine_x.reshape(kernel), enc_fine_h.reshape(kernel), enc_down.reshape(kernel)],
+        [(8 * PATCH, 8 * LANES), wide, wide],
+    )
+    w_up, w_fc, w_head = prepare(
+        prepare_forecaster_body,
+        [jnp.swapaxes(fc_up.reshape(9, C2, C1), 1, 2), fc_fine_x.reshape(kernel), fc_fine_h.reshape(kernel), fc_head.T],
+        [(4 * C2, 2 * LANES), wide, (8 * LANES, 8 * PATCH)],
     )
     coarse_o, coarse_i = outer_swap(coarse), inner_swap(coarse)
 
@@ -591,7 +615,7 @@
     edge = (2, FB // 2, SUB, LANES)
     state_f, low_own, to_outer, to_inner, state_fo, state_fi = call(
         fine_encoder_body,
-        place + on_chip(own, outer, inner, w_stem, w_enc, w_down),
+        on_chip(own, outer, inner, w_stem, w_enc, w_down),
         [(4, FB // 2, SUB, LANES), (4 * ROW_TILES, SUB, LANES), halo, halo, edge, edge],
         [fine_buf(9), fine_buf(9), fine_buf(9), pltpu.VMEM((9, FB, SUB, LANES), BF)],
     )
@@ -599,7 +623,7 @@
 
     acc_first, h_first = call(
         coarse_state_body,
-        place + on_chip(coarse, coarse_o, coarse_i, enc_coarse_h.reshape(flat)),
+        on_chip(coarse, coarse_o, coarse_i, enc_coarse_h.reshape(flat)),
         [jax.ShapeDtypeStruct((4, CB * SUB, 5 * LANES), F32), (4, CB + 2, SUB, 4 * LANES)],
         [coarse_buf(6)],
     )
@@ -607,25 +631,17 @@
 
     (state_c,) = call(
         coarse_encoder_body,
-        place
-        + on_chip(low_own, got_o, got_i, acc_first, h_first, enc_coarse_x.reshape(flat), enc_coarse_h.reshape(flat)),
+        on_chip(low_own, got_o, got_i, acc_first, h_first, enc_coarse_x.reshape(flat), enc_coarse_h.reshape(flat)),
         [(2 * ROW_TILES, SUB, LANES)],
         [coarse_buf(6), coarse_buf(4), coarse_buf(4), acc_buf, acc_buf],
     )
     state_ci = inner_swap(state_c)
-    near = jnp.where(section == 0, state_ci[:ROW_TILES], state_ci[ROW_TILES:])
-    send = jnp.where(
-        section == 0,
-        jnp.concatenate([state_c, near], axis=0),
-        jnp.concatenate([near, state_c], axis=0),
-    )
-    state_co = outer_swap(send)
-    third = inner_swap(jnp.where(section == 0, state_co[2 * ROW_TILES :], state_co[:ROW_TILES]))
+    state_co = outer_swap(jnp.concatenate([state_c, state_ci[ROW_TILES:]], axis=0))
+    third = inner_swap(state_co[:ROW_TILES])
 
     (out,) = call(
         forecaster_body,
-        place
-        + on_chip(state_c, state_co, state_ci, third, state_f, state_fo, state_fi, fc_coarse_h.reshape(flat))
+        on_chip(state_c, state_co, state_ci, third, state_f, state_fo, state_fi, fc_coarse_h.reshape(flat))
         + on_chip(w_up, w_fc, w_head),
         [(HORIZON, 4, SUB, FB * PATCH)],
         [coarse_buf(8), coarse_buf(6), coarse_buf(5), fine_buf(8), fine_buf(6), fine_buf(4), acc_buf],

time: 93.7 us -> 86.7 us (0.925)
  local copies, waits for them, and re-layouts: 10.9 us -> 6.48 us
  Pallas kernels: 44.7 us -> 43 us
    unnamed x41 -> x26, local copies, waits for them, and re-layouts: 8.31 us -> 4.79 us
    pallas_call x5 -> x7, Pallas kernels: 44.7 us -> 43 us  [call(): pl.pallas_call(body, out_shape=[s if isinstance(s, jax.ShapeDtypeStruct)...]
    ppermute x5, starting transfers between devices: 15.2 us -> 16.4 us  [outer_swap(): return lax.ppermute(x, LINE, across)]
  transfers between devices with their start and end apart: 11 -> 11, of which waited for: 5 -> 5; matrix products, arithmetic and copies ran while one was open for 1% -> 0% of each run, Pallas kernels for 5% -> 6%
where the time goes in v3:
time: 86.7 us; the launch traced here: 86 us
  Pallas kernels  43 us (50%)
  waiting for transfers between devices  18.9 us (22%)
  starting transfers between devices  17.3 us (20%)
  local copies, waits for them, and re-layouts  6.48 us (7%)
    pallas_call x7, Pallas kernels, call(): pl.pallas_call(body, out_shape=[s if isinstance(s, jax.ShapeDtypeStruct)...  43 us
    ppermute x5, waiting for transfers between devices, outer_swap(): return lax.ppermute(x, LINE, across)  17.5 us
    ppermute x5, starting transfers between devices, outer_swap(): return lax.ppermute(x, LINE, across)  16.4 us
    unnamed x26, local copies, waits for them, and re-layouts  4.79 us
  transfers between devices with their start and end apart: 11, of which 5 were waited for; matrix products, arithmetic and copies ran while one was open for 0% of the time, Pallas kernels for 6%

profile of v3, /device:TPU:19, one launch (start us, length us, event | category | flops | bytes accessed | tf_op | source)
XLA Modules:
  0.0 86.0 jit_solution(5507662324571092192)
XLA Ops:
  0.0 0.9 %fusion = (bf16[1,4,8192]{2,1,0:T(4,128)(2,1)S(1)}, bf16[1,4,8192]{2,1,0:T(4,128)(2,1)S(1)}) fusion(bf16[2,4,8192]{2,1,0:T(4,128)(2,1)} %param.14), kind=kLoop, calls=%fused_computation.5 | loop fusion | bytes 262144 | tf_op jit(solution)/shard_map/slice | solution.py:588
  0.9 0.0 copy-start.11
  0.9 1.1 %copy.23 = bf16[1,4,16,2048]{3,2,1,0:T(8,128)(2,1)S(1)} copy(bf16[1,4,16,2048]{3,1,2,0:T(4,128)(2,1)} %bitcast.45) | data formatting | bytes 524288
  2.1 0.0 copy-start
  2.1 0.1 shard_map.136
  2.2 3.8 %collective-permute-start = (bf16[3,16,3072]{2,1,0:T(8,128)(2,1)S(1)}, bf16[3,16,3072]{2,1,0:T(8,128)(2,1)S(1)}, u32[]{:S(2)}, u32[]{:S(2)}) collective-permute-start(bf16[3,16,3072]{2,1,0:T(8,128)(2,1)S(1)} %get-tuple-element.23), channel_id=1, source_target_pairs={{1,2},{3,4},{5,6},{7,8},{9,10},{11,12},{13,14},{2,1},{4,3},{6,5},{... | collective-permute-start | bytes 884744 | tf_op jit(solution)/shard_map/ppermute | solution.py:569
  6.1 0.1 collective-permute-start.1
  6.1 1.0 %copy-done.3 = bf16[3,3,64,192]{3,2,1,0:T(8,128)(2,1)S(1)} copy-done((bf16[3,3,64,192]{3,2,1,0:T(8,128)(2,1)S(1)}, bf16[3,3,64,192]{3,2,1,0:T(8,128)(2,1)}, u32[]{:S(2)}) %copy-start.3) | copy-done | bytes 221208
  7.1 1.0 %copy-done.4 = bf16[3,3,64,192]{3,2,1,0:T(8,128)(2,1)S(1)} copy-done((bf16[3,3,64,192]{3,2,1,0:T(8,128)(2,1)S(1)}, bf16[3,3,64,192]{3,2,1,0:T(8,128)(2,1)}, u32[]{:S(2)}) %copy-start.4) | copy-done | bytes 221208
  8.1 1.0 %copy-done.5 = bf16[3,3,64,192]{3,2,1,0:T(8,128)(2,1)S(1)} copy-done((bf16[3,3,64,192]{3,2,1,0:T(8,128)(2,1)S(1)}, bf16[3,3,64,192]{3,2,1,0:T(8,128)(2,1)}, u32[]{:S(2)}) %copy-start.5) | copy-done | bytes 221208
  9.0 0.7 copy-done.9
  9.7 0.5 shard_map.137
  10.2 3.4 %collective-permute-done.outer = bf16[3,16,3072]{2,1,0:T(8,128)(2,1)S(1)} collective-permute-done((bf16[3,16,3072]{2,1,0:T(8,128)(2,1)S(1)}, bf16[3,16,3072]{2,1,0:T(8,128)(2,1)S(1)}, u32[]{:S(2)}, u32[]{:S(2)}) %collective-permute-start) | collective-permute-done | bytes 294944 | tf_op jit(solution)/shard_map/ppermute | solution.py:569
  13.6 10.4 %shard_map.138 = (bf16[4,16,16,128]{3,2,1,0:T(8,128)(2,1)S(1)}, bf16[96,16,128]{2,1,0:T(8,128)(2,1)S(1)}, bf16[72,16,128]{2,1,0:T(8,128)(2,1)S(1)}, bf16[72,16,1...) custom-call(bf16[4,16,3072]{2,1,0:T(8,128)(2,1)S(1)} %get-tuple-element.22.own, ...), custom_call_target="tpu_custom_call" | custom-call | tf_op jit(solution)/shard_map/pallas_call | solution.py:538
  24.0 3.8 %collective-permute-start.2 = (bf16[72,16,128]{2,1,0:T(8,128)(2,1)S(1)}, bf16[72,16,128]{2,1,0:T(8,128)(2,1)S(1)}, u32[]{:S(2)}, u32[]{:S(2)}) collective-permute-start(bf16[72,16,128]{2,1,0:T(8,128)(2,1)S(1)} %get-tuple-element.29), channel_id=1, source_target_pairs={{1,2},{3,4},{5,6},{7,8},{9,10},{11,12},{13,14},{2,1},{4,3},{6,5},{... | collective-permute-start | bytes 884744 | tf_op jit(solution)/shard_map/ppermute | solution.py:569
  27.8 0.1 collective-permute-start.3
  27.9 1.9 %collective-permute-start.4 = (bf16[2,16,3072]{2,1,0:T(8,128)(2,1)S(1)}, bf16[2,16,3072]{2,1,0:T(8,128)(2,1)S(1)}, u32[]{:S(2)}, u32[]{:S(2)}) collective-permute-start(bf16[2,16,3072]{2,1,0:T(8,128)(2,1)S(1)} %bitcast.35), channel_id=1, source_target_pairs={{1,2},{3,4},{5,6},{7,8},{9,10},{11,12},{13,14},{2,1},{4,3},{6,5},{... | collective-permute-start | bytes 589832 | tf_op jit(solution)/shard_map/ppermute | solution.py:569
  29.8 0.5 collective-permute-start.5
  30.4 7.8 %collective-permute-done.4.outer = bf16[2,16,3072]{2,1,0:T(8,128)(2,1)S(1)} collective-permute-done((bf16[2,16,3072]{2,1,0:T(8,128)(2,1)S(1)}, bf16[2,16,3072]{2,1,0:T(8,128)(2,1)S(1)}, u32[]{:S(2)}, u32[]{:S(2)}) %collective-permute-start.4) | collective-permute-done | bytes 196640 | tf_op jit(solution)/shard_map/ppermute | solution.py:569
  38.2 3.9 %shard_map.139 = (f32[4,256,640]{2,1,0:T(8,128)S(1)}, bf16[4,18,16,512]{3,2,1,0:T(8,128)(2,1)S(1)}) custom-call(bf16[2,16,3072]{2,1,0:T(8,128)(2,1)S(1)} %bitcast.37, bf16[2,16,3072]{2,1,0:T(8,128)(2,1)S(1)} %collective-permute-done.4.outer, bf16[2,16,3072]{2,1,0:T(8,128)(2,1)S(1)} %collective-permute-done.5.inner, bf16[1728,576]{1,0:T(8,128)(2,1)S(1)} %bitcast.30), custom_call_target="tpu_custom_call" | custom-call | tf_op jit(solution)/shard_map/pallas_call | solution.py:538
  42.2 8.1 %shard_map.140.c_own = bf16[48,16,128]{2,1,0:T(8,128)(2,1)S(1)} custom-call(bf16[96,16,128]{2,1,0:T(8,128)(2,1)S(1)} %get-tuple-element.28.low_own, bf16[72,16,128]{2,1,0:T(8,128)(2,1)S(1)} %collective-permute-done.2.low_outer, bf16[72,16,128]{2,1,0:T(8,128)(2,1)S(1)} %collective-permute-done.3.low_inner, f32[4,256,640]{2,1,0:T(8,128)S(1)} %get-tuple-element.31.acc_first, ...), custom_call_target="tpu_custom_call" | custom-call | tf_op jit(solution)/shard_map/pallas_call | solution.py:538
  50.3 0.1 collective-permute-start.6
  50.3 1.4 %collective-permute-done.6.c_inner = bf16[48,16,128]{2,1,0:T(8,128)(2,1)S(1)} collective-permute-done((bf16[48,16,128]{2,1,0:T(8,128)(2,1)S(1)}, bf16[48,16,128]{2,1,0:T(8,128)(2,1)S(1)}, u32[]{:S(2)}, u32[]{:S(2)}) %collective-permute-start.6) | collective-permute-done | bytes 196640 | tf_op jit(solution)/shard_map/ppermute | solution.py:572
  51.8 3.7 %collective-permute-start.7 = (bf16[72,16,128]{2,1,0:T(8,128)(2,1)S(1)}, bf16[72,16,128]{2,1,0:T(8,128)(2,1)S(1)}, u32[]{:S(2)}, u32[]{:S(2)}) collective-permute-start(bf16[72,16,128]{2,1,0:T(8,128)(2,1)S(1)} %pad_maximum_fusion), channel_id=1, source_target_pairs={{1,2},{3,4},{5,6},{7,8},{9,10},{11,12},{13,14},{2,1},{4,3},{6,5},{... | collective-permute-start | bytes 884744 | tf_op jit(solution)/shard_map/ppermute | solution.py:569
  55.6 0.1 collective-permute-start.10
  55.6 3.1 %collective-permute-start.9 = (bf16[2,16,16,128]{3,2,1,0:T(8,128)(2,1)S(1)}, bf16[2,16,16,128]{3,2,1,0:T(8,128)(2,1)S(1)}, u32[]{:S(2)}, u32[]{:S(2)}) collective-permute-start(bf16[2,16,16,128]{3,2,1,0:T(8,128)(2,1)S(1)} %get-tuple-element.34), channel_id=1, source_target_pairs={{1,2},{3,4},{5,6},{7,8},{9,10},{11,12},{13,14},{2,1},{4,3},{6,5},{... | collective-permute-start | bytes 393224 | tf_op jit(solution)/shard_map/ppermute | solution.py:569
  58.8 5.7 %collective-permute-done.7.c_outer = bf16[72,16,128]{2,1,0:T(8,128)(2,1)S(1)} collective-permute-done((bf16[72,16,128]{2,1,0:T(8,128)(2,1)S(1)}, bf16[72,16,128]{2,1,0:T(8,128)(2,1)S(1)}, u32[]{:S(2)}, u32[]{:S(2)}) %collective-permute-start.7) | collective-permute-done | bytes 294944 | tf_op jit(solution)/shard_map/ppermute | solution.py:569
  64.5 0.1 collective-permute-start.8
  64.7 0.8 shard_map.141
  65.4 0.5 collective-permute-done.9.f_outer
  65.9 19.3 %shard_map.142 = bf16[2,4,16,512]{3,2,1,0:T(8,128)(2,1)S(1)} custom-call(bf16[48,16,128]{2,1,0:T(8,128)(2,1)S(1)} %shard_map.140.c_own, bf16[72,16,128]{2,1,0:T(8,128)(2,1)S(1)} %collective-permute-done.7.c_outer, bf16[48,16,128]{2,1,0:T(8,128)(2,1)S(1)} %collective-permute-done.6.c_inner, bf16[24,16,128]{2,1,0:T(8,128)(2,1)S(1)} %collective-permute-done.8.c_third, ...), custom_call_target="tpu_custom_call" | custom-call | tf_op jit(solution)/shard_map/pallas_call | solution.py:538
  85.3 0.7 reshape.53
  (29 shorter events, 0.2 us)
Async XLA Ops:
  0.9 26.9 %copy-start.11 = (bf16[2,49152]{1,0:T(2,128)(2,1)S(1)}, bf16[2,49152]{1,0:T(2,128)(2,1)}, u32[]{:S(2)}) copy-start(bf16[2,49152]{1,0:T(2,128)(2,1)} %param.16) | copy-start | bytes 589828
  2.1 36.1 %copy-start = (bf16[3,3,192,576]{3,2,1,0:T(8,128)(2,1)S(1)}, bf16[3,3,192,576]{3,2,1,0:T(8,128)(2,1)}, u32[]{:S(2)}) copy-start(bf16[3,3,192,576]{3,2,1,0:T(8,128)(2,1)} %param.22) | copy-start | bytes 5971972
  2.2 11.4 %collective-permute-start = (bf16[3,16,3072]{2,1,0:T(8,128)(2,1)S(1)}, bf16[3,16,3072]{2,1,0:T(8,128)(2,1)S(1)}, u32[]{:S(2)}, u32[]{:S(2)}) collective-permute-start(bf16[3,16,3072]{2,1,0:T(8,128)(2,1)S(1)} %get-tuple-element.23), channel_id=1, source_target_pairs={{1,2},{3,4},{5,6},{7,8},{9,10},{11,12},{13,14},{2,1},{4,3},{6,5},{... | collective-permute-start | bytes 884744 | tf_op jit(solution)/shard_map/ppermute | solution.py:569
  6.1 7.6 %collective-permute-start.1 = (bf16[3,16,3072]{2,1,0:T(8,128)(2,1)S(1)}, bf16[3,16,3072]{2,1,0:T(8,128)(2,1)S(1)}, u32[]{:S(2)}, u32[]{:S(2)}) collective-permute-start(bf16[3,16,3072]{2,1,0:T(8,128)(2,1)S(1)} %get-tuple-element.24), channel_id=1, source_target_pairs={{0,1},{1,0},{2,3},{3,2},{4,5},{5,4},{6,7},{7,6},{8,9},{9,8},{10,11... | collective-permute-start | bytes 884744 | tf_op jit(solution)/shard_map/ppermute | solution.py:572
  6.1 1.0 %copy-start.3 = (bf16[3,3,64,192]{3,2,1,0:T(8,128)(2,1)S(1)}, bf16[3,3,64,192]{3,2,1,0:T(8,128)(2,1)}, u32[]{:S(2)}) copy-start(bf16[3,3,64,192]{3,2,1,0:T(8,128)(2,1)} %param.18) | copy-start | bytes 663556
  7.1 1.0 %copy-start.4 = (bf16[3,3,64,192]{3,2,1,0:T(8,128)(2,1)S(1)}, bf16[3,3,64,192]{3,2,1,0:T(8,128)(2,1)}, u32[]{:S(2)}) copy-start(bf16[3,3,64,192]{3,2,1,0:T(8,128)(2,1)} %param.19) | copy-start | bytes 663556
  8.1 1.0 %copy-start.5 = (bf16[3,3,64,192]{3,2,1,0:T(8,128)(2,1)S(1)}, bf16[3,3,64,192]{3,2,1,0:T(8,128)(2,1)}, u32[]{:S(2)}) copy-start(bf16[3,3,64,192]{3,2,1,0:T(8,128)(2,1)} %param.20) | copy-start | bytes 663556
  9.0 0.7 copy-start.9
  24.0 18.2 %copy-start.2 = (bf16[3,3,192,576]{3,2,1,0:T(8,128)(2,1)S(1)}, bf16[3,3,192,576]{3,2,1,0:T(8,128)(2,1)}, u32[]{:S(2)}) copy-start(bf16[3,3,192,576]{3,2,1,0:T(8,128)(2,1)} %param.21) | copy-start | bytes 5971972
  24.0 18.1 %collective-permute-start.2 = (bf16[72,16,128]{2,1,0:T(8,128)(2,1)S(1)}, bf16[72,16,128]{2,1,0:T(8,128)(2,1)S(1)}, u32[]{:S(2)}, u32[]{:S(2)}) collective-permute-start(bf16[72,16,128]{2,1,0:T(8,128)(2,1)S(1)} %get-tuple-element.29), channel_id=1, source_target_pairs={{1,2},{3,4},{5,6},{7,8},{9,10},{11,12},{13,14},{2,1},{4,3},{6,5},{... | collective-permute-start | bytes 884744 | tf_op jit(solution)/shard_map/ppermute | solution.py:569
  27.8 14.4 %collective-permute-start.3 = (bf16[72,16,128]{2,1,0:T(8,128)(2,1)S(1)}, bf16[72,16,128]{2,1,0:T(8,128)(2,1)S(1)}, u32[]{:S(2)}, u32[]{:S(2)}) collective-permute-start(bf16[72,16,128]{2,1,0:T(8,128)(2,1)S(1)} %get-tuple-element.30), channel_id=1, source_target_pairs={{0,1},{1,0},{2,3},{3,2},{4,5},{5,4},{6,7},{7,6},{8,9},{9,8},{10,11... | collective-permute-start | bytes 884744 | tf_op jit(solution)/shard_map/ppermute | solution.py:572
  27.9 10.3 %collective-permute-start.4 = (bf16[2,16,3072]{2,1,0:T(8,128)(2,1)S(1)}, bf16[2,16,3072]{2,1,0:T(8,128)(2,1)S(1)}, u32[]{:S(2)}, u32[]{:S(2)}) collective-permute-start(bf16[2,16,3072]{2,1,0:T(8,128)(2,1)S(1)} %bitcast.35), channel_id=1, source_target_pairs={{1,2},{3,4},{5,6},{7,8},{9,10},{11,12},{13,14},{2,1},{4,3},{6,5},{... | collective-permute-start | bytes 589832 | tf_op jit(solution)/shard_map/ppermute | solution.py:569
  29.8 8.4 %collective-permute-start.5 = (bf16[2,16,3072]{2,1,0:T(8,128)(2,1)S(1)}, bf16[2,16,3072]{2,1,0:T(8,128)(2,1)S(1)}, u32[]{:S(2)}, u32[]{:S(2)}) collective-permute-start(bf16[2,16,3072]{2,1,0:T(8,128)(2,1)S(1)} %bitcast.36), channel_id=1, source_target_pairs={{0,1},{1,0},{2,3},{3,2},{4,5},{5,4},{6,7},{7,6},{8,9},{9,8},{10,11... | collective-permute-start | bytes 589832 | tf_op jit(solution)/shard_map/ppermute | solution.py:572
  42.2 22.5 %copy-start.6 = (bf16[3,3,192,64]{2,3,1,0:T(8,128)(2,1)S(1)}, bf16[3,3,192,64]{2,3,1,0:T(8,128)(2,1)}, u32[]{:S(2)}) copy-start(bf16[3,3,192,64]{2,3,1,0:T(8,128)(2,1)} %param.24) | copy-start | bytes 663556
  42.2 22.5 %copy-start.7 = (bf16[3,3,64,192]{3,2,1,0:T(8,128)(2,1)S(1)}, bf16[3,3,64,192]{3,2,1,0:T(8,128)(2,1)}, u32[]{:S(2)}) copy-start(bf16[3,3,64,192]{3,2,1,0:T(8,128)(2,1)} %param.25) | copy-start | bytes 663556
  42.2 22.5 %copy-start.8 = (bf16[3,3,64,192]{3,2,1,0:T(8,128)(2,1)S(1)}, bf16[3,3,64,192]{3,2,1,0:T(8,128)(2,1)}, u32[]{:S(2)}) copy-start(bf16[3,3,64,192]{3,2,1,0:T(8,128)(2,1)} %param.26) | copy-start | bytes 663556
  42.2 22.5 %copy-start.10 = (bf16[64,16]{0,1:T(8,128)(2,1)S(1)}, bf16[64,16]{0,1:T(8,128)(2,1)}, u32[]{:S(2)}) copy-start(bf16[64,16]{0,1:T(8,128)(2,1)} %param.27) | copy-start | bytes 6148
  42.2 23.7 %copy-start.1 = (bf16[3,3,192,576]{3,2,1,0:T(8,128)(2,1)S(1)}, bf16[3,3,192,576]{3,2,1,0:T(8,128)(2,1)}, u32[]{:S(2)}) copy-start(bf16[3,3,192,576]{3,2,1,0:T(8,128)(2,1)} %param.23) | copy-start | bytes 5971972
  50.3 1.5 %collective-permute-start.6 = (bf16[48,16,128]{2,1,0:T(8,128)(2,1)S(1)}, bf16[48,16,128]{2,1,0:T(8,128)(2,1)S(1)}, u32[]{:S(2)}, u32[]{:S(2)}) collective-permute-start(bf16[48,16,128]{2,1,0:T(8,128)(2,1)S(1)} %shard_map.140.c_own), channel_id=1, source_target_pairs={{0,1},{1,0},{2,3},{3,2},{4,5},{5,4},{6,7},{7,6},{8,9},{9,8},{10,11... | collective-permute-start | bytes 589832 | tf_op jit(solution)/shard_map/ppermute | solution.py:572
  51.8 12.7 %collective-permute-start.7 = (bf16[72,16,128]{2,1,0:T(8,128)(2,1)S(1)}, bf16[72,16,128]{2,1,0:T(8,128)(2,1)S(1)}, u32[]{:S(2)}, u32[]{:S(2)}) collective-permute-start(bf16[72,16,128]{2,1,0:T(8,128)(2,1)S(1)} %pad_maximum_fusion), channel_id=1, source_target_pairs={{1,2},{3,4},{5,6},{7,8},{9,10},{11,12},{13,14},{2,1},{4,3},{6,5},{... | collective-permute-start | bytes 884744 | tf_op jit(solution)/shard_map/ppermute | solution.py:569
  55.6 9.9 %collective-permute-start.10 = (bf16[2,16,16,128]{3,2,1,0:T(8,128)(2,1)S(1)}, bf16[2,16,16,128]{3,2,1,0:T(8,128)(2,1)S(1)}, u32[]{:S(2)}, u32[]{:S(2)}) collective-permute-start(bf16[2,16,16,128]{3,2,1,0:T(8,128)(2,1)S(1)} %get-tuple-element.35), channel_id=1, source_target_pairs={{0,1},{1,0},{2,3},{3,2},{4,5},{5,4},{6,7},{7,6},{8,9},{9,8},{10,11... | collective-permute-start | bytes 393224 | tf_op jit(solution)/shard_map/ppermute | solution.py:572
  55.6 10.3 %collective-permute-start.9 = (bf16[2,16,16,128]{3,2,1,0:T(8,128)(2,1)S(1)}, bf16[2,16,16,128]{3,2,1,0:T(8,128)(2,1)S(1)}, u32[]{:S(2)}, u32[]{:S(2)}) collective-permute-start(bf16[2,16,16,128]{3,2,1,0:T(8,128)(2,1)S(1)} %get-tuple-element.34), channel_id=1, source_target_pairs={{1,2},{3,4},{5,6},{7,8},{9,10},{11,12},{13,14},{2,1},{4,3},{6,5},{... | collective-permute-start | bytes 393224 | tf_op jit(solution)/shard_map/ppermute | solution.py:569
  64.5 1.4 %collective-permute-start.8 = (bf16[24,16,128]{2,1,0:T(8,128)(2,1)S(1)}, bf16[24,16,128]{2,1,0:T(8,128)(2,1)S(1)}, u32[]{:S(2)}, u32[]{:S(2)}) collective-permute-start(bf16[24,16,128]{2,1,0:T(8,128)(2,1)S(1)} %slice.19), channel_id=1, source_target_pairs={{0,1},{1,0},{2,3},{3,2},{4,5},{5,4},{6,7},{7,6},{8,9},{9,8},{10,11... | collective-permute-start | bytes 294920 | tf_op jit(solution)/shard_map/ppermute | solution.py:572

commit v4 on v3

--- a/solution.py
+++ b/solution.py
@@ -240,8 +240,7 @@
             p1[idx, 2 + 2 * k] = jnp.where(lo[0], p1[idx, 2 + 2 * k], pair)
         seal(p1, idx, FB)
 
-    @pl.loop(1, 8)
-    def _(idx):
+    for idx in range(1, 8):
         def emit(lo_block, count, new):
             stems = stem2[idx, pl.ds(lo_block, count)]
             p2[idx, pl.ds(1 + lo_block, count)] = jnp.where(lo, stems, new)
@@ -249,8 +248,7 @@
         fine_gru(p1, idx, w_gru, in_grid(first + idx - 3, rows), emit)
         seal(p2, idx, FB)
 
-    @pl.loop(2, 7)
-    def _(idx):
+    for idx in range(2, 7):
         def emit(lo_block, count, new):
             p3[idx, pl.ds(1 + lo_block, count)] = jnp.where(lo, jnp.zeros_like(new), new)
 
@@ -318,16 +316,19 @@
         a, b = (outer, inner) if idx < 2 else (inner, outer)
         put_packed(h0, idx, raw_tiles(lambda lanes: jnp.where(upper, a[r, :, lanes], b[r, :, lanes])))
 
-    @pl.loop(0, 4)
-    def _(idx):
+    for idx in range(0, 4):
         acc_out[idx, :, : 3 * C2] = jnp.dot(coarse_patches(h0, idx + 1), w_h[...], preferred_element_type=F32)
         acc_out[idx, :, 4 * LANES + C1 :] = jnp.zeros((CB * SUB, C1), F32)
         h_out[idx] = h0[idx + 1]
 
 
+def put_row(ref, forms):
+    for k, tile in enumerate(pack_forms(forms)):
+        ref[k * PAIRS : (k + 1) * PAIRS] = tile
+
+
 def coarse_encoder_body(
-    low_own, low_outer, low_inner, acc_first, h_first, w_x, w_h,
-    state_out, x1, x2, h1, acc_x, acc_h,
+    low_own, low_outer, low_inner, acc_first, h_first, w_x, w_h, near, h1, x2, x1, acc_x, acc_h,
 ):
     upper, first, rows = place(2)
     zero_tail(acc_x)
@@ -345,19 +346,22 @@
     put_packed(x2, 0, lambda i: jnp.where(upper, packed_tiles(low_outer, 2)(i), packed_tiles(low_inner, 2)(i)))
     put_packed(x2, 3, lambda i: jnp.where(upper, packed_tiles(low_inner, 2)(i), packed_tiles(low_outer, 2)(i)))
 
-    @pl.loop(0, 4)
-    def _(idx):
+    for idx in range(4):
         forms = coarse_gru(
             x1, idx + 1, h_first, idx, w_x, None, acc_x, acc_first.at[idx], in_grid(first + idx - 1, rows)
         )
         put_forms(h1, idx, forms)
 
-    @pl.loop(0, 2)
-    def _(idx):
-        forms = coarse_gru(x2, idx + 1, h1, idx + 1, w_x, w_h, acc_x, acc_h, in_grid(first + idx, rows))
-        slot = jnp.where(upper, idx, 1 - idx)
-        for k, tile in enumerate(pack_forms(forms)):
-            state_out[pl.ds(slot * ROW_TILES + k * PAIRS, PAIRS)] = tile
+    idx = jnp.where(upper, 1, 0)
+    put_row(near, coarse_gru(x2, idx + 1, h1, idx + 1, w_x, w_h, acc_x, acc_h, True))
+
+
+def coarse_rest_body(h1, x2, w_x, w_h, far, acc_x, acc_h):
+    upper, _, _ = place(2)
+    zero_tail(acc_x)
+    zero_tail(acc_h)
+    idx = jnp.where(upper, 0, 1)
+    put_row(far, coarse_gru(x2, idx + 1, h1, idx + 1, w_x, w_h, acc_x, acc_h, True))
 
 
 def raise_pair(src, idx, weight):
@@ -371,26 +375,45 @@
     return jnp.dot(jnp.concatenate(parts, axis=-1), weight[...], preferred_element_type=F32)
 
 
+def either(upper, a, i, b, j):
+    return lambda t: jnp.where(upper, packed_tiles(a, i)(t), packed_tiles(b, j)(t))
+
+
+def forecast_start_body(far, near, outer, in_far, in_near, w_h, s1, h2, acc_h):
+    upper, first, rows = place(2)
+    zero_tail(acc_h)
+    put_packed(h2, 0, packed_tiles(outer, 2))
+    put_packed(h2, 1, either(upper, outer, 1, in_far, 0))
+    put_packed(h2, 2, either(upper, outer, 0, in_near, 0))
+    put_packed(h2, 3, either(upper, far, 0, near, 0))
+    put_packed(h2, 4, either(upper, near, 0, far, 0))
+    put_packed(h2, 5, either(upper, in_near, 0, outer, 0))
+    put_packed(h2, 6, either(upper, in_far, 0, outer, 1))
+    put_packed(h2, 7, packed_tiles(outer, 2))
+
+    shift = jnp.where(upper, 0, 1)
+    for k in range(5):
+        idx = k + shift
+        forms = coarse_gru(None, 0, h2, idx + 1, None, w_h, None, acc_h, in_grid(first + idx - 2, rows))
+        put_forms(s1, idx, forms)
+
+
 def forecaster_body(
-    c_own, c_outer, c_inner, c_third, f_own, f_outer, f_inner, w_h, w_up, w_gru, w_head,
-    out, h2, s1, s2, pf1, pf2, states, acc_h,
+    s1_given, in_far, in_near, third, f_own, f_outer, f_inner, w_h, w_up, w_gru, w_head,
+    out, s1, h2, s2, pf1, pf2, states, acc_h,
 ):
     upper, first_c, rows_c = place(2)
     _, first_f, rows_f = place(4)
     lo = low_half((1, SUB, LANES))
     zero_tail(acc_h)
 
-    def either(a, i, b, j):
-        return lambda t: jnp.where(upper, packed_tiles(a, i)(t), packed_tiles(b, j)(t))
-
-    put_packed(h2, 0, either(c_outer, 2, c_third, 0))
-    put_packed(h2, 1, either(c_outer, 1, c_inner, 0))
-    put_packed(h2, 2, either(c_outer, 0, c_inner, 1))
-    put_packed(h2, 3, either(c_own, 0, c_own, 1))
-    put_packed(h2, 4, either(c_own, 1, c_own, 0))
-    put_packed(h2, 5, either(c_inner, 1, c_outer, 0))
-    put_packed(h2, 6, either(c_inner, 0, c_outer, 1))
-    put_packed(h2, 7, either(c_third, 0, c_outer, 2))
+    put_packed(h2, 0, either(upper, in_near, 0, third, 0))
+    put_packed(h2, 1, packed_tiles(in_far, 0))
+    put_packed(h2, 2, either(upper, third, 0, in_near, 0))
+    last = jnp.where(upper, 5, 0)
+    put_forms(
+        s1, last, coarse_gru(None, 0, h2, 1, None, w_h, None, acc_h, in_grid(first_c + last - 2, rows_c))
+    )
 
     for idx in range(8):
         for k in range(FB // 2):
@@ -403,13 +426,7 @@
             pf1[idx, 1 + 2 * k] = swap_bf(pair)
             pf1[idx, 2 + 2 * k] = pair
 
-    @pl.loop(0, 6)
-    def _(idx):
-        forms = coarse_gru(None, 0, h2, idx + 1, None, w_h, None, acc_h, in_grid(first_c + idx - 2, rows_c))
-        put_forms(s1, idx, forms)
-
-    @pl.loop(0, 4)
-    def _(idx):
+    for idx in range(0, 4):
         forms = coarse_gru(None, 0, s1, idx + 1, None, w_h, None, acc_h, in_grid(first_c + idx - 1, rows_c))
         put_forms(s2, idx, forms)
 
@@ -427,14 +444,12 @@
             both = jnp.stack([even, odd], axis=1).reshape(FB, SUB, LANES)
             fine[row, 1 : FB + 1] = jnp.where(lo, both, fine[row, 1 : FB + 1])
 
-    @pl.loop(0, 4)
-    def _(k):
+    for k in range(0, 4):
         raise_rows(s1, k + 1, pf1, (2 * k, 2 * k + 1), first_c + k - 1)
         seal(pf1, 2 * k, FB)
         seal(pf1, 2 * k + 1, FB)
 
-    @pl.loop(0, 6)
-    def _(idx):
+    for idx in range(0, 6):
         def emit(lo_block, count, new):
             pf2[idx, pl.ds(1 + lo_block, count)] = new
 
@@ -457,8 +472,7 @@
     for idx in range(6):
         seal(pf2, idx, FB)
 
-    @pl.loop(0, 4)
-    def _(idx):
+    for idx in range(0, 4):
         def emit(lo_block, count, new):
             states[idx, pl.ds(1 + lo_block, count)] = new
 
@@ -534,13 +548,14 @@
         w_head[k * LANES + C1 : (k + 1) * LANES, k * PATCH : (k + 1) * PATCH] = tall
 
 
-def call(body, args, outs, scratch):
+def call(body, args, outs, scratch, aliases={}):
     return pl.pallas_call(
         body,
         out_shape=[s if isinstance(s, jax.ShapeDtypeStruct) else jax.ShapeDtypeStruct(s, BF) for s in outs],
         in_specs=[pl.BlockSpec(memory_space=space) for _, space in args],
         out_specs=[pl.BlockSpec(memory_space=pltpu.VMEM)] * len(outs),
         scratch_shapes=scratch,
+        input_output_aliases=aliases,
         compiler_params=pltpu.CompilerParams(vmem_limit_bytes=24 * 1024 * 1024),
     )(*[arg for arg, _ in args])
 
@@ -629,22 +644,33 @@
     )
     state_fo, state_fi = outer_swap(state_fo), inner_swap(state_fi)
 
-    (state_c,) = call(
+    w_x, w_h = enc_coarse_x.reshape(flat), enc_coarse_h.reshape(flat)
+    four = (4, CB + 2, SUB, 4 * LANES)
+    near, h1, x2 = call(
         coarse_encoder_body,
-        on_chip(low_own, got_o, got_i, acc_first, h_first, enc_coarse_x.reshape(flat), enc_coarse_h.reshape(flat)),
-        [(2 * ROW_TILES, SUB, LANES)],
-        [coarse_buf(6), coarse_buf(4), coarse_buf(4), acc_buf, acc_buf],
-    )
-    state_ci = inner_swap(state_c)
-    state_co = outer_swap(jnp.concatenate([state_c, state_ci[ROW_TILES:]], axis=0))
+        on_chip(low_own, got_o, got_i, acc_first, h_first, w_x, w_h),
+        [(ROW_TILES, SUB, LANES), four, four],
+        [coarse_buf(6), acc_buf, acc_buf],
+    )
+    in_near = inner_swap(near)
+    (far,) = call(coarse_rest_body, on_chip(h1, x2, w_x, w_h), [(ROW_TILES, SUB, LANES)], [acc_buf, acc_buf])
+    in_far = inner_swap(far)
+    state_co = outer_swap(jnp.concatenate([far, near, in_near], axis=0))
     third = inner_swap(state_co[:ROW_TILES])
 
-    (out,) = call(
+    w_f = fc_coarse_h.reshape(flat)
+    (s1,) = call(
+        forecast_start_body,
+        on_chip(far, near, state_co, in_far, in_near, w_f),
+        [(6, CB + 2, SUB, 4 * LANES)],
+        [coarse_buf(8), acc_buf],
+    )
+    out, _ = call(
         forecaster_body,
-        on_chip(state_c, state_co, state_ci, third, state_f, state_fo, state_fi, fc_coarse_h.reshape(flat))
-        + on_chip(w_up, w_fc, w_head),
-        [(HORIZON, 4, SUB, FB * PATCH)],
-        [coarse_buf(8), coarse_buf(6), coarse_buf(5), fine_buf(8), fine_buf(6), fine_buf(4), acc_buf],
+        on_chip(s1, in_far, in_near, third, state_f, state_fo, state_fi, w_f, w_up, w_fc, w_head),
+        [(HORIZON, 4, SUB, FB * PATCH), (6, CB + 2, SUB, 4 * LANES)],
+        [coarse_buf(3), coarse_buf(5), fine_buf(8), fine_buf(6), fine_buf(4), acc_buf],
+        {0: 1},
     )
     return out.reshape(HORIZON, 4, COLS * PATCH)
 

time: 86.7 us -> 74.2 us (0.86)
  Pallas kernels: 43 us -> 32.3 us
  waiting for transfers between devices: 18.9 us -> 16.7 us
    pallas_call x7 -> x9, Pallas kernels: 43 us -> 32.3 us  [call(): pl.pallas_call(body, out_shape=[s if isinstance(s, jax.ShapeDtypeStruct)...]
    ppermute x6 -> x7, waiting for transfers between devices: 1.44 us -> 0.02 us  [inner_swap(): return lax.ppermute(x, 'section', [(0, 1), (1, 0)])]
    ppermute x6 -> x7, starting transfers between devices: 0.9 us -> 2.23 us  [inner_swap(): return lax.ppermute(x, 'section', [(0, 1), (1, 0)])]
    ppermute x5, starting transfers between devices: 16.4 us -> 15.2 us  [outer_swap(): return lax.ppermute(x, LINE, across)]
  transfers between devices with their start and end apart: 11 -> 12, of which waited for: 5 -> 3; matrix products, arithmetic and copies ran while one was open for 0% -> 0% of each run, Pallas kernels for 6% -> 15%
where the time goes in v4:
time: 74.2 us; the launch traced here: 73.3 us
  Pallas kernels  32.3 us (44%)
  starting transfers between devices  17.5 us (24%)
  waiting for transfers between devices  16.7 us (23%)
  local copies, waits for them, and re-layouts  6.44 us (9%)
    pallas_call x9, Pallas kernels, call(): pl.pallas_call(body, out_shape=[s if isinstance(s, jax.ShapeDtypeStruct)...  32.3 us
    ppermute x5, waiting for transfers between devices, outer_swap(): return lax.ppermute(x, LINE, across)  16.7 us
    ppermute x5, starting transfers between devices, outer_swap(): return lax.ppermute(x, LINE, across)  15.2 us
    unnamed x26, local copies, waits for them, and re-layouts  4.75 us
    ppermute x7, starting transfers between devices, inner_swap(): return lax.ppermute(x, 'section', [(0, 1), (1, 0)])  2.23 us
  transfers between devices with their start and end apart: 12, of which 3 were waited for; matrix products, arithmetic and copies ran while one was open for 0% of the time, Pallas kernels for 15%

profile of v4, /device:TPU:19, one launch (start us, length us, event | category | flops | bytes accessed | tf_op | source)
XLA Modules:
  0.0 73.3 jit_solution(8686820077265614459)
XLA Ops:
  0.0 0.9 %fusion = (bf16[1,4,8192]{2,1,0:T(4,128)(2,1)S(1)}, bf16[1,4,8192]{2,1,0:T(4,128)(2,1)S(1)}) fusion(bf16[2,4,8192]{2,1,0:T(4,128)(2,1)} %param.14), kind=kLoop, calls=%fused_computation.5 | loop fusion | bytes 262144 | tf_op jit(solution)/shard_map/slice | solution.py:603
  0.9 1.1 %copy.24 = bf16[1,4,16,2048]{3,2,1,0:T(8,128)(2,1)S(1)} copy(bf16[1,4,16,2048]{3,1,2,0:T(4,128)(2,1)} %bitcast.48) | data formatting | bytes 524288
  2.1 0.0 copy-start.11
  2.1 0.1 shard_map.136
  2.2 3.7 %collective-permute-start = (bf16[3,16,3072]{2,1,0:T(8,128)(2,1)S(1)}, bf16[3,16,3072]{2,1,0:T(8,128)(2,1)S(1)}, u32[]{:S(2)}, u32[]{:S(2)}) collective-permute-start(bf16[3,16,3072]{2,1,0:T(8,128)(2,1)S(1)} %get-tuple-element.27), channel_id=1, source_target_pairs={{1,2},{3,4},{5,6},{7,8},{9,10},{11,12},{13,14},{2,1},{4,3},{6,5},{... | collective-permute-start | bytes 884744 | tf_op jit(solution)/shard_map/ppermute | solution.py:584
  5.9 0.1 collective-permute-start.1
  6.0 1.0 %copy-done.3 = bf16[3,3,64,192]{3,2,1,0:T(8,128)(2,1)S(1)} copy-done((bf16[3,3,64,192]{3,2,1,0:T(8,128)(2,1)S(1)}, bf16[3,3,64,192]{3,2,1,0:T(8,128)(2,1)}, u32[]{:S(2)}) %copy-start.3) | copy-done | bytes 221208
  6.9 1.0 %copy-done.4 = bf16[3,3,64,192]{3,2,1,0:T(8,128)(2,1)S(1)} copy-done((bf16[3,3,64,192]{3,2,1,0:T(8,128)(2,1)S(1)}, bf16[3,3,64,192]{3,2,1,0:T(8,128)(2,1)}, u32[]{:S(2)}) %copy-start.4) | copy-done | bytes 221208
  7.9 1.0 %copy-done.5 = bf16[3,3,64,192]{3,2,1,0:T(8,128)(2,1)S(1)} copy-done((bf16[3,3,64,192]{3,2,1,0:T(8,128)(2,1)S(1)}, bf16[3,3,64,192]{3,2,1,0:T(8,128)(2,1)}, u32[]{:S(2)}) %copy-start.5) | copy-done | bytes 221208
  8.8 0.7 copy-done.9
  9.5 0.5 shard_map.137
  10.0 3.4 %collective-permute-done.outer = bf16[3,16,3072]{2,1,0:T(8,128)(2,1)S(1)} collective-permute-done((bf16[3,16,3072]{2,1,0:T(8,128)(2,1)S(1)}, bf16[3,16,3072]{2,1,0:T(8,128)(2,1)S(1)}, u32[]{:S(2)}, u32[]{:S(2)}) %collective-permute-start) | collective-permute-done | bytes 294944 | tf_op jit(solution)/shard_map/ppermute | solution.py:584
  13.4 7.0 %shard_map.138 = (bf16[4,16,16,128]{3,2,1,0:T(8,128)(2,1)S(1)}, bf16[96,16,128]{2,1,0:T(8,128)(2,1)S(1)}, bf16[72,16,128]{2,1,0:T(8,128)(2,1)S(1)}, bf16[72,16,1...) custom-call(bf16[4,16,3072]{2,1,0:T(8,128)(2,1)S(1)} %get-tuple-element.26.own, ...), custom_call_target="tpu_custom_call" | custom-call | tf_op jit(solution)/shard_map/pallas_call | solution.py:552
  20.5 3.8 %collective-permute-start.2 = (bf16[72,16,128]{2,1,0:T(8,128)(2,1)S(1)}, bf16[72,16,128]{2,1,0:T(8,128)(2,1)S(1)}, u32[]{:S(2)}, u32[]{:S(2)}) collective-permute-start(bf16[72,16,128]{2,1,0:T(8,128)(2,1)S(1)} %get-tuple-element.33), channel_id=1, source_target_pairs={{1,2},{3,4},{5,6},{7,8},{9,10},{11,12},{13,14},{2,1},{4,3},{6,5},{... | collective-permute-start | bytes 884744 | tf_op jit(solution)/shard_map/ppermute | solution.py:584
  24.2 0.1 collective-permute-start.3
  24.4 2.1 %collective-permute-start.4 = (bf16[2,16,3072]{2,1,0:T(8,128)(2,1)S(1)}, bf16[2,16,3072]{2,1,0:T(8,128)(2,1)S(1)}, u32[]{:S(2)}, u32[]{:S(2)}) collective-permute-start(bf16[2,16,3072]{2,1,0:T(8,128)(2,1)S(1)} %bitcast.38), channel_id=1, source_target_pairs={{1,2},{3,4},{5,6},{7,8},{9,10},{11,12},{13,14},{2,1},{4,3},{6,5},{... | collective-permute-start | bytes 589832 | tf_op jit(solution)/shard_map/ppermute | solution.py:584
  26.5 0.5 collective-permute-start.5
  27.0 7.6 %collective-permute-done.4.outer = bf16[2,16,3072]{2,1,0:T(8,128)(2,1)S(1)} collective-permute-done((bf16[2,16,3072]{2,1,0:T(8,128)(2,1)S(1)}, bf16[2,16,3072]{2,1,0:T(8,128)(2,1)S(1)}, u32[]{:S(2)}, u32[]{:S(2)}) %collective-permute-start.4) | collective-permute-done | bytes 196640 | tf_op jit(solution)/shard_map/ppermute | solution.py:584
  34.7 3.2 %shard_map.139 = (f32[4,256,640]{2,1,0:T(8,128)S(1)}, bf16[4,18,16,512]{3,2,1,0:T(8,128)(2,1)S(1)}) custom-call(bf16[2,16,3072]{2,1,0:T(8,128)(2,1)S(1)} %bitcast.40, bf16[2,16,3072]{2,1,0:T(8,128)(2,1)S(1)} %collective-permute-done.4.outer, bf16[2,16,3072]{2,1,0:T(8,128)(2,1)S(1)} %collective-permute-done.5.inner, bf16[1728,576]{1,0:T(8,128)(2,1)S(1)} %bitcast.30), custom_call_target="tpu_custom_call" | custom-call | tf_op jit(solution)/shard_map/pallas_call | solution.py:552
  37.9 5.0 %shard_map.140 = (bf16[24,16,128]{2,1,0:T(8,128)(2,1)S(1)}, bf16[4,18,16,512]{3,2,1,0:T(8,128)(2,1)S(1)}, bf16[4,18,16,512]{3,2,1,0:T(8,128)(2,1)S(1)}) custom-call(bf16[96,16,128]{2,1,0:T(8,128)(2,1)S(1)} %get-tuple-element.32.low_own, bf16[72,16,128]{2,1,0:T(8,128)(2,1)S(1)} %collective-permute-done.2.low_outer, ...), custom_call_target="tpu_custom_call" | custom-call | tf_op jit(solution)/shard_map/pallas_call | solution.py:552
  42.9 0.1 collective-permute-start.6
  43.0 1.7 %shard_map.141.far = bf16[24,16,128]{2,1,0:T(8,128)(2,1)S(1)} custom-call(bf16[4,18,16,512]{3,2,1,0:T(8,128)(2,1)S(1)} %get-tuple-element.37.h1, bf16[4,18,16,512]{3,2,1,0:T(8,128)(2,1)S(1)} %get-tuple-element.38.x2, bf16[1728,576]{1,0:T(8,128)(2,1)S(1)} %bitcast.36, bf16[1728,576]{1,0:T(8,128)(2,1)S(1)} %bitcast.32), custom_call_target="tpu_custom_call" | custom-call | tf_op jit(solution)/shard_map/pallas_call | solution.py:552
  44.8 3.7 %collective-permute-start.7 = (bf16[72,16,128]{2,1,0:T(8,128)(2,1)S(1)}, bf16[72,16,128]{2,1,0:T(8,128)(2,1)S(1)}, u32[]{:S(2)}, u32[]{:S(2)}) collective-permute-start(bf16[72,16,128]{2,1,0:T(8,128)(2,1)S(1)} %pad_maximum_fusion), channel_id=1, source_target_pairs={{1,2},{3,4},{5,6},{7,8},{9,10},{11,12},{13,14},{2,1},{4,3},{6,5},{... | collective-permute-start | bytes 884744 | tf_op jit(solution)/shard_map/ppermute | solution.py:584
  48.5 1.9 %collective-permute-start.10 = (bf16[2,16,16,128]{3,2,1,0:T(8,128)(2,1)S(1)}, bf16[2,16,16,128]{3,2,1,0:T(8,128)(2,1)S(1)}, u32[]{:S(2)}, u32[]{:S(2)}) collective-permute-start(bf16[2,16,16,128]{3,2,1,0:T(8,128)(2,1)S(1)} %get-tuple-element.41), channel_id=1, source_target_pairs={{1,2},{3,4},{5,6},{7,8},{9,10},{11,12},{13,14},{2,1},{4,3},{6,5},{... | collective-permute-start | bytes 393224 | tf_op jit(solution)/shard_map/ppermute | solution.py:584
  50.5 1.3 %collective-permute-start.11 = (bf16[2,16,16,128]{3,2,1,0:T(8,128)(2,1)S(1)}, bf16[2,16,16,128]{3,2,1,0:T(8,128)(2,1)S(1)}, u32[]{:S(2)}, u32[]{:S(2)}) collective-permute-start(bf16[2,16,16,128]{3,2,1,0:T(8,128)(2,1)S(1)} %get-tuple-element.42), channel_id=1, source_target_pairs={{0,1},{1,0},{2,3},{3,2},{4,5},{5,4},{6,7},{7,6},{8,9},{9,8},{10,11... | collective-permute-start | bytes 393224 | tf_op jit(solution)/shard_map/ppermute | solution.py:587
  51.8 0.1 collective-permute-start.8
  51.9 5.6 %collective-permute-done.7.outer = bf16[72,16,128]{2,1,0:T(8,128)(2,1)S(1)} collective-permute-done((bf16[72,16,128]{2,1,0:T(8,128)(2,1)S(1)}, bf16[72,16,128]{2,1,0:T(8,128)(2,1)S(1)}, u32[]{:S(2)}, u32[]{:S(2)}) %collective-permute-start.7) | collective-permute-done | bytes 294944 | tf_op jit(solution)/shard_map/ppermute | solution.py:584
  57.5 0.1 collective-permute-start.9
  57.6 1.0 %shard_map.143 = (bf16[768,256]{1,0:T(8,128)(2,1)S(1)}, bf16[1152,256]{1,0:T(8,128)(2,1)S(1)}, bf16[1024,128]{1,0:T(8,128)(2,1)S(1)}) custom-call(bf16[9,64,192]{2,1,0:T(8,128)(2,1)S(1)} %bitcast.44, bf16[9,64,192]{2,1,0:T(8,128)(2,1)S(1)} %bitcast.45, bf16[9,64,192]{2,1,0:T(8,128)(2,1)S(1)} %bitcast.46, bf16[16,64]{1,0:T(8,128)(2,1)S(1)} %bitcast.47), custom_call_target="tpu_custom_call" | custom-call | tf_op jit(solution)/shard_map/pallas_call | solution.py:552
  58.6 4.5 %shard_map.142.s1_given = bf16[6,18,16,512]{3,2,1,0:T(8,128)(2,1)S(1)} custom-call(bf16[24,16,128]{2,1,0:T(8,128)(2,1)S(1)} %shard_map.141.far, bf16[24,16,128]{2,1,0:T(8,128)(2,1)S(1)} %get-tuple-element.39.near, bf16[72,16,128]{2,1,0:T(8,128)(2,1)S(1)} %collective-permute-done.7.outer, bf16[24,16,128]{2,1,0:T(8,128)(2,1)S(1)} %collective-permute-done.8.in_far, ...), custom_call_target="tpu_custom_call" | custom-call | tf_op jit(solution)/shard_map/pallas_call | solution.py:552
  63.2 9.3 %shard_map.144 = (bf16[2,4,16,512]{3,2,1,0:T(8,128)(2,1)S(1)}, bf16[6,18,16,512]{3,2,1,0:T(8,128)(2,1)S(1)}) custom-call(bf16[6,18,16,512]{3,2,1,0:T(8,128)(2,1)S(1)} %shard_map.142.s1_given, bf16[24,16,128]{2,1,0:T(8,128)(2,1)S(1)} %collective-permute-done.8.in_far, ...), custom_call_target="tpu_custom_call", output_to_operand_aliasing={{1}: (0, {})} | custom-call | tf_op jit(solution)/shard_map/pallas_call | solution.py:552
  72.5 0.7 %reshape.53 = bf16[2,4,8192]{2,1,0:T(4,128)(2,1)} reshape(bf16[2,4,16,512]{3,2,1,0:T(8,128)(2,1)S(1)} %get-tuple-element.46) | data formatting | bytes 262144 | tf_op jit(solution)/shard_map/reshape | solution.py:675
  (32 shorter events, 0.2 us)
Async XLA Ops:
  2.1 22.3 %copy-start.11 = (bf16[2,49152]{1,0:T(2,128)(2,1)S(1)}, bf16[2,49152]{1,0:T(2,128)(2,1)}, u32[]{:S(2)}) copy-start(bf16[2,49152]{1,0:T(2,128)(2,1)} %param.16) | copy-start | bytes 589828
  2.2 11.3 %collective-permute-start = (bf16[3,16,3072]{2,1,0:T(8,128)(2,1)S(1)}, bf16[3,16,3072]{2,1,0:T(8,128)(2,1)S(1)}, u32[]{:S(2)}, u32[]{:S(2)}) collective-permute-start(bf16[3,16,3072]{2,1,0:T(8,128)(2,1)S(1)} %get-tuple-element.27), channel_id=1, source_target_pairs={{1,2},{3,4},{5,6},{7,8},{9,10},{11,12},{13,14},{2,1},{4,3},{6,5},{... | collective-permute-start | bytes 884744 | tf_op jit(solution)/shard_map/ppermute | solution.py:584
  5.9 7.6 %collective-permute-start.1 = (bf16[3,16,3072]{2,1,0:T(8,128)(2,1)S(1)}, bf16[3,16,3072]{2,1,0:T(8,128)(2,1)S(1)}, u32[]{:S(2)}, u32[]{:S(2)}) collective-permute-start(bf16[3,16,3072]{2,1,0:T(8,128)(2,1)S(1)} %get-tuple-element.28), channel_id=1, source_target_pairs={{0,1},{1,0},{2,3},{3,2},{4,5},{5,4},{6,7},{7,6},{8,9},{9,8},{10,11... | collective-permute-start | bytes 884744 | tf_op jit(solution)/shard_map/ppermute | solution.py:587
  6.0 1.0 %copy-start.3 = (bf16[3,3,64,192]{3,2,1,0:T(8,128)(2,1)S(1)}, bf16[3,3,64,192]{3,2,1,0:T(8,128)(2,1)}, u32[]{:S(2)}) copy-start(bf16[3,3,64,192]{3,2,1,0:T(8,128)(2,1)} %param.18) | copy-start | bytes 663556
  6.9 1.0 %copy-start.4 = (bf16[3,3,64,192]{3,2,1,0:T(8,128)(2,1)S(1)}, bf16[3,3,64,192]{3,2,1,0:T(8,128)(2,1)}, u32[]{:S(2)}) copy-start(bf16[3,3,64,192]{3,2,1,0:T(8,128)(2,1)} %param.19) | copy-start | bytes 663556
  7.9 1.0 %copy-start.5 = (bf16[3,3,64,192]{3,2,1,0:T(8,128)(2,1)S(1)}, bf16[3,3,64,192]{3,2,1,0:T(8,128)(2,1)}, u32[]{:S(2)}) copy-start(bf16[3,3,64,192]{3,2,1,0:T(8,128)(2,1)} %param.20) | copy-start | bytes 663556
  8.8 0.7 copy-start.9
  9.5 25.1 %copy-start = (bf16[3,3,192,576]{3,2,1,0:T(8,128)(2,1)S(1)}, bf16[3,3,192,576]{3,2,1,0:T(8,128)(2,1)}, u32[]{:S(2)}) copy-start(bf16[3,3,192,576]{3,2,1,0:T(8,128)(2,1)} %param.22) | copy-start | bytes 5971972
  20.4 17.5 %copy-start.2 = (bf16[3,3,192,576]{3,2,1,0:T(8,128)(2,1)S(1)}, bf16[3,3,192,576]{3,2,1,0:T(8,128)(2,1)}, u32[]{:S(2)}) copy-start(bf16[3,3,192,576]{3,2,1,0:T(8,128)(2,1)} %param.21) | copy-start | bytes 5971972
  20.5 17.5 %collective-permute-start.2 = (bf16[72,16,128]{2,1,0:T(8,128)(2,1)S(1)}, bf16[72,16,128]{2,1,0:T(8,128)(2,1)S(1)}, u32[]{:S(2)}, u32[]{:S(2)}) collective-permute-start(bf16[72,16,128]{2,1,0:T(8,128)(2,1)S(1)} %get-tuple-element.33), channel_id=1, source_target_pairs={{1,2},{3,4},{5,6},{7,8},{9,10},{11,12},{13,14},{2,1},{4,3},{6,5},{... | collective-permute-start | bytes 884744 | tf_op jit(solution)/shard_map/ppermute | solution.py:584
  24.2 13.7 %collective-permute-start.3 = (bf16[72,16,128]{2,1,0:T(8,128)(2,1)S(1)}, bf16[72,16,128]{2,1,0:T(8,128)(2,1)S(1)}, u32[]{:S(2)}, u32[]{:S(2)}) collective-permute-start(bf16[72,16,128]{2,1,0:T(8,128)(2,1)S(1)} %get-tuple-element.34), channel_id=1, source_target_pairs={{0,1},{1,0},{2,3},{3,2},{4,5},{5,4},{6,7},{7,6},{8,9},{9,8},{10,11... | collective-permute-start | bytes 884744 | tf_op jit(solution)/shard_map/ppermute | solution.py:587
  24.4 10.3 %collective-permute-start.4 = (bf16[2,16,3072]{2,1,0:T(8,128)(2,1)S(1)}, bf16[2,16,3072]{2,1,0:T(8,128)(2,1)S(1)}, u32[]{:S(2)}, u32[]{:S(2)}) collective-permute-start(bf16[2,16,3072]{2,1,0:T(8,128)(2,1)S(1)} %bitcast.38), channel_id=1, source_target_pairs={{1,2},{3,4},{5,6},{7,8},{9,10},{11,12},{13,14},{2,1},{4,3},{6,5},{... | collective-permute-start | bytes 589832 | tf_op jit(solution)/shard_map/ppermute | solution.py:584
  26.5 8.2 %collective-permute-start.5 = (bf16[2,16,3072]{2,1,0:T(8,128)(2,1)S(1)}, bf16[2,16,3072]{2,1,0:T(8,128)(2,1)S(1)}, u32[]{:S(2)}, u32[]{:S(2)}) collective-permute-start(bf16[2,16,3072]{2,1,0:T(8,128)(2,1)S(1)} %bitcast.39), channel_id=1, source_target_pairs={{0,1},{1,0},{2,3},{3,2},{4,5},{5,4},{6,7},{7,6},{8,9},{9,8},{10,11... | collective-permute-start | bytes 589832 | tf_op jit(solution)/shard_map/ppermute | solution.py:587
  42.9 1.8 %collective-permute-start.6 = (bf16[24,16,128]{2,1,0:T(8,128)(2,1)S(1)}, bf16[24,16,128]{2,1,0:T(8,128)(2,1)S(1)}, u32[]{:S(2)}, u32[]{:S(2)}) collective-permute-start(bf16[24,16,128]{2,1,0:T(8,128)(2,1)S(1)} %get-tuple-element.39.near), channel_id=1, source_target_pairs={{0,1},{1,0},{2,3},{3,2},{4,5},{5,4},{6,7},{7,6},{8,9},{9,8},{10,11... | collective-permute-start | bytes 294920 | tf_op jit(solution)/shard_map/ppermute | solution.py:587
  43.0 14.6 %copy-start.6 = (bf16[3,3,192,64]{2,3,1,0:T(8,128)(2,1)S(1)}, bf16[3,3,192,64]{2,3,1,0:T(8,128)(2,1)}, u32[]{:S(2)}) copy-start(bf16[3,3,192,64]{2,3,1,0:T(8,128)(2,1)} %param.24) | copy-start | bytes 663556
  43.0 14.6 %copy-start.7 = (bf16[3,3,64,192]{3,2,1,0:T(8,128)(2,1)S(1)}, bf16[3,3,64,192]{3,2,1,0:T(8,128)(2,1)}, u32[]{:S(2)}) copy-start(bf16[3,3,64,192]{3,2,1,0:T(8,128)(2,1)} %param.25) | copy-start | bytes 663556
  43.0 14.6 %copy-start.8 = (bf16[3,3,64,192]{3,2,1,0:T(8,128)(2,1)S(1)}, bf16[3,3,64,192]{3,2,1,0:T(8,128)(2,1)}, u32[]{:S(2)}) copy-start(bf16[3,3,64,192]{3,2,1,0:T(8,128)(2,1)} %param.26) | copy-start | bytes 663556
  43.0 14.6 %copy-start.10 = (bf16[64,16]{0,1:T(8,128)(2,1)S(1)}, bf16[64,16]{0,1:T(8,128)(2,1)}, u32[]{:S(2)}) copy-start(bf16[64,16]{0,1:T(8,128)(2,1)} %param.27) | copy-start | bytes 6148
  43.0 15.6 %copy-start.1 = (bf16[3,3,192,576]{3,2,1,0:T(8,128)(2,1)S(1)}, bf16[3,3,192,576]{3,2,1,0:T(8,128)(2,1)}, u32[]{:S(2)}) copy-start(bf16[3,3,192,576]{3,2,1,0:T(8,128)(2,1)} %param.23) | copy-start | bytes 5971972
  44.8 12.7 %collective-permute-start.7 = (bf16[72,16,128]{2,1,0:T(8,128)(2,1)S(1)}, bf16[72,16,128]{2,1,0:T(8,128)(2,1)S(1)}, u32[]{:S(2)}, u32[]{:S(2)}) collective-permute-start(bf16[72,16,128]{2,1,0:T(8,128)(2,1)S(1)} %pad_maximum_fusion), channel_id=1, source_target_pairs={{1,2},{3,4},{5,6},{7,8},{9,10},{11,12},{13,14},{2,1},{4,3},{6,5},{... | collective-permute-start | bytes 884744 | tf_op jit(solution)/shard_map/ppermute | solution.py:584
  48.5 14.6 %collective-permute-start.10 = (bf16[2,16,16,128]{3,2,1,0:T(8,128)(2,1)S(1)}, bf16[2,16,16,128]{3,2,1,0:T(8,128)(2,1)S(1)}, u32[]{:S(2)}, u32[]{:S(2)}) collective-permute-start(bf16[2,16,16,128]{3,2,1,0:T(8,128)(2,1)S(1)} %get-tuple-element.41), channel_id=1, source_target_pairs={{1,2},{3,4},{5,6},{7,8},{9,10},{11,12},{13,14},{2,1},{4,3},{6,5},{... | collective-permute-start | bytes 393224 | tf_op jit(solution)/shard_map/ppermute | solution.py:584
  50.5 12.7 %collective-permute-start.11 = (bf16[2,16,16,128]{3,2,1,0:T(8,128)(2,1)S(1)}, bf16[2,16,16,128]{3,2,1,0:T(8,128)(2,1)S(1)}, u32[]{:S(2)}, u32[]{:S(2)}) collective-permute-start(bf16[2,16,16,128]{3,2,1,0:T(8,128)(2,1)S(1)} %get-tuple-element.42), channel_id=1, source_target_pairs={{0,1},{1,0},{2,3},{3,2},{4,5},{5,4},{6,7},{7,6},{8,9},{9,8},{10,11... | collective-permute-start | bytes 393224 | tf_op jit(solution)/shard_map/ppermute | solution.py:587
  51.8 6.8 %collective-permute-start.8 = (bf16[24,16,128]{2,1,0:T(8,128)(2,1)S(1)}, bf16[24,16,128]{2,1,0:T(8,128)(2,1)S(1)}, u32[]{:S(2)}, u32[]{:S(2)}) collective-permute-start(bf16[24,16,128]{2,1,0:T(8,128)(2,1)S(1)} %shard_map.141.far), channel_id=1, source_target_pairs={{0,1},{1,0},{2,3},{3,2},{4,5},{5,4},{6,7},{7,6},{8,9},{9,8},{10,11... | collective-permute-start | bytes 294920 | tf_op jit(solution)/shard_map/ppermute | solution.py:587
  57.5 5.7 %collective-permute-start.9 = (bf16[24,16,128]{2,1,0:T(8,128)(2,1)S(1)}, bf16[24,16,128]{2,1,0:T(8,128)(2,1)S(1)}, u32[]{:S(2)}, u32[]{:S(2)}) collective-permute-start(bf16[24,16,128]{2,1,0:T(8,128)(2,1)S(1)} %slice.14), channel_id=1, source_target_pairs={{0,1},{1,0},{2,3},{3,2},{4,5},{5,4},{6,7},{7,6},{8,9},{9,8},{10,11... | collective-permute-start | bytes 294920 | tf_op jit(solution)/shard_map/ppermute | solution.py:587

commit v5 on v4

--- a/solution.py
+++ b/solution.py
@@ -59,9 +59,16 @@
     ref[idx, blocks + 1] = shift_sub(ref[idx, 1], -1)
 
 
-def fine_patches(ref, idx, lo, count):
+def row_of(src, idx):
+    if isinstance(src, list):
+        ref, at = src[idx]
+        return ref.at[at]
+    return src.at[idx]
+
+
+def fine_patches(src, idx, lo, count):
     parts = [
-        ref[idx + dr, pl.ds(lo + dj, count)].reshape(count * SUB, LANES)
+        row_of(src, idx + dr)[pl.ds(lo + dj, count)].reshape(count * SUB, LANES)
         for dr in (-1, 0, 1)
         for dj in (0, 1, 2)
     ]
@@ -75,7 +82,7 @@
         gates = sigmoid(acc[:, :LANES])
         cand = acc[:, LANES:]
         cand = jnp.tanh(cand + swap_halves(gates * cand))
-        old = src[idx, pl.ds(1 + lo, count)].reshape(count * SUB, LANES).astype(F32)
+        old = row_of(src, idx)[pl.ds(1 + lo, count)].reshape(count * SUB, LANES).astype(F32)
         new = (1.0 - gates) * cand + gates * old
         new = jnp.where(valid, new, 0.0).astype(BF)
         emit(lo, count, new.reshape(count, SUB, LANES))
@@ -84,7 +91,7 @@
 def down_row(src, idx, weight):
     parts = []
     for dr in (-1, 0, 1):
-        row = src[idx + dr].reshape(FB // 2 + 1, 2, SUB, LANES)
+        row = row_of(src, idx + dr)[...].reshape(FB // 2 + 1, 2, SUB, LANES)
         for tap in (row[:CB, 0], row[:CB, 1], row[1:, 0]):
             parts.append(tap.reshape(CB * SUB, LANES))
     lhs = jnp.concatenate(parts, axis=-1)
@@ -205,48 +212,66 @@
         to_inner[r] = jnp.where(upper, own[r + 1], own[r])
 
 
-def fine_encoder_body(
-    own, outer, inner, w_stem, w_gru, w_down,
-    state_out, low_own, to_outer, to_inner, state_outer, state_inner, p1, p2, p3, stem2,
-):
-    upper, first, rows = place(4)
-    lo = low_half((1, SUB, LANES))
-
-    def pick(idx, lanes):
-        if 3 <= idx < 7:
-            return own[idx - 3, :, lanes]
-        r = idx if idx < 3 else idx - 7
-        a, b = outer[r, :, lanes], inner[r, :, lanes]
-        return jnp.where(upper, a, b) if idx < 3 else jnp.where(upper, b, a)
-
+def fill_fine(get, count, w_stem, p1, stem2):
+    lo = low_half((SUB, LANES))
     for frame in range(FRAMES):
         for t in range(4):
             at = FB * C1 + frame * FB * PATCH + t * LANES
-            patches = jnp.concatenate([pick(idx, slice(at, at + LANES)) for idx in range(9)], axis=0)
+            patches = jnp.concatenate([get(r, slice(at, at + LANES)) for r in range(count)], axis=0)
             for half in range(2):
                 acc = jnp.dot(patches, w_stem[:, half * 512 : half * 512 + 512], preferred_element_type=F32)
                 acc = leaky(acc).astype(BF)
                 for k in range(4):
-                    block = acc[:, k * LANES : (k + 1) * LANES].reshape(9, SUB, LANES)
-                    at = 8 * t + 4 * half + k
+                    block = acc[:, k * LANES : (k + 1) * LANES].reshape(count, SUB, LANES)
+                    at_block = 8 * t + 4 * half + k
                     if frame == 0:
-                        p1[:, 1 + at] = block
+                        p1[:, 1 + at_block] = block
                     else:
-                        stem2[:, at] = block
-    for idx in range(9):
+                        stem2[:, at_block] = block
+    for r in range(count):
         for k in range(FB // 2):
-            pair = pick(idx, slice(k * LANES, (k + 1) * LANES))
-            p1[idx, 1 + 2 * k] = jnp.where(lo[0], p1[idx, 1 + 2 * k], swap_bf(pair))
-            p1[idx, 2 + 2 * k] = jnp.where(lo[0], p1[idx, 2 + 2 * k], pair)
-        seal(p1, idx, FB)
-
-    for idx in range(1, 8):
-        def emit(lo_block, count, new):
-            stems = stem2[idx, pl.ds(lo_block, count)]
-            p2[idx, pl.ds(1 + lo_block, count)] = jnp.where(lo, stems, new)
-
-        fine_gru(p1, idx, w_gru, in_grid(first + idx - 3, rows), emit)
-        seal(p2, idx, FB)
+            pair = get(r, slice(k * LANES, (k + 1) * LANES))
+            p1[r, 1 + 2 * k] = jnp.where(lo, p1[r, 1 + 2 * k], swap_bf(pair))
+            p1[r, 2 + 2 * k] = jnp.where(lo, p1[r, 2 + 2 * k], pair)
+        seal(p1, r, FB)
+
+
+def first_fine(src, idx, w_gru, valid, stems, dst, at):
+    lo = low_half((1, SUB, LANES))
+
+    def emit(lo_block, count, new):
+        dst[at, pl.ds(1 + lo_block, count)] = jnp.where(lo, stems[pl.ds(lo_block, count)], new)
+
+    fine_gru(src, idx, w_gru, valid, emit)
+    seal(dst, at, FB)
+
+
+def fine_own_body(own, w_stem, w_gru, p1, stem2, inside):
+    fill_fine(lambda r, lanes: own[r, :, lanes], 4, w_stem, p1, stem2)
+    for r in range(2):
+        first_fine(p1, 1 + r, w_gru, True, stem2.at[1 + r], inside, r)
+
+
+def fine_encoder_body(
+    p1_own, stem2_own, inside, outer, inner, w_stem, w_gru, w_down,
+    state_out, low_own, to_outer, to_inner, state_outer, state_inner, p1_halo, stem2_halo, p2_rest, p3,
+):
+    upper, first, rows = place(4)
+    lo = low_half((1, SUB, LANES))
+
+    def get(r, lanes):
+        above = r < 3
+        at = r if above else r - 3
+        a, b = outer[at, :, lanes], inner[at, :, lanes]
+        return jnp.where(upper, a, b) if above else jnp.where(upper, b, a)
+
+    fill_fine(get, 5, w_stem, p1_halo, stem2_halo)
+    p1 = [(p1_halo, r) for r in range(3)] + [(p1_own, r) for r in range(4)] + [(p1_halo, r) for r in (3, 4)]
+    stem2 = [(stem2_halo, r) for r in range(3)] + [(stem2_own, r) for r in range(4)] + [(stem2_halo, 3)]
+    p2 = [None] + [(p2_rest, r) for r in range(3)] + [(inside, 0), (inside, 1), (p2_rest, 3), (p2_rest, 4)]
+    for idx in (1, 2, 3, 6, 7):
+        dst, at = p2[idx]
+        first_fine(p1, idx, w_gru, in_grid(first + idx - 3, rows), row_of(stem2, idx), dst, at)
 
     for idx in range(2, 7):
         def emit(lo_block, count, new):
@@ -379,23 +404,31 @@
     return lambda t: jnp.where(upper, packed_tiles(a, i)(t), packed_tiles(b, j)(t))
 
 
-def forecast_start_body(far, near, outer, in_far, in_near, w_h, s1, h2, acc_h):
+def forecast_inner_body(far, near, in_far, in_near, w_h, s1, h2, acc_h):
     upper, first, rows = place(2)
     zero_tail(acc_h)
-    put_packed(h2, 0, packed_tiles(outer, 2))
-    put_packed(h2, 1, either(upper, outer, 1, in_far, 0))
-    put_packed(h2, 2, either(upper, outer, 0, in_near, 0))
-    put_packed(h2, 3, either(upper, far, 0, near, 0))
-    put_packed(h2, 4, either(upper, near, 0, far, 0))
-    put_packed(h2, 5, either(upper, in_near, 0, outer, 0))
-    put_packed(h2, 6, either(upper, in_far, 0, outer, 1))
-    put_packed(h2, 7, packed_tiles(outer, 2))
-
-    shift = jnp.where(upper, 0, 1)
-    for k in range(5):
-        idx = k + shift
-        forms = coarse_gru(None, 0, h2, idx + 1, None, w_h, None, acc_h, in_grid(first + idx - 2, rows))
-        put_forms(s1, idx, forms)
+    put_packed(h2, 0, either(upper, far, 0, in_far, 0))
+    put_packed(h2, 1, either(upper, near, 0, in_near, 0))
+    put_packed(h2, 2, either(upper, in_near, 0, near, 0))
+    put_packed(h2, 3, either(upper, in_far, 0, far, 0))
+    at = jnp.where(upper, 3, 1)
+    for k in range(2):
+        forms = coarse_gru(None, 0, h2, k + 1, None, w_h, None, acc_h, in_grid(first + at + k - 2, rows))
+        put_forms(s1, at + k, forms)
+
+
+def forecast_outer_body(s1_given, far, near, outer, w_h, s1, h2, acc_h):
+    upper, first, rows = place(2)
+    zero_tail(acc_h)
+    put_packed(h2, 0, either(upper, outer, 2, near, 0))
+    put_packed(h2, 1, either(upper, outer, 1, far, 0))
+    put_packed(h2, 2, packed_tiles(outer, 0))
+    put_packed(h2, 3, either(upper, far, 0, outer, 1))
+    put_packed(h2, 4, either(upper, near, 0, outer, 2))
+    at = jnp.where(upper, 0, 3)
+    for k in range(3):
+        forms = coarse_gru(None, 0, h2, k + 1, None, w_h, None, acc_h, in_grid(first + at + k - 2, rows))
+        put_forms(s1, at + k, forms)
 
 
 def forecaster_body(
@@ -628,11 +661,18 @@
 
     halo = (3 * ROW_TILES, SUB, LANES)
     edge = (2, FB // 2, SUB, LANES)
+
+    def fine_shape(count, blocks=FB + 2):
+        return (count, blocks, SUB, LANES)
+
+    p1_own, stem2_own, inside = call(
+        fine_own_body, on_chip(own, w_stem, w_enc), [fine_shape(4), fine_shape(4, FB), fine_shape(2)], []
+    )
     state_f, low_own, to_outer, to_inner, state_fo, state_fi = call(
         fine_encoder_body,
-        on_chip(own, outer, inner, w_stem, w_enc, w_down),
+        on_chip(p1_own, stem2_own, inside, outer, inner, w_stem, w_enc, w_down),
         [(4, FB // 2, SUB, LANES), (4 * ROW_TILES, SUB, LANES), halo, halo, edge, edge],
-        [fine_buf(9), fine_buf(9), fine_buf(9), pltpu.VMEM((9, FB, SUB, LANES), BF)],
+        [fine_buf(5), pltpu.VMEM(fine_shape(5, FB), BF), fine_buf(5), fine_buf(9)],
     )
     got_o, got_i = outer_swap(to_outer), inner_swap(to_inner)
 
@@ -660,10 +700,17 @@
 
     w_f = fc_coarse_h.reshape(flat)
     (s1,) = call(
-        forecast_start_body,
-        on_chip(far, near, state_co, in_far, in_near, w_f),
+        forecast_inner_body,
+        on_chip(far, near, in_far, in_near, w_f),
         [(6, CB + 2, SUB, 4 * LANES)],
-        [coarse_buf(8), acc_buf],
+        [coarse_buf(4), acc_buf],
+    )
+    (s1,) = call(
+        forecast_outer_body,
+        on_chip(s1, far, near, state_co, w_f),
+        [(6, CB + 2, SUB, 4 * LANES)],
+        [coarse_buf(5), acc_buf],
+        {0: 0},
     )
     out, _ = call(
         forecaster_body,

time: 74.2 us -> 73.3 us (0.988)
  waiting for transfers between devices: 16.7 us -> 15.5 us
    ppermute x5, waiting for transfers between devices: 16.7 us -> 15.5 us  [outer_swap(): return lax.ppermute(x, LINE, across)]
    pallas_call x9 -> x11, Pallas kernels: 32.3 us -> 32.5 us  [call(): pl.pallas_call(body, out_shape=[s if isinstance(s, jax.ShapeDtypeStruct)...]
  transfers between devices with their start and end apart: 12 -> 12, of which waited for: 3 -> 3; matrix products, arithmetic and copies ran while one was open for 0% -> 0% of each run, Pallas kernels for 15% -> 17%
where the time goes in v5:
time: 73.3 us; the launch traced here: 72.3 us
  Pallas kernels  32.5 us (44%)
  starting transfers between devices  17.5 us (24%)
  waiting for transfers between devices  15.5 us (21%)
  local copies, waits for them, and re-layouts  6.44 us (9%)
    pallas_call x11, Pallas kernels, call(): pl.pallas_call(body, out_shape=[s if isinstance(s, jax.ShapeDtypeStruct)...  32.5 us
    ppermute x5, waiting for transfers between devices, outer_swap(): return lax.ppermute(x, LINE, across)  15.5 us
    ppermute x5, starting transfers between devices, outer_swap(): return lax.ppermute(x, LINE, across)  15.4 us
    unnamed x26, local copies, waits for them, and re-layouts  4.75 us
    ppermute x7, starting transfers between devices, inner_swap(): return lax.ppermute(x, 'section', [(0, 1), (1, 0)])  2.04 us
  transfers between devices with their start and end apart: 12, of which 3 were waited for; matrix products, arithmetic and copies ran while one was open for 0% of the time, Pallas kernels for 17%

profile of v5, /device:TPU:19, one launch (start us, length us, event | category | flops | bytes accessed | tf_op | source)
XLA Modules:
  0.0 72.3 jit_solution(5758736169303430547)
XLA Ops:
  0.0 0.9 %fusion = (bf16[1,4,8192]{2,1,0:T(4,128)(2,1)S(1)}, bf16[1,4,8192]{2,1,0:T(4,128)(2,1)S(1)}) fusion(bf16[2,4,8192]{2,1,0:T(4,128)(2,1)} %param.14), kind=kLoop, calls=%fused_computation.5 | loop fusion | bytes 262144 | tf_op jit(solution)/shard_map/slice | solution.py:636
  0.9 1.1 %copy.25 = bf16[1,4,16,2048]{3,2,1,0:T(8,128)(2,1)S(1)} copy(bf16[1,4,16,2048]{3,1,2,0:T(4,128)(2,1)} %bitcast.49) | data formatting | bytes 524288
  2.1 0.1 shard_map.136
  2.1 3.7 %collective-permute-start = (bf16[3,16,3072]{2,1,0:T(8,128)(2,1)S(1)}, bf16[3,16,3072]{2,1,0:T(8,128)(2,1)S(1)}, u32[]{:S(2)}, u32[]{:S(2)}) collective-permute-start(bf16[3,16,3072]{2,1,0:T(8,128)(2,1)S(1)} %get-tuple-element.35), channel_id=1, source_target_pairs={{1,2},{3,4},{5,6},{7,8},{9,10},{11,12},{13,14},{2,1},{4,3},{6,5},{... | collective-permute-start | bytes 884744 | tf_op jit(solution)/shard_map/ppermute | solution.py:617
  5.9 0.1 collective-permute-start.1
  6.0 1.0 %copy-done.3 = bf16[3,3,64,192]{3,2,1,0:T(8,128)(2,1)S(1)} copy-done((bf16[3,3,64,192]{3,2,1,0:T(8,128)(2,1)S(1)}, bf16[3,3,64,192]{3,2,1,0:T(8,128)(2,1)}, u32[]{:S(2)}) %copy-start.3) | copy-done | bytes 221208
  6.9 1.0 %copy-done.4 = bf16[3,3,64,192]{3,2,1,0:T(8,128)(2,1)S(1)} copy-done((bf16[3,3,64,192]{3,2,1,0:T(8,128)(2,1)S(1)}, bf16[3,3,64,192]{3,2,1,0:T(8,128)(2,1)}, u32[]{:S(2)}) %copy-start.4) | copy-done | bytes 221208
  7.9 1.0 %copy-done.5 = bf16[3,3,64,192]{3,2,1,0:T(8,128)(2,1)S(1)} copy-done((bf16[3,3,64,192]{3,2,1,0:T(8,128)(2,1)S(1)}, bf16[3,3,64,192]{3,2,1,0:T(8,128)(2,1)}, u32[]{:S(2)}) %copy-start.5) | copy-done | bytes 221208
  8.8 0.7 copy-done.9
  9.5 0.5 shard_map.137
  10.0 1.5 %shard_map.138 = (bf16[4,34,16,128]{3,2,1,0:T(8,128)(2,1)S(1)}, bf16[4,32,16,128]{3,2,1,0:T(8,128)(2,1)S(1)}, bf16[2,34,16,128]{3,2,1,0:T(8,128)(2,1)S(1)}) custom-call(bf16[4,16,3072]{2,1,0:T(8,128)(2,1)S(1)} %get-tuple-element.29.own, bf16[128,1024]{1,0:T(8,128)(2,1)S(1)} %get-tuple-element.30.w_stem, bf16[1152,256]{1,0:T(8,128)(2,1)S(1)} %get-tuple-element.31.w_gru), custom_call_target="tpu_custom_call" | custom-call | tf_op jit(solution)/shard_map/pallas_call | solution.py:585
  11.5 1.9 %collective-permute-done.outer = bf16[3,16,3072]{2,1,0:T(8,128)(2,1)S(1)} collective-permute-done((bf16[3,16,3072]{2,1,0:T(8,128)(2,1)S(1)}, bf16[3,16,3072]{2,1,0:T(8,128)(2,1)S(1)}, u32[]{:S(2)}, u32[]{:S(2)}) %collective-permute-start) | collective-permute-done | bytes 294944 | tf_op jit(solution)/shard_map/ppermute | solution.py:617
  13.4 5.8 %shard_map.139 = (bf16[4,16,16,128]{3,2,1,0:T(8,128)(2,1)S(1)}, bf16[96,16,128]{2,1,0:T(8,128)(2,1)S(1)}, bf16[72,16,128]{2,1,0:T(8,128)(2,1)S(1)}, bf16[72,16,1...) custom-call(bf16[4,34,16,128]{3,2,1,0:T(8,128)(2,1)S(1)} %get-tuple-element.32.p1_ow, ...), custom_call_target="tpu_custom_call" | custom-call | tf_op jit(solution)/shard_map/pallas_call | solution.py:585
  19.2 3.8 %collective-permute-start.2 = (bf16[72,16,128]{2,1,0:T(8,128)(2,1)S(1)}, bf16[72,16,128]{2,1,0:T(8,128)(2,1)S(1)}, u32[]{:S(2)}, u32[]{:S(2)}) collective-permute-start(bf16[72,16,128]{2,1,0:T(8,128)(2,1)S(1)} %get-tuple-element.39), channel_id=1, source_target_pairs={{1,2},{3,4},{5,6},{7,8},{9,10},{11,12},{13,14},{2,1},{4,3},{6,5},{... | collective-permute-start | bytes 884744 | tf_op jit(solution)/shard_map/ppermute | solution.py:617
  23.0 0.1 collective-permute-start.3
  23.1 2.1 %collective-permute-start.4 = (bf16[2,16,3072]{2,1,0:T(8,128)(2,1)S(1)}, bf16[2,16,3072]{2,1,0:T(8,128)(2,1)S(1)}, u32[]{:S(2)}, u32[]{:S(2)}) collective-permute-start(bf16[2,16,3072]{2,1,0:T(8,128)(2,1)S(1)} %bitcast.39), channel_id=1, source_target_pairs={{1,2},{3,4},{5,6},{7,8},{9,10},{11,12},{13,14},{2,1},{4,3},{6,5},{... | collective-permute-start | bytes 589832 | tf_op jit(solution)/shard_map/ppermute | solution.py:617
  25.3 0.5 collective-permute-start.5
  25.8 7.8 %collective-permute-done.4.outer = bf16[2,16,3072]{2,1,0:T(8,128)(2,1)S(1)} collective-permute-done((bf16[2,16,3072]{2,1,0:T(8,128)(2,1)S(1)}, bf16[2,16,3072]{2,1,0:T(8,128)(2,1)S(1)}, u32[]{:S(2)}, u32[]{:S(2)}) %collective-permute-start.4) | collective-permute-done | bytes 196640 | tf_op jit(solution)/shard_map/ppermute | solution.py:617
  33.6 3.2 %shard_map.140 = (f32[4,256,640]{2,1,0:T(8,128)S(1)}, bf16[4,18,16,512]{3,2,1,0:T(8,128)(2,1)S(1)}) custom-call(bf16[2,16,3072]{2,1,0:T(8,128)(2,1)S(1)} %bitcast.41, bf16[2,16,3072]{2,1,0:T(8,128)(2,1)S(1)} %collective-permute-done.4.outer, bf16[2,16,3072]{2,1,0:T(8,128)(2,1)S(1)} %collective-permute-done.5.inner, bf16[1728,576]{1,0:T(8,128)(2,1)S(1)} %bitcast.33), custom_call_target="tpu_custom_call" | custom-call | tf_op jit(solution)/shard_map/pallas_call | solution.py:585
  36.9 5.0 %shard_map.141 = (bf16[24,16,128]{2,1,0:T(8,128)(2,1)S(1)}, bf16[4,18,16,512]{3,2,1,0:T(8,128)(2,1)S(1)}, bf16[4,18,16,512]{3,2,1,0:T(8,128)(2,1)S(1)}) custom-call(bf16[96,16,128]{2,1,0:T(8,128)(2,1)S(1)} %get-tuple-element.38.low_own, bf16[72,16,128]{2,1,0:T(8,128)(2,1)S(1)} %collective-permute-done.2.low_outer, ...), custom_call_target="tpu_custom_call" | custom-call | tf_op jit(solution)/shard_map/pallas_call | solution.py:585
  42.0 1.7 %shard_map.142.far = bf16[24,16,128]{2,1,0:T(8,128)(2,1)S(1)} custom-call(bf16[4,18,16,512]{3,2,1,0:T(8,128)(2,1)S(1)} %get-tuple-element.43.h1, bf16[4,18,16,512]{3,2,1,0:T(8,128)(2,1)S(1)} %get-tuple-element.44.x2, bf16[1728,576]{1,0:T(8,128)(2,1)S(1)} %bitcast.37, bf16[1728,576]{1,0:T(8,128)(2,1)S(1)} %bitcast.35), custom_call_target="tpu_custom_call" | custom-call | tf_op jit(solution)/shard_map/pallas_call | solution.py:585
  43.7 3.9 %collective-permute-start.8 = (bf16[72,16,128]{2,1,0:T(8,128)(2,1)S(1)}, bf16[72,16,128]{2,1,0:T(8,128)(2,1)S(1)}, u32[]{:S(2)}, u32[]{:S(2)}) collective-permute-start(bf16[72,16,128]{2,1,0:T(8,128)(2,1)S(1)} %pad_maximum_fusion), channel_id=1, source_target_pairs={{1,2},{3,4},{5,6},{7,8},{9,10},{11,12},{13,14},{2,1},{4,3},{6,5},{... | collective-permute-start | bytes 884744 | tf_op jit(solution)/shard_map/ppermute | solution.py:617
  47.7 1.9 %collective-permute-start.10 = (bf16[2,16,16,128]{3,2,1,0:T(8,128)(2,1)S(1)}, bf16[2,16,16,128]{3,2,1,0:T(8,128)(2,1)S(1)}, u32[]{:S(2)}, u32[]{:S(2)}) collective-permute-start(bf16[2,16,16,128]{3,2,1,0:T(8,128)(2,1)S(1)} %get-tuple-element.47), channel_id=1, source_target_pairs={{1,2},{3,4},{5,6},{7,8},{9,10},{11,12},{13,14},{2,1},{4,3},{6,5},{... | collective-permute-start | bytes 393224 | tf_op jit(solution)/shard_map/ppermute | solution.py:617
  49.6 1.1 %collective-permute-start.11 = (bf16[2,16,16,128]{3,2,1,0:T(8,128)(2,1)S(1)}, bf16[2,16,16,128]{3,2,1,0:T(8,128)(2,1)S(1)}, u32[]{:S(2)}, u32[]{:S(2)}) collective-permute-start(bf16[2,16,16,128]{3,2,1,0:T(8,128)(2,1)S(1)} %get-tuple-element.48), channel_id=1, source_target_pairs={{0,1},{1,0},{2,3},{3,2},{4,5},{5,4},{6,7},{7,6},{8,9},{9,8},{10,11... | collective-permute-start | bytes 393224 | tf_op jit(solution)/shard_map/ppermute | solution.py:620
  50.7 0.1 collective-permute-start.6
  50.8 5.8 %collective-permute-done.8.outer = bf16[72,16,128]{2,1,0:T(8,128)(2,1)S(1)} collective-permute-done((bf16[72,16,128]{2,1,0:T(8,128)(2,1)S(1)}, bf16[72,16,128]{2,1,0:T(8,128)(2,1)S(1)}, u32[]{:S(2)}, u32[]{:S(2)}) %collective-permute-start.8) | collective-permute-done | bytes 294944 | tf_op jit(solution)/shard_map/ppermute | solution.py:617
  56.6 0.1 collective-permute-start.9
  56.7 1.0 %shard_map.145 = (bf16[768,256]{1,0:T(8,128)(2,1)S(1)}, bf16[1152,256]{1,0:T(8,128)(2,1)S(1)}, bf16[1024,128]{1,0:T(8,128)(2,1)S(1)}) custom-call(bf16[9,64,192]{2,1,0:T(8,128)(2,1)S(1)} %bitcast.45, bf16[9,64,192]{2,1,0:T(8,128)(2,1)S(1)} %bitcast.46, bf16[9,64,192]{2,1,0:T(8,128)(2,1)S(1)} %bitcast.47, bf16[16,64]{1,0:T(8,128)(2,1)S(1)} %bitcast.48), custom_call_target="tpu_custom_call" | custom-call | tf_op jit(solution)/shard_map/pallas_call | solution.py:585
  57.7 1.8 %shard_map.143.s1_given = bf16[6,18,16,512]{3,2,1,0:T(8,128)(2,1)S(1)} custom-call(bf16[24,16,128]{2,1,0:T(8,128)(2,1)S(1)} %shard_map.142.far, bf16[24,16,128]{2,1,0:T(8,128)(2,1)S(1)} %get-tuple-element.45.near, bf16[24,16,128]{2,1,0:T(8,128)(2,1)S(1)} %collective-permute-done.6.in_far, bf16[24,16,128]{2,1,0:T(8,128)(2,1)S(1)} %collective-permute-done.7.in_near, ...), custom_call_target="tpu_custom_call" | custom-call | tf_op jit(solution)/shard_map/pallas_call | solution.py:585
  59.6 2.6 %shard_map.144.s1_given = bf16[6,18,16,512]{3,2,1,0:T(8,128)(2,1)S(1)} custom-call(bf16[6,18,16,512]{3,2,1,0:T(8,128)(2,1)S(1)} %shard_map.143.s1_given, bf16[24,16,128]{2,1,0:T(8,128)(2,1)S(1)} %shard_map.142.far, bf16[24,16,128]{2,1,0:T(8,128)(2,1)S(1)} %get-tuple-element.45.near, ...), custom_call_target="tpu_custom_call", output_to_operand_aliasing={{}: (0, {})} | custom-call | tf_op jit(solution)/shard_map/pallas_call | solution.py:585
  62.2 9.3 %shard_map.146 = (bf16[2,4,16,512]{3,2,1,0:T(8,128)(2,1)S(1)}, bf16[6,18,16,512]{3,2,1,0:T(8,128)(2,1)S(1)}) custom-call(bf16[6,18,16,512]{3,2,1,0:T(8,128)(2,1)S(1)} %shard_map.144.s1_given, bf16[24,16,128]{2,1,0:T(8,128)(2,1)S(1)} %collective-permute-done.6.in_far, ...), custom_call_target="tpu_custom_call", output_to_operand_aliasing={{1}: (0, {})} | custom-call | tf_op jit(solution)/shard_map/pallas_call | solution.py:585
  71.6 0.7 %reshape.53 = bf16[2,4,8192]{2,1,0:T(4,128)(2,1)} reshape(bf16[2,4,16,512]{3,2,1,0:T(8,128)(2,1)S(1)} %get-tuple-element.52) | data formatting | bytes 262144 | tf_op jit(solution)/shard_map/reshape | solution.py:722
  (34 shorter events, 0.2 us)
Async XLA Ops:
  2.1 11.3 %collective-permute-start = (bf16[3,16,3072]{2,1,0:T(8,128)(2,1)S(1)}, bf16[3,16,3072]{2,1,0:T(8,128)(2,1)S(1)}, u32[]{:S(2)}, u32[]{:S(2)}) collective-permute-start(bf16[3,16,3072]{2,1,0:T(8,128)(2,1)S(1)} %get-tuple-element.35), channel_id=1, source_target_pairs={{1,2},{3,4},{5,6},{7,8},{9,10},{11,12},{13,14},{2,1},{4,3},{6,5},{... | collective-permute-start | bytes 884744 | tf_op jit(solution)/shard_map/ppermute | solution.py:617
  5.9 7.6 %collective-permute-start.1 = (bf16[3,16,3072]{2,1,0:T(8,128)(2,1)S(1)}, bf16[3,16,3072]{2,1,0:T(8,128)(2,1)S(1)}, u32[]{:S(2)}, u32[]{:S(2)}) collective-permute-start(bf16[3,16,3072]{2,1,0:T(8,128)(2,1)S(1)} %get-tuple-element.36), channel_id=1, source_target_pairs={{0,1},{1,0},{2,3},{3,2},{4,5},{5,4},{6,7},{7,6},{8,9},{9,8},{10,11... | collective-permute-start | bytes 884744 | tf_op jit(solution)/shard_map/ppermute | solution.py:620
  5.9 1.0 %copy-start.3 = (bf16[3,3,64,192]{3,2,1,0:T(8,128)(2,1)S(1)}, bf16[3,3,64,192]{3,2,1,0:T(8,128)(2,1)}, u32[]{:S(2)}) copy-start(bf16[3,3,64,192]{3,2,1,0:T(8,128)(2,1)} %param.18) | copy-start | bytes 663556
  6.9 1.0 %copy-start.4 = (bf16[3,3,64,192]{3,2,1,0:T(8,128)(2,1)S(1)}, bf16[3,3,64,192]{3,2,1,0:T(8,128)(2,1)}, u32[]{:S(2)}) copy-start(bf16[3,3,64,192]{3,2,1,0:T(8,128)(2,1)} %param.19) | copy-start | bytes 663556
  7.9 1.0 %copy-start.5 = (bf16[3,3,64,192]{3,2,1,0:T(8,128)(2,1)S(1)}, bf16[3,3,64,192]{3,2,1,0:T(8,128)(2,1)}, u32[]{:S(2)}) copy-start(bf16[3,3,64,192]{3,2,1,0:T(8,128)(2,1)} %param.20) | copy-start | bytes 663556
  8.8 0.7 copy-start.9
  11.5 11.6 %copy-start.11 = (bf16[2,49152]{1,0:T(2,128)(2,1)S(1)}, bf16[2,49152]{1,0:T(2,128)(2,1)}, u32[]{:S(2)}) copy-start(bf16[2,49152]{1,0:T(2,128)(2,1)} %param.16) | copy-start | bytes 589828
  13.4 20.2 %copy-start.1 = (bf16[3,3,192,576]{3,2,1,0:T(8,128)(2,1)S(1)}, bf16[3,3,192,576]{3,2,1,0:T(8,128)(2,1)}, u32[]{:S(2)}) copy-start(bf16[3,3,192,576]{3,2,1,0:T(8,128)(2,1)} %param.22) | copy-start | bytes 5971972
  19.2 17.6 %copy-start.2 = (bf16[3,3,192,576]{3,2,1,0:T(8,128)(2,1)S(1)}, bf16[3,3,192,576]{3,2,1,0:T(8,128)(2,1)}, u32[]{:S(2)}) copy-start(bf16[3,3,192,576]{3,2,1,0:T(8,128)(2,1)} %param.21) | copy-start | bytes 5971972
  19.2 17.6 %collective-permute-start.2 = (bf16[72,16,128]{2,1,0:T(8,128)(2,1)S(1)}, bf16[72,16,128]{2,1,0:T(8,128)(2,1)S(1)}, u32[]{:S(2)}, u32[]{:S(2)}) collective-permute-start(bf16[72,16,128]{2,1,0:T(8,128)(2,1)S(1)} %get-tuple-element.39), channel_id=1, source_target_pairs={{1,2},{3,4},{5,6},{7,8},{9,10},{11,12},{13,14},{2,1},{4,3},{6,5},{... | collective-permute-start | bytes 884744 | tf_op jit(solution)/shard_map/ppermute | solution.py:617
  23.0 13.8 %collective-permute-start.3 = (bf16[72,16,128]{2,1,0:T(8,128)(2,1)S(1)}, bf16[72,16,128]{2,1,0:T(8,128)(2,1)S(1)}, u32[]{:S(2)}, u32[]{:S(2)}) collective-permute-start(bf16[72,16,128]{2,1,0:T(8,128)(2,1)S(1)} %get-tuple-element.40), channel_id=1, source_target_pairs={{0,1},{1,0},{2,3},{3,2},{4,5},{5,4},{6,7},{7,6},{8,9},{9,8},{10,11... | collective-permute-start | bytes 884744 | tf_op jit(solution)/shard_map/ppermute | solution.py:620
  23.1 10.4 %collective-permute-start.4 = (bf16[2,16,3072]{2,1,0:T(8,128)(2,1)S(1)}, bf16[2,16,3072]{2,1,0:T(8,128)(2,1)S(1)}, u32[]{:S(2)}, u32[]{:S(2)}) collective-permute-start(bf16[2,16,3072]{2,1,0:T(8,128)(2,1)S(1)} %bitcast.39), channel_id=1, source_target_pairs={{1,2},{3,4},{5,6},{7,8},{9,10},{11,12},{13,14},{2,1},{4,3},{6,5},{... | collective-permute-start | bytes 589832 | tf_op jit(solution)/shard_map/ppermute | solution.py:617
  25.3 8.3 %collective-permute-start.5 = (bf16[2,16,3072]{2,1,0:T(8,128)(2,1)S(1)}, bf16[2,16,3072]{2,1,0:T(8,128)(2,1)S(1)}, u32[]{:S(2)}, u32[]{:S(2)}) collective-permute-start(bf16[2,16,3072]{2,1,0:T(8,128)(2,1)S(1)} %bitcast.40), channel_id=1, source_target_pairs={{0,1},{1,0},{2,3},{3,2},{4,5},{5,4},{6,7},{7,6},{8,9},{9,8},{10,11... | collective-permute-start | bytes 589832 | tf_op jit(solution)/shard_map/ppermute | solution.py:620
  41.8 1.8 %collective-permute-start.7 = (bf16[24,16,128]{2,1,0:T(8,128)(2,1)S(1)}, bf16[24,16,128]{2,1,0:T(8,128)(2,1)S(1)}, u32[]{:S(2)}, u32[]{:S(2)}) collective-permute-start(bf16[24,16,128]{2,1,0:T(8,128)(2,1)S(1)} %get-tuple-element.45.near), channel_id=1, source_target_pairs={{0,1},{1,0},{2,3},{3,2},{4,5},{5,4},{6,7},{7,6},{8,9},{9,8},{10,11... | collective-permute-start | bytes 294920 | tf_op jit(solution)/shard_map/ppermute | solution.py:620
  41.9 14.8 %copy-start.6 = (bf16[3,3,192,64]{2,3,1,0:T(8,128)(2,1)S(1)}, bf16[3,3,192,64]{2,3,1,0:T(8,128)(2,1)}, u32[]{:S(2)}) copy-start(bf16[3,3,192,64]{2,3,1,0:T(8,128)(2,1)} %param.24) | copy-start | bytes 663556
  41.9 14.8 %copy-start.7 = (bf16[3,3,64,192]{3,2,1,0:T(8,128)(2,1)S(1)}, bf16[3,3,64,192]{3,2,1,0:T(8,128)(2,1)}, u32[]{:S(2)}) copy-start(bf16[3,3,64,192]{3,2,1,0:T(8,128)(2,1)} %param.25) | copy-start | bytes 663556
  41.9 14.8 %copy-start.8 = (bf16[3,3,64,192]{3,2,1,0:T(8,128)(2,1)S(1)}, bf16[3,3,64,192]{3,2,1,0:T(8,128)(2,1)}, u32[]{:S(2)}) copy-start(bf16[3,3,64,192]{3,2,1,0:T(8,128)(2,1)} %param.26) | copy-start | bytes 663556
  41.9 14.8 %copy-start.10 = (bf16[64,16]{0,1:T(8,128)(2,1)S(1)}, bf16[64,16]{0,1:T(8,128)(2,1)}, u32[]{:S(2)}) copy-start(bf16[64,16]{0,1:T(8,128)(2,1)} %param.27) | copy-start | bytes 6148
  42.0 15.8 %copy-start = (bf16[3,3,192,576]{3,2,1,0:T(8,128)(2,1)S(1)}, bf16[3,3,192,576]{3,2,1,0:T(8,128)(2,1)}, u32[]{:S(2)}) copy-start(bf16[3,3,192,576]{3,2,1,0:T(8,128)(2,1)} %param.23) | copy-start | bytes 5971972
  43.7 12.9 %collective-permute-start.8 = (bf16[72,16,128]{2,1,0:T(8,128)(2,1)S(1)}, bf16[72,16,128]{2,1,0:T(8,128)(2,1)S(1)}, u32[]{:S(2)}, u32[]{:S(2)}) collective-permute-start(bf16[72,16,128]{2,1,0:T(8,128)(2,1)S(1)} %pad_maximum_fusion), channel_id=1, source_target_pairs={{1,2},{3,4},{5,6},{7,8},{9,10},{11,12},{13,14},{2,1},{4,3},{6,5},{... | collective-permute-start | bytes 884744 | tf_op jit(solution)/shard_map/ppermute | solution.py:617
  47.7 14.5 %collective-permute-start.10 = (bf16[2,16,16,128]{3,2,1,0:T(8,128)(2,1)S(1)}, bf16[2,16,16,128]{3,2,1,0:T(8,128)(2,1)S(1)}, u32[]{:S(2)}, u32[]{:S(2)}) collective-permute-start(bf16[2,16,16,128]{3,2,1,0:T(8,128)(2,1)S(1)} %get-tuple-element.47), channel_id=1, source_target_pairs={{1,2},{3,4},{5,6},{7,8},{9,10},{11,12},{13,14},{2,1},{4,3},{6,5},{... | collective-permute-start | bytes 393224 | tf_op jit(solution)/shard_map/ppermute | solution.py:617
  49.6 12.6 %collective-permute-start.11 = (bf16[2,16,16,128]{3,2,1,0:T(8,128)(2,1)S(1)}, bf16[2,16,16,128]{3,2,1,0:T(8,128)(2,1)S(1)}, u32[]{:S(2)}, u32[]{:S(2)}) collective-permute-start(bf16[2,16,16,128]{3,2,1,0:T(8,128)(2,1)S(1)} %get-tuple-element.48), channel_id=1, source_target_pairs={{0,1},{1,0},{2,3},{3,2},{4,5},{5,4},{6,7},{7,6},{8,9},{9,8},{10,11... | collective-permute-start | bytes 393224 | tf_op jit(solution)/shard_map/ppermute | solution.py:620
  50.7 7.0 %collective-permute-start.6 = (bf16[24,16,128]{2,1,0:T(8,128)(2,1)S(1)}, bf16[24,16,128]{2,1,0:T(8,128)(2,1)S(1)}, u32[]{:S(2)}, u32[]{:S(2)}) collective-permute-start(bf16[24,16,128]{2,1,0:T(8,128)(2,1)S(1)} %shard_map.142.far), channel_id=1, source_target_pairs={{0,1},{1,0},{2,3},{3,2},{4,5},{5,4},{6,7},{7,6},{8,9},{9,8},{10,11... | collective-permute-start | bytes 294920 | tf_op jit(solution)/shard_map/ppermute | solution.py:620
  56.6 5.6 %collective-permute-start.9 = (bf16[24,16,128]{2,1,0:T(8,128)(2,1)S(1)}, bf16[24,16,128]{2,1,0:T(8,128)(2,1)S(1)}, u32[]{:S(2)}, u32[]{:S(2)}) collective-permute-start(bf16[24,16,128]{2,1,0:T(8,128)(2,1)S(1)} %slice.14), channel_id=1, source_target_pairs={{0,1},{1,0},{2,3},{3,2},{4,5},{5,4},{6,7},{7,6},{8,9},{9,8},{10,11... | collective-permute-start | bytes 294920 | tf_op jit(solution)/shard_map/ppermute | solution.py:620

commit v6 on v5

--- a/solution.py
+++ b/solution.py
@@ -254,7 +254,8 @@
 
 def fine_encoder_body(
     p1_own, stem2_own, inside, outer, inner, w_stem, w_gru, w_down,
-    state_out, low_own, to_outer, to_inner, state_outer, state_inner, p1_halo, stem2_halo, p2_rest, p3,
+    state_out, low_own, to_outer, to_inner, second_outer, second_inner, state_outer, state_inner,
+    p1_halo, stem2_halo, p2_rest, p3,
 ):
     upper, first, rows = place(4)
     lo = low_half((1, SUB, LANES))
@@ -301,11 +302,11 @@
 
         @pl.when(outward)
         def _():
-            put(to_outer, 2, tiles)
+            put(second_outer, 0, tiles)
 
         @pl.when(jnp.logical_not(outward))
         def _():
-            put(to_inner, 2, tiles)
+            put(second_inner, 0, tiles)
 
     for r in range(4):
         for k in range(FB // 2):
@@ -352,31 +353,31 @@
         ref[k * PAIRS : (k + 1) * PAIRS] = tile
 
 
-def coarse_encoder_body(
-    low_own, low_outer, low_inner, acc_first, h_first, w_x, w_h, near, h1, x2, x1, acc_x, acc_h,
-):
+def coarse_encoder_body(low_own, low_outer, low_inner, acc_first, h_first, w_x, h1, x1, acc_x):
     upper, first, rows = place(2)
     zero_tail(acc_x)
-    zero_tail(acc_h)
-
     for idx in range(6):
         if 2 <= idx < 4:
             put_packed(x1, idx, packed_tiles(low_own, idx - 2))
             continue
         r = idx if idx < 2 else idx - 4
         a, b = (low_outer, low_inner) if idx < 2 else (low_inner, low_outer)
-        put_packed(x1, idx, lambda i: jnp.where(upper, packed_tiles(a, r)(i), packed_tiles(b, r)(i)))
-    put_packed(x2, 1, packed_tiles(low_own, 2))
-    put_packed(x2, 2, packed_tiles(low_own, 3))
-    put_packed(x2, 0, lambda i: jnp.where(upper, packed_tiles(low_outer, 2)(i), packed_tiles(low_inner, 2)(i)))
-    put_packed(x2, 3, lambda i: jnp.where(upper, packed_tiles(low_inner, 2)(i), packed_tiles(low_outer, 2)(i)))
-
+        put_packed(x1, idx, either(upper, a, r, b, r))
     for idx in range(4):
         forms = coarse_gru(
             x1, idx + 1, h_first, idx, w_x, None, acc_x, acc_first.at[idx], in_grid(first + idx - 1, rows)
         )
         put_forms(h1, idx, forms)
 
+
+def coarse_near_body(low_own, second_outer, second_inner, h1, w_x, w_h, near, x2, acc_x, acc_h):
+    upper, _, _ = place(2)
+    zero_tail(acc_x)
+    zero_tail(acc_h)
+    put_packed(x2, 0, either(upper, second_outer, 0, second_inner, 0))
+    put_packed(x2, 1, packed_tiles(low_own, 2))
+    put_packed(x2, 2, packed_tiles(low_own, 3))
+    put_packed(x2, 3, either(upper, second_inner, 0, second_outer, 0))
     idx = jnp.where(upper, 1, 0)
     put_row(near, coarse_gru(x2, idx + 1, h1, idx + 1, w_x, w_h, acc_x, acc_h, True))
 
@@ -659,7 +660,8 @@
     )
     coarse_o, coarse_i = outer_swap(coarse), inner_swap(coarse)
 
-    halo = (3 * ROW_TILES, SUB, LANES)
+    halo = (2 * ROW_TILES, SUB, LANES)
+    row = (ROW_TILES, SUB, LANES)
     edge = (2, FB // 2, SUB, LANES)
 
     def fine_shape(count, blocks=FB + 2):
@@ -668,13 +670,14 @@
     p1_own, stem2_own, inside = call(
         fine_own_body, on_chip(own, w_stem, w_enc), [fine_shape(4), fine_shape(4, FB), fine_shape(2)], []
     )
-    state_f, low_own, to_outer, to_inner, state_fo, state_fi = call(
+    state_f, low_own, to_outer, to_inner, second_o, second_i, state_fo, state_fi = call(
         fine_encoder_body,
         on_chip(p1_own, stem2_own, inside, outer, inner, w_stem, w_enc, w_down),
-        [(4, FB // 2, SUB, LANES), (4 * ROW_TILES, SUB, LANES), halo, halo, edge, edge],
+        [(4, FB // 2, SUB, LANES), (4 * ROW_TILES, SUB, LANES), halo, halo, row, row, edge, edge],
         [fine_buf(5), pltpu.VMEM(fine_shape(5, FB), BF), fine_buf(5), fine_buf(9)],
     )
     got_o, got_i = outer_swap(to_outer), inner_swap(to_inner)
+    second_o, second_i = outer_swap(second_o), inner_swap(second_i)
 
     acc_first, h_first = call(
         coarse_state_body,
@@ -686,11 +689,11 @@
 
     w_x, w_h = enc_coarse_x.reshape(flat), enc_coarse_h.reshape(flat)
     four = (4, CB + 2, SUB, 4 * LANES)
-    near, h1, x2 = call(
-        coarse_encoder_body,
-        on_chip(low_own, got_o, got_i, acc_first, h_first, w_x, w_h),
-        [(ROW_TILES, SUB, LANES), four, four],
-        [coarse_buf(6), acc_buf, acc_buf],
+    (h1,) = call(
+        coarse_encoder_body, on_chip(low_own, got_o, got_i, acc_first, h_first, w_x), [four], [coarse_buf(6), acc_buf]
+    )
+    near, x2 = call(
+        coarse_near_body, on_chip(low_own, second_o, second_i, h1, w_x, w_h), [row, four], [acc_buf, acc_buf]
     )
     in_near = inner_swap(near)
     (far,) = call(coarse_rest_body, on_chip(h1, x2, w_x, w_h), [(ROW_TILES, SUB, LANES)], [acc_buf, acc_buf])

time: 73.3 us -> 68.6 us (0.936)
  the two profiles are of different devices: /device:TPU:19 before, /device:TPU:15 now
where the time goes in v6:
time: 68.6 us; the launch traced here: 68.3 us
  Pallas kernels  32.8 us (48%)
  starting transfers between devices  29.2 us (43%)
  local copies, waits for them, and re-layouts  3.88 us (6%)
  waiting for transfers between devices  2.02 us (3%)
    pallas_call x12, Pallas kernels, call(): pl.pallas_call(body, out_shape=[s if isinstance(s, jax.ShapeDtypeStruct)...  32.8 us
    ppermute x6, starting transfers between devices, outer_swap(): return lax.ppermute(x, LINE, across)  22.2 us
    ppermute x8, starting transfers between devices, inner_swap(): return lax.ppermute(x, 'section', [(0, 1), (1, 0)])  7.04 us
    unnamed x24, local copies, waits for them, and re-layouts  2.12 us
    ppermute x6, waiting for transfers between devices, outer_swap(): return lax.ppermute(x, LINE, across)  2 us
  transfers between devices with their start and end apart: 14, of which 1 were waited for; matrix products, arithmetic and copies ran while one was open for 1% of the time, Pallas kernels for 32%

profile of v6, /device:TPU:15, one launch (start us, length us, event | category | flops | bytes accessed | tf_op | source)
XLA Modules:
  0.0 68.3 jit_solution(13638951953903913228)
XLA Ops:
  0.0 1.0 %fusion = (bf16[1,4,8192]{2,1,0:T(4,128)(2,1)S(1)}, bf16[1,4,8192]{2,1,0:T(4,128)(2,1)S(1)}) fusion(bf16[2,4,8192]{2,1,0:T(4,128)(2,1)} %param.14), kind=kLoop, calls=%fused_computation.5 | loop fusion | bytes 262144 | tf_op jit(solution)/shard_map/slice | solution.py:637
  1.0 1.1 %copy.25 = bf16[1,4,16,2048]{3,2,1,0:T(8,128)(2,1)S(1)} copy(bf16[1,4,16,2048]{3,1,2,0:T(4,128)(2,1)} %bitcast.50) | data formatting | bytes 524288
  2.2 0.1 shard_map.136
  2.2 3.7 %collective-permute-start = (bf16[3,16,3072]{2,1,0:T(8,128)(2,1)S(1)}, bf16[3,16,3072]{2,1,0:T(8,128)(2,1)S(1)}, u32[]{:S(2)}, u32[]{:S(2)}) collective-permute-start(bf16[3,16,3072]{2,1,0:T(8,128)(2,1)S(1)} %get-tuple-element.36), channel_id=1, source_target_pairs={{1,2},{3,4},{5,6},{7,8},{9,10},{11,12},{13,14},{2,1},{4,3},{6,5},{... | collective-permute-start | bytes 884744 | tf_op jit(solution)/shard_map/ppermute | solution.py:618
  6.0 0.1 collective-permute-start.1
  6.0 1.0 %copy.26 = bf16[1,2,16,3072]{3,2,1,0:T(8,128)(2,1)S(1)} copy(bf16[1,2,16,3072]{3,1,2,0:T(2,128)(2,1)} %bitcast.53) | data formatting | bytes 393216
  7.0 3.5 %collective-permute-start.4 = (bf16[2,16,3072]{2,1,0:T(8,128)(2,1)S(1)}, bf16[2,16,3072]{2,1,0:T(8,128)(2,1)S(1)}, u32[]{:S(2)}, u32[]{:S(2)}) collective-permute-start(bf16[2,16,3072]{2,1,0:T(8,128)(2,1)S(1)} %bitcast.40), channel_id=1, source_target_pairs={{1,2},{3,4},{5,6},{7,8},{9,10},{11,12},{13,14},{2,1},{4,3},{6,5},{... | collective-permute-start | bytes 589832 | tf_op jit(solution)/shard_map/ppermute | solution.py:618
  10.5 0.1 collective-permute-start.5
  10.7 0.5 shard_map.137
  11.2 1.5 %shard_map.138 = (bf16[4,34,16,128]{3,2,1,0:T(8,128)(2,1)S(1)}, bf16[4,32,16,128]{3,2,1,0:T(8,128)(2,1)S(1)}, bf16[2,34,16,128]{3,2,1,0:T(8,128)(2,1)S(1)}) custom-call(bf16[4,16,3072]{2,1,0:T(8,128)(2,1)S(1)} %get-tuple-element.30.own, bf16[128,1024]{1,0:T(8,128)(2,1)S(1)} %get-tuple-element.31.w_stem, bf16[1152,256]{1,0:T(8,128)(2,1)S(1)} %get-tuple-element.32.w_gru), custom_call_target="tpu_custom_call" | custom-call | tf_op jit(solution)/shard_map/pallas_call | solution.py:586
  12.6 0.0 copy-start.1
  12.7 5.8 %shard_map.139 = (bf16[4,16,16,128]{3,2,1,0:T(8,128)(2,1)S(1)}, bf16[96,16,128]{2,1,0:T(8,128)(2,1)S(1)}, bf16[48,16,128]{2,1,0:T(8,128)(2,1)S(1)}, bf16[48,16,1...) custom-call(bf16[4,34,16,128]{3,2,1,0:T(8,128)(2,1)S(1)} %get-tuple-, ...), custom_call_target="tpu_custom_call" | custom-call | tf_op jit(solution)/shard_map/pallas_call | solution.py:586
  18.5 3.6 %collective-permute-start.2 = (bf16[48,16,128]{2,1,0:T(8,128)(2,1)S(1)}, bf16[48,16,128]{2,1,0:T(8,128)(2,1)S(1)}, u32[]{:S(2)}, u32[]{:S(2)}) collective-permute-start(bf16[48,16,128]{2,1,0:T(8,128)(2,1)S(1)} %get-tuple-element.40), channel_id=1, source_target_pairs={{1,2},{3,4},{5,6},{7,8},{9,10},{11,12},{13,14},{2,1},{4,3},{6,5},{... | collective-permute-start | bytes 589832 | tf_op jit(solution)/shard_map/ppermute | solution.py:618
  22.1 2.0 %collective-permute-start.3 = (bf16[48,16,128]{2,1,0:T(8,128)(2,1)S(1)}, bf16[48,16,128]{2,1,0:T(8,128)(2,1)S(1)}, u32[]{:S(2)}, u32[]{:S(2)}) collective-permute-start(bf16[48,16,128]{2,1,0:T(8,128)(2,1)S(1)} %get-tuple-element.41), channel_id=1, source_target_pairs={{0,1},{1,0},{2,3},{3,2},{4,5},{5,4},{6,7},{7,6},{8,9},{9,8},{10,11... | collective-permute-start | bytes 589832 | tf_op jit(solution)/shard_map/ppermute | solution.py:621
  24.2 4.8 %collective-permute-start.6 = (bf16[24,16,128]{2,1,0:T(8,128)(2,1)S(1)}, bf16[24,16,128]{2,1,0:T(8,128)(2,1)S(1)}, u32[]{:S(2)}, u32[]{:S(2)}) collective-permute-start(bf16[24,16,128]{2,1,0:T(8,128)(2,1)S(1)} %get-tuple-element.44), channel_id=1, source_target_pairs={{1,2},{3,4},{5,6},{7,8},{9,10},{11,12},{13,14},{2,1},{4,3},{6,5},{... | collective-permute-start | bytes 294920 | tf_op jit(solution)/shard_map/ppermute | solution.py:618
  29.0 0.1 collective-permute-start.7
  29.1 3.2 %shard_map.140 = (f32[4,256,640]{2,1,0:T(8,128)S(1)}, bf16[4,18,16,512]{3,2,1,0:T(8,128)(2,1)S(1)}) custom-call(bf16[2,16,3072]{2,1,0:T(8,128)(2,1)S(1)} %bitcast.42, bf16[2,16,3072]{2,1,0:T(8,128)(2,1)S(1)} %collective-permute-done.4.outer, bf16[2,16,3072]{2,1,0:T(8,128)(2,1)S(1)} %collective-permute-done.5.inner, bf16[1728,576]{1,0:T(8,128)(2,1)S(1)} %bitcast.33), custom_call_target="tpu_custom_call" | custom-call | tf_op jit(solution)/shard_map/pallas_call | solution.py:586
  32.4 3.4 %shard_map.141.h1 = bf16[4,18,16,512]{3,2,1,0:T(8,128)(2,1)S(1)} custom-call(bf16[96,16,128]{2,1,0:T(8,128)(2,1)S(1)} %get-tuple-element.39.low_own, bf16[48,16,128]{2,1,0:T(8,128)(2,1)S(1)} %collective-permute-done.2.low_outer, bf16[48,16,128]{2,1,0:T(8,128)(2,1)S(1)} %collective-permute-done.3.low_inner, f32[4,256,640]{2,1,0:T(8,128)S(1)} %get-tuple-element.42.acc_first, ...), custom_call_target="tpu_custom_call" | custom-call | tf_op jit(solution)/shard_map/pallas_call | solution.py:586
  35.8 1.8 %shard_map.142 = (bf16[24,16,128]{2,1,0:T(8,128)(2,1)S(1)}, bf16[4,18,16,512]{3,2,1,0:T(8,128)(2,1)S(1)}) custom-call(bf16[96,16,128]{2,1,0:T(8,128)(2,1)S(1)} %get-tuple-element.39.low_own, bf16[24,16,128]{2,1,0:T(8,128)(2,1)S(1)} %collective-permute-done.6.second_outer, bf16[24,16,128]{2,1,0:T(8,128)(2,1)S(1)} %collective-permute-done.7.second_inner, ...), custom_call_target="tpu_custom_call" | custom-call | tf_op jit(solution)/shard_map/pallas_call | solution.py:586
  37.7 0.5 collective-permute-start.9
  38.2 1.7 %shard_map.143.far = bf16[24,16,128]{2,1,0:T(8,128)(2,1)S(1)} custom-call(bf16[4,18,16,512]{3,2,1,0:T(8,128)(2,1)S(1)} %shard_map.141.h1, bf16[4,18,16,512]{3,2,1,0:T(8,128)(2,1)S(1)} %get-tuple-element.46.x2, bf16[1728,576]{1,0:T(8,128)(2,1)S(1)} %bitcast.38, bf16[1728,576]{1,0:T(8,128)(2,1)S(1)} %bitcast.35), custom_call_target="tpu_custom_call" | custom-call | tf_op jit(solution)/shard_map/pallas_call | solution.py:586
  40.0 1.9 %collective-permute-start.10 = (bf16[72,16,128]{2,1,0:T(8,128)(2,1)S(1)}, bf16[72,16,128]{2,1,0:T(8,128)(2,1)S(1)}, u32[]{:S(2)}, u32[]{:S(2)}) collective-permute-start(bf16[72,16,128]{2,1,0:T(8,128)(2,1)S(1)} %pad_maximum_fusion), channel_id=1, source_target_pairs={{1,2},{3,4},{5,6},{7,8},{9,10},{11,12},{13,14},{2,1},{4,3},{6,5},{... | collective-permute-start | bytes 884744 | tf_op jit(solution)/shard_map/ppermute | solution.py:618
  41.9 4.5 %collective-permute-start.12 = (bf16[2,16,16,128]{3,2,1,0:T(8,128)(2,1)S(1)}, bf16[2,16,16,128]{3,2,1,0:T(8,128)(2,1)S(1)}, u32[]{:S(2)}, u32[]{:S(2)}) collective-permute-start(bf16[2,16,16,128]{3,2,1,0:T(8,128)(2,1)S(1)} %get-tuple-element.49), channel_id=1, source_target_pairs={{1,2},{3,4},{5,6},{7,8},{9,10},{11,12},{13,14},{2,1},{4,3},{6,5},{... | collective-permute-start | bytes 393224 | tf_op jit(solution)/shard_map/ppermute | solution.py:618
  46.4 0.1 collective-permute-start.13
  46.5 0.5 collective-permute-start.8
  47.0 2.0 %collective-permute-done.10.outer = bf16[72,16,128]{2,1,0:T(8,128)(2,1)S(1)} collective-permute-done((bf16[72,16,128]{2,1,0:T(8,128)(2,1)S(1)}, bf16[72,16,128]{2,1,0:T(8,128)(2,1)S(1)}, u32[]{:S(2)}, u32[]{:S(2)}) %collective-permute-start.10) | collective-permute-done | bytes 294944 | tf_op jit(solution)/shard_map/ppermute | solution.py:618
  49.0 3.7 %collective-permute-start.11 = (bf16[24,16,128]{2,1,0:T(8,128)(2,1)S(1)}, bf16[24,16,128]{2,1,0:T(8,128)(2,1)S(1)}, u32[]{:S(2)}, u32[]{:S(2)}) collective-permute-start(bf16[24,16,128]{2,1,0:T(8,128)(2,1)S(1)} %slice.14), channel_id=1, source_target_pairs={{0,1},{1,0},{2,3},{3,2},{4,5},{5,4},{6,7},{7,6},{8,9},{9,8},{10,11... | collective-permute-start | bytes 294920 | tf_op jit(solution)/shard_map/ppermute | solution.py:621
  52.7 1.0 %shard_map.146 = (bf16[768,256]{1,0:T(8,128)(2,1)S(1)}, bf16[1152,256]{1,0:T(8,128)(2,1)S(1)}, bf16[1024,128]{1,0:T(8,128)(2,1)S(1)}) custom-call(bf16[9,64,192]{2,1,0:T(8,128)(2,1)S(1)} %bitcast.46, bf16[9,64,192]{2,1,0:T(8,128)(2,1)S(1)} %bitcast.47, bf16[9,64,192]{2,1,0:T(8,128)(2,1)S(1)} %bitcast.48, bf16[16,64]{1,0:T(8,128)(2,1)S(1)} %bitcast.49), custom_call_target="tpu_custom_call" | custom-call | tf_op jit(solution)/shard_map/pallas_call | solution.py:586
  53.7 1.8 %shard_map.144.s1_given = bf16[6,18,16,512]{3,2,1,0:T(8,128)(2,1)S(1)} custom-call(bf16[24,16,128]{2,1,0:T(8,128)(2,1)S(1)} %shard_map.143.far, bf16[24,16,128]{2,1,0:T(8,128)(2,1)S(1)} %get-tuple-element.47.near, bf16[24,16,128]{2,1,0:T(8,128)(2,1)S(1)} %collective-permute-done.8.in_far, bf16[24,16,128]{2,1,0:T(8,128)(2,1)S(1)} %collective-permute-done.9.in_near, ...), custom_call_target="tpu_custom_call" | custom-call | tf_op jit(solution)/shard_map/pallas_call | solution.py:586
  55.6 2.6 %shard_map.145.s1_given = bf16[6,18,16,512]{3,2,1,0:T(8,128)(2,1)S(1)} custom-call(bf16[6,18,16,512]{3,2,1,0:T(8,128)(2,1)S(1)} %shard_map.144.s1_given, bf16[24,16,128]{2,1,0:T(8,128)(2,1)S(1)} %shard_map.143.far, bf16[24,16,128]{2,1,0:T(8,128)(2,1)S(1)} %get-tuple-element.47.near, ...), custom_call_target="tpu_custom_call", output_to_operand_aliasing={{}: (0, {})} | custom-call | tf_op jit(solution)/shard_map/pallas_call | solution.py:586
  58.2 9.3 %shard_map.147 = (bf16[2,4,16,512]{3,2,1,0:T(8,128)(2,1)S(1)}, bf16[6,18,16,512]{3,2,1,0:T(8,128)(2,1)S(1)}) custom-call(bf16[6,18,16,512]{3,2,1,0:T(8,128)(2,1)S(1)} %shard_map.145.s1_given, bf16[24,16,128]{2,1,0:T(8,128)(2,1)S(1)} %collective-permute-done.8.in_far, ...), custom_call_target="tpu_custom_call", output_to_operand_aliasing={{1}: (0, {})} | custom-call | tf_op jit(solution)/shard_map/pallas_call | solution.py:586
  67.6 0.7 %reshape.53 = bf16[2,4,8192]{2,1,0:T(4,128)(2,1)} reshape(bf16[2,4,16,512]{3,2,1,0:T(8,128)(2,1)S(1)} %get-tuple-element.54) | data formatting | bytes 262144 | tf_op jit(solution)/shard_map/reshape | solution.py:725
  (37 shorter events, 0.1 us)
Async XLA Ops:
  0.0 10.6 %copy-start.3 = (bf16[3,3,64,192]{3,2,1,0:T(8,128)(2,1)S(1)}, bf16[3,3,64,192]{3,2,1,0:T(8,128)(2,1)}, u32[]{:S(2)}) copy-start(bf16[3,3,64,192]{3,2,1,0:T(8,128)(2,1)} %param.18) | copy-start | bytes 663556
  0.0 10.6 %copy-start.4 = (bf16[3,3,64,192]{3,2,1,0:T(8,128)(2,1)S(1)}, bf16[3,3,64,192]{3,2,1,0:T(8,128)(2,1)}, u32[]{:S(2)}) copy-start(bf16[3,3,64,192]{3,2,1,0:T(8,128)(2,1)} %param.19) | copy-start | bytes 663556
  0.0 10.6 %copy-start.5 = (bf16[3,3,64,192]{3,2,1,0:T(8,128)(2,1)S(1)}, bf16[3,3,64,192]{3,2,1,0:T(8,128)(2,1)}, u32[]{:S(2)}) copy-start(bf16[3,3,64,192]{3,2,1,0:T(8,128)(2,1)} %param.20) | copy-start | bytes 663556
  0.0 10.6 %copy-start.9 = (bf16[16,64]{1,0:T(8,128)(2,1)S(1)}, bf16[16,64]{1,0:T(8,128)(2,1)}, u32[]{:S(2)}) copy-start(bf16[16,64]{1,0:T(8,128)(2,1)} %refs_0_.1) | copy-start | bytes 6148
  2.2 10.4 %collective-permute-start = (bf16[3,16,3072]{2,1,0:T(8,128)(2,1)S(1)}, bf16[3,16,3072]{2,1,0:T(8,128)(2,1)S(1)}, u32[]{:S(2)}, u32[]{:S(2)}) collective-permute-start(bf16[3,16,3072]{2,1,0:T(8,128)(2,1)S(1)} %get-tuple-element.36), channel_id=1, source_target_pairs={{1,2},{3,4},{5,6},{7,8},{9,10},{11,12},{13,14},{2,1},{4,3},{6,5},{... | collective-permute-start | bytes 884744 | tf_op jit(solution)/shard_map/ppermute | solution.py:618
  6.0 6.7 %collective-permute-start.1 = (bf16[3,16,3072]{2,1,0:T(8,128)(2,1)S(1)}, bf16[3,16,3072]{2,1,0:T(8,128)(2,1)S(1)}, u32[]{:S(2)}, u32[]{:S(2)}) collective-permute-start(bf16[3,16,3072]{2,1,0:T(8,128)(2,1)S(1)} %get-tuple-element.37), channel_id=1, source_target_pairs={{0,1},{1,0},{2,3},{3,2},{4,5},{5,4},{6,7},{7,6},{8,9},{9,8},{10,11... | collective-permute-start | bytes 884744 | tf_op jit(solution)/shard_map/ppermute | solution.py:621
  7.0 22.0 %collective-permute-start.4 = (bf16[2,16,3072]{2,1,0:T(8,128)(2,1)S(1)}, bf16[2,16,3072]{2,1,0:T(8,128)(2,1)S(1)}, u32[]{:S(2)}, u32[]{:S(2)}) collective-permute-start(bf16[2,16,3072]{2,1,0:T(8,128)(2,1)S(1)} %bitcast.40), channel_id=1, source_target_pairs={{1,2},{3,4},{5,6},{7,8},{9,10},{11,12},{13,14},{2,1},{4,3},{6,5},{... | collective-permute-start | bytes 589832 | tf_op jit(solution)/shard_map/ppermute | solution.py:618
  10.5 18.6 %collective-permute-start.5 = (bf16[2,16,3072]{2,1,0:T(8,128)(2,1)S(1)}, bf16[2,16,3072]{2,1,0:T(8,128)(2,1)S(1)}, u32[]{:S(2)}, u32[]{:S(2)}) collective-permute-start(bf16[2,16,3072]{2,1,0:T(8,128)(2,1)S(1)} %bitcast.41), channel_id=1, source_target_pairs={{0,1},{1,0},{2,3},{3,2},{4,5},{5,4},{6,7},{7,6},{8,9},{9,8},{10,11... | collective-permute-start | bytes 589832 | tf_op jit(solution)/shard_map/ppermute | solution.py:621
  12.6 16.5 %copy-start.1 = (bf16[3,3,192,576]{3,2,1,0:T(8,128)(2,1)S(1)}, bf16[3,3,192,576]{3,2,1,0:T(8,128)(2,1)}, u32[]{:S(2)}) copy-start(bf16[3,3,192,576]{3,2,1,0:T(8,128)(2,1)} %param.22) | copy-start | bytes 5971972
  18.5 13.9 %copy-start.2 = (bf16[3,3,192,576]{3,2,1,0:T(8,128)(2,1)S(1)}, bf16[3,3,192,576]{3,2,1,0:T(8,128)(2,1)}, u32[]{:S(2)}) copy-start(bf16[3,3,192,576]{3,2,1,0:T(8,128)(2,1)} %param.21) | copy-start | bytes 5971972
  18.5 13.9 %collective-permute-start.2 = (bf16[48,16,128]{2,1,0:T(8,128)(2,1)S(1)}, bf16[48,16,128]{2,1,0:T(8,128)(2,1)S(1)}, u32[]{:S(2)}, u32[]{:S(2)}) collective-permute-start(bf16[48,16,128]{2,1,0:T(8,128)(2,1)S(1)} %get-tuple-element.40), channel_id=1, source_target_pairs={{1,2},{3,4},{5,6},{7,8},{9,10},{11,12},{13,14},{2,1},{4,3},{6,5},{... | collective-permute-start | bytes 589832 | tf_op jit(solution)/shard_map/ppermute | solution.py:618
  22.1 10.3 %collective-permute-start.3 = (bf16[48,16,128]{2,1,0:T(8,128)(2,1)S(1)}, bf16[48,16,128]{2,1,0:T(8,128)(2,1)S(1)}, u32[]{:S(2)}, u32[]{:S(2)}) collective-permute-start(bf16[48,16,128]{2,1,0:T(8,128)(2,1)S(1)} %get-tuple-element.41), channel_id=1, source_target_pairs={{0,1},{1,0},{2,3},{3,2},{4,5},{5,4},{6,7},{7,6},{8,9},{9,8},{10,11... | collective-permute-start | bytes 589832 | tf_op jit(solution)/shard_map/ppermute | solution.py:621
  24.2 11.6 %collective-permute-start.6 = (bf16[24,16,128]{2,1,0:T(8,128)(2,1)S(1)}, bf16[24,16,128]{2,1,0:T(8,128)(2,1)S(1)}, u32[]{:S(2)}, u32[]{:S(2)}) collective-permute-start(bf16[24,16,128]{2,1,0:T(8,128)(2,1)S(1)} %get-tuple-element.44), channel_id=1, source_target_pairs={{1,2},{3,4},{5,6},{7,8},{9,10},{11,12},{13,14},{2,1},{4,3},{6,5},{... | collective-permute-start | bytes 294920 | tf_op jit(solution)/shard_map/ppermute | solution.py:618
  29.0 6.8 %collective-permute-start.7 = (bf16[24,16,128]{2,1,0:T(8,128)(2,1)S(1)}, bf16[24,16,128]{2,1,0:T(8,128)(2,1)S(1)}, u32[]{:S(2)}, u32[]{:S(2)}) collective-permute-start(bf16[24,16,128]{2,1,0:T(8,128)(2,1)S(1)} %get-tuple-element.45), channel_id=1, source_target_pairs={{0,1},{1,0},{2,3},{3,2},{4,5},{5,4},{6,7},{7,6},{8,9},{9,8},{10,11... | collective-permute-start | bytes 294920 | tf_op jit(solution)/shard_map/ppermute | solution.py:621
  37.7 2.3 %collective-permute-start.9 = (bf16[24,16,128]{2,1,0:T(8,128)(2,1)S(1)}, bf16[24,16,128]{2,1,0:T(8,128)(2,1)S(1)}, u32[]{:S(2)}, u32[]{:S(2)}) collective-permute-start(bf16[24,16,128]{2,1,0:T(8,128)(2,1)S(1)} %get-tuple-element.47.near), channel_id=1, source_target_pairs={{0,1},{1,0},{2,3},{3,2},{4,5},{5,4},{6,7},{7,6},{8,9},{9,8},{10,11... | collective-permute-start | bytes 294920 | tf_op jit(solution)/shard_map/ppermute | solution.py:621
  38.2 14.5 %copy-start.6 = (bf16[3,3,192,64]{2,3,1,0:T(8,128)(2,1)S(1)}, bf16[3,3,192,64]{2,3,1,0:T(8,128)(2,1)}, u32[]{:S(2)}) copy-start(bf16[3,3,192,64]{2,3,1,0:T(8,128)(2,1)} %param.24) | copy-start | bytes 663556
  38.2 14.5 %copy-start.7 = (bf16[3,3,64,192]{3,2,1,0:T(8,128)(2,1)S(1)}, bf16[3,3,64,192]{3,2,1,0:T(8,128)(2,1)}, u32[]{:S(2)}) copy-start(bf16[3,3,64,192]{3,2,1,0:T(8,128)(2,1)} %param.25) | copy-start | bytes 663556
  38.2 14.5 %copy-start.8 = (bf16[3,3,64,192]{3,2,1,0:T(8,128)(2,1)S(1)}, bf16[3,3,64,192]{3,2,1,0:T(8,128)(2,1)}, u32[]{:S(2)}) copy-start(bf16[3,3,64,192]{3,2,1,0:T(8,128)(2,1)} %param.26) | copy-start | bytes 663556
  38.2 14.5 %copy-start.10 = (bf16[64,16]{0,1:T(8,128)(2,1)S(1)}, bf16[64,16]{0,1:T(8,128)(2,1)}, u32[]{:S(2)}) copy-start(bf16[64,16]{0,1:T(8,128)(2,1)} %param.27) | copy-start | bytes 6148
  38.2 15.5 %copy-start = (bf16[3,3,192,576]{3,2,1,0:T(8,128)(2,1)S(1)}, bf16[3,3,192,576]{3,2,1,0:T(8,128)(2,1)}, u32[]{:S(2)}) copy-start(bf16[3,3,192,576]{3,2,1,0:T(8,128)(2,1)} %param.23) | copy-start | bytes 5971972
  40.0 9.0 %collective-permute-start.10 = (bf16[72,16,128]{2,1,0:T(8,128)(2,1)S(1)}, bf16[72,16,128]{2,1,0:T(8,128)(2,1)S(1)}, u32[]{:S(2)}, u32[]{:S(2)}) collective-permute-start(bf16[72,16,128]{2,1,0:T(8,128)(2,1)S(1)} %pad_maximum_fusion), channel_id=1, source_target_pairs={{1,2},{3,4},{5,6},{7,8},{9,10},{11,12},{13,14},{2,1},{4,3},{6,5},{... | collective-permute-start | bytes 884744 | tf_op jit(solution)/shard_map/ppermute | solution.py:618
  41.9 16.3 %collective-permute-start.12 = (bf16[2,16,16,128]{3,2,1,0:T(8,128)(2,1)S(1)}, bf16[2,16,16,128]{3,2,1,0:T(8,128)(2,1)S(1)}, u32[]{:S(2)}, u32[]{:S(2)}) collective-permute-start(bf16[2,16,16,128]{3,2,1,0:T(8,128)(2,1)S(1)} %get-tuple-element.49), channel_id=1, source_target_pairs={{1,2},{3,4},{5,6},{7,8},{9,10},{11,12},{13,14},{2,1},{4,3},{6,5},{... | collective-permute-start | bytes 393224 | tf_op jit(solution)/shard_map/ppermute | solution.py:618
  46.4 11.7 %collective-permute-start.13 = (bf16[2,16,16,128]{3,2,1,0:T(8,128)(2,1)S(1)}, bf16[2,16,16,128]{3,2,1,0:T(8,128)(2,1)S(1)}, u32[]{:S(2)}, u32[]{:S(2)}) collective-permute-start(bf16[2,16,16,128]{3,2,1,0:T(8,128)(2,1)S(1)} %get-tuple-element.50), channel_id=1, source_target_pairs={{0,1},{1,0},{2,3},{3,2},{4,5},{5,4},{6,7},{7,6},{8,9},{9,8},{10,11... | collective-permute-start | bytes 393224 | tf_op jit(solution)/shard_map/ppermute | solution.py:621
  46.5 7.2 %collective-permute-start.8 = (bf16[24,16,128]{2,1,0:T(8,128)(2,1)S(1)}, bf16[24,16,128]{2,1,0:T(8,128)(2,1)S(1)}, u32[]{:S(2)}, u32[]{:S(2)}) collective-permute-start(bf16[24,16,128]{2,1,0:T(8,128)(2,1)S(1)} %shard_map.143.far), channel_id=1, source_target_pairs={{0,1},{1,0},{2,3},{3,2},{4,5},{5,4},{6,7},{7,6},{8,9},{9,8},{10,11... | collective-permute-start | bytes 294920 | tf_op jit(solution)/shard_map/ppermute | solution.py:621
  49.0 9.2 %collective-permute-start.11 = (bf16[24,16,128]{2,1,0:T(8,128)(2,1)S(1)}, bf16[24,16,128]{2,1,0:T(8,128)(2,1)S(1)}, u32[]{:S(2)}, u32[]{:S(2)}) collective-permute-start(bf16[24,16,128]{2,1,0:T(8,128)(2,1)S(1)} %slice.14), channel_id=1, source_target_pairs={{0,1},{1,0},{2,3},{3,2},{4,5},{5,4},{6,7},{7,6},{8,9},{9,8},{10,11... | collective-permute-start | bytes 294920 | tf_op jit(solution)/shard_map/ppermute | solution.py:621

commit v7 on v6

--- a/solution.py
+++ b/solution.py
@@ -348,9 +348,10 @@
         h_out[idx] = h0[idx + 1]
 
 
-def put_row(ref, forms):
+def put_row(ref, slot, forms):
     for k, tile in enumerate(pack_forms(forms)):
-        ref[k * PAIRS : (k + 1) * PAIRS] = tile
+        base = slot * ROW_TILES + k * PAIRS
+        ref[base : base + PAIRS] = tile
 
 
 def coarse_encoder_body(low_own, low_outer, low_inner, acc_first, h_first, w_x, h1, x1, acc_x):
@@ -370,7 +371,7 @@
         put_forms(h1, idx, forms)
 
 
-def coarse_near_body(low_own, second_outer, second_inner, h1, w_x, w_h, near, x2, acc_x, acc_h):
+def coarse_second_body(low_own, second_outer, second_inner, h1, w_x, w_h, state, x2, acc_x, acc_h):
     upper, _, _ = place(2)
     zero_tail(acc_x)
     zero_tail(acc_h)
@@ -378,16 +379,9 @@
     put_packed(x2, 1, packed_tiles(low_own, 2))
     put_packed(x2, 2, packed_tiles(low_own, 3))
     put_packed(x2, 3, either(upper, second_inner, 0, second_outer, 0))
-    idx = jnp.where(upper, 1, 0)
-    put_row(near, coarse_gru(x2, idx + 1, h1, idx + 1, w_x, w_h, acc_x, acc_h, True))
-
-
-def coarse_rest_body(h1, x2, w_x, w_h, far, acc_x, acc_h):
-    upper, _, _ = place(2)
-    zero_tail(acc_x)
-    zero_tail(acc_h)
-    idx = jnp.where(upper, 0, 1)
-    put_row(far, coarse_gru(x2, idx + 1, h1, idx + 1, w_x, w_h, acc_x, acc_h, True))
+    for slot in range(2):
+        idx = jnp.where(upper, slot, 1 - slot)
+        put_row(state, slot, coarse_gru(x2, idx + 1, h1, idx + 1, w_x, w_h, acc_x, acc_h, True))
 
 
 def raise_pair(src, idx, weight):
@@ -405,48 +399,64 @@
     return lambda t: jnp.where(upper, packed_tiles(a, i)(t), packed_tiles(b, j)(t))
 
 
-def forecast_inner_body(far, near, in_far, in_near, w_h, s1, h2, acc_h):
+def forecast_row(rows_of, w_h, h2, acc_h, dst, at, first, rows):
+    for k, tiles in enumerate(rows_of):
+        put_packed(h2, k, tiles)
+    forms = coarse_gru(None, 0, h2, 1, None, w_h, None, acc_h, in_grid(first + at, rows))
+    put_forms(dst, at, forms)
+    return forms
+
+
+def forecast_inner_body(own, in_near, w_h, s1, sent, h2, acc_h):
     upper, first, rows = place(2)
     zero_tail(acc_h)
-    put_packed(h2, 0, either(upper, far, 0, in_far, 0))
-    put_packed(h2, 1, either(upper, near, 0, in_near, 0))
-    put_packed(h2, 2, either(upper, in_near, 0, near, 0))
-    put_packed(h2, 3, either(upper, in_far, 0, far, 0))
-    at = jnp.where(upper, 3, 1)
-    for k in range(2):
-        forms = coarse_gru(None, 0, h2, k + 1, None, w_h, None, acc_h, in_grid(first + at + k - 2, rows))
-        put_forms(s1, at + k, forms)
-
-
-def forecast_outer_body(s1_given, far, near, outer, w_h, s1, h2, acc_h):
+    given = (either(upper, own, 0, in_near, 0), packed_tiles(own, 1), either(upper, in_near, 0, own, 0))
+    at = jnp.where(upper, 3, 2)
+    put_row(sent, 0, forecast_row(given, w_h, h2, acc_h, s1, at, first - 2, rows))
+
+
+def forecast_outer_body(s1_given, own, outer, w_h, s1, sent, h2, acc_h):
     upper, first, rows = place(2)
     zero_tail(acc_h)
-    put_packed(h2, 0, either(upper, outer, 2, near, 0))
-    put_packed(h2, 1, either(upper, outer, 1, far, 0))
-    put_packed(h2, 2, packed_tiles(outer, 0))
-    put_packed(h2, 3, either(upper, far, 0, outer, 1))
-    put_packed(h2, 4, either(upper, near, 0, outer, 2))
-    at = jnp.where(upper, 0, 3)
+    given = (either(upper, outer, 0, own, 1), packed_tiles(own, 0), either(upper, own, 1, outer, 0))
+    at = jnp.where(upper, 2, 3)
+    put_row(sent, 0, forecast_row(given, w_h, h2, acc_h, s1, at, first - 2, rows))
+
+
+def forecast_halo_body(s1_given, own, outer, w_h, s1, h2, acc_h):
+    upper, first, rows = place(2)
+    zero_tail(acc_h)
+    given = (either(upper, outer, 1, own, 0), packed_tiles(outer, 0), either(upper, own, 0, outer, 1))
+    forecast_row(given, w_h, h2, acc_h, s1, jnp.where(upper, 1, 4), first - 2, rows)
+
+
+def forecast_second_body(s1_given, in_near, in_far, w_h, s1, s2, acc_h):
+    upper, first, rows = place(2)
+    zero_tail(acc_h)
+    put_packed(s1, jnp.where(upper, 4, 1), packed_tiles(in_near, 0))
+    put_packed(s1, jnp.where(upper, 5, 0), packed_tiles(in_far, 0))
+    base = jnp.where(upper, 1, 0)
     for k in range(3):
-        forms = coarse_gru(None, 0, h2, k + 1, None, w_h, None, acc_h, in_grid(first + at + k - 2, rows))
-        put_forms(s1, at + k, forms)
+        at = base + k
+        forms = coarse_gru(None, 0, s1, at + 1, None, w_h, None, acc_h, in_grid(first + at - 1, rows))
+        put_forms(s2, at, forms)
+    s2[4] = jnp.zeros(s2.shape[1:], BF)
 
 
 def forecaster_body(
-    s1_given, in_far, in_near, third, f_own, f_outer, f_inner, w_h, w_up, w_gru, w_head,
-    out, s1, h2, s2, pf1, pf2, states, acc_h,
+    s1_given, s2_given, outer, rest, f_own, f_inner, w_h, w_up, w_gru, w_head,
+    out, s1, s2, h2, pf1, pf2, states, acc_h,
 ):
     upper, first_c, rows_c = place(2)
     _, first_f, rows_f = place(4)
     lo = low_half((1, SUB, LANES))
     zero_tail(acc_h)
 
-    put_packed(h2, 0, either(upper, in_near, 0, third, 0))
-    put_packed(h2, 1, packed_tiles(in_far, 0))
-    put_packed(h2, 2, either(upper, third, 0, in_near, 0))
-    last = jnp.where(upper, 5, 0)
+    given = (either(upper, rest, 0, outer, 0), packed_tiles(outer, 1), either(upper, outer, 0, rest, 0))
+    forecast_row(given, w_h, h2, acc_h, s1, jnp.where(upper, 0, 5), first_c - 2, rows_c)
+    at = jnp.where(upper, 0, 3)
     put_forms(
-        s1, last, coarse_gru(None, 0, h2, 1, None, w_h, None, acc_h, in_grid(first_c + last - 2, rows_c))
+        s2, at, coarse_gru(None, 0, s1, at + 1, None, w_h, None, acc_h, in_grid(first_c + at - 1, rows_c))
     )
 
     for idx in range(8):
@@ -454,17 +464,11 @@
             if 2 <= idx < 6:
                 pair = f_own[idx - 2, k]
             elif idx < 2:
-                pair = jnp.where(upper, f_outer[idx, k], f_inner[idx, k])
+                pair = jnp.where(upper, rest[ROW_TILES + idx * FB // 2 + k], f_inner[idx, k])
             else:
-                pair = jnp.where(upper, f_inner[idx - 6, k], f_outer[idx - 6, k])
+                pair = jnp.where(upper, f_inner[idx - 6, k], rest[ROW_TILES + (idx - 6) * FB // 2 + k])
             pf1[idx, 1 + 2 * k] = swap_bf(pair)
             pf1[idx, 2 + 2 * k] = pair
-
-    for idx in range(0, 4):
-        forms = coarse_gru(None, 0, s1, idx + 1, None, w_h, None, acc_h, in_grid(first_c + idx - 1, rows_c))
-        put_forms(s2, idx, forms)
-
-    s2[4] = jnp.zeros(s2.shape[1:], BF)
 
     def raise_rows(src, idx, fine, at, coarse_row):
         acc = raise_pair(src, idx, w_up)
@@ -685,42 +689,38 @@
         [jax.ShapeDtypeStruct((4, CB * SUB, 5 * LANES), F32), (4, CB + 2, SUB, 4 * LANES)],
         [coarse_buf(6)],
     )
-    state_fo, state_fi = outer_swap(state_fo), inner_swap(state_fi)
+    state_fi = inner_swap(state_fi)
 
     w_x, w_h = enc_coarse_x.reshape(flat), enc_coarse_h.reshape(flat)
     four = (4, CB + 2, SUB, 4 * LANES)
     (h1,) = call(
         coarse_encoder_body, on_chip(low_own, got_o, got_i, acc_first, h_first, w_x), [four], [coarse_buf(6), acc_buf]
     )
-    near, x2 = call(
-        coarse_near_body, on_chip(low_own, second_o, second_i, h1, w_x, w_h), [row, four], [acc_buf, acc_buf]
-    )
-    in_near = inner_swap(near)
-    (far,) = call(coarse_rest_body, on_chip(h1, x2, w_x, w_h), [(ROW_TILES, SUB, LANES)], [acc_buf, acc_buf])
-    in_far = inner_swap(far)
-    state_co = outer_swap(jnp.concatenate([far, near, in_near], axis=0))
-    third = inner_swap(state_co[:ROW_TILES])
+    (state_c,) = call(
+        coarse_second_body,
+        on_chip(low_own, second_o, second_i, h1, w_x, w_h),
+        [(2 * ROW_TILES, SUB, LANES)],
+        [coarse_buf(4), acc_buf, acc_buf],
+    )
+    in_near = inner_swap(state_c[ROW_TILES:])
+    state_o = outer_swap(state_c)
+    rest = outer_swap(jnp.concatenate([in_near, state_fo.reshape(FB, SUB, LANES)], axis=0))
 
     w_f = fc_coarse_h.reshape(flat)
-    (s1,) = call(
-        forecast_inner_body,
-        on_chip(far, near, in_far, in_near, w_f),
-        [(6, CB + 2, SUB, 4 * LANES)],
-        [coarse_buf(4), acc_buf],
-    )
-    (s1,) = call(
-        forecast_outer_body,
-        on_chip(s1, far, near, state_co, w_f),
-        [(6, CB + 2, SUB, 4 * LANES)],
-        [coarse_buf(5), acc_buf],
-        {0: 0},
-    )
-    out, _ = call(
+    six, five = (6,) + four[1:], (5,) + four[1:]
+    small = [coarse_buf(3), acc_buf]
+    s1, sent = call(forecast_inner_body, on_chip(state_c, in_near, w_f), [six, row], small)
+    in_near = inner_swap(sent)
+    s1, sent = call(forecast_outer_body, on_chip(s1, state_c, state_o, w_f), [six, row], small, {0: 0})
+    in_far = inner_swap(sent)
+    (s1,) = call(forecast_halo_body, on_chip(s1, state_c, state_o, w_f), [six], small, {0: 0})
+    s1, s2 = call(forecast_second_body, on_chip(s1, in_near, in_far, w_f), [six, five], [acc_buf], {0: 0})
+    out, _, _ = call(
         forecaster_body,
-        on_chip(s1, in_far, in_near, third, state_f, state_fo, state_fi, w_f, w_up, w_fc, w_head),
-        [(HORIZON, 4, SUB, FB * PATCH), (6, CB + 2, SUB, 4 * LANES)],
-        [coarse_buf(3), coarse_buf(5), fine_buf(8), fine_buf(6), fine_buf(4), acc_buf],
-        {0: 1},
+        on_chip(s1, s2, state_o, rest, state_f, state_fi, w_f, w_up, w_fc, w_head),
+        [(HORIZON, 4, SUB, FB * PATCH), six, five],
+        [coarse_buf(3), fine_buf(8), fine_buf(6), fine_buf(4), acc_buf],
+        {0: 1, 1: 2},
     )
     return out.reshape(HORIZON, 4, COLS * PATCH)
 

time: 68.6 us -> 64 us (0.933)
  the two profiles are of different devices: /device:TPU:15 before, /device:TPU:19 now
where the time goes in v7:
time: 64 us; the launch traced here: 63.7 us
  Pallas kernels  32 us (50%)
  starting transfers between devices  21 us (33%)
  waiting for transfers between devices  6.42 us (10%)
  local copies, waits for them, and re-layouts  3.88 us (6%)
    pallas_call x13, Pallas kernels, call(): pl.pallas_call(body, out_shape=[s if isinstance(s, jax.ShapeDtypeStruct)...  32 us
    ppermute x6, starting transfers between devices, outer_swap(): return lax.ppermute(x, LINE, across)  18.2 us
    ppermute x6, waiting for transfers between devices, outer_swap(): return lax.ppermute(x, LINE, across)  6.4 us
    ppermute x8, starting transfers between devices, inner_swap(): return lax.ppermute(x, 'section', [(0, 1), (1, 0)])  2.83 us
    unnamed x24, local copies, waits for them, and re-layouts  2.12 us
  transfers between devices with their start and end apart: 14, of which 2 were waited for; matrix products, arithmetic and copies ran while one was open for 2% of the time, Pallas kernels for 33%

profile of v7, /device:TPU:19, one launch (start us, length us, event | category | flops | bytes accessed | tf_op | source)
XLA Modules:
  0.0 63.7 jit_solution(9651611630119441157)
XLA Ops:
  0.0 1.0 %fusion = (bf16[1,4,8192]{2,1,0:T(4,128)(2,1)S(1)}, bf16[1,4,8192]{2,1,0:T(4,128)(2,1)S(1)}) fusion(bf16[2,4,8192]{2,1,0:T(4,128)(2,1)} %param.14), kind=kLoop, calls=%fused_computation.5 | loop fusion | bytes 262144 | tf_op jit(solution)/shard_map/slice | solution.py:641
  1.0 1.1 %copy.28 = bf16[1,4,16,2048]{3,2,1,0:T(8,128)(2,1)S(1)} copy(bf16[1,4,16,2048]{3,1,2,0:T(4,128)(2,1)} %bitcast.52) | data formatting | bytes 524288
  2.2 0.1 shard_map.136
  2.2 3.7 %collective-permute-start = (bf16[3,16,3072]{2,1,0:T(8,128)(2,1)S(1)}, bf16[3,16,3072]{2,1,0:T(8,128)(2,1)S(1)}, u32[]{:S(2)}, u32[]{:S(2)}) collective-permute-start(bf16[3,16,3072]{2,1,0:T(8,128)(2,1)S(1)} %get-tuple-element.40), channel_id=1, source_target_pairs={{1,2},{3,4},{5,6},{7,8},{9,10},{11,12},{13,14},{2,1},{4,3},{6,5},{... | collective-permute-start | bytes 884744 | tf_op jit(solution)/shard_map/ppermute | solution.py:622
  6.0 0.1 collective-permute-start.1
  6.0 1.0 %copy.29 = bf16[1,2,16,3072]{3,2,1,0:T(8,128)(2,1)S(1)} copy(bf16[1,2,16,3072]{3,1,2,0:T(2,128)(2,1)} %bitcast.55) | data formatting | bytes 393216
  7.0 0.6 collective-permute-start.7
  7.6 3.0 %collective-permute-start.6 = (bf16[2,16,3072]{2,1,0:T(8,128)(2,1)S(1)}, bf16[2,16,3072]{2,1,0:T(8,128)(2,1)S(1)}, u32[]{:S(2)}, u32[]{:S(2)}) collective-permute-start(bf16[2,16,3072]{2,1,0:T(8,128)(2,1)S(1)} %bitcast.42), channel_id=1, source_target_pairs={{1,2},{3,4},{5,6},{7,8},{9,10},{11,12},{13,14},{2,1},{4,3},{6,5},{... | collective-permute-start | bytes 589832 | tf_op jit(solution)/shard_map/ppermute | solution.py:622
  10.7 0.5 shard_map.137
  11.2 1.5 %shard_map.138 = (bf16[4,34,16,128]{3,2,1,0:T(8,128)(2,1)S(1)}, bf16[4,32,16,128]{3,2,1,0:T(8,128)(2,1)S(1)}, bf16[2,34,16,128]{3,2,1,0:T(8,128)(2,1)S(1)}) custom-call(bf16[4,16,3072]{2,1,0:T(8,128)(2,1)S(1)} %get-tuple-element.34.own, bf16[128,1024]{1,0:T(8,128)(2,1)S(1)} %get-tuple-element.35.w_stem, bf16[1152,256]{1,0:T(8,128)(2,1)S(1)} %get-tuple-element.36.w_gru), custom_call_target="tpu_custom_call" | custom-call | tf_op jit(solution)/shard_map/pallas_call | solution.py:590
  12.6 3.0 %collective-permute-done.outer = bf16[3,16,3072]{2,1,0:T(8,128)(2,1)S(1)} collective-permute-done((bf16[3,16,3072]{2,1,0:T(8,128)(2,1)S(1)}, bf16[3,16,3072]{2,1,0:T(8,128)(2,1)S(1)}, u32[]{:S(2)}, u32[]{:S(2)}) %collective-permute-start) | collective-permute-done | bytes 294944 | tf_op jit(solution)/shard_map/ppermute | solution.py:622
  15.6 5.8 %shard_map.139 = (bf16[4,16,16,128]{3,2,1,0:T(8,128)(2,1)S(1)}, bf16[96,16,128]{2,1,0:T(8,128)(2,1)S(1)}, bf16[48,16,128]{2,1,0:T(8,128)(2,1)S(1)}, bf16[48,16,1...) custom-call(bf16[4,34,16,128]{3,2,1,0:T(8,128)(2,1)S(1)} %get-tuple-, ...), custom_call_target="tpu_custom_call" | custom-call | tf_op jit(solution)/shard_map/pallas_call | solution.py:590
  21.4 2.1 %collective-permute-start.4 = (bf16[48,16,128]{2,1,0:T(8,128)(2,1)S(1)}, bf16[48,16,128]{2,1,0:T(8,128)(2,1)S(1)}, u32[]{:S(2)}, u32[]{:S(2)}) collective-permute-start(bf16[48,16,128]{2,1,0:T(8,128)(2,1)S(1)} %get-tuple-element.46), channel_id=1, source_target_pairs={{1,2},{3,4},{5,6},{7,8},{9,10},{11,12},{13,14},{2,1},{4,3},{6,5},{... | collective-permute-start | bytes 589832 | tf_op jit(solution)/shard_map/ppermute | solution.py:622
  23.5 0.1 collective-permute-start.5
  23.6 3.8 %collective-permute-start.2 = (bf16[24,16,128]{2,1,0:T(8,128)(2,1)S(1)}, bf16[24,16,128]{2,1,0:T(8,128)(2,1)S(1)}, u32[]{:S(2)}, u32[]{:S(2)}) collective-permute-start(bf16[24,16,128]{2,1,0:T(8,128)(2,1)S(1)} %get-tuple-element.44), channel_id=1, source_target_pairs={{1,2},{3,4},{5,6},{7,8},{9,10},{11,12},{13,14},{2,1},{4,3},{6,5},{... | collective-permute-start | bytes 294920 | tf_op jit(solution)/shard_map/ppermute | solution.py:622
  27.4 0.4 collective-permute-start.3
  27.9 3.2 %shard_map.140 = (f32[4,256,640]{2,1,0:T(8,128)S(1)}, bf16[4,18,16,512]{3,2,1,0:T(8,128)(2,1)S(1)}) custom-call(bf16[2,16,3072]{2,1,0:T(8,128)(2,1)S(1)} %bitcast.43, bf16[2,16,3072]{2,1,0:T(8,128)(2,1)S(1)} %collective-permute-done.6.outer, bf16[2,16,3072]{2,1,0:T(8,128)(2,1)S(1)} %collective-permute-done.7.inner, bf16[1728,576]{1,0:T(8,128)(2,1)S(1)} %bitcast.36), custom_call_target="tpu_custom_call" | custom-call | tf_op jit(solution)/shard_map/pallas_call | solution.py:590
  31.1 3.4 %shard_map.141.h1 = bf16[4,18,16,512]{3,2,1,0:T(8,128)(2,1)S(1)} custom-call(bf16[96,16,128]{2,1,0:T(8,128)(2,1)S(1)} %get-tuple-element.43.low_own, bf16[48,16,128]{2,1,0:T(8,128)(2,1)S(1)} %collective-permute-done.4.low_outer, bf16[48,16,128]{2,1,0:T(8,128)(2,1)S(1)} %collective-permute-done.5.low_inner, f32[4,256,640]{2,1,0:T(8,128)S(1)} %get-tuple-element.48.acc_first, ...), custom_call_target="tpu_custom_call" | custom-call | tf_op jit(solution)/shard_map/pallas_call | solution.py:590
  34.5 3.3 %shard_map.142.own = bf16[48,16,128]{2,1,0:T(8,128)(2,1)S(1)} custom-call(bf16[96,16,128]{2,1,0:T(8,128)(2,1)S(1)} %get-tuple-element.43.low_own, bf16[24,16,128]{2,1,0:T(8,128)(2,1)S(1)} %collective-permute-done.2.second_outer, bf16[24,16,128]{2,1,0:T(8,128)(2,1)S(1)} %collective-permute-done.3.second_inner, bf16[4,18,16,512]{3,2,1,0:T(8,128)(2,1)S(1)} %shard_map.141.h1, ...), custom_call_target="tpu_custom_call" | custom-call | tf_op jit(solution)/shard_map/pallas_call | solution.py:590
  37.9 0.2 collective-permute-start.8
  38.1 2.9 %collective-permute-start.9 = (bf16[48,16,128]{2,1,0:T(8,128)(2,1)S(1)}, bf16[48,16,128]{2,1,0:T(8,128)(2,1)S(1)}, u32[]{:S(2)}, u32[]{:S(2)}) collective-permute-start(bf16[48,16,128]{2,1,0:T(8,128)(2,1)S(1)} %shard_map.142.own), channel_id=1, source_target_pairs={{1,2},{3,4},{5,6},{7,8},{9,10},{11,12},{13,14},{2,1},{4,3},{6,5},{... | collective-permute-start | bytes 589832 | tf_op jit(solution)/shard_map/ppermute | solution.py:622
  41.0 2.6 %collective-permute-start.12 = (bf16[56,16,128]{2,1,0:T(8,128)(2,1)S(1)}, bf16[56,16,128]{2,1,0:T(8,128)(2,1)S(1)}, u32[]{:S(2)}, u32[]{:S(2)}) collective-permute-start(bf16[56,16,128]{2,1,0:T(8,128)(2,1)S(1)} %pad_maximum_fusion), channel_id=1, source_target_pairs={{1,2},{3,4},{5,6},{7,8},{9,10},{11,12},{13,14},{2,1},{4,3},{6,5},{... | collective-permute-start | bytes 688136 | tf_op jit(solution)/shard_map/ppermute | solution.py:622
  43.7 1.3 %collective-permute-start.13 = (bf16[2,16,16,128]{3,2,1,0:T(8,128)(2,1)S(1)}, bf16[2,16,16,128]{3,2,1,0:T(8,128)(2,1)S(1)}, u32[]{:S(2)}, u32[]{:S(2)}) collective-permute-start(bf16[2,16,16,128]{3,2,1,0:T(8,128)(2,1)S(1)} %get-tuple-element.58), channel_id=1, source_target_pairs={{0,1},{1,0},{2,3},{3,2},{4,5},{5,4},{6,7},{7,6},{8,9},{9,8},{10,11... | collective-permute-start | bytes 393224 | tf_op jit(solution)/shard_map/ppermute | solution.py:625
  45.0 1.1 %shard_map.143 = (bf16[6,18,16,512]{3,2,1,0:T(8,128)(2,1)S(1)}, bf16[24,16,128]{2,1,0:T(8,128)(2,1)S(1)}) custom-call(bf16[48,16,128]{2,1,0:T(8,128)(2,1)S(1)} %shard_map.142.own, bf16[24,16,128]{2,1,0:T(8,128)(2,1)S(1)} %collective-permute-done.8.in_near, bf16[1728,576]{1,0:T(8,128)(2,1)S(1)} %bitcast.31), custom_call_target="tpu_custom_call" | custom-call | tf_op jit(solution)/shard_map/pallas_call | solution.py:590
  46.1 0.1 collective-permute-start.10
  46.2 3.4 %collective-permute-done.9.outer = bf16[48,16,128]{2,1,0:T(8,128)(2,1)S(1)} collective-permute-done((bf16[48,16,128]{2,1,0:T(8,128)(2,1)S(1)}, bf16[48,16,128]{2,1,0:T(8,128)(2,1)S(1)}, u32[]{:S(2)}, u32[]{:S(2)}) %collective-permute-start.9) | collective-permute-done | bytes 196640 | tf_op jit(solution)/shard_map/ppermute | solution.py:622
  49.6 1.1 %shard_map.144 = (bf16[6,18,16,512]{3,2,1,0:T(8,128)(2,1)S(1)}, bf16[24,16,128]{2,1,0:T(8,128)(2,1)S(1)}) custom-call(bf16[6,18,16,512]{3,2,1,0:T(8,128)(2,1)S(1)} %get-tuple-element.50.s1_given, bf16[48,16,128]{2,1,0:T(8,128)(2,1)S(1)} %shard_map.142.own, bf16[48,16,128]{2,1,0:T(8,128)(2,1)S(1)} %collective-permute-done.9.outer, ...), custom_call_target="tpu_custom_call", output_to_operand_aliasing={{0}: (0, {})} | custom-call | tf_op jit(solution)/shard_map/pallas_call | solution.py:590
  50.8 1.0 %shard_map.147 = (bf16[768,256]{1,0:T(8,128)(2,1)S(1)}, bf16[1152,256]{1,0:T(8,128)(2,1)S(1)}, bf16[1024,128]{1,0:T(8,128)(2,1)S(1)}) custom-call(bf16[9,64,192]{2,1,0:T(8,128)(2,1)S(1)} %bitcast.47, bf16[9,64,192]{2,1,0:T(8,128)(2,1)S(1)} %bitcast.48, bf16[9,64,192]{2,1,0:T(8,128)(2,1)S(1)} %bitcast.49, bf16[16,64]{1,0:T(8,128)(2,1)S(1)} %bitcast.51), custom_call_target="tpu_custom_call" | custom-call | tf_op jit(solution)/shard_map/pallas_call | solution.py:590
  51.8 1.1 %shard_map.145.s1_given = bf16[6,18,16,512]{3,2,1,0:T(8,128)(2,1)S(1)} custom-call(bf16[6,18,16,512]{3,2,1,0:T(8,128)(2,1)S(1)} %get-tuple-element.51.s1_given, bf16[48,16,128]{2,1,0:T(8,128)(2,1)S(1)} %shard_map.142.own, bf16[48,16,128]{2,1,0:T(8,128)(2,1)S(1)} %collective-permute-done.9.outer, ...), custom_call_target="tpu_custom_call", output_to_operand_aliasing={{}: (0, {})} | custom-call | tf_op jit(solution)/shard_map/pallas_call | solution.py:590
  52.9 2.7 %shard_map.146 = (bf16[6,18,16,512]{3,2,1,0:T(8,128)(2,1)S(1)}, bf16[5,18,16,512]{3,2,1,0:T(8,128)(2,1)S(1)}) custom-call(bf16[6,18,16,512]{3,2,1,0:T(8,128)(2,1)S(1)} %shard_map.145.s1_given, bf16[24,16,128]{2,1,0:T(8,128)(2,1)S(1)} %collective-permute-done.10.in_near, ...), custom_call_target="tpu_custom_call", output_to_operand_aliasing={{0}: (0, {})} | custom-call | tf_op jit(solution)/shard_map/pallas_call | solution.py:590
  55.7 7.3 %shard_map.148 = (bf16[2,4,16,512]{3,2,1,0:T(8,128)(2,1)S(1)}, bf16[6,18,16,512]{3,2,1,0:T(8,128)(2,1)S(1)}, bf16[5,18,16,512]{3,2,1,0:T(8,128)(2,1)S(1)}) custom-call(bf16[6,18,16,512]{3,2,1,0:T(8,128)(2,1)S(1)} %get-tuple-element.54.s1_given, ...), custom_call_target="tpu_custom_call", output_to_operand_aliasing={{1}: (0, {}), {2}: (1, {})} | custom-call | tf_op jit(solution)/shard_map/pallas_call | solution.py:590
  63.0 0.7 %reshape.57 = bf16[2,4,8192]{2,1,0:T(4,128)(2,1)} reshape(bf16[2,4,16,512]{3,2,1,0:T(8,128)(2,1)S(1)} %get-tuple-element.62) | data formatting | bytes 262144 | tf_op jit(solution)/shard_map/reshape | solution.py:725
  (38 shorter events, 0.2 us)
Async XLA Ops:
  0.0 10.6 %copy-start.5 = (bf16[3,3,64,192]{3,2,1,0:T(8,128)(2,1)S(1)}, bf16[3,3,64,192]{3,2,1,0:T(8,128)(2,1)}, u32[]{:S(2)}) copy-start(bf16[3,3,64,192]{3,2,1,0:T(8,128)(2,1)} %param.20) | copy-start | bytes 663556
  0.0 10.6 %copy-start.4 = (bf16[3,3,64,192]{3,2,1,0:T(8,128)(2,1)S(1)}, bf16[3,3,64,192]{3,2,1,0:T(8,128)(2,1)}, u32[]{:S(2)}) copy-start(bf16[3,3,64,192]{3,2,1,0:T(8,128)(2,1)} %param.19) | copy-start | bytes 663556
  0.0 10.6 %copy-start.3 = (bf16[3,3,64,192]{3,2,1,0:T(8,128)(2,1)S(1)}, bf16[3,3,64,192]{3,2,1,0:T(8,128)(2,1)}, u32[]{:S(2)}) copy-start(bf16[3,3,64,192]{3,2,1,0:T(8,128)(2,1)} %param.18) | copy-start | bytes 663556
  0.0 10.6 %copy-start.9 = (bf16[16,64]{1,0:T(8,128)(2,1)S(1)}, bf16[16,64]{1,0:T(8,128)(2,1)}, u32[]{:S(2)}) copy-start(bf16[16,64]{1,0:T(8,128)(2,1)} %refs_0_.1) | copy-start | bytes 6148
  2.2 13.4 %collective-permute-start = (bf16[3,16,3072]{2,1,0:T(8,128)(2,1)S(1)}, bf16[3,16,3072]{2,1,0:T(8,128)(2,1)S(1)}, u32[]{:S(2)}, u32[]{:S(2)}) collective-permute-start(bf16[3,16,3072]{2,1,0:T(8,128)(2,1)S(1)} %get-tuple-element.40), channel_id=1, source_target_pairs={{1,2},{3,4},{5,6},{7,8},{9,10},{11,12},{13,14},{2,1},{4,3},{6,5},{... | collective-permute-start | bytes 884744 | tf_op jit(solution)/shard_map/ppermute | solution.py:622
  6.0 9.7 %collective-permute-start.1 = (bf16[3,16,3072]{2,1,0:T(8,128)(2,1)S(1)}, bf16[3,16,3072]{2,1,0:T(8,128)(2,1)S(1)}, u32[]{:S(2)}, u32[]{:S(2)}) collective-permute-start(bf16[3,16,3072]{2,1,0:T(8,128)(2,1)S(1)} %get-tuple-element.41), channel_id=1, source_target_pairs={{0,1},{1,0},{2,3},{3,2},{4,5},{5,4},{6,7},{7,6},{8,9},{9,8},{10,11... | collective-permute-start | bytes 884744 | tf_op jit(solution)/shard_map/ppermute | solution.py:625
  7.0 20.4 %collective-permute-start.7 = (bf16[2,16,3072]{2,1,0:T(8,128)(2,1)S(1)}, bf16[2,16,3072]{2,1,0:T(8,128)(2,1)S(1)}, u32[]{:S(2)}, u32[]{:S(2)}) collective-permute-start(bf16[2,16,3072]{2,1,0:T(8,128)(2,1)S(1)} %bitcast.41), channel_id=1, source_target_pairs={{0,1},{1,0},{2,3},{3,2},{4,5},{5,4},{6,7},{7,6},{8,9},{9,8},{10,11... | collective-permute-start | bytes 589832 | tf_op jit(solution)/shard_map/ppermute | solution.py:625
  7.6 20.3 %collective-permute-start.6 = (bf16[2,16,3072]{2,1,0:T(8,128)(2,1)S(1)}, bf16[2,16,3072]{2,1,0:T(8,128)(2,1)S(1)}, u32[]{:S(2)}, u32[]{:S(2)}) collective-permute-start(bf16[2,16,3072]{2,1,0:T(8,128)(2,1)S(1)} %bitcast.42), channel_id=1, source_target_pairs={{1,2},{3,4},{5,6},{7,8},{9,10},{11,12},{13,14},{2,1},{4,3},{6,5},{... | collective-permute-start | bytes 589832 | tf_op jit(solution)/shard_map/ppermute | solution.py:622
  12.6 15.2 %copy-start.1 = (bf16[3,3,192,576]{3,2,1,0:T(8,128)(2,1)S(1)}, bf16[3,3,192,576]{3,2,1,0:T(8,128)(2,1)}, u32[]{:S(2)}) copy-start(bf16[3,3,192,576]{3,2,1,0:T(8,128)(2,1)} %param.22) | copy-start | bytes 5971972
  21.4 9.7 %copy-start.2 = (bf16[3,3,192,576]{3,2,1,0:T(8,128)(2,1)S(1)}, bf16[3,3,192,576]{3,2,1,0:T(8,128)(2,1)}, u32[]{:S(2)}) copy-start(bf16[3,3,192,576]{3,2,1,0:T(8,128)(2,1)} %param.21) | copy-start | bytes 5971972
  21.4 9.7 %collective-permute-start.4 = (bf16[48,16,128]{2,1,0:T(8,128)(2,1)S(1)}, bf16[48,16,128]{2,1,0:T(8,128)(2,1)S(1)}, u32[]{:S(2)}, u32[]{:S(2)}) collective-permute-start(bf16[48,16,128]{2,1,0:T(8,128)(2,1)S(1)} %get-tuple-element.46), channel_id=1, source_target_pairs={{1,2},{3,4},{5,6},{7,8},{9,10},{11,12},{13,14},{2,1},{4,3},{6,5},{... | collective-permute-start | bytes 589832 | tf_op jit(solution)/shard_map/ppermute | solution.py:622
  23.5 7.6 %collective-permute-start.5 = (bf16[48,16,128]{2,1,0:T(8,128)(2,1)S(1)}, bf16[48,16,128]{2,1,0:T(8,128)(2,1)S(1)}, u32[]{:S(2)}, u32[]{:S(2)}) collective-permute-start(bf16[48,16,128]{2,1,0:T(8,128)(2,1)S(1)} %get-tuple-element.47), channel_id=1, source_target_pairs={{0,1},{1,0},{2,3},{3,2},{4,5},{5,4},{6,7},{7,6},{8,9},{9,8},{10,11... | collective-permute-start | bytes 589832 | tf_op jit(solution)/shard_map/ppermute | solution.py:625
  23.6 10.9 %collective-permute-start.2 = (bf16[24,16,128]{2,1,0:T(8,128)(2,1)S(1)}, bf16[24,16,128]{2,1,0:T(8,128)(2,1)S(1)}, u32[]{:S(2)}, u32[]{:S(2)}) collective-permute-start(bf16[24,16,128]{2,1,0:T(8,128)(2,1)S(1)} %get-tuple-element.44), channel_id=1, source_target_pairs={{1,2},{3,4},{5,6},{7,8},{9,10},{11,12},{13,14},{2,1},{4,3},{6,5},{... | collective-permute-start | bytes 294920 | tf_op jit(solution)/shard_map/ppermute | solution.py:622
  27.4 7.1 %collective-permute-start.3 = (bf16[24,16,128]{2,1,0:T(8,128)(2,1)S(1)}, bf16[24,16,128]{2,1,0:T(8,128)(2,1)S(1)}, u32[]{:S(2)}, u32[]{:S(2)}) collective-permute-start(bf16[24,16,128]{2,1,0:T(8,128)(2,1)S(1)} %get-tuple-element.45), channel_id=1, source_target_pairs={{0,1},{1,0},{2,3},{3,2},{4,5},{5,4},{6,7},{7,6},{8,9},{9,8},{10,11... | collective-permute-start | bytes 294920 | tf_op jit(solution)/shard_map/ppermute | solution.py:625
  34.5 10.5 %copy-start = (bf16[3,3,192,576]{3,2,1,0:T(8,128)(2,1)S(1)}, bf16[3,3,192,576]{3,2,1,0:T(8,128)(2,1)}, u32[]{:S(2)}) copy-start(bf16[3,3,192,576]{3,2,1,0:T(8,128)(2,1)} %param.23) | copy-start | bytes 5971972
  37.9 3.2 %collective-permute-start.8 = (bf16[24,16,128]{2,1,0:T(8,128)(2,1)S(1)}, bf16[24,16,128]{2,1,0:T(8,128)(2,1)S(1)}, u32[]{:S(2)}, u32[]{:S(2)}) collective-permute-start(bf16[24,16,128]{2,1,0:T(8,128)(2,1)S(1)} %slice.14), channel_id=1, source_target_pairs={{0,1},{1,0},{2,3},{3,2},{4,5},{5,4},{6,7},{7,6},{8,9},{9,8},{10,11... | collective-permute-start | bytes 294920 | tf_op jit(solution)/shard_map/ppermute | solution.py:625
  38.1 11.5 %collective-permute-start.9 = (bf16[48,16,128]{2,1,0:T(8,128)(2,1)S(1)}, bf16[48,16,128]{2,1,0:T(8,128)(2,1)S(1)}, u32[]{:S(2)}, u32[]{:S(2)}) collective-permute-start(bf16[48,16,128]{2,1,0:T(8,128)(2,1)S(1)} %shard_map.142.own), channel_id=1, source_target_pairs={{1,2},{3,4},{5,6},{7,8},{9,10},{11,12},{13,14},{2,1},{4,3},{6,5},{... | collective-permute-start | bytes 589832 | tf_op jit(solution)/shard_map/ppermute | solution.py:622
  41.0 14.6 %collective-permute-start.12 = (bf16[56,16,128]{2,1,0:T(8,128)(2,1)S(1)}, bf16[56,16,128]{2,1,0:T(8,128)(2,1)S(1)}, u32[]{:S(2)}, u32[]{:S(2)}) collective-permute-start(bf16[56,16,128]{2,1,0:T(8,128)(2,1)S(1)} %pad_maximum_fusion), channel_id=1, source_target_pairs={{1,2},{3,4},{5,6},{7,8},{9,10},{11,12},{13,14},{2,1},{4,3},{6,5},{... | collective-permute-start | bytes 688136 | tf_op jit(solution)/shard_map/ppermute | solution.py:622
  43.7 12.0 %collective-permute-start.13 = (bf16[2,16,16,128]{3,2,1,0:T(8,128)(2,1)S(1)}, bf16[2,16,16,128]{3,2,1,0:T(8,128)(2,1)S(1)}, u32[]{:S(2)}, u32[]{:S(2)}) collective-permute-start(bf16[2,16,16,128]{3,2,1,0:T(8,128)(2,1)S(1)} %get-tuple-element.58), channel_id=1, source_target_pairs={{0,1},{1,0},{2,3},{3,2},{4,5},{5,4},{6,7},{7,6},{8,9},{9,8},{10,11... | collective-permute-start | bytes 393224 | tf_op jit(solution)/shard_map/ppermute | solution.py:625
  46.1 6.8 %collective-permute-start.10 = (bf16[24,16,128]{2,1,0:T(8,128)(2,1)S(1)}, bf16[24,16,128]{2,1,0:T(8,128)(2,1)S(1)}, u32[]{:S(2)}, u32[]{:S(2)}) collective-permute-start(bf16[24,16,128]{2,1,0:T(8,128)(2,1)S(1)} %get-tuple-element.52), channel_id=1, source_target_pairs={{0,1},{1,0},{2,3},{3,2},{4,5},{5,4},{6,7},{7,6},{8,9},{9,8},{10,11... | collective-permute-start | bytes 294920 | tf_op jit(solution)/shard_map/ppermute | solution.py:625
  49.6 1.2 %copy-start.6 = (bf16[3,3,192,64]{2,3,1,0:T(8,128)(2,1)S(1)}, bf16[3,3,192,64]{2,3,1,0:T(8,128)(2,1)}, u32[]{:S(2)}) copy-start(bf16[3,3,192,64]{2,3,1,0:T(8,128)(2,1)} %param.24) | copy-start | bytes 663556
  49.6 1.2 %copy-start.7 = (bf16[3,3,64,192]{3,2,1,0:T(8,128)(2,1)S(1)}, bf16[3,3,64,192]{3,2,1,0:T(8,128)(2,1)}, u32[]{:S(2)}) copy-start(bf16[3,3,64,192]{3,2,1,0:T(8,128)(2,1)} %param.25) | copy-start | bytes 663556
  49.6 1.2 %copy-start.8 = (bf16[3,3,64,192]{3,2,1,0:T(8,128)(2,1)S(1)}, bf16[3,3,64,192]{3,2,1,0:T(8,128)(2,1)}, u32[]{:S(2)}) copy-start(bf16[3,3,64,192]{3,2,1,0:T(8,128)(2,1)} %param.26) | copy-start | bytes 663556
  49.6 1.2 %copy-start.10 = (bf16[64,16]{0,1:T(8,128)(2,1)S(1)}, bf16[64,16]{0,1:T(8,128)(2,1)}, u32[]{:S(2)}) copy-start(bf16[64,16]{0,1:T(8,128)(2,1)} %param.27) | copy-start | bytes 6148
  50.7 2.2 %collective-permute-start.11 = (bf16[24,16,128]{2,1,0:T(8,128)(2,1)S(1)}, bf16[24,16,128]{2,1,0:T(8,128)(2,1)S(1)}, u32[]{:S(2)}, u32[]{:S(2)}) collective-permute-start(bf16[24,16,128]{2,1,0:T(8,128)(2,1)S(1)} %get-tuple-element.53), channel_id=1, source_target_pairs={{0,1},{1,0},{2,3},{3,2},{4,5},{5,4},{6,7},{7,6},{8,9},{9,8},{10,11... | collective-permute-start | bytes 294920 | tf_op jit(solution)/shard_map/ppermute | solution.py:625

commit v8 on v7

--- a/solution.py
+++ b/solution.py
@@ -342,10 +342,11 @@
         a, b = (outer, inner) if idx < 2 else (inner, outer)
         put_packed(h0, idx, raw_tiles(lambda lanes: jnp.where(upper, a[r, :, lanes], b[r, :, lanes])))
 
-    for idx in range(0, 4):
-        acc_out[idx, :, : 3 * C2] = jnp.dot(coarse_patches(h0, idx + 1), w_h[...], preferred_element_type=F32)
-        acc_out[idx, :, 4 * LANES + C1 :] = jnp.zeros((CB * SUB, C1), F32)
-        h_out[idx] = h0[idx + 1]
+    base = jnp.where(upper, 1, 2)
+    for k in range(3):
+        acc_out[k, :, : 3 * C2] = jnp.dot(coarse_patches(h0, base + k), w_h[...], preferred_element_type=F32)
+        acc_out[k, :, 4 * LANES + C1 :] = jnp.zeros((CB * SUB, C1), F32)
+        h_out[k] = h0[base + k]
 
 
 def put_row(ref, slot, forms):
@@ -354,24 +355,37 @@
         ref[base : base + PAIRS] = tile
 
 
-def coarse_encoder_body(low_own, low_outer, low_inner, acc_first, h_first, w_x, h1, x1, acc_x):
+def first_inner_body(low_own, low_inner, acc_first, h_first, w_x, h1, sent, x1, acc_x):
+    upper, _, _ = place(2)
+    zero_tail(acc_x)
+    put_packed(x1, 0, either(upper, low_own, 0, low_inner, 1))
+    put_packed(x1, 1, either(upper, low_own, 1, low_own, 0))
+    put_packed(x1, 2, either(upper, low_inner, 0, low_own, 1))
+    k = jnp.where(upper, 2, 0)
+    forms = coarse_gru(x1, 1, h_first, k, w_x, None, acc_x, acc_first.at[k], True)
+    put_forms(h1, jnp.where(upper, 2, 1), forms)
+    put_row(sent, 0, forms)
+
+
+def first_outer_body(h1_given, low_own, low_outer, acc_first, h_first, w_x, h1, x1, acc_x):
     upper, first, rows = place(2)
     zero_tail(acc_x)
-    for idx in range(6):
-        if 2 <= idx < 4:
-            put_packed(x1, idx, packed_tiles(low_own, idx - 2))
-            continue
-        r = idx if idx < 2 else idx - 4
-        a, b = (low_outer, low_inner) if idx < 2 else (low_inner, low_outer)
-        put_packed(x1, idx, either(upper, a, r, b, r))
-    for idx in range(4):
+    put_packed(x1, 0, either(upper, low_outer, 0, low_own, 0))
+    put_packed(x1, 1, either(upper, low_outer, 1, low_own, 1))
+    put_packed(x1, 2, either(upper, low_own, 0, low_outer, 0))
+    put_packed(x1, 3, either(upper, low_own, 1, low_outer, 1))
+    for c in (1, 2):
+        k = jnp.where(upper, c - 1, c)
+        row = jnp.where(upper, c - 2, c)
         forms = coarse_gru(
-            x1, idx + 1, h_first, idx, w_x, None, acc_x, acc_first.at[idx], in_grid(first + idx - 1, rows)
+            x1, c, h_first, k, w_x, None, acc_x, acc_first.at[k], in_grid(first + row, rows)
         )
-        put_forms(h1, idx, forms)
-
-
-def coarse_second_body(low_own, second_outer, second_inner, h1, w_x, w_h, state, x2, acc_x, acc_h):
+        put_forms(h1, row + 1, forms)
+
+
+def coarse_second_body(
+    low_own, second_outer, second_inner, h1_given, h1_inner, w_x, w_h, state, h1, x2, acc_x, acc_h
+):
     upper, _, _ = place(2)
     zero_tail(acc_x)
     zero_tail(acc_h)
@@ -379,6 +393,7 @@
     put_packed(x2, 1, packed_tiles(low_own, 2))
     put_packed(x2, 2, packed_tiles(low_own, 3))
     put_packed(x2, 3, either(upper, second_inner, 0, second_outer, 0))
+    put_packed(h1, jnp.where(upper, 3, 0), packed_tiles(h1_inner, 0))
     for slot in range(2):
         idx = jnp.where(upper, slot, 1 - slot)
         put_row(state, slot, coarse_gru(x2, idx + 1, h1, idx + 1, w_x, w_h, acc_x, acc_h, True))
@@ -624,19 +639,19 @@
     def inner_swap(x):
         return lax.ppermute(x, "section", [(0, 1), (1, 0)])
 
+    coarse = start_coarse.reshape(2, SUB, CB * C2)
+
+    def on_chip(*values):
+        return [(value, pltpu.VMEM) for value in values]
+
+    def fine_buf(rows):
+        return pltpu.VMEM((rows, FB + 2, SUB, LANES), BF)
+
+    def coarse_buf(rows):
+        return pltpu.VMEM((rows, CB + 2, SUB, 4 * LANES), BF)
+
     fine = start_fine.reshape(4, SUB, FB * C1)
     patches = frames.reshape(FRAMES, 4, SUB, FB * PATCH)
-    coarse = start_coarse.reshape(2, SUB, CB * C2)
-
-    def on_chip(*values):
-        return [(value, pltpu.VMEM) for value in values]
-
-    def fine_buf(rows):
-        return pltpu.VMEM((rows, FB + 2, SUB, LANES), BF)
-
-    def coarse_buf(rows):
-        return pltpu.VMEM((rows, CB + 2, SUB, 4 * LANES), BF)
-
     rows = (3, SUB, FB * (C1 + FRAMES * PATCH))
     own, to_outer, to_inner = call(pack_body, on_chip(fine, patches[0], patches[1]), [(4,) + rows[1:], rows, rows], [])
     outer, inner = outer_swap(to_outer), inner_swap(to_inner)
@@ -686,21 +701,26 @@
     acc_first, h_first = call(
         coarse_state_body,
         on_chip(coarse, coarse_o, coarse_i, enc_coarse_h.reshape(flat)),
-        [jax.ShapeDtypeStruct((4, CB * SUB, 5 * LANES), F32), (4, CB + 2, SUB, 4 * LANES)],
+        [jax.ShapeDtypeStruct((3, CB * SUB, 5 * LANES), F32), (3, CB + 2, SUB, 4 * LANES)],
         [coarse_buf(6)],
     )
     state_fi = inner_swap(state_fi)
 
     w_x, w_h = enc_coarse_x.reshape(flat), enc_coarse_h.reshape(flat)
     four = (4, CB + 2, SUB, 4 * LANES)
+    h1, sent = call(
+        first_inner_body, on_chip(low_own, got_i, acc_first, h_first, w_x), [four, row], [coarse_buf(3), acc_buf]
+    )
+    h1_inner = inner_swap(sent)
     (h1,) = call(
-        coarse_encoder_body, on_chip(low_own, got_o, got_i, acc_first, h_first, w_x), [four], [coarse_buf(6), acc_buf]
-    )
-    (state_c,) = call(
+        first_outer_body, on_chip(h1, low_own, got_o, acc_first, h_first, w_x), [four], [coarse_buf(4), acc_buf], {0: 0}
+    )
+    state_c, _ = call(
         coarse_second_body,
-        on_chip(low_own, second_o, second_i, h1, w_x, w_h),
-        [(2 * ROW_TILES, SUB, LANES)],
+        on_chip(low_own, second_o, second_i, h1, h1_inner, w_x, w_h),
+        [(2 * ROW_TILES, SUB, LANES), four],
         [coarse_buf(4), acc_buf, acc_buf],
+        {3: 1},
     )
     in_near = inner_swap(state_c[ROW_TILES:])
     state_o = outer_swap(state_c)

time: 64 us -> 64.6 us (level)
  starting transfers between devices: 21 us -> 22 us
  Pallas kernels: 32 us -> 31.2 us
    ppermute x8 -> x9, starting transfers between devices: 2.83 us -> 3.82 us  [inner_swap(): return lax.ppermute(x, 'section', [(0, 1), (1, 0)])]
    pallas_call x13 -> x14, Pallas kernels: 32 us -> 31.2 us  [call(): pl.pallas_call(body, out_shape=[s if isinstance(s, jax.ShapeDtypeStruct)...]
  transfers between devices with their start and end apart: 14 -> 15, of which waited for: 2 -> 2; matrix products, arithmetic and copies ran while one was open for 2% -> 2% of each run, Pallas kernels for 33% -> 32%
where the time goes in v8:
time: 64.6 us; the launch traced here: 64.3 us
  Pallas kernels  31.2 us (48%)
  starting transfers between devices  22 us (34%)
  waiting for transfers between devices  6.76 us (10%)
  local copies, waits for them, and re-layouts  3.88 us (6%)
    pallas_call x14, Pallas kernels, call(): pl.pallas_call(body, out_shape=[s if isinstance(s, jax.ShapeDtypeStruct)...  31.2 us
    ppermute x6, starting transfers between devices, outer_swap(): return lax.ppermute(x, LINE, across)  18.2 us
    ppermute x6, waiting for transfers between devices, outer_swap(): return lax.ppermute(x, LINE, across)  6.73 us
    ppermute x9, starting transfers between devices, inner_swap(): return lax.ppermute(x, 'section', [(0, 1), (1, 0)])  3.82 us
    unnamed x24, local copies, waits for them, and re-layouts  2.12 us
  transfers between devices with their start and end apart: 15, of which 2 were waited for; matrix products, arithmetic and copies ran while one was open for 2% of the time, Pallas kernels for 32%

profile of v8, /device:TPU:19, one launch (start us, length us, event | category | flops | bytes accessed | tf_op | source)
XLA Modules:
  0.0 64.3 jit_solution(7406435735278406768)
XLA Ops:
  0.0 1.0 %fusion = (bf16[1,4,8192]{2,1,0:T(4,128)(2,1)S(1)}, bf16[1,4,8192]{2,1,0:T(4,128)(2,1)S(1)}) fusion(bf16[2,4,8192]{2,1,0:T(4,128)(2,1)} %param.14), kind=kLoop, calls=%fused_computation.5 | loop fusion | bytes 262144 | tf_op jit(solution)/shard_map/slice | solution.py:656
  1.0 1.1 %copy.30 = bf16[1,4,16,2048]{3,2,1,0:T(8,128)(2,1)S(1)} copy(bf16[1,4,16,2048]{3,1,2,0:T(4,128)(2,1)} %bitcast.53) | data formatting | bytes 524288
  2.2 0.1 shard_map.136
  2.2 3.7 %collective-permute-start = (bf16[3,16,3072]{2,1,0:T(8,128)(2,1)S(1)}, bf16[3,16,3072]{2,1,0:T(8,128)(2,1)S(1)}, u32[]{:S(2)}, u32[]{:S(2)}) collective-permute-start(bf16[3,16,3072]{2,1,0:T(8,128)(2,1)S(1)} %get-tuple-element.43), channel_id=1, source_target_pairs={{1,2},{3,4},{5,6},{7,8},{9,10},{11,12},{13,14},{2,1},{4,3},{6,5},{... | collective-permute-start | bytes 884744 | tf_op jit(solution)/shard_map/ppermute | solution.py:637
  6.0 1.0 %copy.31 = bf16[1,2,16,3072]{3,2,1,0:T(8,128)(2,1)S(1)} copy(bf16[1,2,16,3072]{3,1,2,0:T(2,128)(2,1)} %bitcast.56) | data formatting | bytes 393216
  7.0 0.6 collective-permute-start.6
  7.6 3.0 %collective-permute-start.5 = (bf16[2,16,3072]{2,1,0:T(8,128)(2,1)S(1)}, bf16[2,16,3072]{2,1,0:T(8,128)(2,1)S(1)}, u32[]{:S(2)}, u32[]{:S(2)}) collective-permute-start(bf16[2,16,3072]{2,1,0:T(8,128)(2,1)S(1)} %bitcast.43), channel_id=1, source_target_pairs={{1,2},{3,4},{5,6},{7,8},{9,10},{11,12},{13,14},{2,1},{4,3},{6,5},{... | collective-permute-start | bytes 589832 | tf_op jit(solution)/shard_map/ppermute | solution.py:637
  10.7 0.5 shard_map.137
  11.2 1.5 %shard_map.138 = (bf16[4,34,16,128]{3,2,1,0:T(8,128)(2,1)S(1)}, bf16[4,32,16,128]{3,2,1,0:T(8,128)(2,1)S(1)}, bf16[2,34,16,128]{3,2,1,0:T(8,128)(2,1)S(1)}) custom-call(bf16[4,16,3072]{2,1,0:T(8,128)(2,1)S(1)} %get-tuple-element.37.own, bf16[128,1024]{1,0:T(8,128)(2,1)S(1)} %get-tuple-element.38.w_stem, bf16[1152,256]{1,0:T(8,128)(2,1)S(1)} %get-tuple-element.39.w_gru), custom_call_target="tpu_custom_call" | custom-call | tf_op jit(solution)/shard_map/pallas_call | solution.py:605
  12.6 3.0 %collective-permute-done.outer = bf16[3,16,3072]{2,1,0:T(8,128)(2,1)S(1)} collective-permute-done((bf16[3,16,3072]{2,1,0:T(8,128)(2,1)S(1)}, bf16[3,16,3072]{2,1,0:T(8,128)(2,1)S(1)}, u32[]{:S(2)}, u32[]{:S(2)}) %collective-permute-start) | collective-permute-done | bytes 294944 | tf_op jit(solution)/shard_map/ppermute | solution.py:637
  15.6 5.8 %shard_map.139 = (bf16[4,16,16,128]{3,2,1,0:T(8,128)(2,1)S(1)}, bf16[96,16,128]{2,1,0:T(8,128)(2,1)S(1)}, bf16[48,16,128]{2,1,0:T(8,128)(2,1)S(1)}, bf16[48,16,1...) custom-call(bf16[4,34,16,128]{3,2,1,0:T(8,128)(2,1)S(1)} %get-tuple-, ...), custom_call_target="tpu_custom_call" | custom-call | tf_op jit(solution)/shard_map/pallas_call | solution.py:605
  21.5 2.1 %collective-permute-start.7 = (bf16[48,16,128]{2,1,0:T(8,128)(2,1)S(1)}, bf16[48,16,128]{2,1,0:T(8,128)(2,1)S(1)}, u32[]{:S(2)}, u32[]{:S(2)}) collective-permute-start(bf16[48,16,128]{2,1,0:T(8,128)(2,1)S(1)} %get-tuple-element.53), channel_id=1, source_target_pairs={{1,2},{3,4},{5,6},{7,8},{9,10},{11,12},{13,14},{2,1},{4,3},{6,5},{... | collective-permute-start | bytes 589832 | tf_op jit(solution)/shard_map/ppermute | solution.py:637
  23.6 2.9 %shard_map.140 = (f32[3,256,640]{2,1,0:T(8,128)S(1)}, bf16[3,18,16,512]{3,2,1,0:T(8,128)(2,1)S(1)}) custom-call(bf16[2,16,3072]{2,1,0:T(8,128)(2,1)S(1)} %bitcast.44, bf16[2,16,3072]{2,1,0:T(8,128)(2,1)S(1)} %collective-permute-done.5.outer, bf16[2,16,3072]{2,1,0:T(8,128)(2,1)S(1)} %collective-permute-done.6.inner, bf16[1728,576]{1,0:T(8,128)(2,1)S(1)} %bitcast.39), custom_call_target="tpu_custom_call" | custom-call | tf_op jit(solution)/shard_map/pallas_call | solution.py:605
  26.5 3.8 %collective-permute-start.2 = (bf16[24,16,128]{2,1,0:T(8,128)(2,1)S(1)}, bf16[24,16,128]{2,1,0:T(8,128)(2,1)S(1)}, u32[]{:S(2)}, u32[]{:S(2)}) collective-permute-start(bf16[24,16,128]{2,1,0:T(8,128)(2,1)S(1)} %get-tuple-element.47), channel_id=1, source_target_pairs={{1,2},{3,4},{5,6},{7,8},{9,10},{11,12},{13,14},{2,1},{4,3},{6,5},{... | collective-permute-start | bytes 294920 | tf_op jit(solution)/shard_map/ppermute | solution.py:637
  30.3 1.3 %collective-permute-start.3 = (bf16[24,16,128]{2,1,0:T(8,128)(2,1)S(1)}, bf16[24,16,128]{2,1,0:T(8,128)(2,1)S(1)}, u32[]{:S(2)}, u32[]{:S(2)}) collective-permute-start(bf16[24,16,128]{2,1,0:T(8,128)(2,1)S(1)} %get-tuple-element.48), channel_id=1, source_target_pairs={{0,1},{1,0},{2,3},{3,2},{4,5},{5,4},{6,7},{7,6},{8,9},{9,8},{10,11... | collective-permute-start | bytes 294920 | tf_op jit(solution)/shard_map/ppermute | solution.py:640
  31.6 1.1 %shard_map.141 = (bf16[4,18,16,512]{3,2,1,0:T(8,128)(2,1)S(1)}, bf16[24,16,128]{2,1,0:T(8,128)(2,1)S(1)}) custom-call(bf16[96,16,128]{2,1,0:T(8,128)(2,1)S(1)} %get-tuple-element.46.low_own, bf16[48,16,128]{2,1,0:T(8,128)(2,1)S(1)} %collective-permute-done.4.low_inner, f32[3,256,640]{2,1,0:T(8,128)S(1)} %get-tuple-element.50.acc_first, ...), custom_call_target="tpu_custom_call" | custom-call | tf_op jit(solution)/shard_map/pallas_call | solution.py:605
  32.7 0.1 collective-permute-start.8
  32.8 1.8 %shard_map.142.h1_given = bf16[4,18,16,512]{3,2,1,0:T(8,128)(2,1)S(1)} custom-call(bf16[4,18,16,512]{3,2,1,0:T(8,128)(2,1)S(1)} %get-tuple-element.52.h1_given, bf16[96,16,128]{2,1,0:T(8,128)(2,1)S(1)} %get-tuple-element.46.low_own, bf16[48,16,128]{2,1,0:T(8,128)(2,1)S(1)} %collective-permute-done.7.low_outer, ...), custom_call_target="tpu_custom_call", output_to_operand_aliasing={{}: (0, {})} | custom-call | tf_op jit(solution)/shard_map/pallas_call | solution.py:605
  34.7 3.4 %shard_map.143 = (bf16[48,16,128]{2,1,0:T(8,128)(2,1)S(1)}, bf16[4,18,16,512]{3,2,1,0:T(8,128)(2,1)S(1)}) custom-call(bf16[96,16,128]{2,1,0:T(8,128)(2,1)S(1)} %get-tuple-element.46.low_own, bf16[24,16,128]{2,1,0:T(8,128)(2,1)S(1)} %collective-permute-done.2.second_outer, ...), custom_call_target="tpu_custom_call", output_to_operand_aliasing={{1}: (3, {})} | custom-call | tf_op jit(solution)/shard_map/pallas_call | solution.py:605
  38.1 0.5 collective-permute-start.9
  38.7 3.1 %collective-permute-start.10 = (bf16[48,16,128]{2,1,0:T(8,128)(2,1)S(1)}, bf16[48,16,128]{2,1,0:T(8,128)(2,1)S(1)}, u32[]{:S(2)}, u32[]{:S(2)}) collective-permute-start(bf16[48,16,128]{2,1,0:T(8,128)(2,1)S(1)} %get-tuple-element.55.own), channel_id=1, source_target_pairs={{1,2},{3,4},{5,6},{7,8},{9,10},{11,12},{13,14},{2,1},{4,3},{6,5},{... | collective-permute-start | bytes 589832 | tf_op jit(solution)/shard_map/ppermute | solution.py:637
  41.8 2.4 %collective-permute-start.13 = (bf16[56,16,128]{2,1,0:T(8,128)(2,1)S(1)}, bf16[56,16,128]{2,1,0:T(8,128)(2,1)S(1)}, u32[]{:S(2)}, u32[]{:S(2)}) collective-permute-start(bf16[56,16,128]{2,1,0:T(8,128)(2,1)S(1)} %pad_maximum_fusion), channel_id=1, source_target_pairs={{1,2},{3,4},{5,6},{7,8},{9,10},{11,12},{13,14},{2,1},{4,3},{6,5},{... | collective-permute-start | bytes 688136 | tf_op jit(solution)/shard_map/ppermute | solution.py:637
  44.3 1.0 %collective-permute-start.14 = (bf16[2,16,16,128]{3,2,1,0:T(8,128)(2,1)S(1)}, bf16[2,16,16,128]{3,2,1,0:T(8,128)(2,1)S(1)}, u32[]{:S(2)}, u32[]{:S(2)}) collective-permute-start(bf16[2,16,16,128]{3,2,1,0:T(8,128)(2,1)S(1)} %get-tuple-element.64), channel_id=1, source_target_pairs={{0,1},{1,0},{2,3},{3,2},{4,5},{5,4},{6,7},{7,6},{8,9},{9,8},{10,11... | collective-permute-start | bytes 393224 | tf_op jit(solution)/shard_map/ppermute | solution.py:640
  45.3 1.1 %shard_map.144 = (bf16[6,18,16,512]{3,2,1,0:T(8,128)(2,1)S(1)}, bf16[24,16,128]{2,1,0:T(8,128)(2,1)S(1)}) custom-call(bf16[48,16,128]{2,1,0:T(8,128)(2,1)S(1)} %get-tuple-element.55.own, bf16[24,16,128]{2,1,0:T(8,128)(2,1)S(1)} %collective-permute-done.9.in_near, bf16[1728,576]{1,0:T(8,128)(2,1)S(1)} %bitcast.31), custom_call_target="tpu_custom_call" | custom-call | tf_op jit(solution)/shard_map/pallas_call | solution.py:605
  46.4 0.1 collective-permute-start.11
  46.4 3.7 %collective-permute-done.10.outer = bf16[48,16,128]{2,1,0:T(8,128)(2,1)S(1)} collective-permute-done((bf16[48,16,128]{2,1,0:T(8,128)(2,1)S(1)}, bf16[48,16,128]{2,1,0:T(8,128)(2,1)S(1)}, u32[]{:S(2)}, u32[]{:S(2)}) %collective-permute-start.10) | collective-permute-done | bytes 196640 | tf_op jit(solution)/shard_map/ppermute | solution.py:637
  50.2 1.1 %shard_map.145 = (bf16[6,18,16,512]{3,2,1,0:T(8,128)(2,1)S(1)}, bf16[24,16,128]{2,1,0:T(8,128)(2,1)S(1)}) custom-call(bf16[6,18,16,512]{3,2,1,0:T(8,128)(2,1)S(1)} %get-tuple-element.56.s1_given, bf16[48,16,128]{2,1,0:T(8,128)(2,1)S(1)} %get-tuple-element.55.own, ...), custom_call_target="tpu_custom_call", output_to_operand_aliasing={{0}: (0, {})} | custom-call | tf_op jit(solution)/shard_map/pallas_call | solution.py:605
  51.4 1.0 %shard_map.148 = (bf16[768,256]{1,0:T(8,128)(2,1)S(1)}, bf16[1152,256]{1,0:T(8,128)(2,1)S(1)}, bf16[1024,128]{1,0:T(8,128)(2,1)S(1)}) custom-call(bf16[9,64,192]{2,1,0:T(8,128)(2,1)S(1)} %bitcast.48, bf16[9,64,192]{2,1,0:T(8,128)(2,1)S(1)} %bitcast.49, bf16[9,64,192]{2,1,0:T(8,128)(2,1)S(1)} %bitcast.50, bf16[16,64]{1,0:T(8,128)(2,1)S(1)} %bitcast.52), custom_call_target="tpu_custom_call" | custom-call | tf_op jit(solution)/shard_map/pallas_call | solution.py:605
  52.4 1.1 %shard_map.146.s1_given = bf16[6,18,16,512]{3,2,1,0:T(8,128)(2,1)S(1)} custom-call(bf16[6,18,16,512]{3,2,1,0:T(8,128)(2,1)S(1)} %get-tuple-element.57.s1_given, bf16[48,16,128]{2,1,0:T(8,128)(2,1)S(1)} %get-tuple-element.55.own, bf16[48,16,128]{2,1,0:T(8,128)(2,1)S(1)} %collective-permute-done.10.outer, ...), custom_call_target="tpu_custom_call", output_to_operand_aliasing={{}: (0, {})} | custom-call | tf_op jit(solution)/shard_map/pallas_call | solution.py:605
  53.5 2.7 %shard_map.147 = (bf16[6,18,16,512]{3,2,1,0:T(8,128)(2,1)S(1)}, bf16[5,18,16,512]{3,2,1,0:T(8,128)(2,1)S(1)}) custom-call(bf16[6,18,16,512]{3,2,1,0:T(8,128)(2,1)S(1)} %shard_map.146.s1_given, bf16[24,16,128]{2,1,0:T(8,128)(2,1)S(1)} %collective-permute-done.11.in_near, ...), custom_call_target="tpu_custom_call", output_to_operand_aliasing={{0}: (0, {})} | custom-call | tf_op jit(solution)/shard_map/pallas_call | solution.py:605
  56.3 7.3 %shard_map.149 = (bf16[2,4,16,512]{3,2,1,0:T(8,128)(2,1)S(1)}, bf16[6,18,16,512]{3,2,1,0:T(8,128)(2,1)S(1)}, bf16[5,18,16,512]{3,2,1,0:T(8,128)(2,1)S(1)}) custom-call(bf16[6,18,16,512]{3,2,1,0:T(8,128)(2,1)S(1)} %get-tuple-element.60.s1_given, ...), custom_call_target="tpu_custom_call", output_to_operand_aliasing={{1}: (0, {}), {2}: (1, {})} | custom-call | tf_op jit(solution)/shard_map/pallas_call | solution.py:605
  63.5 0.7 %reshape.57 = bf16[2,4,8192]{2,1,0:T(4,128)(2,1)} reshape(bf16[2,4,16,512]{3,2,1,0:T(8,128)(2,1)S(1)} %get-tuple-element.68) | data formatting | bytes 262144 | tf_op jit(solution)/shard_map/reshape | solution.py:745
  (41 shorter events, 0.4 us)
Async XLA Ops:
  0.0 10.6 %copy-start.5 = (bf16[3,3,64,192]{3,2,1,0:T(8,128)(2,1)S(1)}, bf16[3,3,64,192]{3,2,1,0:T(8,128)(2,1)}, u32[]{:S(2)}) copy-start(bf16[3,3,64,192]{3,2,1,0:T(8,128)(2,1)} %param.20) | copy-start | bytes 663556
  0.0 10.6 %copy-start.4 = (bf16[3,3,64,192]{3,2,1,0:T(8,128)(2,1)S(1)}, bf16[3,3,64,192]{3,2,1,0:T(8,128)(2,1)}, u32[]{:S(2)}) copy-start(bf16[3,3,64,192]{3,2,1,0:T(8,128)(2,1)} %param.19) | copy-start | bytes 663556
  0.0 10.6 %copy-start.3 = (bf16[3,3,64,192]{3,2,1,0:T(8,128)(2,1)S(1)}, bf16[3,3,64,192]{3,2,1,0:T(8,128)(2,1)}, u32[]{:S(2)}) copy-start(bf16[3,3,64,192]{3,2,1,0:T(8,128)(2,1)} %param.18) | copy-start | bytes 663556
  0.0 10.6 %copy-start.9 = (bf16[16,64]{1,0:T(8,128)(2,1)S(1)}, bf16[16,64]{1,0:T(8,128)(2,1)}, u32[]{:S(2)}) copy-start(bf16[16,64]{1,0:T(8,128)(2,1)} %refs_0_.1) | copy-start | bytes 6148
  2.2 13.4 %collective-permute-start = (bf16[3,16,3072]{2,1,0:T(8,128)(2,1)S(1)}, bf16[3,16,3072]{2,1,0:T(8,128)(2,1)S(1)}, u32[]{:S(2)}, u32[]{:S(2)}) collective-permute-start(bf16[3,16,3072]{2,1,0:T(8,128)(2,1)S(1)} %get-tuple-element.43), channel_id=1, source_target_pairs={{1,2},{3,4},{5,6},{7,8},{9,10},{11,12},{13,14},{2,1},{4,3},{6,5},{... | collective-permute-start | bytes 884744 | tf_op jit(solution)/shard_map/ppermute | solution.py:637
  6.0 9.7 %collective-permute-start.1 = (bf16[3,16,3072]{2,1,0:T(8,128)(2,1)S(1)}, bf16[3,16,3072]{2,1,0:T(8,128)(2,1)S(1)}, u32[]{:S(2)}, u32[]{:S(2)}) collective-permute-start(bf16[3,16,3072]{2,1,0:T(8,128)(2,1)S(1)} %get-tuple-element.44), channel_id=1, source_target_pairs={{0,1},{1,0},{2,3},{3,2},{4,5},{5,4},{6,7},{7,6},{8,9},{9,8},{10,11... | collective-permute-start | bytes 884744 | tf_op jit(solution)/shard_map/ppermute | solution.py:640
  7.0 16.6 %collective-permute-start.6 = (bf16[2,16,3072]{2,1,0:T(8,128)(2,1)S(1)}, bf16[2,16,3072]{2,1,0:T(8,128)(2,1)S(1)}, u32[]{:S(2)}, u32[]{:S(2)}) collective-permute-start(bf16[2,16,3072]{2,1,0:T(8,128)(2,1)S(1)} %bitcast.42), channel_id=1, source_target_pairs={{0,1},{1,0},{2,3},{3,2},{4,5},{5,4},{6,7},{7,6},{8,9},{9,8},{10,11... | collective-permute-start | bytes 589832 | tf_op jit(solution)/shard_map/ppermute | solution.py:640
  7.6 16.0 %collective-permute-start.5 = (bf16[2,16,3072]{2,1,0:T(8,128)(2,1)S(1)}, bf16[2,16,3072]{2,1,0:T(8,128)(2,1)S(1)}, u32[]{:S(2)}, u32[]{:S(2)}) collective-permute-start(bf16[2,16,3072]{2,1,0:T(8,128)(2,1)S(1)} %bitcast.43), channel_id=1, source_target_pairs={{1,2},{3,4},{5,6},{7,8},{9,10},{11,12},{13,14},{2,1},{4,3},{6,5},{... | collective-permute-start | bytes 589832 | tf_op jit(solution)/shard_map/ppermute | solution.py:637
  12.6 11.0 %copy-start.2 = (bf16[3,3,192,576]{3,2,1,0:T(8,128)(2,1)S(1)}, bf16[3,3,192,576]{3,2,1,0:T(8,128)(2,1)}, u32[]{:S(2)}) copy-start(bf16[3,3,192,576]{3,2,1,0:T(8,128)(2,1)} %param.22) | copy-start | bytes 5971972
  21.4 10.2 %copy-start.1 = (bf16[3,3,192,576]{3,2,1,0:T(8,128)(2,1)S(1)}, bf16[3,3,192,576]{3,2,1,0:T(8,128)(2,1)}, u32[]{:S(2)}) copy-start(bf16[3,3,192,576]{3,2,1,0:T(8,128)(2,1)} %param.21) | copy-start | bytes 5971972
  21.4 10.2 %collective-permute-start.4 = (bf16[48,16,128]{2,1,0:T(8,128)(2,1)S(1)}, bf16[48,16,128]{2,1,0:T(8,128)(2,1)S(1)}, u32[]{:S(2)}, u32[]{:S(2)}) collective-permute-start(bf16[48,16,128]{2,1,0:T(8,128)(2,1)S(1)} %get-tuple-element.49), channel_id=1, source_target_pairs={{0,1},{1,0},{2,3},{3,2},{4,5},{5,4},{6,7},{7,6},{8,9},{9,8},{10,11... | collective-permute-start | bytes 589832 | tf_op jit(solution)/shard_map/ppermute | solution.py:640
  21.5 11.3 %collective-permute-start.7 = (bf16[48,16,128]{2,1,0:T(8,128)(2,1)S(1)}, bf16[48,16,128]{2,1,0:T(8,128)(2,1)S(1)}, u32[]{:S(2)}, u32[]{:S(2)}) collective-permute-start(bf16[48,16,128]{2,1,0:T(8,128)(2,1)S(1)} %get-tuple-element.53), channel_id=1, source_target_pairs={{1,2},{3,4},{5,6},{7,8},{9,10},{11,12},{13,14},{2,1},{4,3},{6,5},{... | collective-permute-start | bytes 589832 | tf_op jit(solution)/shard_map/ppermute | solution.py:637
  26.5 8.2 %collective-permute-start.2 = (bf16[24,16,128]{2,1,0:T(8,128)(2,1)S(1)}, bf16[24,16,128]{2,1,0:T(8,128)(2,1)S(1)}, u32[]{:S(2)}, u32[]{:S(2)}) collective-permute-start(bf16[24,16,128]{2,1,0:T(8,128)(2,1)S(1)} %get-tuple-element.47), channel_id=1, source_target_pairs={{1,2},{3,4},{5,6},{7,8},{9,10},{11,12},{13,14},{2,1},{4,3},{6,5},{... | collective-permute-start | bytes 294920 | tf_op jit(solution)/shard_map/ppermute | solution.py:637
  30.3 4.4 %collective-permute-start.3 = (bf16[24,16,128]{2,1,0:T(8,128)(2,1)S(1)}, bf16[24,16,128]{2,1,0:T(8,128)(2,1)S(1)}, u32[]{:S(2)}, u32[]{:S(2)}) collective-permute-start(bf16[24,16,128]{2,1,0:T(8,128)(2,1)S(1)} %get-tuple-element.48), channel_id=1, source_target_pairs={{0,1},{1,0},{2,3},{3,2},{4,5},{5,4},{6,7},{7,6},{8,9},{9,8},{10,11... | collective-permute-start | bytes 294920 | tf_op jit(solution)/shard_map/ppermute | solution.py:640
  32.7 2.0 %collective-permute-start.8 = (bf16[24,16,128]{2,1,0:T(8,128)(2,1)S(1)}, bf16[24,16,128]{2,1,0:T(8,128)(2,1)S(1)}, u32[]{:S(2)}, u32[]{:S(2)}) collective-permute-start(bf16[24,16,128]{2,1,0:T(8,128)(2,1)S(1)} %get-tuple-element.54), channel_id=1, source_target_pairs={{0,1},{1,0},{2,3},{3,2},{4,5},{5,4},{6,7},{7,6},{8,9},{9,8},{10,11... | collective-permute-start | bytes 294920 | tf_op jit(solution)/shard_map/ppermute | solution.py:640
  34.7 10.5 %copy-start = (bf16[3,3,192,576]{3,2,1,0:T(8,128)(2,1)S(1)}, bf16[3,3,192,576]{3,2,1,0:T(8,128)(2,1)}, u32[]{:S(2)}) copy-start(bf16[3,3,192,576]{3,2,1,0:T(8,128)(2,1)} %param.23) | copy-start | bytes 5971972
  38.1 3.7 %collective-permute-start.9 = (bf16[24,16,128]{2,1,0:T(8,128)(2,1)S(1)}, bf16[24,16,128]{2,1,0:T(8,128)(2,1)S(1)}, u32[]{:S(2)}, u32[]{:S(2)}) collective-permute-start(bf16[24,16,128]{2,1,0:T(8,128)(2,1)S(1)} %slice.13), channel_id=1, source_target_pairs={{0,1},{1,0},{2,3},{3,2},{4,5},{5,4},{6,7},{7,6},{8,9},{9,8},{10,11... | collective-permute-start | bytes 294920 | tf_op jit(solution)/shard_map/ppermute | solution.py:640
  38.7 11.5 %collective-permute-start.10 = (bf16[48,16,128]{2,1,0:T(8,128)(2,1)S(1)}, bf16[48,16,128]{2,1,0:T(8,128)(2,1)S(1)}, u32[]{:S(2)}, u32[]{:S(2)}) collective-permute-start(bf16[48,16,128]{2,1,0:T(8,128)(2,1)S(1)} %get-tuple-element.55.own), channel_id=1, source_target_pairs={{1,2},{3,4},{5,6},{7,8},{9,10},{11,12},{13,14},{2,1},{4,3},{6,5},{... | collective-permute-start | bytes 589832 | tf_op jit(solution)/shard_map/ppermute | solution.py:637
  41.8 14.4 %collective-permute-start.13 = (bf16[56,16,128]{2,1,0:T(8,128)(2,1)S(1)}, bf16[56,16,128]{2,1,0:T(8,128)(2,1)S(1)}, u32[]{:S(2)}, u32[]{:S(2)}) collective-permute-start(bf16[56,16,128]{2,1,0:T(8,128)(2,1)S(1)} %pad_maximum_fusion), channel_id=1, source_target_pairs={{1,2},{3,4},{5,6},{7,8},{9,10},{11,12},{13,14},{2,1},{4,3},{6,5},{... | collective-permute-start | bytes 688136 | tf_op jit(solution)/shard_map/ppermute | solution.py:637
  44.3 12.0 %collective-permute-start.14 = (bf16[2,16,16,128]{3,2,1,0:T(8,128)(2,1)S(1)}, bf16[2,16,16,128]{3,2,1,0:T(8,128)(2,1)S(1)}, u32[]{:S(2)}, u32[]{:S(2)}) collective-permute-start(bf16[2,16,16,128]{3,2,1,0:T(8,128)(2,1)S(1)} %get-tuple-element.64), channel_id=1, source_target_pairs={{0,1},{1,0},{2,3},{3,2},{4,5},{5,4},{6,7},{7,6},{8,9},{9,8},{10,11... | collective-permute-start | bytes 393224 | tf_op jit(solution)/shard_map/ppermute | solution.py:640
  46.4 7.2 %collective-permute-start.11 = (bf16[24,16,128]{2,1,0:T(8,128)(2,1)S(1)}, bf16[24,16,128]{2,1,0:T(8,128)(2,1)S(1)}, u32[]{:S(2)}, u32[]{:S(2)}) collective-permute-start(bf16[24,16,128]{2,1,0:T(8,128)(2,1)S(1)} %get-tuple-element.58), channel_id=1, source_target_pairs={{0,1},{1,0},{2,3},{3,2},{4,5},{5,4},{6,7},{7,6},{8,9},{9,8},{10,11... | collective-permute-start | bytes 294920 | tf_op jit(solution)/shard_map/ppermute | solution.py:640
  50.2 1.2 %copy-start.6 = (bf16[3,3,192,64]{2,3,1,0:T(8,128)(2,1)S(1)}, bf16[3,3,192,64]{2,3,1,0:T(8,128)(2,1)}, u32[]{:S(2)}) copy-start(bf16[3,3,192,64]{2,3,1,0:T(8,128)(2,1)} %param.24) | copy-start | bytes 663556
  50.2 1.2 %copy-start.7 = (bf16[3,3,64,192]{3,2,1,0:T(8,128)(2,1)S(1)}, bf16[3,3,64,192]{3,2,1,0:T(8,128)(2,1)}, u32[]{:S(2)}) copy-start(bf16[3,3,64,192]{3,2,1,0:T(8,128)(2,1)} %param.25) | copy-start | bytes 663556
  50.2 1.2 %copy-start.8 = (bf16[3,3,64,192]{3,2,1,0:T(8,128)(2,1)S(1)}, bf16[3,3,64,192]{3,2,1,0:T(8,128)(2,1)}, u32[]{:S(2)}) copy-start(bf16[3,3,64,192]{3,2,1,0:T(8,128)(2,1)} %param.26) | copy-start | bytes 663556
  50.2 1.2 %copy-start.10 = (bf16[64,16]{0,1:T(8,128)(2,1)S(1)}, bf16[64,16]{0,1:T(8,128)(2,1)}, u32[]{:S(2)}) copy-start(bf16[64,16]{0,1:T(8,128)(2,1)} %param.27) | copy-start | bytes 6148
  51.3 2.2 %collective-permute-start.12 = (bf16[24,16,128]{2,1,0:T(8,128)(2,1)S(1)}, bf16[24,16,128]{2,1,0:T(8,128)(2,1)S(1)}, u32[]{:S(2)}, u32[]{:S(2)}) collective-permute-start(bf16[24,16,128]{2,1,0:T(8,128)(2,1)S(1)} %get-tuple-element.59), channel_id=1, source_target_pairs={{0,1},{1,0},{2,3},{3,2},{4,5},{5,4},{6,7},{7,6},{8,9},{9,8},{10,11... | collective-permute-start | bytes 294920 | tf_op jit(solution)/shard_map/ppermute | solution.py:640

commit v9 on v8

--- a/solution.py
+++ b/solution.py
@@ -479,9 +479,11 @@
             if 2 <= idx < 6:
                 pair = f_own[idx - 2, k]
             elif idx < 2:
-                pair = jnp.where(upper, rest[ROW_TILES + idx * FB // 2 + k], f_inner[idx, k])
+                at = ROW_TILES + idx * FB // 2 + k
+                pair = jnp.where(upper, rest[at], f_inner[at])
             else:
-                pair = jnp.where(upper, f_inner[idx - 6, k], rest[ROW_TILES + (idx - 6) * FB // 2 + k])
+                at = ROW_TILES + (idx - 6) * FB // 2 + k
+                pair = jnp.where(upper, f_inner[at], rest[at])
             pf1[idx, 1 + 2 * k] = swap_bf(pair)
             pf1[idx, 2 + 2 * k] = pair
 
@@ -704,7 +706,6 @@
         [jax.ShapeDtypeStruct((3, CB * SUB, 5 * LANES), F32), (3, CB + 2, SUB, 4 * LANES)],
         [coarse_buf(6)],
     )
-    state_fi = inner_swap(state_fi)
 
     w_x, w_h = enc_coarse_x.reshape(flat), enc_coarse_h.reshape(flat)
     four = (4, CB + 2, SUB, 4 * LANES)
@@ -722,14 +723,16 @@
         [coarse_buf(4), acc_buf, acc_buf],
         {3: 1},
     )
-    in_near = inner_swap(state_c[ROW_TILES:])
+    edge_i = jnp.concatenate([state_c[ROW_TILES:], state_fi.reshape(FB, SUB, LANES)], axis=0)
+    edge_i = inner_swap(edge_i)
+    in_near = edge_i[:ROW_TILES]
     state_o = outer_swap(state_c)
     rest = outer_swap(jnp.concatenate([in_near, state_fo.reshape(FB, SUB, LANES)], axis=0))
 
     w_f = fc_coarse_h.reshape(flat)
     six, five = (6,) + four[1:], (5,) + four[1:]
     small = [coarse_buf(3), acc_buf]
-    s1, sent = call(forecast_inner_body, on_chip(state_c, in_near, w_f), [six, row], small)
+    s1, sent = call(forecast_inner_body, on_chip(state_c, edge_i, w_f), [six, row], small)
     in_near = inner_swap(sent)
     s1, sent = call(forecast_outer_body, on_chip(s1, state_c, state_o, w_f), [six, row], small, {0: 0})
     in_far = inner_swap(sent)
@@ -737,7 +740,7 @@
     s1, s2 = call(forecast_second_body, on_chip(s1, in_near, in_far, w_f), [six, five], [acc_buf], {0: 0})
     out, _, _ = call(
         forecaster_body,
-        on_chip(s1, s2, state_o, rest, state_f, state_fi, w_f, w_up, w_fc, w_head),
+        on_chip(s1, s2, state_o, rest, state_f, edge_i, w_f, w_up, w_fc, w_head),
         [(HORIZON, 4, SUB, FB * PATCH), six, five],
         [coarse_buf(3), fine_buf(8), fine_buf(6), fine_buf(4), acc_buf],
         {0: 1, 1: 2},

time: 64.6 us -> 64.9 us (level)
  waiting for transfers between devices: 6.76 us -> 7.81 us
    ppermute x6, waiting for transfers between devices: 6.73 us -> 7.79 us  [outer_swap(): return lax.ppermute(x, LINE, across)]
    ppermute x9 -> x8, starting transfers between devices: 3.82 us -> 3.23 us  [inner_swap(): return lax.ppermute(x, 'section', [(0, 1), (1, 0)])]
  transfers between devices with their start and end apart: 15 -> 14, of which waited for: 2 -> 2; matrix products, arithmetic and copies ran while one was open for 2% -> 2% of each run, Pallas kernels for 32% -> 32%
where the time goes in v9:
time: 64.9 us; the launch traced here: 64.6 us
  Pallas kernels  31 us (48%)
  starting transfers between devices  21.4 us (33%)
  waiting for transfers between devices  7.81 us (12%)
  local copies, waits for them, and re-layouts  3.89 us (6%)
    pallas_call x14, Pallas kernels, call(): pl.pallas_call(body, out_shape=[s if isinstance(s, jax.ShapeDtypeStruct)...  31 us
    ppermute x6, starting transfers between devices, outer_swap(): return lax.ppermute(x, LINE, across)  18.2 us
    ppermute x6, waiting for transfers between devices, outer_swap(): return lax.ppermute(x, LINE, across)  7.79 us
    ppermute x8, starting transfers between devices, inner_swap(): return lax.ppermute(x, 'section', [(0, 1), (1, 0)])  3.23 us
    unnamed x24, local copies, waits for them, and re-layouts  2.12 us
  transfers between devices with their start and end apart: 14, of which 2 were waited for; matrix products, arithmetic and copies ran while one was open for 2% of the time, Pallas kernels for 32%

profile of v9, /device:TPU:19, one launch (start us, length us, event | category | flops | bytes accessed | tf_op | source)
XLA Modules:
  0.0 64.6 jit_solution(16837386784125093393)
XLA Ops:
  0.0 1.0 %fusion = (bf16[1,4,8192]{2,1,0:T(4,128)(2,1)S(1)}, bf16[1,4,8192]{2,1,0:T(4,128)(2,1)S(1)}) fusion(bf16[2,4,8192]{2,1,0:T(4,128)(2,1)} %param.14), kind=kLoop, calls=%fused_computation.6 | loop fusion | bytes 262144 | tf_op jit(solution)/shard_map/slice | solution.py:658
  1.0 1.1 %copy.30 = bf16[1,4,16,2048]{3,2,1,0:T(8,128)(2,1)S(1)} copy(bf16[1,4,16,2048]{3,1,2,0:T(4,128)(2,1)} %bitcast.55) | data formatting | bytes 524288
  2.2 0.1 shard_map.136
  2.2 3.7 %collective-permute-start = (bf16[3,16,3072]{2,1,0:T(8,128)(2,1)S(1)}, bf16[3,16,3072]{2,1,0:T(8,128)(2,1)S(1)}, u32[]{:S(2)}, u32[]{:S(2)}) collective-permute-start(bf16[3,16,3072]{2,1,0:T(8,128)(2,1)S(1)} %get-tuple-element.43), channel_id=1, source_target_pairs={{1,2},{3,4},{5,6},{7,8},{9,10},{11,12},{13,14},{2,1},{4,3},{6,5},{... | collective-permute-start | bytes 884744 | tf_op jit(solution)/shard_map/ppermute | solution.py:639
  6.0 0.1 collective-permute-start.1
  6.0 1.0 %copy.31 = bf16[1,2,16,3072]{3,2,1,0:T(8,128)(2,1)S(1)} copy(bf16[1,2,16,3072]{3,1,2,0:T(2,128)(2,1)} %bitcast.58) | data formatting | bytes 393216
  7.0 0.6 collective-permute-start.6
  7.6 3.0 %collective-permute-start.5 = (bf16[2,16,3072]{2,1,0:T(8,128)(2,1)S(1)}, bf16[2,16,3072]{2,1,0:T(8,128)(2,1)S(1)}, u32[]{:S(2)}, u32[]{:S(2)}) collective-permute-start(bf16[2,16,3072]{2,1,0:T(8,128)(2,1)S(1)} %bitcast.44), channel_id=1, source_target_pairs={{1,2},{3,4},{5,6},{7,8},{9,10},{11,12},{13,14},{2,1},{4,3},{6,5},{... | collective-permute-start | bytes 589832 | tf_op jit(solution)/shard_map/ppermute | solution.py:639
  10.7 0.5 shard_map.137
  11.2 1.5 %shard_map.138 = (bf16[4,34,16,128]{3,2,1,0:T(8,128)(2,1)S(1)}, bf16[4,32,16,128]{3,2,1,0:T(8,128)(2,1)S(1)}, bf16[2,34,16,128]{3,2,1,0:T(8,128)(2,1)S(1)}) custom-call(bf16[4,16,3072]{2,1,0:T(8,128)(2,1)S(1)} %get-tuple-element.37.own, bf16[128,1024]{1,0:T(8,128)(2,1)S(1)} %get-tuple-element.38.w_stem, bf16[1152,256]{1,0:T(8,128)(2,1)S(1)} %get-tuple-element.39.w_gru), custom_call_target="tpu_custom_call" | custom-call | tf_op jit(solution)/shard_map/pallas_call | solution.py:607
  12.6 3.0 %collective-permute-done.outer = bf16[3,16,3072]{2,1,0:T(8,128)(2,1)S(1)} collective-permute-done((bf16[3,16,3072]{2,1,0:T(8,128)(2,1)S(1)}, bf16[3,16,3072]{2,1,0:T(8,128)(2,1)S(1)}, u32[]{:S(2)}, u32[]{:S(2)}) %collective-permute-start) | collective-permute-done | bytes 294944 | tf_op jit(solution)/shard_map/ppermute | solution.py:639
  15.6 5.8 %shard_map.139 = (bf16[4,16,16,128]{3,2,1,0:T(8,128)(2,1)S(1)}, bf16[96,16,128]{2,1,0:T(8,128)(2,1)S(1)}, bf16[48,16,128]{2,1,0:T(8,128)(2,1)S(1)}, bf16[48,16,1...) custom-call(bf16[4,34,16,128]{3,2,1,0:T(8,128)(2,1)S(1)} %get-tuple-, ...), custom_call_target="tpu_custom_call" | custom-call | tf_op jit(solution)/shard_map/pallas_call | solution.py:607
  21.5 2.1 %collective-permute-start.7 = (bf16[48,16,128]{2,1,0:T(8,128)(2,1)S(1)}, bf16[48,16,128]{2,1,0:T(8,128)(2,1)S(1)}, u32[]{:S(2)}, u32[]{:S(2)}) collective-permute-start(bf16[48,16,128]{2,1,0:T(8,128)(2,1)S(1)} %get-tuple-element.53), channel_id=1, source_target_pairs={{1,2},{3,4},{5,6},{7,8},{9,10},{11,12},{13,14},{2,1},{4,3},{6,5},{... | collective-permute-start | bytes 589832 | tf_op jit(solution)/shard_map/ppermute | solution.py:639
  23.6 2.9 %shard_map.140 = (f32[3,256,640]{2,1,0:T(8,128)S(1)}, bf16[3,18,16,512]{3,2,1,0:T(8,128)(2,1)S(1)}) custom-call(bf16[2,16,3072]{2,1,0:T(8,128)(2,1)S(1)} %bitcast.45, bf16[2,16,3072]{2,1,0:T(8,128)(2,1)S(1)} %collective-permute-done.5.outer, bf16[2,16,3072]{2,1,0:T(8,128)(2,1)S(1)} %collective-permute-done.6.inner, bf16[1728,576]{1,0:T(8,128)(2,1)S(1)} %bitcast.40), custom_call_target="tpu_custom_call" | custom-call | tf_op jit(solution)/shard_map/pallas_call | solution.py:607
  26.5 3.8 %collective-permute-start.2 = (bf16[24,16,128]{2,1,0:T(8,128)(2,1)S(1)}, bf16[24,16,128]{2,1,0:T(8,128)(2,1)S(1)}, u32[]{:S(2)}, u32[]{:S(2)}) collective-permute-start(bf16[24,16,128]{2,1,0:T(8,128)(2,1)S(1)} %get-tuple-element.47), channel_id=1, source_target_pairs={{1,2},{3,4},{5,6},{7,8},{9,10},{11,12},{13,14},{2,1},{4,3},{6,5},{... | collective-permute-start | bytes 294920 | tf_op jit(solution)/shard_map/ppermute | solution.py:639
  30.3 1.3 %collective-permute-start.3 = (bf16[24,16,128]{2,1,0:T(8,128)(2,1)S(1)}, bf16[24,16,128]{2,1,0:T(8,128)(2,1)S(1)}, u32[]{:S(2)}, u32[]{:S(2)}) collective-permute-start(bf16[24,16,128]{2,1,0:T(8,128)(2,1)S(1)} %get-tuple-element.48), channel_id=1, source_target_pairs={{0,1},{1,0},{2,3},{3,2},{4,5},{5,4},{6,7},{7,6},{8,9},{9,8},{10,11... | collective-permute-start | bytes 294920 | tf_op jit(solution)/shard_map/ppermute | solution.py:642
  31.6 1.1 %shard_map.141 = (bf16[4,18,16,512]{3,2,1,0:T(8,128)(2,1)S(1)}, bf16[24,16,128]{2,1,0:T(8,128)(2,1)S(1)}) custom-call(bf16[96,16,128]{2,1,0:T(8,128)(2,1)S(1)} %get-tuple-element.46.low_own, bf16[48,16,128]{2,1,0:T(8,128)(2,1)S(1)} %collective-permute-done.4.low_inner, f32[3,256,640]{2,1,0:T(8,128)S(1)} %get-tuple-element.50.acc_first, ...), custom_call_target="tpu_custom_call" | custom-call | tf_op jit(solution)/shard_map/pallas_call | solution.py:607
  32.7 0.1 collective-permute-start.8
  32.8 1.8 %shard_map.142.h1_given = bf16[4,18,16,512]{3,2,1,0:T(8,128)(2,1)S(1)} custom-call(bf16[4,18,16,512]{3,2,1,0:T(8,128)(2,1)S(1)} %get-tuple-element.52.h1_given, bf16[96,16,128]{2,1,0:T(8,128)(2,1)S(1)} %get-tuple-element.46.low_own, bf16[48,16,128]{2,1,0:T(8,128)(2,1)S(1)} %collective-permute-done.7.low_outer, ...), custom_call_target="tpu_custom_call", output_to_operand_aliasing={{}: (0, {})} | custom-call | tf_op jit(solution)/shard_map/pallas_call | solution.py:607
  34.7 3.4 %shard_map.143 = (bf16[48,16,128]{2,1,0:T(8,128)(2,1)S(1)}, bf16[4,18,16,512]{3,2,1,0:T(8,128)(2,1)S(1)}) custom-call(bf16[96,16,128]{2,1,0:T(8,128)(2,1)S(1)} %get-tuple-element.46.low_own, bf16[24,16,128]{2,1,0:T(8,128)(2,1)S(1)} %collective-permute-done.2.second_outer, ...), custom_call_target="tpu_custom_call", output_to_operand_aliasing={{1}: (3, {})} | custom-call | tf_op jit(solution)/shard_map/pallas_call | solution.py:607
  38.1 0.5 collective-permute-start.9
  38.7 3.1 %collective-permute-start.10 = (bf16[48,16,128]{2,1,0:T(8,128)(2,1)S(1)}, bf16[48,16,128]{2,1,0:T(8,128)(2,1)S(1)}, u32[]{:S(2)}, u32[]{:S(2)}) collective-permute-start(bf16[48,16,128]{2,1,0:T(8,128)(2,1)S(1)} %get-tuple-element.55.own), channel_id=1, source_target_pairs={{1,2},{3,4},{5,6},{7,8},{9,10},{11,12},{13,14},{2,1},{4,3},{6,5},{... | collective-permute-start | bytes 589832 | tf_op jit(solution)/shard_map/ppermute | solution.py:639
  41.9 2.4 %collective-permute-start.13 = (bf16[56,16,128]{2,1,0:T(8,128)(2,1)S(1)}, bf16[56,16,128]{2,1,0:T(8,128)(2,1)S(1)}, u32[]{:S(2)}, u32[]{:S(2)}) collective-permute-start(bf16[56,16,128]{2,1,0:T(8,128)(2,1)S(1)} %pad_maximum_fusion.1), channel_id=1, source_target_pairs={{1,2},{3,4},{5,6},{7,8},{9,10},{11,12},{13,14},{2,1},{4,3},{6,5},{... | collective-permute-start | bytes 688136 | tf_op jit(solution)/shard_map/ppermute | solution.py:639
  44.3 1.1 %shard_map.144 = (bf16[6,18,16,512]{3,2,1,0:T(8,128)(2,1)S(1)}, bf16[24,16,128]{2,1,0:T(8,128)(2,1)S(1)}) custom-call(bf16[48,16,128]{2,1,0:T(8,128)(2,1)S(1)} %get-tuple-element.55.own, bf16[56,16,128]{2,1,0:T(8,128)(2,1)S(1)} %collective-permute-done.9.in_near.f_inner, bf16[1728,576]{1,0:T(8,128)(2,1)S(1)} %bitcast.32), custom_call_target="tpu_custom_call" | custom-call | tf_op jit(solution)/shard_map/pallas_call | solution.py:607
  45.4 4.8 %collective-permute-done.10.outer = bf16[48,16,128]{2,1,0:T(8,128)(2,1)S(1)} collective-permute-done((bf16[48,16,128]{2,1,0:T(8,128)(2,1)S(1)}, bf16[48,16,128]{2,1,0:T(8,128)(2,1)S(1)}, u32[]{:S(2)}, u32[]{:S(2)}) %collective-permute-start.10) | collective-permute-done | bytes 196640 | tf_op jit(solution)/shard_map/ppermute | solution.py:639
  50.2 1.1 %shard_map.145 = (bf16[6,18,16,512]{3,2,1,0:T(8,128)(2,1)S(1)}, bf16[24,16,128]{2,1,0:T(8,128)(2,1)S(1)}) custom-call(bf16[6,18,16,512]{3,2,1,0:T(8,128)(2,1)S(1)} %get-tuple-element.57.s1_given, bf16[48,16,128]{2,1,0:T(8,128)(2,1)S(1)} %get-tuple-element.55.own, ...), custom_call_target="tpu_custom_call", output_to_operand_aliasing={{0}: (0, {})} | custom-call | tf_op jit(solution)/shard_map/pallas_call | solution.py:607
  51.4 0.5 collective-permute-start.11
  51.9 1.0 %shard_map.148 = (bf16[768,256]{1,0:T(8,128)(2,1)S(1)}, bf16[1152,256]{1,0:T(8,128)(2,1)S(1)}, bf16[1024,128]{1,0:T(8,128)(2,1)S(1)}) custom-call(bf16[9,64,192]{2,1,0:T(8,128)(2,1)S(1)} %bitcast.49, bf16[9,64,192]{2,1,0:T(8,128)(2,1)S(1)} %bitcast.50, bf16[9,64,192]{2,1,0:T(8,128)(2,1)S(1)} %bitcast.51, bf16[16,64]{1,0:T(8,128)(2,1)S(1)} %bitcast.54), custom_call_target="tpu_custom_call" | custom-call | tf_op jit(solution)/shard_map/pallas_call | solution.py:607
  52.9 1.1 %shard_map.146.s1_given = bf16[6,18,16,512]{3,2,1,0:T(8,128)(2,1)S(1)} custom-call(bf16[6,18,16,512]{3,2,1,0:T(8,128)(2,1)S(1)} %get-tuple-element.58.s1_given, bf16[48,16,128]{2,1,0:T(8,128)(2,1)S(1)} %get-tuple-element.55.own, bf16[48,16,128]{2,1,0:T(8,128)(2,1)S(1)} %collective-permute-done.10.outer, ...), custom_call_target="tpu_custom_call", output_to_operand_aliasing={{}: (0, {})} | custom-call | tf_op jit(solution)/shard_map/pallas_call | solution.py:607
  54.0 2.7 %shard_map.147 = (bf16[6,18,16,512]{3,2,1,0:T(8,128)(2,1)S(1)}, bf16[5,18,16,512]{3,2,1,0:T(8,128)(2,1)S(1)}) custom-call(bf16[6,18,16,512]{3,2,1,0:T(8,128)(2,1)S(1)} %shard_map.146.s1_given, bf16[24,16,128]{2,1,0:T(8,128)(2,1)S(1)} %collective-permute-done.11.in_near, ...), custom_call_target="tpu_custom_call", output_to_operand_aliasing={{0}: (0, {})} | custom-call | tf_op jit(solution)/shard_map/pallas_call | solution.py:607
  56.7 7.1 %shard_map.149 = (bf16[2,4,16,512]{3,2,1,0:T(8,128)(2,1)S(1)}, bf16[6,18,16,512]{3,2,1,0:T(8,128)(2,1)S(1)}, bf16[5,18,16,512]{3,2,1,0:T(8,128)(2,1)S(1)}) custom-call(bf16[6,18,16,512]{3,2,1,0:T(8,128)(2,1)S(1)} %get-tuple-element.61.s1_given, ...), custom_call_target="tpu_custom_call", output_to_operand_aliasing={{1}: (0, {}), {2}: (1, {})} | custom-call | tf_op jit(solution)/shard_map/pallas_call | solution.py:607
  63.8 0.7 %reshape.61 = bf16[2,4,8192]{2,1,0:T(4,128)(2,1)} reshape(bf16[2,4,16,512]{3,2,1,0:T(8,128)(2,1)S(1)} %get-tuple-element.68) | data formatting | bytes 262144 | tf_op jit(solution)/shard_map/reshape | solution.py:748
  (41 shorter events, 0.3 us)
Async XLA Ops:
  0.0 10.6 %copy-start.5 = (bf16[3,3,64,192]{3,2,1,0:T(8,128)(2,1)S(1)}, bf16[3,3,64,192]{3,2,1,0:T(8,128)(2,1)}, u32[]{:S(2)}) copy-start(bf16[3,3,64,192]{3,2,1,0:T(8,128)(2,1)} %param.20) | copy-start | bytes 663556
  0.0 10.6 %copy-start.4 = (bf16[3,3,64,192]{3,2,1,0:T(8,128)(2,1)S(1)}, bf16[3,3,64,192]{3,2,1,0:T(8,128)(2,1)}, u32[]{:S(2)}) copy-start(bf16[3,3,64,192]{3,2,1,0:T(8,128)(2,1)} %param.19) | copy-start | bytes 663556
  0.0 10.6 %copy-start.3 = (bf16[3,3,64,192]{3,2,1,0:T(8,128)(2,1)S(1)}, bf16[3,3,64,192]{3,2,1,0:T(8,128)(2,1)}, u32[]{:S(2)}) copy-start(bf16[3,3,64,192]{3,2,1,0:T(8,128)(2,1)} %param.18) | copy-start | bytes 663556
  0.0 10.6 %copy-start.9 = (bf16[16,64]{1,0:T(8,128)(2,1)S(1)}, bf16[16,64]{1,0:T(8,128)(2,1)}, u32[]{:S(2)}) copy-start(bf16[16,64]{1,0:T(8,128)(2,1)} %refs_0_.1) | copy-start | bytes 6148
  2.2 13.4 %collective-permute-start = (bf16[3,16,3072]{2,1,0:T(8,128)(2,1)S(1)}, bf16[3,16,3072]{2,1,0:T(8,128)(2,1)S(1)}, u32[]{:S(2)}, u32[]{:S(2)}) collective-permute-start(bf16[3,16,3072]{2,1,0:T(8,128)(2,1)S(1)} %get-tuple-element.43), channel_id=1, source_target_pairs={{1,2},{3,4},{5,6},{7,8},{9,10},{11,12},{13,14},{2,1},{4,3},{6,5},{... | collective-permute-start | bytes 884744 | tf_op jit(solution)/shard_map/ppermute | solution.py:639
  6.0 9.7 %collective-permute-start.1 = (bf16[3,16,3072]{2,1,0:T(8,128)(2,1)S(1)}, bf16[3,16,3072]{2,1,0:T(8,128)(2,1)S(1)}, u32[]{:S(2)}, u32[]{:S(2)}) collective-permute-start(bf16[3,16,3072]{2,1,0:T(8,128)(2,1)S(1)} %get-tuple-element.44), channel_id=1, source_target_pairs={{0,1},{1,0},{2,3},{3,2},{4,5},{5,4},{6,7},{7,6},{8,9},{9,8},{10,11... | collective-permute-start | bytes 884744 | tf_op jit(solution)/shard_map/ppermute | solution.py:642
  7.0 16.6 %collective-permute-start.6 = (bf16[2,16,3072]{2,1,0:T(8,128)(2,1)S(1)}, bf16[2,16,3072]{2,1,0:T(8,128)(2,1)S(1)}, u32[]{:S(2)}, u32[]{:S(2)}) collective-permute-start(bf16[2,16,3072]{2,1,0:T(8,128)(2,1)S(1)} %bitcast.43), channel_id=1, source_target_pairs={{0,1},{1,0},{2,3},{3,2},{4,5},{5,4},{6,7},{7,6},{8,9},{9,8},{10,11... | collective-permute-start | bytes 589832 | tf_op jit(solution)/shard_map/ppermute | solution.py:642
  7.6 16.0 %collective-permute-start.5 = (bf16[2,16,3072]{2,1,0:T(8,128)(2,1)S(1)}, bf16[2,16,3072]{2,1,0:T(8,128)(2,1)S(1)}, u32[]{:S(2)}, u32[]{:S(2)}) collective-permute-start(bf16[2,16,3072]{2,1,0:T(8,128)(2,1)S(1)} %bitcast.44), channel_id=1, source_target_pairs={{1,2},{3,4},{5,6},{7,8},{9,10},{11,12},{13,14},{2,1},{4,3},{6,5},{... | collective-permute-start | bytes 589832 | tf_op jit(solution)/shard_map/ppermute | solution.py:639
  12.6 11.0 %copy-start.2 = (bf16[3,3,192,576]{3,2,1,0:T(8,128)(2,1)S(1)}, bf16[3,3,192,576]{3,2,1,0:T(8,128)(2,1)}, u32[]{:S(2)}) copy-start(bf16[3,3,192,576]{3,2,1,0:T(8,128)(2,1)} %param.22) | copy-start | bytes 5971972
  21.4 10.2 %copy-start.1 = (bf16[3,3,192,576]{3,2,1,0:T(8,128)(2,1)S(1)}, bf16[3,3,192,576]{3,2,1,0:T(8,128)(2,1)}, u32[]{:S(2)}) copy-start(bf16[3,3,192,576]{3,2,1,0:T(8,128)(2,1)} %param.21) | copy-start | bytes 5971972
  21.4 10.2 %collective-permute-start.4 = (bf16[48,16,128]{2,1,0:T(8,128)(2,1)S(1)}, bf16[48,16,128]{2,1,0:T(8,128)(2,1)S(1)}, u32[]{:S(2)}, u32[]{:S(2)}) collective-permute-start(bf16[48,16,128]{2,1,0:T(8,128)(2,1)S(1)} %get-tuple-element.49), channel_id=1, source_target_pairs={{0,1},{1,0},{2,3},{3,2},{4,5},{5,4},{6,7},{7,6},{8,9},{9,8},{10,11... | collective-permute-start | bytes 589832 | tf_op jit(solution)/shard_map/ppermute | solution.py:642
  21.5 11.3 %collective-permute-start.7 = (bf16[48,16,128]{2,1,0:T(8,128)(2,1)S(1)}, bf16[48,16,128]{2,1,0:T(8,128)(2,1)S(1)}, u32[]{:S(2)}, u32[]{:S(2)}) collective-permute-start(bf16[48,16,128]{2,1,0:T(8,128)(2,1)S(1)} %get-tuple-element.53), channel_id=1, source_target_pairs={{1,2},{3,4},{5,6},{7,8},{9,10},{11,12},{13,14},{2,1},{4,3},{6,5},{... | collective-permute-start | bytes 589832 | tf_op jit(solution)/shard_map/ppermute | solution.py:639
  26.5 8.2 %collective-permute-start.2 = (bf16[24,16,128]{2,1,0:T(8,128)(2,1)S(1)}, bf16[24,16,128]{2,1,0:T(8,128)(2,1)S(1)}, u32[]{:S(2)}, u32[]{:S(2)}) collective-permute-start(bf16[24,16,128]{2,1,0:T(8,128)(2,1)S(1)} %get-tuple-element.47), channel_id=1, source_target_pairs={{1,2},{3,4},{5,6},{7,8},{9,10},{11,12},{13,14},{2,1},{4,3},{6,5},{... | collective-permute-start | bytes 294920 | tf_op jit(solution)/shard_map/ppermute | solution.py:639
  30.3 4.4 %collective-permute-start.3 = (bf16[24,16,128]{2,1,0:T(8,128)(2,1)S(1)}, bf16[24,16,128]{2,1,0:T(8,128)(2,1)S(1)}, u32[]{:S(2)}, u32[]{:S(2)}) collective-permute-start(bf16[24,16,128]{2,1,0:T(8,128)(2,1)S(1)} %get-tuple-element.48), channel_id=1, source_target_pairs={{0,1},{1,0},{2,3},{3,2},{4,5},{5,4},{6,7},{7,6},{8,9},{9,8},{10,11... | collective-permute-start | bytes 294920 | tf_op jit(solution)/shard_map/ppermute | solution.py:642
  32.7 2.0 %collective-permute-start.8 = (bf16[24,16,128]{2,1,0:T(8,128)(2,1)S(1)}, bf16[24,16,128]{2,1,0:T(8,128)(2,1)S(1)}, u32[]{:S(2)}, u32[]{:S(2)}) collective-permute-start(bf16[24,16,128]{2,1,0:T(8,128)(2,1)S(1)} %get-tuple-element.54), channel_id=1, source_target_pairs={{0,1},{1,0},{2,3},{3,2},{4,5},{5,4},{6,7},{7,6},{8,9},{9,8},{10,11... | collective-permute-start | bytes 294920 | tf_op jit(solution)/shard_map/ppermute | solution.py:642
  34.7 9.6 %copy-start = (bf16[3,3,192,576]{3,2,1,0:T(8,128)(2,1)S(1)}, bf16[3,3,192,576]{3,2,1,0:T(8,128)(2,1)}, u32[]{:S(2)}) copy-start(bf16[3,3,192,576]{3,2,1,0:T(8,128)(2,1)} %param.23) | copy-start | bytes 5971972
  38.1 3.7 %collective-permute-start.9 = (bf16[56,16,128]{2,1,0:T(8,128)(2,1)S(1)}, bf16[56,16,128]{2,1,0:T(8,128)(2,1)S(1)}, u32[]{:S(2)}, u32[]{:S(2)}) collective-permute-start(bf16[56,16,128]{2,1,0:T(8,128)(2,1)S(1)} %pad_maximum_fusion), channel_id=1, source_target_pairs={{0,1},{1,0},{2,3},{3,2},{4,5},{5,4},{6,7},{7,6},{8,9},{9,8},{10,11... | collective-permute-start | bytes 688136 | tf_op jit(solution)/shard_map/ppermute | solution.py:642
  38.7 11.5 %collective-permute-start.10 = (bf16[48,16,128]{2,1,0:T(8,128)(2,1)S(1)}, bf16[48,16,128]{2,1,0:T(8,128)(2,1)S(1)}, u32[]{:S(2)}, u32[]{:S(2)}) collective-permute-start(bf16[48,16,128]{2,1,0:T(8,128)(2,1)S(1)} %get-tuple-element.55.own), channel_id=1, source_target_pairs={{1,2},{3,4},{5,6},{7,8},{9,10},{11,12},{13,14},{2,1},{4,3},{6,5},{... | collective-permute-start | bytes 589832 | tf_op jit(solution)/shard_map/ppermute | solution.py:639
  41.9 14.9 %collective-permute-start.13 = (bf16[56,16,128]{2,1,0:T(8,128)(2,1)S(1)}, bf16[56,16,128]{2,1,0:T(8,128)(2,1)S(1)}, u32[]{:S(2)}, u32[]{:S(2)}) collective-permute-start(bf16[56,16,128]{2,1,0:T(8,128)(2,1)S(1)} %pad_maximum_fusion.1), channel_id=1, source_target_pairs={{1,2},{3,4},{5,6},{7,8},{9,10},{11,12},{13,14},{2,1},{4,3},{6,5},{... | collective-permute-start | bytes 688136 | tf_op jit(solution)/shard_map/ppermute | solution.py:639
  50.2 1.7 %copy-start.6 = (bf16[3,3,192,64]{2,3,1,0:T(8,128)(2,1)S(1)}, bf16[3,3,192,64]{2,3,1,0:T(8,128)(2,1)}, u32[]{:S(2)}) copy-start(bf16[3,3,192,64]{2,3,1,0:T(8,128)(2,1)} %param.24) | copy-start | bytes 663556
  50.2 1.7 %copy-start.7 = (bf16[3,3,64,192]{3,2,1,0:T(8,128)(2,1)S(1)}, bf16[3,3,64,192]{3,2,1,0:T(8,128)(2,1)}, u32[]{:S(2)}) copy-start(bf16[3,3,64,192]{3,2,1,0:T(8,128)(2,1)} %param.25) | copy-start | bytes 663556
  50.2 1.7 %copy-start.8 = (bf16[3,3,64,192]{3,2,1,0:T(8,128)(2,1)S(1)}, bf16[3,3,64,192]{3,2,1,0:T(8,128)(2,1)}, u32[]{:S(2)}) copy-start(bf16[3,3,64,192]{3,2,1,0:T(8,128)(2,1)} %param.26) | copy-start | bytes 663556
  50.2 1.7 %copy-start.10 = (bf16[64,16]{0,1:T(8,128)(2,1)S(1)}, bf16[64,16]{0,1:T(8,128)(2,1)}, u32[]{:S(2)}) copy-start(bf16[64,16]{0,1:T(8,128)(2,1)} %param.27) | copy-start | bytes 6148
  51.3 2.7 %collective-permute-start.12 = (bf16[24,16,128]{2,1,0:T(8,128)(2,1)S(1)}, bf16[24,16,128]{2,1,0:T(8,128)(2,1)S(1)}, u32[]{:S(2)}, u32[]{:S(2)}) collective-permute-start(bf16[24,16,128]{2,1,0:T(8,128)(2,1)S(1)} %get-tuple-element.60), channel_id=1, source_target_pairs={{0,1},{1,0},{2,3},{3,2},{4,5},{5,4},{6,7},{7,6},{8,9},{9,8},{10,11... | collective-permute-start | bytes 294920 | tf_op jit(solution)/shard_map/ppermute | solution.py:642
  51.4 2.6 %collective-permute-start.11 = (bf16[24,16,128]{2,1,0:T(8,128)(2,1)S(1)}, bf16[24,16,128]{2,1,0:T(8,128)(2,1)S(1)}, u32[]{:S(2)}, u32[]{:S(2)}) collective-permute-start(bf16[24,16,128]{2,1,0:T(8,128)(2,1)S(1)} %get-tuple-element.59), channel_id=1, source_target_pairs={{0,1},{1,0},{2,3},{3,2},{4,5},{5,4},{6,7},{7,6},{8,9},{9,8},{10,11... | collective-permute-start | bytes 294920 | tf_op jit(solution)/shard_map/ppermute | solution.py:642

commit v10 on v9

--- a/solution.py
+++ b/solution.py
@@ -218,16 +218,15 @@
         for t in range(4):
             at = FB * C1 + frame * FB * PATCH + t * LANES
             patches = jnp.concatenate([get(r, slice(at, at + LANES)) for r in range(count)], axis=0)
-            for half in range(2):
-                acc = jnp.dot(patches, w_stem[:, half * 512 : half * 512 + 512], preferred_element_type=F32)
-                acc = leaky(acc).astype(BF)
-                for k in range(4):
-                    block = acc[:, k * LANES : (k + 1) * LANES].reshape(count, SUB, LANES)
-                    at_block = 8 * t + 4 * half + k
-                    if frame == 0:
-                        p1[:, 1 + at_block] = block
-                    else:
-                        stem2[:, at_block] = block
+            acc = leaky(jnp.dot(patches, w_stem[...], preferred_element_type=F32))
+            for k in range(8):
+                tile = acc[:, k // 2 * LANES : (k // 2 + 1) * LANES]
+                tile = swap_halves(tile) if k % 2 else tile
+                block = tile.astype(BF).reshape(count, SUB, LANES)
+                if frame == 0:
+                    p1[:, 1 + 8 * t + k] = block
+                else:
+                    stem2[:, 8 * t + k] = block
     for r in range(count):
         for k in range(FB // 2):
             pair = get(r, slice(k * LANES, (k + 1) * LANES))
@@ -254,7 +253,7 @@
 
 def fine_encoder_body(
     p1_own, stem2_own, inside, outer, inner, w_stem, w_gru, w_down,
-    state_out, low_own, to_outer, to_inner, second_outer, second_inner, state_outer, state_inner,
+    state_out, low_own, to_outer, to_inner, state_outer, state_inner,
     p1_halo, stem2_halo, p2_rest, p3,
 ):
     upper, first, rows = place(4)
@@ -302,11 +301,11 @@
 
         @pl.when(outward)
         def _():
-            put(second_outer, 0, tiles)
+            put(to_outer, 2, tiles)
 
         @pl.when(jnp.logical_not(outward))
         def _():
-            put(second_inner, 0, tiles)
+            put(to_inner, 2, tiles)
 
     for r in range(4):
         for k in range(FB // 2):
@@ -384,15 +383,15 @@
 
 
 def coarse_second_body(
-    low_own, second_outer, second_inner, h1_given, h1_inner, w_x, w_h, state, h1, x2, acc_x, acc_h
+    low_own, low_outer, low_inner, h1_given, h1_inner, w_x, w_h, state, h1, x2, acc_x, acc_h
 ):
     upper, _, _ = place(2)
     zero_tail(acc_x)
     zero_tail(acc_h)
-    put_packed(x2, 0, either(upper, second_outer, 0, second_inner, 0))
+    put_packed(x2, 0, either(upper, low_outer, 2, low_inner, 2))
     put_packed(x2, 1, packed_tiles(low_own, 2))
     put_packed(x2, 2, packed_tiles(low_own, 3))
-    put_packed(x2, 3, either(upper, second_inner, 0, second_outer, 0))
+    put_packed(x2, 3, either(upper, low_inner, 2, low_outer, 2))
     put_packed(h1, jnp.where(upper, 3, 0), packed_tiles(h1_inner, 0))
     for slot in range(2):
         idx = jnp.where(upper, slot, 1 - slot)
@@ -572,9 +571,9 @@
         w_down[at + C1 : at + LANES, :LANES] = down[k, :, :LANES]
         w_down[at + C1 : at + LANES, LANES:] = to_lower(down[k, :, LANES:])
     w_stem[...] = jnp.zeros(w_stem.shape, BF)
-    wide = to_lower(stem[...])
     for k in range(8):
-        w_stem[k * PATCH : (k + 1) * PATCH, k * LANES : (k + 1) * LANES] = wide
+        wide = to_upper(stem[...]) if k % 2 else to_lower(stem[...])
+        w_stem[k * PATCH : (k + 1) * PATCH, k // 2 * LANES : (k // 2 + 1) * LANES] = wide
 
 
 def prepare_forecaster_body(*refs):
@@ -672,7 +671,7 @@
     w_stem, w_enc, w_down = prepare(
         prepare_encoder_body,
         [enc_stem, enc_fine_x.reshape(kernel), enc_fine_h.reshape(kernel), enc_down.reshape(kernel)],
-        [(8 * PATCH, 8 * LANES), wide, wide],
+        [(8 * PATCH, 4 * LANES), wide, wide],
     )
     w_up, w_fc, w_head = prepare(
         prepare_forecaster_body,
@@ -681,7 +680,7 @@
     )
     coarse_o, coarse_i = outer_swap(coarse), inner_swap(coarse)
 
-    halo = (2 * ROW_TILES, SUB, LANES)
+    halo = (3 * ROW_TILES, SUB, LANES)
     row = (ROW_TILES, SUB, LANES)
     edge = (2, FB // 2, SUB, LANES)
 
@@ -691,14 +690,13 @@
     p1_own, stem2_own, inside = call(
         fine_own_body, on_chip(own, w_stem, w_enc), [fine_shape(4), fine_shape(4, FB), fine_shape(2)], []
     )
-    state_f, low_own, to_outer, to_inner, second_o, second_i, state_fo, state_fi = call(
+    state_f, low_own, to_outer, to_inner, state_fo, state_fi = call(
         fine_encoder_body,
         on_chip(p1_own, stem2_own, inside, outer, inner, w_stem, w_enc, w_down),
-        [(4, FB // 2, SUB, LANES), (4 * ROW_TILES, SUB, LANES), halo, halo, row, row, edge, edge],
+        [(4, FB // 2, SUB, LANES), (4 * ROW_TILES, SUB, LANES), halo, halo, edge, edge],
         [fine_buf(5), pltpu.VMEM(fine_shape(5, FB), BF), fine_buf(5), fine_buf(9)],
     )
     got_o, got_i = outer_swap(to_outer), inner_swap(to_inner)
-    second_o, second_i = outer_swap(second_o), inner_swap(second_i)
 
     acc_first, h_first = call(
         coarse_state_body,
@@ -718,7 +716,7 @@
     )
     state_c, _ = call(
         coarse_second_body,
-        on_chip(low_own, second_o, second_i, h1, h1_inner, w_x, w_h),
+        on_chip(low_own, got_o, got_i, h1, h1_inner, w_x, w_h),
         [(2 * ROW_TILES, SUB, LANES), four],
         [coarse_buf(4), acc_buf, acc_buf],
         {3: 1},

time: 64.9 us -> 68.3 us (1.052)
  waiting for transfers between devices: 7.81 us -> 13.4 us
  starting transfers between devices: 21.4 us -> 16.9 us
  local copies, waits for them, and re-layouts: 3.89 us -> 6.43 us
    ppermute x6 -> x5, waiting for transfers between devices: 7.79 us -> 13.4 us  [outer_swap(): return lax.ppermute(x, LINE, across)]
    ppermute x6 -> x5, starting transfers between devices: 18.2 us -> 15 us  [outer_swap(): return lax.ppermute(x, LINE, across)]
    unnamed x24 -> x26, local copies, waits for them, and re-layouts: 2.12 us -> 4.74 us
    ppermute x8 -> x7, starting transfers between devices: 3.23 us -> 1.88 us  [inner_swap(): return lax.ppermute(x, 'section', [(0, 1), (1, 0)])]
  transfers between devices with their start and end apart: 14 -> 12, of which waited for: 2 -> 3; matrix products, arithmetic and copies ran while one was open for 2% -> 0% of each run, Pallas kernels for 32% -> 21%
where the time goes in v10:
time: 68.3 us; the launch traced here: 67.7 us
  Pallas kernels  30.6 us (45%)
  starting transfers between devices  16.9 us (25%)
  waiting for transfers between devices  13.4 us (20%)
  local copies, waits for them, and re-layouts  6.43 us (9%)
    pallas_call x14, Pallas kernels, call(): pl.pallas_call(body, out_shape=[s if isinstance(s, jax.ShapeDtypeStruct)...  30.6 us
    ppermute x5, starting transfers between devices, outer_swap(): return lax.ppermute(x, LINE, across)  15 us
    ppermute x5, waiting for transfers between devices, outer_swap(): return lax.ppermute(x, LINE, across)  13.4 us
    unnamed x26, local copies, waits for them, and re-layouts  4.74 us
    ppermute x7, starting transfers between devices, inner_swap(): return lax.ppermute(x, 'section', [(0, 1), (1, 0)])  1.88 us
  transfers between devices with their start and end apart: 12, of which 3 were waited for; matrix products, arithmetic and copies ran while one was open for 0% of the time, Pallas kernels for 21%

profile of v10, /device:TPU:19, one launch (start us, length us, event | category | flops | bytes accessed | tf_op | source)
XLA Modules:
  0.0 67.7 jit_solution(9768691644228366096)
XLA Ops:
  0.0 0.9 %fusion = (bf16[1,4,8192]{2,1,0:T(4,128)(2,1)S(1)}, bf16[1,4,8192]{2,1,0:T(4,128)(2,1)S(1)}) fusion(bf16[2,4,8192]{2,1,0:T(4,128)(2,1)} %param.14), kind=kLoop, calls=%fused_computation.6 | loop fusion | bytes 262144 | tf_op jit(solution)/shard_map/slice | solution.py:657
  0.9 1.1 %copy.30 = bf16[1,4,16,2048]{3,2,1,0:T(8,128)(2,1)S(1)} copy(bf16[1,4,16,2048]{3,1,2,0:T(4,128)(2,1)} %bitcast.55) | data formatting | bytes 524288
  2.1 0.1 shard_map.136
  2.1 3.7 %collective-permute-start = (bf16[3,16,3072]{2,1,0:T(8,128)(2,1)S(1)}, bf16[3,16,3072]{2,1,0:T(8,128)(2,1)S(1)}, u32[]{:S(2)}, u32[]{:S(2)}) collective-permute-start(bf16[3,16,3072]{2,1,0:T(8,128)(2,1)S(1)} %get-tuple-element.41), channel_id=1, source_target_pairs={{1,2},{3,4},{5,6},{7,8},{9,10},{11,12},{13,14},{2,1},{4,3},{6,5},{... | collective-permute-start | bytes 884744 | tf_op jit(solution)/shard_map/ppermute | solution.py:638
  6.0 1.0 %copy-done.3 = bf16[3,3,64,192]{3,2,1,0:T(8,128)(2,1)S(1)} copy-done((bf16[3,3,64,192]{3,2,1,0:T(8,128)(2,1)S(1)}, bf16[3,3,64,192]{3,2,1,0:T(8,128)(2,1)}, u32[]{:S(2)}) %copy-start.3) | copy-done | bytes 221208
  6.9 1.0 %copy-done.4 = bf16[3,3,64,192]{3,2,1,0:T(8,128)(2,1)S(1)} copy-done((bf16[3,3,64,192]{3,2,1,0:T(8,128)(2,1)S(1)}, bf16[3,3,64,192]{3,2,1,0:T(8,128)(2,1)}, u32[]{:S(2)}) %copy-start.4) | copy-done | bytes 221208
  7.9 1.0 %copy-done.5 = bf16[3,3,64,192]{3,2,1,0:T(8,128)(2,1)S(1)} copy-done((bf16[3,3,64,192]{3,2,1,0:T(8,128)(2,1)S(1)}, bf16[3,3,64,192]{3,2,1,0:T(8,128)(2,1)}, u32[]{:S(2)}) %copy-start.5) | copy-done | bytes 221208
  8.8 0.7 %copy-done.9 = bf16[16,64]{1,0:T(8,128)(2,1)S(1)} copy-done((bf16[16,64]{1,0:T(8,128)(2,1)S(1)}, bf16[16,64]{1,0:T(8,128)(2,1)}, u32[]{:S(2)}) %copy-start.9) | copy-done | bytes 2072
  9.5 0.5 shard_map.137
  10.0 1.3 %shard_map.138 = (bf16[4,34,16,128]{3,2,1,0:T(8,128)(2,1)S(1)}, bf16[4,32,16,128]{3,2,1,0:T(8,128)(2,1)S(1)}, bf16[2,34,16,128]{3,2,1,0:T(8,128)(2,1)S(1)}) custom-call(bf16[4,16,3072]{2,1,0:T(8,128)(2,1)S(1)} %get-tuple-element.35.own, bf16[128,512]{1,0:T(8,128)(2,1)S(1)} %get-tuple-element.36.w_stem, bf16[1152,256]{1,0:T(8,128)(2,1)S(1)} %get-tuple-element.37.w_gru), custom_call_target="tpu_custom_call" | custom-call | tf_op jit(solution)/shard_map/pallas_call | solution.py:606
  11.3 2.1 %collective-permute-done.outer = bf16[3,16,3072]{2,1,0:T(8,128)(2,1)S(1)} collective-permute-done((bf16[3,16,3072]{2,1,0:T(8,128)(2,1)S(1)}, bf16[3,16,3072]{2,1,0:T(8,128)(2,1)S(1)}, u32[]{:S(2)}, u32[]{:S(2)}) %collective-permute-start) | collective-permute-done | bytes 294944 | tf_op jit(solution)/shard_map/ppermute | solution.py:638
  13.4 5.5 %shard_map.139 = (bf16[4,16,16,128]{3,2,1,0:T(8,128)(2,1)S(1)}, bf16[96,16,128]{2,1,0:T(8,128)(2,1)S(1)}, bf16[72,16,128]{2,1,0:T(8,128)(2,1)S(1)}, bf16[72,16,1...) custom-call(bf16[4,34,16,128]{3,2,1,0:T(8,128)(2,1)S(1)} %get-tuple-element.38.p1_ow, ...), custom_call_target="tpu_custom_call" | custom-call | tf_op jit(solution)/shard_map/pallas_call | solution.py:606
  19.1 0.5 collective-permute-start.5
  19.6 3.6 %collective-permute-start.4 = (bf16[2,16,3072]{2,1,0:T(8,128)(2,1)S(1)}, bf16[2,16,3072]{2,1,0:T(8,128)(2,1)S(1)}, u32[]{:S(2)}, u32[]{:S(2)}) collective-permute-start(bf16[2,16,3072]{2,1,0:T(8,128)(2,1)S(1)} %bitcast.44), channel_id=1, source_target_pairs={{1,2},{3,4},{5,6},{7,8},{9,10},{11,12},{13,14},{2,1},{4,3},{6,5},{... | collective-permute-start | bytes 589832 | tf_op jit(solution)/shard_map/ppermute | solution.py:638
  23.3 2.1 %collective-permute-start.2 = (bf16[72,16,128]{2,1,0:T(8,128)(2,1)S(1)}, bf16[72,16,128]{2,1,0:T(8,128)(2,1)S(1)}, u32[]{:S(2)}, u32[]{:S(2)}) collective-permute-start(bf16[72,16,128]{2,1,0:T(8,128)(2,1)S(1)} %get-tuple-element.45), channel_id=1, source_target_pairs={{1,2},{3,4},{5,6},{7,8},{9,10},{11,12},{13,14},{2,1},{4,3},{6,5},{... | collective-permute-start | bytes 884744 | tf_op jit(solution)/shard_map/ppermute | solution.py:638
  25.4 6.5 %collective-permute-done.4.outer = bf16[2,16,3072]{2,1,0:T(8,128)(2,1)S(1)} collective-permute-done((bf16[2,16,3072]{2,1,0:T(8,128)(2,1)S(1)}, bf16[2,16,3072]{2,1,0:T(8,128)(2,1)S(1)}, u32[]{:S(2)}, u32[]{:S(2)}) %collective-permute-start.4) | collective-permute-done | bytes 196640 | tf_op jit(solution)/shard_map/ppermute | solution.py:638
  31.9 2.9 %shard_map.140 = (f32[3,256,640]{2,1,0:T(8,128)S(1)}, bf16[3,18,16,512]{3,2,1,0:T(8,128)(2,1)S(1)}) custom-call(bf16[2,16,3072]{2,1,0:T(8,128)(2,1)S(1)} %bitcast.45, bf16[2,16,3072]{2,1,0:T(8,128)(2,1)S(1)} %collective-permute-done.4.outer, bf16[2,16,3072]{2,1,0:T(8,128)(2,1)S(1)} %collective-permute-done.5.inner, bf16[1728,576]{1,0:T(8,128)(2,1)S(1)} %bitcast.40), custom_call_target="tpu_custom_call" | custom-call | tf_op jit(solution)/shard_map/pallas_call | solution.py:606
  34.8 1.1 %shard_map.141 = (bf16[4,18,16,512]{3,2,1,0:T(8,128)(2,1)S(1)}, bf16[24,16,128]{2,1,0:T(8,128)(2,1)S(1)}) custom-call(bf16[96,16,128]{2,1,0:T(8,128)(2,1)S(1)} %get-tuple-element.44.low_own, bf16[72,16,128]{2,1,0:T(8,128)(2,1)S(1)} %collective-permute-done.3.low_inner, f32[3,256,640]{2,1,0:T(8,128)S(1)} %get-tuple-element.47.acc_first, ...), custom_call_target="tpu_custom_call" | custom-call | tf_op jit(solution)/shard_map/pallas_call | solution.py:606
  36.0 1.8 %shard_map.142.h1_given = bf16[4,18,16,512]{3,2,1,0:T(8,128)(2,1)S(1)} custom-call(bf16[4,18,16,512]{3,2,1,0:T(8,128)(2,1)S(1)} %get-tuple-element.49.h1_given, bf16[96,16,128]{2,1,0:T(8,128)(2,1)S(1)} %get-tuple-element.44.low_own, bf16[72,16,128]{2,1,0:T(8,128)(2,1)S(1)} %collective-permute-done.2.low_outer, ...), custom_call_target="tpu_custom_call", output_to_operand_aliasing={{}: (0, {})} | custom-call | tf_op jit(solution)/shard_map/pallas_call | solution.py:606
  37.9 3.4 %shard_map.143 = (bf16[48,16,128]{2,1,0:T(8,128)(2,1)S(1)}, bf16[4,18,16,512]{3,2,1,0:T(8,128)(2,1)S(1)}) custom-call(bf16[96,16,128]{2,1,0:T(8,128)(2,1)S(1)} %get-tuple-element.44.low_own, bf16[72,16,128]{2,1,0:T(8,128)(2,1)S(1)} %collective-permute-done.2.low_outer, ...), custom_call_target="tpu_custom_call", output_to_operand_aliasing={{1}: (3, {})} | custom-call | tf_op jit(solution)/shard_map/pallas_call | solution.py:606
  41.3 0.6 collective-permute-start.7
  41.8 3.6 %collective-permute-start.8 = (bf16[48,16,128]{2,1,0:T(8,128)(2,1)S(1)}, bf16[48,16,128]{2,1,0:T(8,128)(2,1)S(1)}, u32[]{:S(2)}, u32[]{:S(2)}) collective-permute-start(bf16[48,16,128]{2,1,0:T(8,128)(2,1)S(1)} %get-tuple-element.51.own), channel_id=1, source_target_pairs={{1,2},{3,4},{5,6},{7,8},{9,10},{11,12},{13,14},{2,1},{4,3},{6,5},{... | collective-permute-start | bytes 589832 | tf_op jit(solution)/shard_map/ppermute | solution.py:638
  45.5 1.9 %collective-permute-start.11 = (bf16[56,16,128]{2,1,0:T(8,128)(2,1)S(1)}, bf16[56,16,128]{2,1,0:T(8,128)(2,1)S(1)}, u32[]{:S(2)}, u32[]{:S(2)}) collective-permute-start(bf16[56,16,128]{2,1,0:T(8,128)(2,1)S(1)} %pad_maximum_fusion.1), channel_id=1, source_target_pairs={{1,2},{3,4},{5,6},{7,8},{9,10},{11,12},{13,14},{2,1},{4,3},{6,5},{... | collective-permute-start | bytes 688136 | tf_op jit(solution)/shard_map/ppermute | solution.py:638
  47.5 1.1 %shard_map.144 = (bf16[6,18,16,512]{3,2,1,0:T(8,128)(2,1)S(1)}, bf16[24,16,128]{2,1,0:T(8,128)(2,1)S(1)}) custom-call(bf16[48,16,128]{2,1,0:T(8,128)(2,1)S(1)} %get-tuple-element.51.own, bf16[56,16,128]{2,1,0:T(8,128)(2,1)S(1)} %collective-permute-done.7.in_near.f_inner, bf16[1728,576]{1,0:T(8,128)(2,1)S(1)} %bitcast.32), custom_call_target="tpu_custom_call" | custom-call | tf_op jit(solution)/shard_map/pallas_call | solution.py:606
  48.6 4.8 %collective-permute-done.8.outer = bf16[48,16,128]{2,1,0:T(8,128)(2,1)S(1)} collective-permute-done((bf16[48,16,128]{2,1,0:T(8,128)(2,1)S(1)}, bf16[48,16,128]{2,1,0:T(8,128)(2,1)S(1)}, u32[]{:S(2)}, u32[]{:S(2)}) %collective-permute-start.8) | collective-permute-done | bytes 196640 | tf_op jit(solution)/shard_map/ppermute | solution.py:638
  53.4 1.1 %shard_map.145 = (bf16[6,18,16,512]{3,2,1,0:T(8,128)(2,1)S(1)}, bf16[24,16,128]{2,1,0:T(8,128)(2,1)S(1)}) custom-call(bf16[6,18,16,512]{3,2,1,0:T(8,128)(2,1)S(1)} %get-tuple-element.53.s1_given, bf16[48,16,128]{2,1,0:T(8,128)(2,1)S(1)} %get-tuple-element.51.own, ...), custom_call_target="tpu_custom_call", output_to_operand_aliasing={{0}: (0, {})} | custom-call | tf_op jit(solution)/shard_map/pallas_call | solution.py:606
  54.6 0.5 collective-permute-start.9
  55.1 1.0 %shard_map.148 = (bf16[768,256]{1,0:T(8,128)(2,1)S(1)}, bf16[1152,256]{1,0:T(8,128)(2,1)S(1)}, bf16[1024,128]{1,0:T(8,128)(2,1)S(1)}) custom-call(bf16[9,64,192]{2,1,0:T(8,128)(2,1)S(1)} %bitcast.49, bf16[9,64,192]{2,1,0:T(8,128)(2,1)S(1)} %bitcast.50, bf16[9,64,192]{2,1,0:T(8,128)(2,1)S(1)} %bitcast.51, bf16[16,64]{1,0:T(8,128)(2,1)S(1)} %bitcast.54), custom_call_target="tpu_custom_call" | custom-call | tf_op jit(solution)/shard_map/pallas_call | solution.py:606
  56.1 1.1 %shard_map.146.s1_given = bf16[6,18,16,512]{3,2,1,0:T(8,128)(2,1)S(1)} custom-call(bf16[6,18,16,512]{3,2,1,0:T(8,128)(2,1)S(1)} %get-tuple-element.54.s1_given, bf16[48,16,128]{2,1,0:T(8,128)(2,1)S(1)} %get-tuple-element.51.own, bf16[48,16,128]{2,1,0:T(8,128)(2,1)S(1)} %collective-permute-done.8.outer, ...), custom_call_target="tpu_custom_call", output_to_operand_aliasing={{}: (0, {})} | custom-call | tf_op jit(solution)/shard_map/pallas_call | solution.py:606
  57.2 2.7 %shard_map.147 = (bf16[6,18,16,512]{3,2,1,0:T(8,128)(2,1)S(1)}, bf16[5,18,16,512]{3,2,1,0:T(8,128)(2,1)S(1)}) custom-call(bf16[6,18,16,512]{3,2,1,0:T(8,128)(2,1)S(1)} %shard_map.146.s1_given, bf16[24,16,128]{2,1,0:T(8,128)(2,1)S(1)} %collective-permute-done.9.in_near, ...), custom_call_target="tpu_custom_call", output_to_operand_aliasing={{0}: (0, {})} | custom-call | tf_op jit(solution)/shard_map/pallas_call | solution.py:606
  59.9 7.0 %shard_map.149 = (bf16[2,4,16,512]{3,2,1,0:T(8,128)(2,1)S(1)}, bf16[6,18,16,512]{3,2,1,0:T(8,128)(2,1)S(1)}, bf16[5,18,16,512]{3,2,1,0:T(8,128)(2,1)S(1)}) custom-call(bf16[6,18,16,512]{3,2,1,0:T(8,128)(2,1)S(1)} %get-tuple-element.57.s1_given, ...), custom_call_target="tpu_custom_call", output_to_operand_aliasing={{1}: (0, {}), {2}: (1, {})} | custom-call | tf_op jit(solution)/shard_map/pallas_call | solution.py:606
  66.9 0.7 %reshape.61 = bf16[2,4,8192]{2,1,0:T(4,128)(2,1)} reshape(bf16[2,4,16,512]{3,2,1,0:T(8,128)(2,1)S(1)} %get-tuple-element.64) | data formatting | bytes 262144 | tf_op jit(solution)/shard_map/reshape | solution.py:746
  (39 shorter events, 0.5 us)
Async XLA Ops:
  2.1 11.3 %collective-permute-start = (bf16[3,16,3072]{2,1,0:T(8,128)(2,1)S(1)}, bf16[3,16,3072]{2,1,0:T(8,128)(2,1)S(1)}, u32[]{:S(2)}, u32[]{:S(2)}) collective-permute-start(bf16[3,16,3072]{2,1,0:T(8,128)(2,1)S(1)} %get-tuple-element.41), channel_id=1, source_target_pairs={{1,2},{3,4},{5,6},{7,8},{9,10},{11,12},{13,14},{2,1},{4,3},{6,5},{... | collective-permute-start | bytes 884744 | tf_op jit(solution)/shard_map/ppermute | solution.py:638
  5.9 7.6 %collective-permute-start.1 = (bf16[3,16,3072]{2,1,0:T(8,128)(2,1)S(1)}, bf16[3,16,3072]{2,1,0:T(8,128)(2,1)S(1)}, u32[]{:S(2)}, u32[]{:S(2)}) collective-permute-start(bf16[3,16,3072]{2,1,0:T(8,128)(2,1)S(1)} %get-tuple-element.42), channel_id=1, source_target_pairs={{0,1},{1,0},{2,3},{3,2},{4,5},{5,4},{6,7},{7,6},{8,9},{9,8},{10,11... | collective-permute-start | bytes 884744 | tf_op jit(solution)/shard_map/ppermute | solution.py:641
  5.9 1.0 %copy-start.3 = (bf16[3,3,64,192]{3,2,1,0:T(8,128)(2,1)S(1)}, bf16[3,3,64,192]{3,2,1,0:T(8,128)(2,1)}, u32[]{:S(2)}) copy-start(bf16[3,3,64,192]{3,2,1,0:T(8,128)(2,1)} %param.18) | copy-start | bytes 663556
  6.9 1.0 %copy-start.4 = (bf16[3,3,64,192]{3,2,1,0:T(8,128)(2,1)S(1)}, bf16[3,3,64,192]{3,2,1,0:T(8,128)(2,1)}, u32[]{:S(2)}) copy-start(bf16[3,3,64,192]{3,2,1,0:T(8,128)(2,1)} %param.19) | copy-start | bytes 663556
  7.9 1.0 %copy-start.5 = (bf16[3,3,64,192]{3,2,1,0:T(8,128)(2,1)S(1)}, bf16[3,3,64,192]{3,2,1,0:T(8,128)(2,1)}, u32[]{:S(2)}) copy-start(bf16[3,3,64,192]{3,2,1,0:T(8,128)(2,1)} %param.20) | copy-start | bytes 663556
  8.8 0.7 %copy-start.9 = (bf16[16,64]{1,0:T(8,128)(2,1)S(1)}, bf16[16,64]{1,0:T(8,128)(2,1)}, u32[]{:S(2)}) copy-start(bf16[16,64]{1,0:T(8,128)(2,1)} %refs_0_.1) | copy-start | bytes 6148
  11.3 7.7 %copy-start.11 = (bf16[2,49152]{1,0:T(2,128)(2,1)S(1)}, bf16[2,49152]{1,0:T(2,128)(2,1)}, u32[]{:S(2)}) copy-start(bf16[2,49152]{1,0:T(2,128)(2,1)} %param.16) | copy-start | bytes 589828
  13.4 18.5 %copy-start.2 = (bf16[3,3,192,576]{3,2,1,0:T(8,128)(2,1)S(1)}, bf16[3,3,192,576]{3,2,1,0:T(8,128)(2,1)}, u32[]{:S(2)}) copy-start(bf16[3,3,192,576]{3,2,1,0:T(8,128)(2,1)} %param.22) | copy-start | bytes 5971972
  19.0 15.8 %copy-start.1 = (bf16[3,3,192,576]{3,2,1,0:T(8,128)(2,1)S(1)}, bf16[3,3,192,576]{3,2,1,0:T(8,128)(2,1)}, u32[]{:S(2)}) copy-start(bf16[3,3,192,576]{3,2,1,0:T(8,128)(2,1)} %param.21) | copy-start | bytes 5971972
  19.0 15.8 %collective-permute-start.3 = (bf16[72,16,128]{2,1,0:T(8,128)(2,1)S(1)}, bf16[72,16,128]{2,1,0:T(8,128)(2,1)S(1)}, u32[]{:S(2)}, u32[]{:S(2)}) collective-permute-start(bf16[72,16,128]{2,1,0:T(8,128)(2,1)S(1)} %get-tuple-element.46), channel_id=1, source_target_pairs={{0,1},{1,0},{2,3},{3,2},{4,5},{5,4},{6,7},{7,6},{8,9},{9,8},{10,11... | collective-permute-start | bytes 884744 | tf_op jit(solution)/shard_map/ppermute | solution.py:641
  19.1 6.3 %collective-permute-start.5 = (bf16[2,16,3072]{2,1,0:T(8,128)(2,1)S(1)}, bf16[2,16,3072]{2,1,0:T(8,128)(2,1)S(1)}, u32[]{:S(2)}, u32[]{:S(2)}) collective-permute-start(bf16[2,16,3072]{2,1,0:T(8,128)(2,1)S(1)} %bitcast.43), channel_id=1, source_target_pairs={{0,1},{1,0},{2,3},{3,2},{4,5},{5,4},{6,7},{7,6},{8,9},{9,8},{10,11... | collective-permute-start | bytes 589832 | tf_op jit(solution)/shard_map/ppermute | solution.py:641
  19.6 12.2 %collective-permute-start.4 = (bf16[2,16,3072]{2,1,0:T(8,128)(2,1)S(1)}, bf16[2,16,3072]{2,1,0:T(8,128)(2,1)S(1)}, u32[]{:S(2)}, u32[]{:S(2)}) collective-permute-start(bf16[2,16,3072]{2,1,0:T(8,128)(2,1)S(1)} %bitcast.44), channel_id=1, source_target_pairs={{1,2},{3,4},{5,6},{7,8},{9,10},{11,12},{13,14},{2,1},{4,3},{6,5},{... | collective-permute-start | bytes 589832 | tf_op jit(solution)/shard_map/ppermute | solution.py:638
  23.3 12.7 %collective-permute-start.2 = (bf16[72,16,128]{2,1,0:T(8,128)(2,1)S(1)}, bf16[72,16,128]{2,1,0:T(8,128)(2,1)S(1)}, u32[]{:S(2)}, u32[]{:S(2)}) collective-permute-start(bf16[72,16,128]{2,1,0:T(8,128)(2,1)S(1)} %get-tuple-element.45), channel_id=1, source_target_pairs={{1,2},{3,4},{5,6},{7,8},{9,10},{11,12},{13,14},{2,1},{4,3},{6,5},{... | collective-permute-start | bytes 884744 | tf_op jit(solution)/shard_map/ppermute | solution.py:638
  35.9 1.9 %collective-permute-start.6 = (bf16[24,16,128]{2,1,0:T(8,128)(2,1)S(1)}, bf16[24,16,128]{2,1,0:T(8,128)(2,1)S(1)}, u32[]{:S(2)}, u32[]{:S(2)}) collective-permute-start(bf16[24,16,128]{2,1,0:T(8,128)(2,1)S(1)} %get-tuple-element.50), channel_id=1, source_target_pairs={{0,1},{1,0},{2,3},{3,2},{4,5},{5,4},{6,7},{7,6},{8,9},{9,8},{10,11... | collective-permute-start | bytes 294920 | tf_op jit(solution)/shard_map/ppermute | solution.py:641
  37.9 9.6 %copy-start = (bf16[3,3,192,576]{3,2,1,0:T(8,128)(2,1)S(1)}, bf16[3,3,192,576]{3,2,1,0:T(8,128)(2,1)}, u32[]{:S(2)}) copy-start(bf16[3,3,192,576]{3,2,1,0:T(8,128)(2,1)} %param.23) | copy-start | bytes 5971972
  41.3 4.2 %collective-permute-start.7 = (bf16[56,16,128]{2,1,0:T(8,128)(2,1)S(1)}, bf16[56,16,128]{2,1,0:T(8,128)(2,1)S(1)}, u32[]{:S(2)}, u32[]{:S(2)}) collective-permute-start(bf16[56,16,128]{2,1,0:T(8,128)(2,1)S(1)} %pad_maximum_fusion), channel_id=1, source_target_pairs={{0,1},{1,0},{2,3},{3,2},{4,5},{5,4},{6,7},{7,6},{8,9},{9,8},{10,11... | collective-permute-start | bytes 688136 | tf_op jit(solution)/shard_map/ppermute | solution.py:641
  41.8 11.5 %collective-permute-start.8 = (bf16[48,16,128]{2,1,0:T(8,128)(2,1)S(1)}, bf16[48,16,128]{2,1,0:T(8,128)(2,1)S(1)}, u32[]{:S(2)}, u32[]{:S(2)}) collective-permute-start(bf16[48,16,128]{2,1,0:T(8,128)(2,1)S(1)} %get-tuple-element.51.own), channel_id=1, source_target_pairs={{1,2},{3,4},{5,6},{7,8},{9,10},{11,12},{13,14},{2,1},{4,3},{6,5},{... | collective-permute-start | bytes 589832 | tf_op jit(solution)/shard_map/ppermute | solution.py:638
  45.5 14.4 %collective-permute-start.11 = (bf16[56,16,128]{2,1,0:T(8,128)(2,1)S(1)}, bf16[56,16,128]{2,1,0:T(8,128)(2,1)S(1)}, u32[]{:S(2)}, u32[]{:S(2)}) collective-permute-start(bf16[56,16,128]{2,1,0:T(8,128)(2,1)S(1)} %pad_maximum_fusion.1), channel_id=1, source_target_pairs={{1,2},{3,4},{5,6},{7,8},{9,10},{11,12},{13,14},{2,1},{4,3},{6,5},{... | collective-permute-start | bytes 688136 | tf_op jit(solution)/shard_map/ppermute | solution.py:638
  53.4 1.7 %copy-start.6 = (bf16[3,3,192,64]{2,3,1,0:T(8,128)(2,1)S(1)}, bf16[3,3,192,64]{2,3,1,0:T(8,128)(2,1)}, u32[]{:S(2)}) copy-start(bf16[3,3,192,64]{2,3,1,0:T(8,128)(2,1)} %param.24) | copy-start | bytes 663556
  53.4 1.7 %copy-start.7 = (bf16[3,3,64,192]{3,2,1,0:T(8,128)(2,1)S(1)}, bf16[3,3,64,192]{3,2,1,0:T(8,128)(2,1)}, u32[]{:S(2)}) copy-start(bf16[3,3,64,192]{3,2,1,0:T(8,128)(2,1)} %param.25) | copy-start | bytes 663556
  53.4 1.7 %copy-start.8 = (bf16[3,3,64,192]{3,2,1,0:T(8,128)(2,1)S(1)}, bf16[3,3,64,192]{3,2,1,0:T(8,128)(2,1)}, u32[]{:S(2)}) copy-start(bf16[3,3,64,192]{3,2,1,0:T(8,128)(2,1)} %param.26) | copy-start | bytes 663556
  53.4 1.7 %copy-start.10 = (bf16[64,16]{0,1:T(8,128)(2,1)S(1)}, bf16[64,16]{0,1:T(8,128)(2,1)}, u32[]{:S(2)}) copy-start(bf16[64,16]{0,1:T(8,128)(2,1)} %param.27) | copy-start | bytes 6148
  54.5 2.7 %collective-permute-start.10 = (bf16[24,16,128]{2,1,0:T(8,128)(2,1)S(1)}, bf16[24,16,128]{2,1,0:T(8,128)(2,1)S(1)}, u32[]{:S(2)}, u32[]{:S(2)}) collective-permute-start(bf16[24,16,128]{2,1,0:T(8,128)(2,1)S(1)} %get-tuple-element.56), channel_id=1, source_target_pairs={{0,1},{1,0},{2,3},{3,2},{4,5},{5,4},{6,7},{7,6},{8,9},{9,8},{10,11... | collective-permute-start | bytes 294920 | tf_op jit(solution)/shard_map/ppermute | solution.py:641
  54.6 2.6 %collective-permute-start.9 = (bf16[24,16,128]{2,1,0:T(8,128)(2,1)S(1)}, bf16[24,16,128]{2,1,0:T(8,128)(2,1)S(1)}, u32[]{:S(2)}, u32[]{:S(2)}) collective-permute-start(bf16[24,16,128]{2,1,0:T(8,128)(2,1)S(1)} %get-tuple-element.55), channel_id=1, source_target_pairs={{0,1},{1,0},{2,3},{3,2},{4,5},{5,4},{6,7},{7,6},{8,9},{9,8},{10,11... | collective-permute-start | bytes 294920 | tf_op jit(solution)/shard_map/ppermute | solution.py:641

commit v11 on v10

--- a/solution.py
+++ b/solution.py
@@ -253,8 +253,7 @@
 
 def fine_encoder_body(
     p1_own, stem2_own, inside, outer, inner, w_stem, w_gru, w_down,
-    state_out, low_own, to_outer, to_inner, state_outer, state_inner,
-    p1_halo, stem2_halo, p2_rest, p3,
+    low_own, to_outer, to_inner, p3, p1_halo, stem2_halo, p2_rest,
 ):
     upper, first, rows = place(4)
     lo = low_half((1, SUB, LANES))
@@ -307,6 +306,10 @@
         def _():
             put(to_inner, 2, tiles)
 
+
+def fine_state_body(p3, state_out, state_outer, state_inner):
+    upper, _, _ = place(4)
+    lo = low_half((1, SUB, LANES))
     for r in range(4):
         for k in range(FB // 2):
             state_out[r, k] = jnp.where(lo[0], swap_bf(p3[3 + r, 1 + 2 * k]), p3[3 + r, 2 + 2 * k])
@@ -690,12 +693,13 @@
     p1_own, stem2_own, inside = call(
         fine_own_body, on_chip(own, w_stem, w_enc), [fine_shape(4), fine_shape(4, FB), fine_shape(2)], []
     )
-    state_f, low_own, to_outer, to_inner, state_fo, state_fi = call(
+    low_own, to_outer, to_inner, p3 = call(
         fine_encoder_body,
         on_chip(p1_own, stem2_own, inside, outer, inner, w_stem, w_enc, w_down),
-        [(4, FB // 2, SUB, LANES), (4 * ROW_TILES, SUB, LANES), halo, halo, edge, edge],
-        [fine_buf(5), pltpu.VMEM(fine_shape(5, FB), BF), fine_buf(5), fine_buf(9)],
-    )
+        [(4 * ROW_TILES, SUB, LANES), halo, halo, fine_shape(9)],
+        [fine_buf(5), pltpu.VMEM(fine_shape(5, FB), BF), fine_buf(5)],
+    )
+    state_f, state_fo, state_fi = call(fine_state_body, on_chip(p3), [(4, FB // 2, SUB, LANES), edge, edge], [])
     got_o, got_i = outer_swap(to_outer), inner_swap(to_inner)
 
     acc_first, h_first = call(

time: 68.3 us -> 68.3 us (level)
    pallas_call x14 -> x15, Pallas kernels: 30.6 us -> 30.5 us  [call(): pl.pallas_call(body, out_shape=[s if isinstance(s, jax.ShapeDtypeStruct)...]
  transfers between devices with their start and end apart: 12 -> 12, of which waited for: 3 -> 3; matrix products, arithmetic and copies ran while one was open for 0% -> 0% of each run, Pallas kernels for 21% -> 22%
where the time goes in v11:
time: 68.3 us; the launch traced here: 67.7 us
  Pallas kernels  30.5 us (45%)
  starting transfers between devices  16.9 us (25%)
  waiting for transfers between devices  13.4 us (20%)
  local copies, waits for them, and re-layouts  6.43 us (9%)
    pallas_call x15, Pallas kernels, call(): pl.pallas_call(body, out_shape=[s if isinstance(s, jax.ShapeDtypeStruct)...  30.5 us
    ppermute x5, starting transfers between devices, outer_swap(): return lax.ppermute(x, LINE, across)  15 us
    ppermute x5, waiting for transfers between devices, outer_swap(): return lax.ppermute(x, LINE, across)  13.4 us
    unnamed x26, local copies, waits for them, and re-layouts  4.74 us
    ppermute x7, starting transfers between devices, inner_swap(): return lax.ppermute(x, 'section', [(0, 1), (1, 0)])  1.89 us
  transfers between devices with their start and end apart: 12, of which 3 were waited for; matrix products, arithmetic and copies ran while one was open for 0% of the time, Pallas kernels for 22%

profile of v11, /device:TPU:19, one launch (start us, length us, event | category | flops | bytes accessed | tf_op | source)
XLA Modules:
  0.0 67.7 jit_solution(14403852835515901736)
XLA Ops:
  0.0 0.9 %fusion = (bf16[1,4,8192]{2,1,0:T(4,128)(2,1)S(1)}, bf16[1,4,8192]{2,1,0:T(4,128)(2,1)S(1)}) fusion(bf16[2,4,8192]{2,1,0:T(4,128)(2,1)} %param.14), kind=kLoop, calls=%fused_computation.6 | loop fusion | bytes 262144 | tf_op jit(solution)/shard_map/slice | solution.py:660
  0.9 1.1 %copy.30 = bf16[1,4,16,2048]{3,2,1,0:T(8,128)(2,1)S(1)} copy(bf16[1,4,16,2048]{3,1,2,0:T(4,128)(2,1)} %bitcast.55) | data formatting | bytes 524288
  2.1 3.7 %collective-permute-start = (bf16[3,16,3072]{2,1,0:T(8,128)(2,1)S(1)}, bf16[3,16,3072]{2,1,0:T(8,128)(2,1)S(1)}, u32[]{:S(2)}, u32[]{:S(2)}) collective-permute-start(bf16[3,16,3072]{2,1,0:T(8,128)(2,1)S(1)} %get-tuple-element.42), channel_id=1, source_target_pairs={{1,2},{3,4},{5,6},{7,8},{9,10},{11,12},{13,14},{2,1},{4,3},{6,5},{... | collective-permute-start | bytes 884744 | tf_op jit(solution)/shard_map/ppermute | solution.py:641
  6.0 1.0 %copy-done.3 = bf16[3,3,64,192]{3,2,1,0:T(8,128)(2,1)S(1)} copy-done((bf16[3,3,64,192]{3,2,1,0:T(8,128)(2,1)S(1)}, bf16[3,3,64,192]{3,2,1,0:T(8,128)(2,1)}, u32[]{:S(2)}) %copy-start.3) | copy-done | bytes 221208
  6.9 1.0 %copy-done.4 = bf16[3,3,64,192]{3,2,1,0:T(8,128)(2,1)S(1)} copy-done((bf16[3,3,64,192]{3,2,1,0:T(8,128)(2,1)S(1)}, bf16[3,3,64,192]{3,2,1,0:T(8,128)(2,1)}, u32[]{:S(2)}) %copy-start.4) | copy-done | bytes 221208
  7.9 1.0 %copy-done.5 = bf16[3,3,64,192]{3,2,1,0:T(8,128)(2,1)S(1)} copy-done((bf16[3,3,64,192]{3,2,1,0:T(8,128)(2,1)S(1)}, bf16[3,3,64,192]{3,2,1,0:T(8,128)(2,1)}, u32[]{:S(2)}) %copy-start.5) | copy-done | bytes 221208
  8.8 0.7 %copy-done.9 = bf16[16,64]{1,0:T(8,128)(2,1)S(1)} copy-done((bf16[16,64]{1,0:T(8,128)(2,1)S(1)}, bf16[16,64]{1,0:T(8,128)(2,1)}, u32[]{:S(2)}) %copy-start.9) | copy-done | bytes 2072
  9.5 0.5 shard_map.137
  10.0 1.3 %shard_map.138 = (bf16[4,34,16,128]{3,2,1,0:T(8,128)(2,1)S(1)}, bf16[4,32,16,128]{3,2,1,0:T(8,128)(2,1)S(1)}, bf16[2,34,16,128]{3,2,1,0:T(8,128)(2,1)S(1)}) custom-call(bf16[4,16,3072]{2,1,0:T(8,128)(2,1)S(1)} %get-tuple-element.36.own, bf16[128,512]{1,0:T(8,128)(2,1)S(1)} %get-tuple-element.37.w_stem, bf16[1152,256]{1,0:T(8,128)(2,1)S(1)} %get-tuple-element.38.w_gru), custom_call_target="tpu_custom_call" | custom-call | tf_op jit(solution)/shard_map/pallas_call | solution.py:609
  11.3 2.1 %collective-permute-done.outer = bf16[3,16,3072]{2,1,0:T(8,128)(2,1)S(1)} collective-permute-done((bf16[3,16,3072]{2,1,0:T(8,128)(2,1)S(1)}, bf16[3,16,3072]{2,1,0:T(8,128)(2,1)S(1)}, u32[]{:S(2)}, u32[]{:S(2)}) %collective-permute-start) | collective-permute-done | bytes 294944 | tf_op jit(solution)/shard_map/ppermute | solution.py:641
  13.4 5.3 %shard_map.139 = (bf16[96,16,128]{2,1,0:T(8,128)(2,1)S(1)}, bf16[72,16,128]{2,1,0:T(8,128)(2,1)S(1)}, bf16[72,16,128]{2,1,0:T(8,128)(2,1)S(1)}, bf16[9,34,16,128]{3,2,1,0:T(8,128)(2,1)S(1)}) custom-call(bf16[4,34,16,128]{3,2,1,0:T(8,128)(2,1)S(1)} %get-tuple-element.39.p1_own, bf16[4,32,16,128]{3,2,1,0:T(8,128)(2,1)S(1)} %get-tuple-element.40.stem2_own, ...), custom_call_target="tpu_custom_call" | custom-call | tf_op jit(solution)/shard_map/pallas_call | solution.py:609
  18.9 0.5 collective-permute-start.5
  19.5 3.6 %collective-permute-start.4 = (bf16[2,16,3072]{2,1,0:T(8,128)(2,1)S(1)}, bf16[2,16,3072]{2,1,0:T(8,128)(2,1)S(1)}, u32[]{:S(2)}, u32[]{:S(2)}) collective-permute-start(bf16[2,16,3072]{2,1,0:T(8,128)(2,1)S(1)} %bitcast.44), channel_id=1, source_target_pairs={{1,2},{3,4},{5,6},{7,8},{9,10},{11,12},{13,14},{2,1},{4,3},{6,5},{... | collective-permute-start | bytes 589832 | tf_op jit(solution)/shard_map/ppermute | solution.py:641
  23.1 2.1 %collective-permute-start.2 = (bf16[72,16,128]{2,1,0:T(8,128)(2,1)S(1)}, bf16[72,16,128]{2,1,0:T(8,128)(2,1)S(1)}, u32[]{:S(2)}, u32[]{:S(2)}) collective-permute-start(bf16[72,16,128]{2,1,0:T(8,128)(2,1)S(1)} %get-tuple-element.46), channel_id=1, source_target_pairs={{1,2},{3,4},{5,6},{7,8},{9,10},{11,12},{13,14},{2,1},{4,3},{6,5},{... | collective-permute-start | bytes 884744 | tf_op jit(solution)/shard_map/ppermute | solution.py:641
  25.2 6.5 %collective-permute-done.4.outer = bf16[2,16,3072]{2,1,0:T(8,128)(2,1)S(1)} collective-permute-done((bf16[2,16,3072]{2,1,0:T(8,128)(2,1)S(1)}, bf16[2,16,3072]{2,1,0:T(8,128)(2,1)S(1)}, u32[]{:S(2)}, u32[]{:S(2)}) %collective-permute-start.4) | collective-permute-done | bytes 196640 | tf_op jit(solution)/shard_map/ppermute | solution.py:641
  31.7 2.9 %shard_map.140 = (f32[3,256,640]{2,1,0:T(8,128)S(1)}, bf16[3,18,16,512]{3,2,1,0:T(8,128)(2,1)S(1)}) custom-call(bf16[2,16,3072]{2,1,0:T(8,128)(2,1)S(1)} %bitcast.45, bf16[2,16,3072]{2,1,0:T(8,128)(2,1)S(1)} %collective-permute-done.4.outer, bf16[2,16,3072]{2,1,0:T(8,128)(2,1)S(1)} %collective-permute-done.5.inner, bf16[1728,576]{1,0:T(8,128)(2,1)S(1)} %bitcast.40), custom_call_target="tpu_custom_call" | custom-call | tf_op jit(solution)/shard_map/pallas_call | solution.py:609
  34.6 1.1 %shard_map.141 = (bf16[4,18,16,512]{3,2,1,0:T(8,128)(2,1)S(1)}, bf16[24,16,128]{2,1,0:T(8,128)(2,1)S(1)}) custom-call(bf16[96,16,128]{2,1,0:T(8,128)(2,1)S(1)} %get-tuple-element.45.low_own, bf16[72,16,128]{2,1,0:T(8,128)(2,1)S(1)} %collective-permute-done.3.low_inner, f32[3,256,640]{2,1,0:T(8,128)S(1)} %get-tuple-element.48.acc_first, ...), custom_call_target="tpu_custom_call" | custom-call | tf_op jit(solution)/shard_map/pallas_call | solution.py:609
  35.8 0.2 shard_map.144
  36.0 1.8 %shard_map.142.h1_given = bf16[4,18,16,512]{3,2,1,0:T(8,128)(2,1)S(1)} custom-call(bf16[4,18,16,512]{3,2,1,0:T(8,128)(2,1)S(1)} %get-tuple-element.50.h1_given, bf16[96,16,128]{2,1,0:T(8,128)(2,1)S(1)} %get-tuple-element.45.low_own, bf16[72,16,128]{2,1,0:T(8,128)(2,1)S(1)} %collective-permute-done.2.low_outer, ...), custom_call_target="tpu_custom_call", output_to_operand_aliasing={{}: (0, {})} | custom-call | tf_op jit(solution)/shard_map/pallas_call | solution.py:609
  37.9 3.4 %shard_map.143 = (bf16[48,16,128]{2,1,0:T(8,128)(2,1)S(1)}, bf16[4,18,16,512]{3,2,1,0:T(8,128)(2,1)S(1)}) custom-call(bf16[96,16,128]{2,1,0:T(8,128)(2,1)S(1)} %get-tuple-element.45.low_own, bf16[72,16,128]{2,1,0:T(8,128)(2,1)S(1)} %collective-permute-done.2.low_outer, ...), custom_call_target="tpu_custom_call", output_to_operand_aliasing={{1}: (3, {})} | custom-call | tf_op jit(solution)/shard_map/pallas_call | solution.py:609
  41.3 0.6 collective-permute-start.7
  41.8 3.6 %collective-permute-start.8 = (bf16[48,16,128]{2,1,0:T(8,128)(2,1)S(1)}, bf16[48,16,128]{2,1,0:T(8,128)(2,1)S(1)}, u32[]{:S(2)}, u32[]{:S(2)}) collective-permute-start(bf16[48,16,128]{2,1,0:T(8,128)(2,1)S(1)} %get-tuple-element.52.own), channel_id=1, source_target_pairs={{1,2},{3,4},{5,6},{7,8},{9,10},{11,12},{13,14},{2,1},{4,3},{6,5},{... | collective-permute-start | bytes 589832 | tf_op jit(solution)/shard_map/ppermute | solution.py:641
  45.5 1.9 %collective-permute-start.11 = (bf16[56,16,128]{2,1,0:T(8,128)(2,1)S(1)}, bf16[56,16,128]{2,1,0:T(8,128)(2,1)S(1)}, u32[]{:S(2)}, u32[]{:S(2)}) collective-permute-start(bf16[56,16,128]{2,1,0:T(8,128)(2,1)S(1)} %pad_maximum_fusion.1), channel_id=1, source_target_pairs={{1,2},{3,4},{5,6},{7,8},{9,10},{11,12},{13,14},{2,1},{4,3},{6,5},{... | collective-permute-start | bytes 688136 | tf_op jit(solution)/shard_map/ppermute | solution.py:641
  47.5 1.1 %shard_map.145 = (bf16[6,18,16,512]{3,2,1,0:T(8,128)(2,1)S(1)}, bf16[24,16,128]{2,1,0:T(8,128)(2,1)S(1)}) custom-call(bf16[48,16,128]{2,1,0:T(8,128)(2,1)S(1)} %get-tuple-element.52.own, bf16[56,16,128]{2,1,0:T(8,128)(2,1)S(1)} %collective-permute-done.7.in_near.f_inner, bf16[1728,576]{1,0:T(8,128)(2,1)S(1)} %bitcast.32), custom_call_target="tpu_custom_call" | custom-call | tf_op jit(solution)/shard_map/pallas_call | solution.py:609
  48.6 4.8 %collective-permute-done.8.outer = bf16[48,16,128]{2,1,0:T(8,128)(2,1)S(1)} collective-permute-done((bf16[48,16,128]{2,1,0:T(8,128)(2,1)S(1)}, bf16[48,16,128]{2,1,0:T(8,128)(2,1)S(1)}, u32[]{:S(2)}, u32[]{:S(2)}) %collective-permute-start.8) | collective-permute-done | bytes 196640 | tf_op jit(solution)/shard_map/ppermute | solution.py:641
  53.4 1.1 %shard_map.146 = (bf16[6,18,16,512]{3,2,1,0:T(8,128)(2,1)S(1)}, bf16[24,16,128]{2,1,0:T(8,128)(2,1)S(1)}) custom-call(bf16[6,18,16,512]{3,2,1,0:T(8,128)(2,1)S(1)} %get-tuple-element.55.s1_given, bf16[48,16,128]{2,1,0:T(8,128)(2,1)S(1)} %get-tuple-element.52.own, ...), custom_call_target="tpu_custom_call", output_to_operand_aliasing={{0}: (0, {})} | custom-call | tf_op jit(solution)/shard_map/pallas_call | solution.py:609
  54.6 0.5 collective-permute-start.9
  55.1 1.0 %shard_map.149 = (bf16[768,256]{1,0:T(8,128)(2,1)S(1)}, bf16[1152,256]{1,0:T(8,128)(2,1)S(1)}, bf16[1024,128]{1,0:T(8,128)(2,1)S(1)}) custom-call(bf16[9,64,192]{2,1,0:T(8,128)(2,1)S(1)} %bitcast.49, bf16[9,64,192]{2,1,0:T(8,128)(2,1)S(1)} %bitcast.50, bf16[9,64,192]{2,1,0:T(8,128)(2,1)S(1)} %bitcast.51, bf16[16,64]{1,0:T(8,128)(2,1)S(1)} %bitcast.54), custom_call_target="tpu_custom_call" | custom-call | tf_op jit(solution)/shard_map/pallas_call | solution.py:609
  56.1 1.1 %shard_map.147.s1_given = bf16[6,18,16,512]{3,2,1,0:T(8,128)(2,1)S(1)} custom-call(bf16[6,18,16,512]{3,2,1,0:T(8,128)(2,1)S(1)} %get-tuple-element.56.s1_given, bf16[48,16,128]{2,1,0:T(8,128)(2,1)S(1)} %get-tuple-element.52.own, bf16[48,16,128]{2,1,0:T(8,128)(2,1)S(1)} %collective-permute-done.8.outer, ...), custom_call_target="tpu_custom_call", output_to_operand_aliasing={{}: (0, {})} | custom-call | tf_op jit(solution)/shard_map/pallas_call | solution.py:609
  57.2 2.7 %shard_map.148 = (bf16[6,18,16,512]{3,2,1,0:T(8,128)(2,1)S(1)}, bf16[5,18,16,512]{3,2,1,0:T(8,128)(2,1)S(1)}) custom-call(bf16[6,18,16,512]{3,2,1,0:T(8,128)(2,1)S(1)} %shard_map.147.s1_given, bf16[24,16,128]{2,1,0:T(8,128)(2,1)S(1)} %collective-permute-done.9.in_near, ...), custom_call_target="tpu_custom_call", output_to_operand_aliasing={{0}: (0, {})} | custom-call | tf_op jit(solution)/shard_map/pallas_call | solution.py:609
  59.9 7.0 %shard_map.150 = (bf16[2,4,16,512]{3,2,1,0:T(8,128)(2,1)S(1)}, bf16[6,18,16,512]{3,2,1,0:T(8,128)(2,1)S(1)}, bf16[5,18,16,512]{3,2,1,0:T(8,128)(2,1)S(1)}) custom-call(bf16[6,18,16,512]{3,2,1,0:T(8,128)(2,1)S(1)} %get-tuple-element.59.s1_given, ...), custom_call_target="tpu_custom_call", output_to_operand_aliasing={{1}: (0, {}), {2}: (1, {})} | custom-call | tf_op jit(solution)/shard_map/pallas_call | solution.py:609
  66.9 0.7 %reshape.61 = bf16[2,4,8192]{2,1,0:T(4,128)(2,1)} reshape(bf16[2,4,16,512]{3,2,1,0:T(8,128)(2,1)S(1)} %get-tuple-element.66) | data formatting | bytes 262144 | tf_op jit(solution)/shard_map/reshape | solution.py:750
  (40 shorter events, 0.6 us)
Async XLA Ops:
  2.1 11.3 %collective-permute-start = (bf16[3,16,3072]{2,1,0:T(8,128)(2,1)S(1)}, bf16[3,16,3072]{2,1,0:T(8,128)(2,1)S(1)}, u32[]{:S(2)}, u32[]{:S(2)}) collective-permute-start(bf16[3,16,3072]{2,1,0:T(8,128)(2,1)S(1)} %get-tuple-element.42), channel_id=1, source_target_pairs={{1,2},{3,4},{5,6},{7,8},{9,10},{11,12},{13,14},{2,1},{4,3},{6,5},{... | collective-permute-start | bytes 884744 | tf_op jit(solution)/shard_map/ppermute | solution.py:641
  5.9 7.6 %collective-permute-start.1 = (bf16[3,16,3072]{2,1,0:T(8,128)(2,1)S(1)}, bf16[3,16,3072]{2,1,0:T(8,128)(2,1)S(1)}, u32[]{:S(2)}, u32[]{:S(2)}) collective-permute-start(bf16[3,16,3072]{2,1,0:T(8,128)(2,1)S(1)} %get-tuple-element.43), channel_id=1, source_target_pairs={{0,1},{1,0},{2,3},{3,2},{4,5},{5,4},{6,7},{7,6},{8,9},{9,8},{10,11... | collective-permute-start | bytes 884744 | tf_op jit(solution)/shard_map/ppermute | solution.py:644
  5.9 1.0 %copy-start.3 = (bf16[3,3,64,192]{3,2,1,0:T(8,128)(2,1)S(1)}, bf16[3,3,64,192]{3,2,1,0:T(8,128)(2,1)}, u32[]{:S(2)}) copy-start(bf16[3,3,64,192]{3,2,1,0:T(8,128)(2,1)} %param.18) | copy-start | bytes 663556
  6.9 1.0 %copy-start.4 = (bf16[3,3,64,192]{3,2,1,0:T(8,128)(2,1)S(1)}, bf16[3,3,64,192]{3,2,1,0:T(8,128)(2,1)}, u32[]{:S(2)}) copy-start(bf16[3,3,64,192]{3,2,1,0:T(8,128)(2,1)} %param.19) | copy-start | bytes 663556
  7.9 1.0 %copy-start.5 = (bf16[3,3,64,192]{3,2,1,0:T(8,128)(2,1)S(1)}, bf16[3,3,64,192]{3,2,1,0:T(8,128)(2,1)}, u32[]{:S(2)}) copy-start(bf16[3,3,64,192]{3,2,1,0:T(8,128)(2,1)} %param.20) | copy-start | bytes 663556
  8.8 0.7 %copy-start.9 = (bf16[16,64]{1,0:T(8,128)(2,1)S(1)}, bf16[16,64]{1,0:T(8,128)(2,1)}, u32[]{:S(2)}) copy-start(bf16[16,64]{1,0:T(8,128)(2,1)} %refs_0_.1) | copy-start | bytes 6148
  11.3 7.6 %copy-start.11 = (bf16[2,49152]{1,0:T(2,128)(2,1)S(1)}, bf16[2,49152]{1,0:T(2,128)(2,1)}, u32[]{:S(2)}) copy-start(bf16[2,49152]{1,0:T(2,128)(2,1)} %param.16) | copy-start | bytes 589828
  13.4 18.3 %copy-start.2 = (bf16[3,3,192,576]{3,2,1,0:T(8,128)(2,1)S(1)}, bf16[3,3,192,576]{3,2,1,0:T(8,128)(2,1)}, u32[]{:S(2)}) copy-start(bf16[3,3,192,576]{3,2,1,0:T(8,128)(2,1)} %param.22) | copy-start | bytes 5971972
  18.8 15.8 %copy-start.1 = (bf16[3,3,192,576]{3,2,1,0:T(8,128)(2,1)S(1)}, bf16[3,3,192,576]{3,2,1,0:T(8,128)(2,1)}, u32[]{:S(2)}) copy-start(bf16[3,3,192,576]{3,2,1,0:T(8,128)(2,1)} %param.21) | copy-start | bytes 5971972
  18.8 15.8 %collective-permute-start.3 = (bf16[72,16,128]{2,1,0:T(8,128)(2,1)S(1)}, bf16[72,16,128]{2,1,0:T(8,128)(2,1)S(1)}, u32[]{:S(2)}, u32[]{:S(2)}) collective-permute-start(bf16[72,16,128]{2,1,0:T(8,128)(2,1)S(1)} %get-tuple-element.47), channel_id=1, source_target_pairs={{0,1},{1,0},{2,3},{3,2},{4,5},{5,4},{6,7},{7,6},{8,9},{9,8},{10,11... | collective-permute-start | bytes 884744 | tf_op jit(solution)/shard_map/ppermute | solution.py:644
  18.9 6.3 %collective-permute-start.5 = (bf16[2,16,3072]{2,1,0:T(8,128)(2,1)S(1)}, bf16[2,16,3072]{2,1,0:T(8,128)(2,1)S(1)}, u32[]{:S(2)}, u32[]{:S(2)}) collective-permute-start(bf16[2,16,3072]{2,1,0:T(8,128)(2,1)S(1)} %bitcast.43), channel_id=1, source_target_pairs={{0,1},{1,0},{2,3},{3,2},{4,5},{5,4},{6,7},{7,6},{8,9},{9,8},{10,11... | collective-permute-start | bytes 589832 | tf_op jit(solution)/shard_map/ppermute | solution.py:644
  19.5 12.2 %collective-permute-start.4 = (bf16[2,16,3072]{2,1,0:T(8,128)(2,1)S(1)}, bf16[2,16,3072]{2,1,0:T(8,128)(2,1)S(1)}, u32[]{:S(2)}, u32[]{:S(2)}) collective-permute-start(bf16[2,16,3072]{2,1,0:T(8,128)(2,1)S(1)} %bitcast.44), channel_id=1, source_target_pairs={{1,2},{3,4},{5,6},{7,8},{9,10},{11,12},{13,14},{2,1},{4,3},{6,5},{... | collective-permute-start | bytes 589832 | tf_op jit(solution)/shard_map/ppermute | solution.py:641
  23.1 12.9 %collective-permute-start.2 = (bf16[72,16,128]{2,1,0:T(8,128)(2,1)S(1)}, bf16[72,16,128]{2,1,0:T(8,128)(2,1)S(1)}, u32[]{:S(2)}, u32[]{:S(2)}) collective-permute-start(bf16[72,16,128]{2,1,0:T(8,128)(2,1)S(1)} %get-tuple-element.46), channel_id=1, source_target_pairs={{1,2},{3,4},{5,6},{7,8},{9,10},{11,12},{13,14},{2,1},{4,3},{6,5},{... | collective-permute-start | bytes 884744 | tf_op jit(solution)/shard_map/ppermute | solution.py:641
  35.7 2.1 %collective-permute-start.6 = (bf16[24,16,128]{2,1,0:T(8,128)(2,1)S(1)}, bf16[24,16,128]{2,1,0:T(8,128)(2,1)S(1)}, u32[]{:S(2)}, u32[]{:S(2)}) collective-permute-start(bf16[24,16,128]{2,1,0:T(8,128)(2,1)S(1)} %get-tuple-element.51), channel_id=1, source_target_pairs={{0,1},{1,0},{2,3},{3,2},{4,5},{5,4},{6,7},{7,6},{8,9},{9,8},{10,11... | collective-permute-start | bytes 294920 | tf_op jit(solution)/shard_map/ppermute | solution.py:644
  37.8 9.6 %copy-start = (bf16[3,3,192,576]{3,2,1,0:T(8,128)(2,1)S(1)}, bf16[3,3,192,576]{3,2,1,0:T(8,128)(2,1)}, u32[]{:S(2)}) copy-start(bf16[3,3,192,576]{3,2,1,0:T(8,128)(2,1)} %param.23) | copy-start | bytes 5971972
  41.3 4.2 %collective-permute-start.7 = (bf16[56,16,128]{2,1,0:T(8,128)(2,1)S(1)}, bf16[56,16,128]{2,1,0:T(8,128)(2,1)S(1)}, u32[]{:S(2)}, u32[]{:S(2)}) collective-permute-start(bf16[56,16,128]{2,1,0:T(8,128)(2,1)S(1)} %pad_maximum_fusion), channel_id=1, source_target_pairs={{0,1},{1,0},{2,3},{3,2},{4,5},{5,4},{6,7},{7,6},{8,9},{9,8},{10,11... | collective-permute-start | bytes 688136 | tf_op jit(solution)/shard_map/ppermute | solution.py:644
  41.8 11.6 %collective-permute-start.8 = (bf16[48,16,128]{2,1,0:T(8,128)(2,1)S(1)}, bf16[48,16,128]{2,1,0:T(8,128)(2,1)S(1)}, u32[]{:S(2)}, u32[]{:S(2)}) collective-permute-start(bf16[48,16,128]{2,1,0:T(8,128)(2,1)S(1)} %get-tuple-element.52.own), channel_id=1, source_target_pairs={{1,2},{3,4},{5,6},{7,8},{9,10},{11,12},{13,14},{2,1},{4,3},{6,5},{... | collective-permute-start | bytes 589832 | tf_op jit(solution)/shard_map/ppermute | solution.py:641
  45.5 14.3 %collective-permute-start.11 = (bf16[56,16,128]{2,1,0:T(8,128)(2,1)S(1)}, bf16[56,16,128]{2,1,0:T(8,128)(2,1)S(1)}, u32[]{:S(2)}, u32[]{:S(2)}) collective-permute-start(bf16[56,16,128]{2,1,0:T(8,128)(2,1)S(1)} %pad_maximum_fusion.1), channel_id=1, source_target_pairs={{1,2},{3,4},{5,6},{7,8},{9,10},{11,12},{13,14},{2,1},{4,3},{6,5},{... | collective-permute-start | bytes 688136 | tf_op jit(solution)/shard_map/ppermute | solution.py:641
  53.4 1.7 %copy-start.6 = (bf16[3,3,192,64]{2,3,1,0:T(8,128)(2,1)S(1)}, bf16[3,3,192,64]{2,3,1,0:T(8,128)(2,1)}, u32[]{:S(2)}) copy-start(bf16[3,3,192,64]{2,3,1,0:T(8,128)(2,1)} %param.24) | copy-start | bytes 663556
  53.4 1.7 %copy-start.7 = (bf16[3,3,64,192]{3,2,1,0:T(8,128)(2,1)S(1)}, bf16[3,3,64,192]{3,2,1,0:T(8,128)(2,1)}, u32[]{:S(2)}) copy-start(bf16[3,3,64,192]{3,2,1,0:T(8,128)(2,1)} %param.25) | copy-start | bytes 663556
  53.4 1.7 %copy-start.8 = (bf16[3,3,64,192]{3,2,1,0:T(8,128)(2,1)S(1)}, bf16[3,3,64,192]{3,2,1,0:T(8,128)(2,1)}, u32[]{:S(2)}) copy-start(bf16[3,3,64,192]{3,2,1,0:T(8,128)(2,1)} %param.26) | copy-start | bytes 663556
  53.4 1.7 %copy-start.10 = (bf16[64,16]{0,1:T(8,128)(2,1)S(1)}, bf16[64,16]{0,1:T(8,128)(2,1)}, u32[]{:S(2)}) copy-start(bf16[64,16]{0,1:T(8,128)(2,1)} %param.27) | copy-start | bytes 6148
  54.5 2.7 %collective-permute-start.10 = (bf16[24,16,128]{2,1,0:T(8,128)(2,1)S(1)}, bf16[24,16,128]{2,1,0:T(8,128)(2,1)S(1)}, u32[]{:S(2)}, u32[]{:S(2)}) collective-permute-start(bf16[24,16,128]{2,1,0:T(8,128)(2,1)S(1)} %get-tuple-element.58), channel_id=1, source_target_pairs={{0,1},{1,0},{2,3},{3,2},{4,5},{5,4},{6,7},{7,6},{8,9},{9,8},{10,11... | collective-permute-start | bytes 294920 | tf_op jit(solution)/shard_map/ppermute | solution.py:644
  54.6 2.6 %collective-permute-start.9 = (bf16[24,16,128]{2,1,0:T(8,128)(2,1)S(1)}, bf16[24,16,128]{2,1,0:T(8,128)(2,1)S(1)}, u32[]{:S(2)}, u32[]{:S(2)}) collective-permute-start(bf16[24,16,128]{2,1,0:T(8,128)(2,1)S(1)} %get-tuple-element.57), channel_id=1, source_target_pairs={{0,1},{1,0},{2,3},{3,2},{4,5},{5,4},{6,7},{7,6},{8,9},{9,8},{10,11... | collective-permute-start | bytes 294920 | tf_op jit(solution)/shard_map/ppermute | solution.py:644
